TPU v7x, 128 devices: a whole 4x4x4 slice. The times are simulated.
128 devices in a mesh: scan: 64 (over x, y, z_lo, core), mode: 2 (over z_hi).
Axes of the slice: x: 4, y: 4, z: 4 (z_hi: 2, z_lo: 2; z = z_hi * 2 + z_lo), core: 2. Of those that a mesh axis runs over, the one named last changes fastest.
Arguments:
- object_tiles: float32 [64, 2, 512, 512], P('scan'), may hold values from -5 to 5
- probe_modes: float32 [4, 2, 512, 512], P('mode'), may hold values from -5 to 5
- amplitudes: float32 [64, 3, 512, 512], P('scan'), may hold values from 0.5 to 3
- offsets: int32 [64, 3, 2], P('scan'), may hold values from 1 to 511, as said below
- counts: int32 [64], P('scan'), may hold values from 1 to 3, as said below
Outputs:
- object_grad: float32 [64, 2, 512, 512], P('scan', 'mode')
- probe_grad: float32 [4, 2, 512, 512], P('mode')
- position_grad: float32 [64, 3, 2], P('scan')
Inputs may be any that keep to these rules, and one draw needn't show every extreme that they name: `offsets`: A slot's window lies within its device's 2 x 2 arrangement of tiles. Slots s >= counts[d] of device d are empty.
All inputs are finite; a program needn't handle non-finite values.
Results may differ from a plain program's by a relative error of at most 0.006.
The roundings to bfloat16 on the way count: a program that leaves them out, or rounds other values in their place, can miss the bound.
Values sent between devices are 32-bit elements; how exact they have to be, the bound alone decides.
A program may use at most 192 MiB of HBM per device.

v0:
```python
import math

import jax
import jax.numpy as jnp
from jax import lax
from jax.sharding import PartitionSpec as P

GCOLS = 8


amp_floor = 1.0


def from_behind(value, axis, steps):
    count = lax.axis_size(axis)
    pairs = [(source, (source + steps) % count) for source in range(count)]
    return lax.ppermute(value, axis, pairs)


def dft_tables(length_side, direction_sign):
    index_row = jnp.arange(length_side, dtype=jnp.int32)
    product = index_row[:, None] * index_row[None, :] % length_side
    angles = product.astype(jnp.float32) * (2.0 * math.pi / length_side)
    scale_factor = 1.0 / math.sqrt(length_side)
    real_part = jnp.cos(angles) * scale_factor
    imag_part = direction_sign * jnp.sin(angles) * scale_factor
    matrix_table = jnp.stack(
        [jnp.stack([real_part, -imag_part]), jnp.stack([imag_part, real_part])]
    )
    return matrix_table.astype(jnp.bfloat16)


def transform(field, matrix_table):
    first_section = jnp.einsum(
        "dcpq,bcqk->bdpk", matrix_table, field, preferred_element_type=jnp.float32
    ).astype(jnp.bfloat16)
    return jnp.einsum(
        "bcpq,dcqk->bdpk", first_section, matrix_table, preferred_element_type=jnp.float32
    )


def shards(object_tiles, probe_modes, amplitudes, offsets, counts):
    side = probe_modes.shape[-1]
    tile_side = object_tiles.shape[-1]
    slots = offsets.shape[1]
    modes_here = probe_modes.shape[0]
    own_tile = object_tiles[0]
    east_tile = from_behind(own_tile, "scan", -1)
    south_tile = from_behind(own_tile, "scan", -GCOLS)
    corner_tile = from_behind(own_tile, "scan", -(GCOLS + 1))
    upper_band = jnp.concatenate([own_tile, east_tile], axis=2)
    lower_band = jnp.concatenate([south_tile, corner_tile], axis=2)
    extended = jnp.concatenate([upper_band, lower_band], axis=1)
    slot_offsets = offsets[0]
    windows = jnp.stack(
        [
            lax.dynamic_slice(
                extended,
                (0, slot_offsets[slot_id, 0] - 1, slot_offsets[slot_id, 1] - 1),
                (2, side + 2, side + 2),
            )
            for slot_id in range(slots)
        ]
    )
    patch = windows[:, :, 1:-1, 1:-1]
    grad_y = (windows[:, :, 2:, 1:-1] - windows[:, :, :-2, 1:-1]) * 0.5
    grad_x = (windows[:, :, 1:-1, 2:] - windows[:, :, 1:-1, :-2]) * 0.5
    obj_real = patch[:, 0][:, None]
    obj_imag = patch[:, 1][:, None]
    probe_real = probe_modes[:, 0][None]
    probe_imag = probe_modes[:, 1][None]
    exit_real = obj_real * probe_real - obj_imag * probe_imag
    exit_imag = obj_real * probe_imag + obj_imag * probe_real
    exit_wave = jnp.stack([exit_real, exit_imag], axis=2).astype(jnp.bfloat16)
    forward_table = dft_tables(side, -1.0)
    inverse_table = dft_tables(side, 1.0)
    far_field = transform(exit_wave.reshape(slots * modes_here, 2, side, side), forward_table)
    far_field = far_field.reshape(slots, modes_here, 2, side, side)
    local_intensity = jnp.sum(far_field * far_field, axis=(1, 2))
    intensity = lax.psum(local_intensity, "mode")
    ratio = amplitudes[0] / jnp.maximum(jnp.sqrt(intensity), amp_floor)
    correction = (far_field * (ratio - 1.0)[:, None, None]).astype(jnp.bfloat16)
    back_wave = transform(correction.reshape(slots * modes_here, 2, side, side), inverse_table)
    back_wave = back_wave.reshape(slots, modes_here, 2, side, side)
    live_slots = (jnp.arange(slots, dtype=jnp.int32) < counts[0]).astype(jnp.float32)
    back_wave = back_wave * live_slots[:, None, None, None, None]
    back_real = back_wave[:, :, 0]
    back_imag = back_wave[:, :, 1]
    grad_real = jnp.sum(probe_real * back_real + probe_imag * back_imag, axis=1)
    grad_imag = jnp.sum(probe_real * back_imag - probe_imag * back_real, axis=1)
    probe_real_grad = jnp.sum(obj_real * back_real + obj_imag * back_imag, axis=0)
    probe_imag_grad = jnp.sum(obj_real * back_imag - obj_imag * back_real, axis=0)
    local_patch_grad = jnp.stack([grad_real, grad_imag], axis=1)
    component = lax.axis_index("mode")
    whole_grad = lax.psum(local_patch_grad, "mode")
    position_y = jnp.sum(whole_grad * grad_y, axis=(1, 2, 3))
    position_x = jnp.sum(whole_grad * grad_x, axis=(1, 2, 3))
    positions = jnp.stack([position_y, position_x], axis=1) / side
    mine = lax.dynamic_slice_in_dim(whole_grad, component, 1, axis=1)
    probe_grad = lax.psum(jnp.stack([probe_real_grad, probe_imag_grad], axis=1), "scan")
    gradient_plane = jnp.zeros((2 * tile_side, 2 * tile_side), jnp.float32)
    for slot_id in range(slots):
        start = (slot_offsets[slot_id, 0], slot_offsets[slot_id, 1])
        current = lax.dynamic_slice(gradient_plane, start, (side, side))
        gradient_plane = lax.dynamic_update_slice(gradient_plane, current + mine[slot_id, 0], start)
    received_east = from_behind(gradient_plane[:tile_side, tile_side:], "scan", 1)
    received_south = from_behind(gradient_plane[tile_side:, :tile_side], "scan", GCOLS)
    received_corner = from_behind(gradient_plane[tile_side:, tile_side:], "scan", GCOLS + 1)
    total_grad = (
        gradient_plane[:tile_side, :tile_side] + received_east + received_south + received_corner
    )
    return (total_grad[None, None], probe_grad, positions[None])


def solution(mesh):
    return jax.shard_map(
        shards,
        mesh=mesh,
        in_specs=(
            P("scan", None, None, None),
            P("mode", None, None, None),
            P("scan", None, None, None),
            P("scan", None, None),
            P("scan"),
        ),
        out_specs=(
            P("scan", "mode", None, None),
            P("mode", None, None, None),
            P("scan", None, None),
        ),
        check_vma=False,
    )
```

profile of v0, /device:TPU:20, one launch (start us, length us, event | category | flops | bytes accessed | tf_op | source)
XLA Modules:
  0.0 1201.2 jit_solution(7075233157555547276)
XLA Ops:
  8.5 2.9 collective-permute-start.1
  20.6 4.2 slice_bitcast_fusion.5
  24.8 2.9 copy.23
  27.7 1.9 copy.27
  29.5 4.0 multiply_convert_fusion.2
  33.5 4.0 negate_convert_fusion
  37.6 4.4 multiply_convert_fusion
  42.0 2.2 fusion.34
  44.2 11.0 collective-permute-done
  55.2 73.0 %collective-permute-done.1 = f32[2,512,512]{2,1,0:T(8,128)} collective-permute-done((f32[2,512,512]{2,1,0:T(8,128)}, f32[2,512,512]{2,1,0:T(8,128)}, u32[]{:S(2)}, u32[]{:S(2)}) %collective-permute-start.1) | collective-permute-done | bytes 2097184 | tf_op jit(solution)/shard_map/ppermute | solution.py:17
  128.2 3.2 maximum_maximum_fusion
  131.4 4.6 constant_dynamic-slice_fusion.2
  136.0 3.3 copy.24
  139.3 3.3 copy.25
  142.7 2.2 copy.26
  144.9 3.6 pad_maximum_fusion
  148.5 2.3 slice_bitcast_fusion.3
  150.8 1.8 copy-done
  153.8 3.7 subtract_convert_fusion
  157.5 23.7 %fusion = (f32[6,512,512]{1,2,0:T(8,128)}, f32[2,512,6,512,1]{3,1,4,2,0:T(8,128)}) fusion(bf16[6,1,512,512]{2,3,1,0:T(8,128)(2,1)} %bitcast.171, bf16[6,1,512,512]{2,3,1,0:T(8,128)(2,1)} %bitcast.170, bf16[1,2,512,512]{3,2,1,0:T(8,128)(2,1)} %get-tuple-element.30, bf16[1,2,512,512]{3,2,1,0:T(8,128)(2,1)} %get-tuple-element.31), kind=kOutput, calls=%fused_computation.3 | convolution fusion | flops 12913737728 | bytes 27262976 | tf_op jit(solution)/shard_map/bcpq,dcqk->bdpk/dot_general | solution.py:37
  181.3 5.5 reduce_sum.72
  186.8 3.7 copy.30
  191.2 111.4 %all-reduce.4.cloned.1.call-done = f32[3,512,512]{1,2,0:T(8,128)} async-done(((f32[3,512,512]{1,2,0:T(8,128)}), f32[3,512,512]{1,2,0:T(8,128)}) %all-reduce.4.cloned.1.call-update) | async-done | bytes 3145744 | tf_op jit(solution)/shard_map/psum | solution.py:80
  302.7 4.0 fusion.25
  306.6 3.4 mul.373
  310.1 23.6 %fusion.9 = f32[2,512,6,512,1]{3,1,4,2,0:T(8,128)} fusion(bf16[1,2,512,512]{3,2,1,0:T(8,128)(2,1)} %get-tuple-element.32, bf16[1,2,512,512]{3,2,1,0:T(8,128)(2,1)} %get-tuple-element.29, f32[2,512,6,512,1]{3,1,4,2,0:T(8,128)} %get-tuple-element.40, f32[6,512,512]{1,2,0:T(8,128)} %bitcast.169), kind=kOutput, calls=%fused_computation.13 | convolution fusion | flops 12902727680 | bytes 33554432 | tf_op jit(solution)/shard_map/bcpq,dcqk->bdpk/dot_general | solution.py:37
  333.7 11.0 broadcast_multiply_fusion
  344.7 12.0 %add_reduce_fusion = (f32[2,512,512]{1,2,0:T(8,128)S(1)}, f32[2,512,512]{1,2,0:T(8,128)}, f32[3,512,512]{1,2,0:T(8,128)}, f32[3,512,512]{1,2,0:T(8,128)}) fusion(f32[3,2,2,512,512]{3,4,1,0,2:T(8,128)} %broadcast_multiply_fusion, f32[3,512,512]{1,2,0:T(8,128)S(1)} %copy-done.2, f32[3,512,512]{1,2,0:T(8,128)S(1)} %get-tuple-element.22, ...), kind=kLoop, calls=%fused_computation.31 | loop fusion | flops 22544384 | bytes 33554432 | tf_op jit(solution)/shard_map/reduce_sum | solution.py:91
  356.7 4.1 pad_maximum_fusion.2
  360.9 1.8 copy-done.5
  362.7 5.6 pad_maximum_fusion.1
  379.7 494.5 %all-reduce.8.cloned.1.call-done = f32[2,2,512,512]{2,3,0,1:T(8,128)} async-done(((f32[2,2,512,512]{2,3,0,1:T(8,128)}), f32[2,2,512,512]{2,3,0,1:T(8,128)}) %all-reduce.8.cloned.1.call-update) | async-done | bytes 4194320 | tf_op jit(solution)/shard_map/psum | solution.py:100
  874.2 5.2 copy.37
  879.4 203.7 %all-reduce.6.cloned.1.call-done = f32[3,2,512,512]{2,3,0,1:T(8,128)} async-done(((f32[3,2,512,512]{2,3,0,1:T(8,128)}), f32[3,2,512,512]{2,3,0,1:T(8,128)}) %all-reduce.6.cloned.1.call-update) | async-done | bytes 6291472 | tf_op jit(solution)/shard_map/psum | solution.py:95
  1083.1 2.2 dynamic-slice_bitcast_fusion
  1086.3 2.6 broadcast_in_dim.4
  1088.9 7.7 dynamic_update_slice.9
  1096.6 2.6 fusion.43
  1099.2 7.8 dynamic_update_slice.10
  1107.1 2.0 fusion.42
  1109.1 7.5 dynamic_update_slice.11
  1116.6 2.2 fusion.52
  1120.4 3.1 collective-permute-start.5
  1123.5 14.8 %fusion.18 = (f32[3]{0:T(128)S(1)}, f32[3]{0:T(128)S(1)}) fusion(f32[3,2,512,512]{2,3,0,1:T(8,128)} %all-reduce.6.cloned.1.call-done, f32[3,2,514,514]{2,3,0,1:T(8,128)} %copy-done), kind=kLoop, calls=%fused_computation.22 | loop fusion | flops 12582906 | bytes 31457304 | tf_op jit(solution)/shard_map/reduce_sum | solution.py:96
  1138.9 4.4 collective-permute-done.3
  1143.2 3.2 collective-permute-done.4
  1146.5 45.0 %collective-permute-done.5 = f32[512,512]{0,1:T(8,128)S(1)} collective-permute-done((f32[512,512]{0,1:T(8,128)S(1)}, f32[512,512]{0,1:T(8,128)S(1)}, u32[]{:S(2)}, u32[]{:S(2)}) %collective-permute-start.5) | collective-permute-done | bytes 1048608 | tf_op jit(solution)/shard_map/ppermute | solution.py:17
  1191.4 1.7 fusion.41
  (28 shorter events, 8.9 us)
Async XLA Ops:
  7.2 295.5 %all-reduce.4.cloned.1.call-start = ((), (), s32[]{:S(2)}) async-start(), calls=%async_computation | async-start | bytes 6291456 | tf_op jit(solution)/shard_map/psum | solution.py:80
  7.2 48.0 %collective-permute-start = (f32[2,512,512]{2,1,0:T(8,128)}, f32[2,512,512]{2,1,0:T(8,128)}, u32[]{:S(2)}, u32[]{:S(2)}) collective-permute-start(f32[2,512,512]{2,1,0:T(8,128)} %bitcast.172), channel_id=1, source_target_pairs={{0,126},{2,0},{4,2},{6,4},{8,6},{10,8},{12,10},{14,12},{16,14},{18... | collective-permute-start | bytes 6291464 | tf_op jit(solution)/shard_map/ppermute | solution.py:17
  8.5 119.7 %collective-permute-start.1 = (f32[2,512,512]{2,1,0:T(8,128)}, f32[2,512,512]{2,1,0:T(8,128)}, u32[]{:S(2)}, u32[]{:S(2)}) collective-permute-start(f32[2,512,512]{2,1,0:T(8,128)} %bitcast.173), channel_id=1, source_target_pairs={{0,112},{2,114},{4,116},{6,118},{8,120},{10,122},{12,124},{14,126}... | collective-permute-start | bytes 6291464 | tf_op jit(solution)/shard_map/ppermute | solution.py:17
  11.4 116.8 %collective-permute-start.2 = (f32[2,512,512]{2,1,0:T(8,128)}, f32[2,512,512]{2,1,0:T(8,128)}, u32[]{:S(2)}, u32[]{:S(2)}) collective-permute-start(f32[2,512,512]{2,1,0:T(8,128)} %bitcast.174), channel_id=1, source_target_pairs={{0,110},{2,112},{4,114},{6,116},{8,118},{10,120},{12,122},{14,124}... | collective-permute-start | bytes 6291464 | tf_op jit(solution)/shard_map/ppermute | solution.py:17
  37.6 90.6 %copy-start.6 = (f32[1,2,512,512]{3,2,1,0:T(8,128)S(1)}, f32[1,2,512,512]{3,2,1,0:T(8,128)}, u32[]{:S(2)}) copy-start(f32[1,2,512,512]{3,2,1,0:T(8,128)} %param.5) | copy-start | bytes 6291460
  148.5 4.1 copy-start
  148.5 4.0 copy-start.3
  148.5 5.3 copy-start.4
  152.5 5.0 copy-start.1
  186.8 687.4 %all-reduce.8.cloned.1.call-start = ((), (), s32[]{:S(2)}) async-start(), calls=%async_computation.2 | async-start | bytes 8388608 | tf_op jit(solution)/shard_map/psum | solution.py:100
  333.7 11.0 copy-start.2
  360.8 1.9 copy-start.5
  360.8 722.3 %all-reduce.6.cloned.1.call-start = ((), (), s32[]{:S(2)}) async-start(), calls=%async_computation.1 | async-start | bytes 12582912 | tf_op jit(solution)/shard_map/psum | solution.py:95
  1118.7 24.5 %collective-permute-start.3 = (f32[512,512]{0,1:T(8,128)S(1)}, f32[512,512]{0,1:T(8,128)S(1)}, u32[]{:S(2)}, u32[]{:S(2)}) collective-permute-start(f32[512,512]{0,1:T(8,128)S(1)} %get-tuple-element.24), channel_id=1, source_target_pairs={{0,2},{2,4},{4,6},{6,8},{8,10},{10,12},{12,14},{14,16},{16,18},{18... | collective-permute-start | bytes 3145736 | tf_op jit(solution)/shard_map/ppermute | solution.py:17
  1119.0 27.4 %collective-permute-start.4 = (f32[512,512]{0,1:T(8,128)S(1)}, f32[512,512]{0,1:T(8,128)S(1)}, u32[]{:S(2)}, u32[]{:S(2)}) collective-permute-start(f32[512,512]{0,1:T(8,128)S(1)} %get-tuple-element.26), channel_id=1, source_target_pairs={{0,16},{2,18},{4,20},{6,22},{8,24},{10,26},{12,28},{14,30},{16,32}... | collective-permute-start | bytes 3145736 | tf_op jit(solution)/shard_map/ppermute | solution.py:17
  1120.4 71.1 %collective-permute-start.5 = (f32[512,512]{0,1:T(8,128)S(1)}, f32[512,512]{0,1:T(8,128)S(1)}, u32[]{:S(2)}, u32[]{:S(2)}) collective-permute-start(f32[512,512]{0,1:T(8,128)S(1)} %get-tuple-element.25), channel_id=1, source_target_pairs={{0,18},{2,20},{4,22},{6,24},{8,26},{10,28},{12,30},{14,32},{16,34}... | collective-permute-start | bytes 3145736 | tf_op jit(solution)/shard_map/ppermute | solution.py:17
Sparse Core Ops, SparseCore 0:
  186.9 115.7 all-reduce.3
  360.9 513.1 all-reduce.7
  876.8 206.2 all-reduce.5
where the time goes:
time: 1210 us; the launch traced here: 1200 us
  waiting for transfers between devices  946 us (78%)
  other arithmetic  89 us (7%)
  local copies, waits for them, and re-layouts  75.8 us (6%)
  matrix products  47.3 us (4%)
  between operations  33.7 us (3%)
    psum x1, waiting for transfers between devices, shards(): lax.psum(jnp.stack([probe_real_grad, probe_imag_grad], axis=1), 'scan')  494 us
    psum x1, waiting for transfers between devices, shards(): whole_grad = lax.psum(local_patch_grad, 'mode')  204 us
    ppermute x6, waiting for transfers between devices, from_behind(): return lax.ppermute(value, axis, pairs)  137 us
    psum x1, waiting for transfers between devices, shards(): intensity = lax.psum(local_intensity, 'mode')  111 us
    dot_general x2, matrix products, transform(): jnp.einsum('bcpq,dcqk->bdpk', first_section, matrix_table, preferred_elem...  47.3 us
  transfers between devices with their start and end apart: 9, of which 8 were waited for; matrix products, arithmetic and copies ran while one was open for 5% of the time, Pallas kernels for 0%

commit v1 on v0

--- a/solution.py
+++ b/solution.py
@@ -6,6 +6,10 @@
 from jax.sharding import PartitionSpec as P
 
 GCOLS = 8
+CORE = (1, 2)
+ZLO = (2, 2)
+YAX = (4, 4)
+XAX = (16, 4)
 
 
 amp_floor = 1.0
@@ -15,6 +19,85 @@
     count = lax.axis_size(axis)
     pairs = [(source, (source + steps) % count) for source in range(count)]
     return lax.ppermute(value, axis, pairs)
+
+
+def sub_shift(value, sub, shift):
+    stride, size = sub
+    count = lax.axis_size("scan")
+    pairs = []
+    for source in range(count):
+        coord = (source // stride) % size
+        pairs.append((source, source + (((coord + shift) % size) - coord) * stride))
+    return lax.ppermute(value, "scan", pairs)
+
+
+def sub_coord(sub):
+    stride, size = sub
+    return (lax.axis_index("scan") // stride) % size
+
+
+def pair_reduce_scatter(data, sub):
+    coord = sub_coord(sub)
+    half = data.shape[0] // 2
+    mine = lax.dynamic_slice_in_dim(data, coord * half, half, axis=0)
+    other = lax.dynamic_slice_in_dim(data, (1 - coord) * half, half, axis=0)
+    return mine + sub_shift(other, sub, 1)
+
+
+def pair_all_gather(data, sub):
+    coord = sub_coord(sub)
+    got = sub_shift(data, sub, 1)
+    first = jnp.where(coord == 0, data, got)
+    second = jnp.where(coord == 0, got, data)
+    return jnp.concatenate([first, second], axis=0)
+
+
+def ring_reduce_scatter(data, sub):
+    size = sub[1]
+    coord = sub_coord(sub)
+    rows = data.shape[0] // (2 * size)
+    fwd = data[: rows * size].reshape(size, rows, -1)
+    bwd = data[rows * size :].reshape(size, rows, -1)
+    part_f = fwd[(coord - 1) % size]
+    part_b = bwd[(coord + 1) % size]
+    for step in range(size - 1):
+        got_f = sub_shift(part_f, sub, 1)
+        got_b = sub_shift(part_b, sub, -1)
+        part_f = got_f + fwd[(coord - step - 2) % size]
+        part_b = got_b + bwd[(coord + step + 2) % size]
+    return jnp.concatenate([part_f, part_b], axis=0)
+
+
+def ring_all_gather(data, sub):
+    size = sub[1]
+    coord = sub_coord(sub)
+    rows = data.shape[0] // 2
+    piece_f = data[:rows]
+    piece_b = data[rows:]
+    out_f = jnp.zeros((size, rows, data.shape[1]), data.dtype)
+    out_b = jnp.zeros((size, rows, data.shape[1]), data.dtype)
+    out_f = lax.dynamic_update_index_in_dim(out_f, piece_f, coord, 0)
+    out_b = lax.dynamic_update_index_in_dim(out_b, piece_b, coord, 0)
+    for step in range(size - 1):
+        piece_f = sub_shift(piece_f, sub, 1)
+        piece_b = sub_shift(piece_b, sub, -1)
+        out_f = lax.dynamic_update_index_in_dim(out_f, piece_f, (coord - step - 1) % size, 0)
+        out_b = lax.dynamic_update_index_in_dim(out_b, piece_b, (coord + step + 1) % size, 0)
+    return jnp.concatenate([out_f.reshape(size * rows, -1), out_b.reshape(size * rows, -1)], axis=0)
+
+
+def scan_all_reduce(value):
+    shape = value.shape
+    data = value.reshape(-1, shape[-1])
+    data = pair_reduce_scatter(data, CORE)
+    data = ring_reduce_scatter(data, XAX)
+    data = ring_reduce_scatter(data, YAX)
+    data = pair_reduce_scatter(data, ZLO)
+    data = pair_all_gather(data, ZLO)
+    data = ring_all_gather(data, YAX)
+    data = ring_all_gather(data, XAX)
+    data = pair_all_gather(data, CORE)
+    return data.reshape(shape)
 
 
 def dft_tables(length_side, direction_sign):
@@ -43,7 +126,10 @@
     side = probe_modes.shape[-1]
     tile_side = object_tiles.shape[-1]
     slots = offsets.shape[1]
-    modes_here = probe_modes.shape[0]
+    own_modes = probe_modes.shape[0]
+    partner_modes = lax.ppermute(probe_modes, "mode", [(0, 1), (1, 0)])
+    all_modes = jnp.concatenate([probe_modes, partner_modes], axis=0)
+    modes_here = all_modes.shape[0]
     own_tile = object_tiles[0]
     east_tile = from_behind(own_tile, "scan", -1)
     south_tile = from_behind(own_tile, "scan", -GCOLS)
@@ -67,8 +153,8 @@
     grad_x = (windows[:, :, 1:-1, 2:] - windows[:, :, 1:-1, :-2]) * 0.5
     obj_real = patch[:, 0][:, None]
     obj_imag = patch[:, 1][:, None]
-    probe_real = probe_modes[:, 0][None]
-    probe_imag = probe_modes[:, 1][None]
+    probe_real = all_modes[:, 0][None]
+    probe_imag = all_modes[:, 1][None]
     exit_real = obj_real * probe_real - obj_imag * probe_imag
     exit_imag = obj_real * probe_imag + obj_imag * probe_real
     exit_wave = jnp.stack([exit_real, exit_imag], axis=2).astype(jnp.bfloat16)
@@ -76,28 +162,33 @@
     inverse_table = dft_tables(side, 1.0)
     far_field = transform(exit_wave.reshape(slots * modes_here, 2, side, side), forward_table)
     far_field = far_field.reshape(slots, modes_here, 2, side, side)
-    local_intensity = jnp.sum(far_field * far_field, axis=(1, 2))
-    intensity = lax.psum(local_intensity, "mode")
+    intensity = jnp.sum(far_field * far_field, axis=(1, 2))
     ratio = amplitudes[0] / jnp.maximum(jnp.sqrt(intensity), amp_floor)
     correction = (far_field * (ratio - 1.0)[:, None, None]).astype(jnp.bfloat16)
-    back_wave = transform(correction.reshape(slots * modes_here, 2, side, side), inverse_table)
-    back_wave = back_wave.reshape(slots, modes_here, 2, side, side)
     live_slots = (jnp.arange(slots, dtype=jnp.int32) < counts[0]).astype(jnp.float32)
-    back_wave = back_wave * live_slots[:, None, None, None, None]
+    back_own = transform(
+        correction[:, :own_modes].reshape(slots * own_modes, 2, side, side), inverse_table
+    ).reshape(slots, own_modes, 2, side, side)
+    back_own = back_own * live_slots[:, None, None, None, None]
+    probe_real_grad = jnp.sum(obj_real * back_own[:, :, 0] + obj_imag * back_own[:, :, 1], axis=0)
+    probe_imag_grad = jnp.sum(obj_real * back_own[:, :, 1] - obj_imag * back_own[:, :, 0], axis=0)
+    probe_grad = scan_all_reduce(jnp.stack([probe_real_grad, probe_imag_grad], axis=1))
+    back_other = transform(
+        correction[:, own_modes:].reshape(slots * (modes_here - own_modes), 2, side, side),
+        inverse_table,
+    ).reshape(slots, modes_here - own_modes, 2, side, side)
+    back_other = back_other * live_slots[:, None, None, None, None]
+    back_wave = jnp.concatenate([back_own, back_other], axis=1)
     back_real = back_wave[:, :, 0]
     back_imag = back_wave[:, :, 1]
     grad_real = jnp.sum(probe_real * back_real + probe_imag * back_imag, axis=1)
     grad_imag = jnp.sum(probe_real * back_imag - probe_imag * back_real, axis=1)
-    probe_real_grad = jnp.sum(obj_real * back_real + obj_imag * back_imag, axis=0)
-    probe_imag_grad = jnp.sum(obj_real * back_imag - obj_imag * back_real, axis=0)
-    local_patch_grad = jnp.stack([grad_real, grad_imag], axis=1)
+    whole_grad = jnp.stack([grad_real, grad_imag], axis=1)
     component = lax.axis_index("mode")
-    whole_grad = lax.psum(local_patch_grad, "mode")
     position_y = jnp.sum(whole_grad * grad_y, axis=(1, 2, 3))
     position_x = jnp.sum(whole_grad * grad_x, axis=(1, 2, 3))
     positions = jnp.stack([position_y, position_x], axis=1) / side
     mine = lax.dynamic_slice_in_dim(whole_grad, component, 1, axis=1)
-    probe_grad = lax.psum(jnp.stack([probe_real_grad, probe_imag_grad], axis=1), "scan")
     gradient_plane = jnp.zeros((2 * tile_side, 2 * tile_side), jnp.float32)
     for slot_id in range(slots):
         start = (slot_offsets[slot_id, 0], slot_offsets[slot_id, 1])

time: 1210 us -> 597 us (0.49)
  the two profiles are of different devices: /device:TPU:20 before, /device:TPU:22 now
where the time goes in v1:
time: 597 us; the launch traced here: 585 us
  waiting for transfers between devices  180 us (30%)
  other arithmetic  124 us (21%)
  local copies, waits for them, and re-layouts  100 us (17%)
  starting transfers between devices  80.1 us (13%)
  matrix products  79.9 us (13%)
  between operations  21.1 us (4%)
    ppermute x6, waiting for transfers between devices, from_behind(): return lax.ppermute(value, axis, pairs)  137 us
    dot_general x3, matrix products, transform(): jnp.einsum('bcpq,dcqk->bdpk', first_section, matrix_table, preferred_elem...  79.9 us
    ppermute x28, starting transfers between devices, sub_shift(): return lax.ppermute(value, 'scan', pairs)  65.9 us
    ppermute x28, waiting for transfers between devices, sub_shift(): return lax.ppermute(value, 'scan', pairs)  42.2 us
    dynamic_update_slice x3, local copies, waits for them, and re-layouts, shards(): lax.dynamic_update_slice(gradient_plane, current + mine[slot_id, 0], start)  23.7 us
    another operation x4, other arithmetic  23.4 us
    reduce_sum x1, other arithmetic, shards(): grad_imag = jnp.sum(probe_real * back_imag - probe_imag * back_real, axis=1)  17.1 us
    mul x1, other arithmetic, shards(): back_own = back_own * live_slots[:, None, None, None, None]  14.7 us
  transfers between devices with their start and end apart: 35, of which 26 were waited for; matrix products, arithmetic and copies ran while one was open for 21% of the time, Pallas kernels for 0%

profile of v1, /device:TPU:22, one launch (start us, length us, event | category | flops | bytes accessed | tf_op | source)
XLA Modules:
  0.0 585.5 jit_solution(3048560016616830968)
XLA Ops:
  0.6 4.0 collective-permute-start
  16.8 3.5 copy.49
  21.6 4.0 multiply_convert_fusion.3
  25.6 4.0 negate_convert_fusion
  29.7 4.4 multiply_convert_fusion.1
  34.1 4.6 constant_dynamic-update-slice_fusion.1
  40.8 8.8 %collective-permute-done.1 = f32[2,512,512]{2,1,0:T(8,128)S(1)} collective-permute-done((f32[2,512,512]{2,1,0:T(8,128)}, f32[2,512,512]{2,1,0:T(8,128)S(1)}, u32[]{:S(2)}, u32[]{:S(2)}) %collective-permute-start.1) | collective-permute-done | bytes 2097184 | tf_op jit(solution)/shard_map/ppermute | solution.py:21
  49.6 72.1 %collective-permute-done.2 = f32[2,512,512]{2,1,0:T(8,128)} collective-permute-done((f32[2,512,512]{2,1,0:T(8,128)}, f32[2,512,512]{2,1,0:T(8,128)}, u32[]{:S(2)}, u32[]{:S(2)}) %collective-permute-start.2) | collective-permute-done | bytes 2097184 | tf_op jit(solution)/shard_map/ppermute | solution.py:21
  124.5 4.6 constant_dynamic-slice_fusion.3
  129.0 3.3 copy.43
  132.4 3.4 copy.44
  137.9 3.6 pad_maximum_fusion.1
  141.5 4.1 slice_bitcast_fusion.5
  145.6 4.6 constant_dynamic-update-slice_fusion
  150.3 7.8 %slice_bitcast_fusion.3 = (f32[4,512,512]{2,1,0:T(8,128)}, f32[4,512,512]{2,1,0:T(8,128)}) fusion(f32[4,2,512,512]{3,2,1,0:T(8,128)} %constant_dynamic-update-slice_fusion), kind=kLoop, calls=%fused_computation.48 | loop fusion | bytes 16777216 | tf_op jit(solution)/shard_map/mul | solution.py:184
  158.0 5.4 copy.42
  163.5 5.2 copy.46
  168.7 11.0 %subtract_convert_fusion = (bf16[3,4,512,512]{2,3,1,0:T(8,128)(2,1)}, bf16[3,4,512,512]{2,3,1,0:T(8,128)(2,1)}) fusion(f32[4,512,512]{1,2,0:T(8,128)} %copy.46, f32[3,512,512]{1,2,0:T(8,128)} %get-tuple-element.32, f32[3,512,512]{1,2,0:T(8,128)S(1)} %get-tuple-element.31, f32[4,512,512]{1,2,0:T(8,128)} %copy.42), kind=kLoop, calls=%fused_computation.21 | loop fusion | flops 25165824 | bytes 27262976 | tf_op jit(solution)/shard_map/convert.3
  179.7 39.6 %fusion = (f32[12,512,512]{1,2,0:T(8,128)}, f32[2,512,12,512,1]{3,1,4,2,0:T(8,128)}) fusion(bf16[12,1,512,512]{2,3,1,0:T(8,128)(2,1)} %bitcast.289, bf16[12,1,512,512]{2,3,1,0:T(8,128)(2,1)} %bitcast.288, bf16[1,2,512,512]{3,2,1,0:T(8,128)(2,1)} %get-tuple-element.41, bf16[1,2,512,512]{3,2,1,0:T(8,128)(2,1)} %get-tuple-element.42), kind=kOutput, calls=%fused_computation.3 | convolution fusion | flops 25819086848 | bytes 52428800 | tf_op jit(solution)/shard_map/bcpq,dcqk->bdpk/dot_general | solution.py:120
  219.2 8.2 %reduce_sum.72 = f32[3,512,512]{1,2,0:T(8,128)} reduce(f32[3,4,512,512]{2,3,1,0:T(8,128)} %bitcast.272, f32[]{:T(128)} %constant.289.clone.1), dimensions={1}, to_apply=%region_1.2 | reduce | flops 2359296 | bytes 15728644 | tf_op jit(solution)/shard_map/reduce_sum | solution.py:165
  227.4 4.0 fusion.27
  231.4 10.8 %multiply_convert_fusion = bf16[3,4,2,512,512]{3,4,1,0,2:T(8,128)(2,1)S(1)} fusion(f32[3,4,2,512,512]{3,4,1,0,2:T(8,128)} %bitcast.269, f32[3,512,512]{1,2,0:T(8,128)S(1)} %fusion.27), kind=kLoop, calls=%fused_computation.5 | loop fusion | flops 12582912 | bytes 40894464 | tf_op jit(solution)/shard_map/convert_element_type | solution.py:167
  243.1 3.5 copy.53
  246.5 3.5 copy.50
  250.0 20.2 %fusion.16 = f32[2,512,6,512,1]{3,1,4,2,0:T(8,128)} fusion(bf16[6,2,512,512,1]{2,3,1,4,0:T(8,128)(2,1)} %bitcast.287, bf16[1,2,512,512]{3,2,1,0:T(8,128)(2,1)} %get-tuple-element.43, bf16[1,2,512,512]{3,2,1,0:T(8,128)(2,1)} %get-tuple-element.40), kind=kOutput, calls=%fused_computation.31 | convolution fusion | flops 12896436224 | bytes 20971520 | tf_op jit(solution)/shard_map/bcpq,dcqk->bdpk/dot_general | solution.py:120
  270.1 20.2 %fusion.11 = f32[2,512,6,512,1]{3,1,4,2,0:T(8,128)} fusion(bf16[6,2,512,512,1]{2,3,1,4,0:T(8,128)(2,1)} %bitcast.286, bf16[1,2,512,512]{3,2,1,0:T(8,128)(2,1)} %get-tuple-element.43, bf16[1,2,512,512]{3,2,1,0:T(8,128)(2,1)} %get-tuple-element.40), kind=kOutput, calls=%fused_computation.28 | convolution fusion | flops 12896436224 | bytes 20971520 | tf_op jit(solution)/shard_map/bcpq,dcqk->bdpk/dot_general | solution.py:120
  290.4 14.7 %broadcast_multiply_fusion.1 = (f32[3,2,2,512,512]{3,4,1,0,2:T(8,128)S(1)}, f32[3,2,2,512,512]{3,4,1,0,2:T(8,128)}) fusion(f32[3,2,2,512,512]{3,4,1,0,2:T(8,128)} %bitcast.274, f32[3]{0:T(128)S(1)} %copy-done.14, f32[3,2,2,512,512]{3,4,1,0,2:T(8,128)} %bitcast.273), kind=kLoop, calls=%fused_computation.46 | loop fusion | flops 6291456 | bytes 50331660 | tf_op jit(solution)/shard_map/mul | solution.py:172
  312.1 5.3 copy.58
  320.4 18.9 %collective-permute-start.7 = (f32[1024,512]{1,0:T(8,128)}, f32[1024,512]{1,0:T(8,128)S(1)}, u32[]{:S(2)}, u32[]{:S(2)}) collective-permute-start(f32[1024,512]{1,0:T(8,128)} %constant_dynamic-slice_fusion), channel_id=1, source_target_pairs={{0,2},{2,0},{4,6},{6,4},{8,10},{10,8},{12,14},{14,12},{16,18},{18,... | collective-permute-start | bytes 6291464 | tf_op jit(solution)/shard_map/ppermute | solution.py:31
  339.3 4.0 collective-permute-done.7
  349.0 6.5 %collective-permute-done.14 = f32[128,512]{1,0:T(8,128)S(1)} collective-permute-done((f32[128,512]{1,0:T(8,128)S(1)}, f32[128,512]{1,0:T(8,128)S(1)}, u32[]{:S(2)}, u32[]{:S(2)}) %collective-permute-start.14) | collective-permute-done | bytes 262176 | tf_op jit(solution)/shard_map/ppermute | solution.py:31
  370.5 17.1 %subtract_reduce_fusion = (f32[3,512,512]{1,2,0:T(8,128)S(1)}, f32[3,512,512]{1,2,0:T(8,128)S(1)}) fusion(f32[4,512,512]{1,2,0:T(8,128)} %copy.46, f32[4,512,512]{1,2,0:T(8,128)} %copy.42, f32[3,2,2,512,512]{3,4,1,0,2:T(8,128)} %get-tuple-element.51, f32[3,2,2,512,512]{3,4,1,0,2:T(8,128)} %copy-done.1), kind=kLoop, calls=%fused_computation.18 | loop fusion | flops 33030144 | bytes 39845888 | tf_op jit(solution)/shard_map/reduce_sum | solution.py:185
  396.8 3.8 collective-permute-start.18
  401.0 3.4 collective-permute-start.12
  406.8 3.6 collective-permute-start.13
  422.0 7.9 %dynamic_update_slice.59 = f32[1024,1024]{0,1:T(8,128)} dynamic-update-slice(f32[1024,1024]{0,1:T(8,128)} %broadcast_in_dim.64, f32[512,512]{0,1:T(8,128)} %slice_bitcast_fusion.8, s32[]{:T(128)S(6)} %select_n.332, s32[]{:T(128)S(6)} %select_n.333) | dynamic-update-slice | bytes 2097156 | tf_op jit(solution)/shard_map/dynamic_update_slice | solution.py:196
  439.4 3.5 collective-permute-start.24
  444.9 3.9 collective-permute-start.25
  449.3 3.6 collective-permute-done.25
  452.9 3.9 collective-permute-start.26
  460.7 3.7 collective-permute-start.27
  468.3 5.3 collective-permute-done.33
  479.2 7.9 %dynamic_update_slice.60 = f32[1024,1024]{0,1:T(8,128)} dynamic-update-slice(f32[1024,1024]{0,1:T(8,128)} %dynamic_update_slice.59, f32[512,512]{0,1:T(8,128)} %fusion.48, s32[]{:T(128)S(6)} %select_n.334, s32[]{:T(128)S(6)} %select_n.335) | dynamic-update-slice | bytes 2097156 | tf_op jit(solution)/shard_map/dynamic_update_slice | solution.py:196
  490.0 8.0 %dynamic_update_slice.61 = f32[1024,1024]{0,1:T(8,128)} dynamic-update-slice(f32[1024,1024]{0,1:T(8,128)} %dynamic_update_slice.60, f32[512,512]{0,1:T(8,128)} %fusion.47, s32[]{:T(128)S(6)} %select_n.336, s32[]{:T(128)S(6)} %select_n.337) | dynamic-update-slice | bytes 2097156 | tf_op jit(solution)/shard_map/dynamic_update_slice | solution.py:196
  500.8 4.4 collective-permute-start.5
  507.3 13.3 %fusion.25 = (f32[3]{0:T(128)S(1)}, f32[3]{0:T(128)S(1)}) fusion(f32[3,2,514,514]{2,3,0,1:T(8,128)} %copy-done, f32[3,1,512,512]{2,3,0,1:T(8,128)S(1)} %bitcast.266, f32[3,1,512,512]{2,3,0,1:T(8,128)S(1)} %bitcast.268), kind=kLoop, calls=%fused_computation.40 | loop fusion | flops 14155770 | bytes 31457304 | tf_op jit(solution)/shard_map/reduce_sum | solution.py:188
  521.2 4.0 collective-permute-done.4
  528.2 49.3 %collective-permute-done.6 = f32[512,512]{0,1:T(8,128)S(1)} collective-permute-done((f32[512,512]{0,1:T(8,128)S(1)}, f32[512,512]{0,1:T(8,128)S(1)}, u32[]{:S(2)}, u32[]{:S(2)}) %collective-permute-start.6) | collective-permute-done | bytes 1048608 | tf_op jit(solution)/shard_map/ppermute | solution.py:21
  (143 shorter events, 100.3 us)
Async XLA Ops:
  0.6 145.0 %collective-permute-start = (f32[2,2,512,512]{3,2,1,0:T(8,128)}, f32[2,2,512,512]{3,2,1,0:T(8,128)}, u32[]{:S(2)}, u32[]{:S(2)}) collective-permute-start(f32[2,2,512,512]{3,2,1,0:T(8,128)} %param.6), channel_id=1, source_target_pairs={{0,1},{1,0},{2,3},{3,2},{4,5},{5,4},{6,7},{7,6},{8,9},{9,8},{10,11... | collective-permute-start | bytes 12582920 | tf_op jit(solution)/shard_map/ppermute | solution.py:130
  4.6 45.0 %collective-permute-start.1 = (f32[2,512,512]{2,1,0:T(8,128)}, f32[2,512,512]{2,1,0:T(8,128)S(1)}, u32[]{:S(2)}, u32[]{:S(2)}) collective-permute-start(f32[2,512,512]{2,1,0:T(8,128)} %bitcast.299), channel_id=1, source_target_pairs={{0,126},{2,0},{4,2},{6,4},{8,6},{10,8},{12,10},{14,12},{16,14},{18... | collective-permute-start | bytes 6291464 | tf_op jit(solution)/shard_map/ppermute | solution.py:21
  4.7 117.0 %collective-permute-start.2 = (f32[2,512,512]{2,1,0:T(8,128)}, f32[2,512,512]{2,1,0:T(8,128)}, u32[]{:S(2)}, u32[]{:S(2)}) collective-permute-start(f32[2,512,512]{2,1,0:T(8,128)} %bitcast.300), channel_id=1, source_target_pairs={{0,112},{2,114},{4,116},{6,118},{8,120},{10,122},{12,124},{14,126}... | collective-permute-start | bytes 6291464 | tf_op jit(solution)/shard_map/ppermute | solution.py:21
  7.8 114.1 %collective-permute-start.3 = (f32[2,512,512]{2,1,0:T(8,128)}, f32[2,512,512]{2,1,0:T(8,128)}, u32[]{:S(2)}, u32[]{:S(2)}) collective-permute-start(f32[2,512,512]{2,1,0:T(8,128)} %bitcast.301), channel_id=1, source_target_pairs={{0,110},{2,112},{4,114},{6,116},{8,118},{10,120},{12,122},{14,124}... | collective-permute-start | bytes 6291464 | tf_op jit(solution)/shard_map/ppermute | solution.py:21
  38.7 83.2 %copy-start.13 = (f32[1,2,512,512]{3,2,1,0:T(8,128)S(1)}, f32[1,2,512,512]{3,2,1,0:T(8,128)}, u32[]{:S(2)}) copy-start(f32[1,2,512,512]{3,2,1,0:T(8,128)} %param.5) | copy-start | bytes 6291460
  141.5 4.1 copy-start
  270.1 20.2 %copy-start.14 = (f32[3]{0:T(128)S(1)}, f32[3]{0:T(128)}, u32[]{:S(2)}) copy-start(f32[3]{0:T(128)} %compare_convert_fusion) | copy-start | bytes 40
  290.4 14.7 %copy-start.4 = (f32[3,512,512]{1,2,0:T(8,128)S(1)}, f32[3,512,512]{1,2,0:T(8,128)}, u32[]{:S(2)}) copy-start(f32[3,512,512]{1,2,0:T(8,128)} %get-tuple-element.32) | copy-start | bytes 9437188
  305.1 4.5 copy-start.1
  320.4 22.9 %collective-permute-start.7 = (f32[1024,512]{1,0:T(8,128)}, f32[1024,512]{1,0:T(8,128)S(1)}, u32[]{:S(2)}, u32[]{:S(2)}) collective-permute-start(f32[1024,512]{1,0:T(8,128)} %constant_dynamic-slice_fusion), channel_id=1, source_target_pairs={{0,2},{2,0},{4,6},{6,4},{8,10},{10,8},{12,14},{14,12},{16,18},{18,... | collective-permute-start | bytes 6291464 | tf_op jit(solution)/shard_map/ppermute | solution.py:31
  345.6 24.9 %copy-start.10 = (f32[512,512]{1,0:T(8,128)}, f32[512,512]{1,0:T(8,128)S(1)}, u32[]{:S(2)}) copy-start(f32[512,512]{1,0:T(8,128)S(1)} %get-tuple-element.39) | copy-start | bytes 3145732
  345.6 24.9 %copy-start.12 = (f32[512,512]{1,0:T(8,128)}, f32[512,512]{1,0:T(8,128)S(1)}, u32[]{:S(2)}) copy-start(f32[512,512]{1,0:T(8,128)S(1)} %get-tuple-element.38) | copy-start | bytes 3145732
  345.6 9.9 %collective-permute-start.14 = (f32[128,512]{1,0:T(8,128)S(1)}, f32[128,512]{1,0:T(8,128)S(1)}, u32[]{:S(2)}, u32[]{:S(2)}) collective-permute-start(f32[128,512]{1,0:T(8,128)S(1)} %dynamic-slice_bitcast_fusion), channel_id=1, source_target_pairs={{0,96},{2,98},{4,100},{6,102},{8,104},{10,106},{12,108},{14,110},{... | collective-permute-start | bytes 786440 | tf_op jit(solution)/shard_map/ppermute | solution.py:31
  346.6 20.6 %collective-permute-start.8 = (f32[128,512]{1,0:T(8,128)S(1)}, f32[128,512]{1,0:T(8,128)S(1)}, u32[]{:S(2)}, u32[]{:S(2)}) collective-permute-start(f32[128,512]{1,0:T(8,128)S(1)} %dynamic-slice_bitcast_fusion.1), channel_id=1, source_target_pairs={{0,32},{2,34},{4,36},{6,38},{8,40},{10,42},{12,44},{14,46},{16,48}... | collective-permute-start | bytes 786440 | tf_op jit(solution)/shard_map/ppermute | solution.py:31
  355.5 14.8 %collective-permute-start.15 = (f32[128,512]{1,0:T(8,128)S(1)}, f32[128,512]{1,0:T(8,128)S(1)}, u32[]{:S(2)}, u32[]{:S(2)}) collective-permute-start(f32[128,512]{1,0:T(8,128)S(1)} %bitcast_add_fusion.2), channel_id=1, source_target_pairs={{0,96},{2,98},{4,100},{6,102},{8,104},{10,106},{12,108},{14,110},{... | collective-permute-start | bytes 786440 | tf_op jit(solution)/shard_map/ppermute | solution.py:31
  367.3 20.3 %collective-permute-start.9 = (f32[128,512]{1,0:T(8,128)S(1)}, f32[128,512]{1,0:T(8,128)S(1)}, u32[]{:S(2)}, u32[]{:S(2)}) collective-permute-start(f32[128,512]{1,0:T(8,128)S(1)} %bitcast_add_fusion.5), channel_id=1, source_target_pairs={{0,32},{2,34},{4,36},{6,38},{8,40},{10,42},{12,44},{14,46},{16,48}... | collective-permute-start | bytes 786440 | tf_op jit(solution)/shard_map/ppermute | solution.py:31
  370.3 20.5 %collective-permute-start.16 = (f32[128,512]{1,0:T(8,128)S(1)}, f32[128,512]{1,0:T(8,128)S(1)}, u32[]{:S(2)}, u32[]{:S(2)}) collective-permute-start(f32[128,512]{1,0:T(8,128)S(1)} %bitcast_add_fusion.1), channel_id=1, source_target_pairs={{0,96},{2,98},{4,100},{6,102},{8,104},{10,106},{12,108},{14,110},{... | collective-permute-start | bytes 786440 | tf_op jit(solution)/shard_map/ppermute | solution.py:31
  370.4 17.1 %copy-start.11 = (f32[512,512]{1,0:T(8,128)S(1)}, f32[512,512]{1,0:T(8,128)}, u32[]{:S(2)}) copy-start(f32[512,512]{1,0:T(8,128)} %copy-done.10) | copy-start | bytes 3145732
  387.5 27.3 %copy-start.2 = (f32[3,512,512]{1,2,0:T(8,128)}, f32[3,512,512]{1,2,0:T(8,128)S(1)}, u32[]{:S(2)}) copy-start(f32[3,512,512]{1,2,0:T(8,128)S(1)} %get-tuple-element.13) | copy-start | bytes 9437188
  387.6 7.7 %collective-permute-start.10 = (f32[128,512]{1,0:T(8,128)S(1)}, f32[128,512]{1,0:T(8,128)S(1)}, u32[]{:S(2)}, u32[]{:S(2)}) collective-permute-start(f32[128,512]{1,0:T(8,128)S(1)} %bitcast_add_fusion.4), channel_id=1, source_target_pairs={{0,32},{2,34},{4,36},{6,38},{8,40},{10,42},{12,44},{14,46},{16,48}... | collective-permute-start | bytes 786440 | tf_op jit(solution)/shard_map/ppermute | solution.py:31
  391.9 4.9 collective-permute-start.17
  395.4 5.6 collective-permute-start.11
  396.8 8.0 %collective-permute-start.18 = (f32[32,512]{1,0:T(8,128)S(1)}, f32[32,512]{1,0:T(8,128)S(1)}, u32[]{:S(2)}, u32[]{:S(2)}) collective-permute-start(f32[32,512]{1,0:T(8,128)S(1)} %bitcast_add_fusion.8), channel_id=1, source_target_pairs={{0,24},{2,26},{4,28},{6,30},{8,0},{10,2},{12,4},{14,6},{16,8},{18,... | collective-permute-start | bytes 196616 | tf_op jit(solution)/shard_map/ppermute | solution.py:31
  401.0 5.8 collective-permute-start.12
  404.8 5.6 collective-permute-start.19
  406.8 5.8 collective-permute-start.13
  412.6 4.3 collective-permute-start.20
  417.0 12.9 %collective-permute-start.21 = (f32[32,512]{1,0:T(8,128)S(1)}, f32[32,512]{1,0:T(8,128)S(1)}, u32[]{:S(2)}, u32[]{:S(2)}) collective-permute-start(f32[32,512]{1,0:T(8,128)S(1)} %fusion.55), channel_id=1, source_target_pairs={{0,4},{2,6},{4,0},{6,2},{8,12},{10,14},{12,8},{14,10},{16,20},{18,... | collective-permute-start | bytes 196616 | tf_op jit(solution)/shard_map/ppermute | solution.py:31
  430.0 4.3 collective-permute-start.22
  432.0 5.9 %collective-permute-start.28 = (f32[32,512]{1,0:T(8,128)S(1)}, f32[32,512]{1,0:T(8,128)S(1)}, u32[]{:S(2)}, u32[]{:S(2)}) collective-permute-start(f32[32,512]{1,0:T(8,128)S(1)} %get-tuple-element.21), channel_id=1, source_target_pairs={{0,24},{2,26},{4,28},{6,30},{8,0},{10,2},{12,4},{14,6},{16,8},{18,... | collective-permute-start | bytes 196616 | tf_op jit(solution)/shard_map/ppermute | solution.py:31
  434.3 5.1 collective-permute-start.23
  437.9 5.6 collective-permute-start.29
  439.4 5.5 collective-permute-start.24
  443.4 5.5 collective-permute-start.30
  444.9 8.0 %collective-permute-start.25 = (f32[128,512]{1,0:T(8,128)S(1)}, f32[128,512]{1,0:T(8,128)S(1)}, u32[]{:S(2)}, u32[]{:S(2)}) collective-permute-start(f32[128,512]{1,0:T(8,128)S(1)} %bitcast.305), channel_id=1, source_target_pairs={{0,32},{2,34},{4,36},{6,38},{8,40},{10,42},{12,44},{14,46},{16,48}... | collective-permute-start | bytes 786440 | tf_op jit(solution)/shard_map/ppermute | solution.py:31
  448.9 8.6 %collective-permute-start.31 = (f32[128,512]{1,0:T(8,128)S(1)}, f32[128,512]{1,0:T(8,128)S(1)}, u32[]{:S(2)}, u32[]{:S(2)}) collective-permute-start(f32[128,512]{1,0:T(8,128)S(1)} %bitcast.303), channel_id=1, source_target_pairs={{0,96},{2,98},{4,100},{6,102},{8,104},{10,106},{12,108},{14,110},{... | collective-permute-start | bytes 786440 | tf_op jit(solution)/shard_map/ppermute | solution.py:31
  452.9 7.8 %collective-permute-start.26 = (f32[128,512]{1,0:T(8,128)S(1)}, f32[128,512]{1,0:T(8,128)S(1)}, u32[]{:S(2)}, u32[]{:S(2)}) collective-permute-start(f32[128,512]{1,0:T(8,128)S(1)} %collective-permute-done.25), channel_id=1, source_target_pairs={{0,32},{2,34},{4,36},{6,38},{8,40},{10,42},{12,44},{14,46},{16,48}... | collective-permute-start | bytes 786440 | tf_op jit(solution)/shard_map/ppermute | solution.py:31
  457.5 8.5 %collective-permute-start.32 = (f32[128,512]{1,0:T(8,128)S(1)}, f32[128,512]{1,0:T(8,128)S(1)}, u32[]{:S(2)}, u32[]{:S(2)}) collective-permute-start(f32[128,512]{1,0:T(8,128)S(1)} %collective-permute-done.31), channel_id=1, source_target_pairs={{0,96},{2,98},{4,100},{6,102},{8,104},{10,106},{12,108},{14,110},{... | collective-permute-start | bytes 786440 | tf_op jit(solution)/shard_map/ppermute | solution.py:31
  460.7 7.6 %collective-permute-start.27 = (f32[128,512]{1,0:T(8,128)S(1)}, f32[128,512]{1,0:T(8,128)S(1)}, u32[]{:S(2)}, u32[]{:S(2)}) collective-permute-start(f32[128,512]{1,0:T(8,128)S(1)} %collective-permute-done.26), channel_id=1, source_target_pairs={{0,32},{2,34},{4,36},{6,38},{8,40},{10,42},{12,44},{14,46},{16,48}... | collective-permute-start | bytes 786440 | tf_op jit(solution)/shard_map/ppermute | solution.py:31
  466.1 7.6 %collective-permute-start.33 = (f32[128,512]{1,0:T(8,128)S(1)}, f32[128,512]{1,0:T(8,128)S(1)}, u32[]{:S(2)}, u32[]{:S(2)}) collective-permute-start(f32[128,512]{1,0:T(8,128)S(1)} %collective-permute-done.32), channel_id=1, source_target_pairs={{0,96},{2,98},{4,100},{6,102},{8,104},{10,106},{12,108},{14,110},{... | collective-permute-start | bytes 786440 | tf_op jit(solution)/shard_map/ppermute | solution.py:31
  468.3 7.9 %copy-start.8 = (f32[4,128,512]{2,1,0:T(8,128)}, f32[4,128,512]{2,1,0:T(8,128)S(1)}, u32[]{:S(2)}) copy-start(f32[4,128,512]{2,1,0:T(8,128)S(1)} %bitcast_dynamic-update-slice_fusion.4) | copy-start | bytes 3145732
  476.2 104.2 %collective-permute-start.34 = (f32[1024,512]{1,0:T(8,128)}, f32[1024,512]{1,0:T(8,128)}, u32[]{:S(2)}, u32[]{:S(2)}) collective-permute-start(f32[1024,512]{1,0:T(8,128)} %pad_maximum_fusion.7), channel_id=1, source_target_pairs={{0,2},{2,0},{4,6},{6,4},{8,10},{10,8},{12,14},{14,12},{16,18},{18,... | collective-permute-start | bytes 6291464 | tf_op jit(solution)/shard_map/ppermute | solution.py:31
  497.9 9.3 %copy-start.3 = (f32[3,512,512]{1,2,0:T(8,128)S(1)}, f32[3,512,512]{1,2,0:T(8,128)}, u32[]{:S(2)}) copy-start(f32[3,512,512]{1,2,0:T(8,128)} %copy-done.2) | copy-start | bytes 9437188
  500.3 24.9 %collective-permute-start.4 = (f32[512,512]{0,1:T(8,128)S(1)}, f32[512,512]{0,1:T(8,128)S(1)}, u32[]{:S(2)}, u32[]{:S(2)}) collective-permute-start(f32[512,512]{0,1:T(8,128)S(1)} %get-tuple-element.35), channel_id=1, source_target_pairs={{0,2},{2,4},{4,6},{6,8},{8,10},{10,12},{12,14},{14,16},{16,18},{18... | collective-permute-start | bytes 3145736 | tf_op jit(solution)/shard_map/ppermute | solution.py:21
  500.8 27.4 %collective-permute-start.5 = (f32[512,512]{0,1:T(8,128)S(1)}, f32[512,512]{0,1:T(8,128)S(1)}, u32[]{:S(2)}, u32[]{:S(2)}) collective-permute-start(f32[512,512]{0,1:T(8,128)S(1)} %get-tuple-element.37), channel_id=1, source_target_pairs={{0,16},{2,18},{4,20},{6,22},{8,24},{10,26},{12,28},{14,30},{16,32}... | collective-permute-start | bytes 3145736 | tf_op jit(solution)/shard_map/ppermute | solution.py:21
  505.2 72.2 %collective-permute-start.6 = (f32[512,512]{0,1:T(8,128)S(1)}, f32[512,512]{0,1:T(8,128)S(1)}, u32[]{:S(2)}, u32[]{:S(2)}) collective-permute-start(f32[512,512]{0,1:T(8,128)S(1)} %get-tuple-element.36), channel_id=1, source_target_pairs={{0,18},{2,20},{4,22},{6,24},{8,26},{10,28},{12,30},{14,32},{16,34}... | collective-permute-start | bytes 3145736 | tf_op jit(solution)/shard_map/ppermute | solution.py:21
  520.6 59.9 %copy-start.7 = (f32[4,128,512]{2,1,0:T(8,128)S(1)}, f32[4,128,512]{2,1,0:T(8,128)}, u32[]{:S(2)}) copy-start(f32[4,128,512]{2,1,0:T(8,128)} %copy-done.6) | copy-start | bytes 3145732
  520.6 59.9 %copy-start.9 = (f32[4,128,512]{2,1,0:T(8,128)S(1)}, f32[4,128,512]{2,1,0:T(8,128)}, u32[]{:S(2)}) copy-start(f32[4,128,512]{2,1,0:T(8,128)} %copy-done.8) | copy-start | bytes 3145732
  (2 other events, 4.6 us)

commit v2 on v1

--- a/solution.py
+++ b/solution.py
@@ -50,6 +50,27 @@
     first = jnp.where(coord == 0, data, got)
     second = jnp.where(coord == 0, got, data)
     return jnp.concatenate([first, second], axis=0)
+
+
+def direct_reduce_scatter(data, sub):
+    size = sub[1]
+    coord = sub_coord(sub)
+    chunks = data.reshape(size, data.shape[0] // size, -1)
+    total = chunks[coord]
+    for shift in range(1, size):
+        total = total + sub_shift(chunks[(coord + shift) % size], sub, shift)
+    return total
+
+
+def direct_all_gather(data, sub):
+    size = sub[1]
+    coord = sub_coord(sub)
+    out = jnp.zeros((size,) + data.shape, data.dtype)
+    out = lax.dynamic_update_index_in_dim(out, data, coord, 0)
+    for shift in range(1, size):
+        got = sub_shift(data, sub, shift)
+        out = lax.dynamic_update_index_in_dim(out, got, (coord - shift) % size, 0)
+    return out.reshape(size * data.shape[0], -1)
 
 
 def ring_reduce_scatter(data, sub):
@@ -86,18 +107,19 @@
     return jnp.concatenate([out_f.reshape(size * rows, -1), out_b.reshape(size * rows, -1)], axis=0)
 
 
-def scan_all_reduce(value):
+def scan_all_reduce(value, tied):
     shape = value.shape
     data = value.reshape(-1, shape[-1])
     data = pair_reduce_scatter(data, CORE)
-    data = ring_reduce_scatter(data, XAX)
-    data = ring_reduce_scatter(data, YAX)
+    data = direct_reduce_scatter(data, XAX)
+    data = direct_reduce_scatter(data, YAX)
     data = pair_reduce_scatter(data, ZLO)
+    data, tied = lax.optimization_barrier((data, tied))
     data = pair_all_gather(data, ZLO)
-    data = ring_all_gather(data, YAX)
-    data = ring_all_gather(data, XAX)
+    data = direct_all_gather(data, YAX)
+    data = direct_all_gather(data, XAX)
     data = pair_all_gather(data, CORE)
-    return data.reshape(shape)
+    return data.reshape(shape), tied
 
 
 def dft_tables(length_side, direction_sign):
@@ -127,13 +149,29 @@
     tile_side = object_tiles.shape[-1]
     slots = offsets.shape[1]
     own_modes = probe_modes.shape[0]
-    partner_modes = lax.ppermute(probe_modes, "mode", [(0, 1), (1, 0)])
-    all_modes = jnp.concatenate([probe_modes, partner_modes], axis=0)
+    count = lax.axis_size("scan")
+    core = lax.axis_index("scan") % 2
+    sent = lax.dynamic_index_in_dim(probe_modes, core, 0, keepdims=False)
+    pairs = [(s * 2 + m, (s ^ 2) * 2 + 1 - m) for s in range(count) for m in range(2)]
+    got = lax.ppermute(sent, ("scan", "mode"), pairs)
+    mate = lax.ppermute(got, "scan", [(s, s ^ 1) for s in range(count)])
+    partner_modes = jnp.stack([jnp.where(core == 0, got, mate), jnp.where(core == 0, mate, got)])
+    component = lax.axis_index("mode")
+    all_modes = jnp.where(
+        component == 0,
+        jnp.concatenate([probe_modes, partner_modes], axis=0),
+        jnp.concatenate([partner_modes, probe_modes], axis=0),
+    )
     modes_here = all_modes.shape[0]
     own_tile = object_tiles[0]
     east_tile = from_behind(own_tile, "scan", -1)
     south_tile = from_behind(own_tile, "scan", -GCOLS)
-    corner_tile = from_behind(own_tile, "scan", -(GCOLS + 1))
+    far_corner = lax.ppermute(
+        own_tile, "scan", [(s, s - GCOLS - 1) for s in range(count) if (s - GCOLS - 1) % 2 == 1 and s >= GCOLS + 1]
+        + [(s, s - GCOLS - 1 + count) for s in range(count) if (s - GCOLS - 1) % 2 == 1 and s < GCOLS + 1]
+    )
+    near_corner = lax.ppermute(south_tile, "scan", [(s, s - 1) for s in range(count) if s % 2 == 1])
+    corner_tile = jnp.where(lax.axis_index("scan") % 2 == 0, near_corner, far_corner)
     upper_band = jnp.concatenate([own_tile, east_tile], axis=2)
     lower_band = jnp.concatenate([south_tile, corner_tile], axis=2)
     extended = jnp.concatenate([upper_band, lower_band], axis=1)
@@ -166,25 +204,19 @@
     ratio = amplitudes[0] / jnp.maximum(jnp.sqrt(intensity), amp_floor)
     correction = (far_field * (ratio - 1.0)[:, None, None]).astype(jnp.bfloat16)
     live_slots = (jnp.arange(slots, dtype=jnp.int32) < counts[0]).astype(jnp.float32)
-    back_own = transform(
-        correction[:, :own_modes].reshape(slots * own_modes, 2, side, side), inverse_table
-    ).reshape(slots, own_modes, 2, side, side)
-    back_own = back_own * live_slots[:, None, None, None, None]
+    back_wave = transform(
+        correction.reshape(slots * modes_here, 2, side, side), inverse_table
+    ).reshape(slots, modes_here, 2, side, side)
+    back_wave = back_wave * live_slots[:, None, None, None, None]
+    back_own = lax.dynamic_slice_in_dim(back_wave, component * own_modes, own_modes, axis=1)
     probe_real_grad = jnp.sum(obj_real * back_own[:, :, 0] + obj_imag * back_own[:, :, 1], axis=0)
     probe_imag_grad = jnp.sum(obj_real * back_own[:, :, 1] - obj_imag * back_own[:, :, 0], axis=0)
-    probe_grad = scan_all_reduce(jnp.stack([probe_real_grad, probe_imag_grad], axis=1))
-    back_other = transform(
-        correction[:, own_modes:].reshape(slots * (modes_here - own_modes), 2, side, side),
-        inverse_table,
-    ).reshape(slots, modes_here - own_modes, 2, side, side)
-    back_other = back_other * live_slots[:, None, None, None, None]
-    back_wave = jnp.concatenate([back_own, back_other], axis=1)
+    probe_partial = jnp.stack([probe_real_grad, probe_imag_grad], axis=1)
     back_real = back_wave[:, :, 0]
     back_imag = back_wave[:, :, 1]
     grad_real = jnp.sum(probe_real * back_real + probe_imag * back_imag, axis=1)
     grad_imag = jnp.sum(probe_real * back_imag - probe_imag * back_real, axis=1)
     whole_grad = jnp.stack([grad_real, grad_imag], axis=1)
-    component = lax.axis_index("mode")
     position_y = jnp.sum(whole_grad * grad_y, axis=(1, 2, 3))
     position_x = jnp.sum(whole_grad * grad_x, axis=(1, 2, 3))
     positions = jnp.stack([position_y, position_x], axis=1) / side
@@ -194,9 +226,13 @@
         start = (slot_offsets[slot_id, 0], slot_offsets[slot_id, 1])
         current = lax.dynamic_slice(gradient_plane, start, (side, side))
         gradient_plane = lax.dynamic_update_slice(gradient_plane, current + mine[slot_id, 0], start)
+    probe_partial, gradient_plane = lax.optimization_barrier((probe_partial, gradient_plane))
     received_east = from_behind(gradient_plane[:tile_side, tile_side:], "scan", 1)
     received_south = from_behind(gradient_plane[tile_side:, :tile_side], "scan", GCOLS)
     received_corner = from_behind(gradient_plane[tile_side:, tile_side:], "scan", GCOLS + 1)
+    probe_grad, (received_east, received_south, received_corner) = scan_all_reduce(
+        probe_partial, (received_east, received_south, received_corner)
+    )
     total_grad = (
         gradient_plane[:tile_side, :tile_side] + received_east + received_south + received_corner
     )

time: 597 us -> 519 us (0.87)
  the two profiles are of different devices: /device:TPU:22 before, /device:TPU:65 now
where the time goes in v2:
time: 519 us; the launch traced here: 512 us
  waiting for transfers between devices  154 us (30%)
  other arithmetic  131 us (25%)
  local copies, waits for them, and re-layouts  102 us (20%)
  matrix products  73.5 us (14%)
  starting transfers between devices  32.1 us (6%)
  between operations  20.1 us (4%)
    ppermute x16, waiting for transfers between devices, sub_shift(): return lax.ppermute(value, 'scan', pairs)  91.6 us
    dot_general x2, matrix products, transform(): jnp.einsum('bcpq,dcqk->bdpk', first_section, matrix_table, preferred_elem...  73.5 us
    ppermute x5, waiting for transfers between devices, from_behind(): return lax.ppermute(value, axis, pairs)  62.6 us
    another operation x4, other arithmetic  25.9 us
    dynamic_update_slice x3, local copies, waits for them, and re-layouts, shards(): lax.dynamic_update_slice(gradient_plane, current + mine[slot_id, 0], start)  23.8 us
    mul x1, other arithmetic, shards(): back_wave = back_wave * live_slots[:, None, None, None, None]  19.3 us
    ppermute x16, starting transfers between devices, sub_shift(): return lax.ppermute(value, 'scan', pairs)  16.4 us
    mul x3, local copies, waits for them, and re-layouts, shards(): exit_real = obj_real * probe_real - obj_imag * probe_imag  14.9 us
  transfers between devices with their start and end apart: 25, of which 13 were waited for; matrix products, arithmetic and copies ran while one was open for 16% of the time, Pallas kernels for 0%

profile of v2, /device:TPU:65, one launch (start us, length us, event | category | flops | bytes accessed | tf_op | source)
XLA Modules:
  0.0 512.3 jit_solution(8875439366487573031)
XLA Ops:
  0.7 5.2 %collective-permute-start.1 = (f32[2,512,512]{2,1,0:T(8,128)}, f32[2,512,512]{2,1,0:T(8,128)}, u32[]{:S(2)}, u32[]{:S(2)}) collective-permute-start(f32[2,512,512]{2,1,0:T(8,128)} %bitcast.244), channel_id=1, source_target_pairs={{0,112},{2,114},{4,116},{6,118},{8,120},{10,122},{12,124},{14,126}... | collective-permute-start | bytes 6291464 | tf_op jit(solution)/shard_map/ppermute | solution.py:21
  9.0 62.6 %collective-permute-done.1 = f32[2,512,512]{2,1,0:T(8,128)} collective-permute-done((f32[2,512,512]{2,1,0:T(8,128)}, f32[2,512,512]{2,1,0:T(8,128)}, u32[]{:S(2)}, u32[]{:S(2)}) %collective-permute-start.1) | collective-permute-done | bytes 2097184 | tf_op jit(solution)/shard_map/ppermute | solution.py:21
  71.6 4.8 collective-permute-start.2
  77.7 4.7 multiply_convert_fusion.2
  82.3 4.7 negate_convert_fusion
  87.1 5.3 %multiply_convert_fusion = (bf16[1,512,512]{2,1,0:T(8,128)(2,1)}, bf16[1,512,512]{2,1,0:T(8,128)(2,1)}) fusion(), kind=kLoop, calls=%fused_computation.83 | loop fusion | flops 4718592 | bytes 1048576 | tf_op jit(solution)/shard_map/convert.18
  113.7 4.0 fusion.34
  122.6 4.6 constant_dynamic-slice_fusion.4
  127.2 3.4 copy.41
  130.5 3.4 copy.39
  136.1 3.6 pad_maximum_fusion
  139.7 4.1 slice_bitcast_fusion.5
  143.8 3.9 select_bitcast_fusion.1
  150.1 4.4 slice_bitcast_fusion.3
  154.5 5.3 %copy.42 = f32[4,512,512]{1,2,0:T(8,128)} copy(f32[4,512,512]{2,1,0:T(8,128)} %get-tuple-element.32) | data formatting | bytes 8388608 | tf_op jit(solution)/shard_map/mul | solution.py:196
  159.8 5.2 %copy.43 = f32[4,512,512]{1,2,0:T(8,128)} copy(f32[4,512,512]{2,1,0:T(8,128)} %get-tuple-element.33) | data formatting | bytes 8388608 | tf_op jit(solution)/shard_map/mul | solution.py:196
  165.0 11.2 %subtract_convert_fusion = (bf16[3,4,512,512]{2,3,1,0:T(8,128)(2,1)}, bf16[3,4,512,512]{2,3,1,0:T(8,128)(2,1)}) fusion(f32[4,512,512]{1,2,0:T(8,128)} %copy.43, f32[3,512,512]{1,2,0:T(8,128)} %get-tuple-element.38, f32[4,512,512]{1,2,0:T(8,128)} %copy.42, f32[3,512,512]{1,2,0:T(8,128)S(1)} %get-tuple-element.37), kind=kLoop, calls=%fused_computation.23 | loop fusion | flops 25165824 | bytes 27262976 | tf_op jit(solution)/shard_map/convert.3
  176.2 39.6 %fusion = (f32[12,512,512]{1,2,0:T(8,128)}, f32[2,512,12,512,1]{3,1,4,2,0:T(8,128)}) fusion(bf16[12,1,512,512]{2,3,1,0:T(8,128)(2,1)} %bitcast.240, bf16[12,1,512,512]{2,3,1,0:T(8,128)(2,1)} %bitcast.239, bf16[1,2,512,512]{3,2,1,0:T(8,128)(2,1)} %get-tuple-element.53, bf16[1,2,512,512]{3,2,1,0:T(8,128)(2,1)} %get-tuple-element.54), kind=kOutput, calls=%fused_computation.3 | convolution fusion | flops 25819086848 | bytes 52428800 | tf_op jit(solution)/shard_map/bcpq,dcqk->bdpk/dot_general | solution.py:142
  215.8 8.3 %reduce_sum.72 = f32[3,512,512]{1,2,0:T(8,128)} reduce(f32[3,4,512,512]{2,3,1,0:T(8,128)} %bitcast.228, f32[]{:T(128)} %constant.226.clone.1), dimensions={1}, to_apply=%region_1.2 | reduce | flops 2359296 | bytes 15728644 | tf_op jit(solution)/shard_map/reduce_sum | solution.py:203
  224.1 3.0 fusion.25
  227.2 6.1 %mul.393 = f32[3,4,512,512]{2,3,1,0:T(8,128)} broadcast(f32[3,512,512]{1,2,0:T(8,128)S(1)} %fusion.25), dimensions={0,2,3} | broadcast | bytes 15728640 | tf_op jit(solution)/shard_map/mul | solution.py:205
  233.2 33.9 %fusion.7 = f32[2,512,12,512,1]{3,1,4,2,0:T(8,128)} fusion(bf16[1,2,512,512]{3,2,1,0:T(8,128)(2,1)S(1)} %copy-done.14, bf16[1,2,512,512]{3,2,1,0:T(8,128)(2,1)S(1)} %copy-done.13, f32[2,512,12,512,1]{3,1,4,2,0:T(8,128)} %get-tuple-element.65, f32[12,512,512]{1,2,0:T(8,128)} %bitcast.229), kind=kOutput, calls=%fused_computation.10 | convolution fusion | flops 25797066752 | bytes 65011712 | tf_op jit(solution)/shard_map/bcpq,dcqk->bdpk/dot_general | solution.py:142
  267.1 19.3 %broadcast_multiply_fusion = f32[3,4,2,512,512]{3,4,1,0,2:T(8,128)} fusion(f32[3,4,2,512,512]{3,4,1,0,2:T(8,128)} %bitcast.225, f32[3]{0:T(128)S(1)} %copy-done.16), kind=kLoop, calls=%fused_computation.21 | loop fusion | flops 6291456 | bytes 50331660 | tf_op jit(solution)/shard_map/mul | solution.py:210
  286.4 10.6 %subtract_reduce_fusion = (f32[3,512,512]{1,2,0:T(8,128)S(1)}, f32[3,512,512]{1,2,0:T(8,128)S(1)}) fusion(f32[3,4,2,512,512]{3,4,1,0,2:T(8,128)} %broadcast_multiply_fusion, f32[4,512,512]{1,2,0:T(8,128)S(1)} %copy-done.2, f32[4,512,512]{1,2,0:T(8,128)S(1)} %copy-done.1), kind=kLoop, calls=%fused_computation.19 | loop fusion | flops 23592960 | bytes 39845888 | tf_op jit(solution)/shard_map/reduce_sum | solution.py:218
  303.8 7.9 %dynamic_update_slice.35 = f32[1024,1024]{0,1:T(8,128)} dynamic-update-slice(f32[1024,1024]{0,1:T(8,128)} %broadcast_in_dim.45, f32[512,512]{0,1:T(8,128)} %slice_bitcast_fusion.8, s32[]{:T(128)S(6)} %select_n.312, s32[]{:T(128)S(6)} %select_n.313) | dynamic-update-slice | bytes 2097156 | tf_op jit(solution)/shard_map/dynamic_update_slice | solution.py:228
  311.7 3.0 fusion.40
  314.6 7.9 %dynamic_update_slice.36 = f32[1024,1024]{0,1:T(8,128)} dynamic-update-slice(f32[1024,1024]{0,1:T(8,128)} %dynamic_update_slice.35, f32[512,512]{0,1:T(8,128)} %fusion.40, s32[]{:T(128)S(6)} %select_n.314, s32[]{:T(128)S(6)} %select_n.315) | dynamic-update-slice | bytes 2097156 | tf_op jit(solution)/shard_map/dynamic_update_slice | solution.py:228
  322.5 3.0 fusion.39
  325.5 8.1 %dynamic_update_slice.37 = f32[1024,1024]{0,1:T(8,128)} dynamic-update-slice(f32[1024,1024]{0,1:T(8,128)} %dynamic_update_slice.36, f32[512,512]{0,1:T(8,128)} %fusion.39, s32[]{:T(128)S(6)} %select_n.316, s32[]{:T(128)S(6)} %select_n.317) | dynamic-update-slice | bytes 2097156 | tf_op jit(solution)/shard_map/dynamic_update_slice | solution.py:228
  333.6 8.3 %add_reduce_fusion.1 = (f32[2,512,512]{1,2,0:T(8,128)S(1)}, f32[2,512,512]{1,2,0:T(8,128)S(1)}) fusion(f32[3,4,2,512,512]{3,4,1,0,2:T(8,128)} %broadcast_multiply_fusion, s32[]{:T(128)S(6)} %select_n.310, s32[]{:T(128)S(6)} %add.391, f32[3,512,512]{1,2,0:T(8,128)} %get-tuple-element.38, f32[3,512,512]{1,2,0:T(8,128)} %copy-done.5), kind=kLoop, calls=%fused_computation.41 | loop fusion | flops 11534336 | bytes 23068680 | tf_op jit(solution)/shard_map/reduce_sum | solution.py:212
  344.3 5.2 %copy.52 = f32[2,2,512,512]{3,2,1,0:T(8,128)} copy(f32[2,2,512,512]{2,3,0,1:T(8,128)} %pad_maximum_fusion.2) | data formatting | bytes 8388608 | tf_op jit(solution)/shard_map/optimization_barrier | solution.py:229
  349.5 3.2 constant_dynamic-slice_fusion.1
  353.0 4.2 collective-permute-done.6
  357.2 2.7 dynamic-slice_add_fusion
  367.3 3.6 fusion.53
  373.6 3.6 collective-permute-done.7
  378.9 10.5 %collective-permute-done.8 = f32[256,512]{1,0:T(8,128)} collective-permute-done((f32[256,512]{1,0:T(8,128)}, f32[256,512]{1,0:T(8,128)}, u32[]{:S(2)}, u32[]{:S(2)}) %collective-permute-start.8) | collective-permute-done | bytes 524320 | tf_op jit(solution)/shard_map/ppermute | solution.py:31
  392.1 44.7 %collective-permute-done.10 = f32[64,512]{1,0:T(8,128)S(1)} collective-permute-done((f32[64,512]{1,0:T(8,128)S(1)}, f32[64,512]{1,0:T(8,128)S(1)}, u32[]{:S(2)}, u32[]{:S(2)}) %collective-permute-start.10) | collective-permute-done | bytes 131104 | tf_op jit(solution)/shard_map/ppermute | solution.py:31
  436.9 2.7 collective-permute-done.11
  442.7 3.1 collective-permute-done.13
  445.9 3.1 collective-permute-done.17
  463.7 4.9 collective-permute-done.21
  470.6 7.6 %collective-permute-done.22 = f32[256,512]{1,0:T(8,128)} collective-permute-done((f32[256,512]{1,0:T(8,128)}, f32[256,512]{1,0:T(8,128)}, u32[]{:S(2)}, u32[]{:S(2)}) %collective-permute-start.22) | collective-permute-done | bytes 524320 | tf_op jit(solution)/shard_map/ppermute | solution.py:31
  480.0 3.1 collective-permute-done.23
  483.9 5.3 %collective-permute-start.24 = (f32[1024,512]{1,0:T(8,128)}, f32[1024,512]{1,0:T(8,128)}, u32[]{:S(2)}, u32[]{:S(2)}) collective-permute-start(f32[1024,512]{1,0:T(8,128)} %bitcast.85), channel_id=1, source_target_pairs={{0,2},{2,0},{4,6},{6,4},{8,10},{10,8},{12,14},{14,12},{16,18},{18,... | collective-permute-start | bytes 6291464 | tf_op jit(solution)/shard_map/ppermute | solution.py:31
  489.3 13.1 %fusion.19 = (f32[3]{0:T(128)S(1)}, f32[3]{0:T(128)S(1)}) fusion(f32[3,2,514,514]{2,3,0,1:T(8,128)} %copy-done, f32[3,1,512,512]{2,3,0,1:T(8,128)S(1)} %bitcast.222, f32[3,1,512,512]{2,3,0,1:T(8,128)S(1)} %bitcast.224), kind=kLoop, calls=%fused_computation.37 | loop fusion | flops 14155770 | bytes 31457304 | tf_op jit(solution)/shard_map/reduce_sum | solution.py:220
  503.0 2.7 add_bitcast_fusion
  506.9 2.7 broadcast_select_fusion.1
  (103 shorter events, 67.2 us)
Async XLA Ops:
  0.6 76.4 %copy-start.15 = (s32[1,3,2]{1,2,0:T(2,128)S(1)}, s32[1,3,2]{1,2,0:T(2,128)}, u32[]{:S(2)}) copy-start(s32[1,3,2]{1,2,0:T(2,128)} %param.8) | copy-start | bytes 76
  0.6 106.9 %copy-start.10 = (f32[1,3,512,512]{3,2,1,0:T(8,128)S(1)}, f32[1,3,512,512]{3,2,1,0:T(8,128)}, u32[]{:S(2)}) copy-start(f32[1,3,512,512]{3,2,1,0:T(8,128)} %param.7) | copy-start | bytes 9437188
  0.7 70.9 %collective-permute-start.1 = (f32[2,512,512]{2,1,0:T(8,128)}, f32[2,512,512]{2,1,0:T(8,128)}, u32[]{:S(2)}, u32[]{:S(2)}) collective-permute-start(f32[2,512,512]{2,1,0:T(8,128)} %bitcast.244), channel_id=1, source_target_pairs={{0,112},{2,114},{4,116},{6,118},{8,120},{10,122},{12,124},{14,126}... | collective-permute-start | bytes 6291464 | tf_op jit(solution)/shard_map/ppermute | solution.py:21
  7.6 84.8 %collective-permute-start.4 = (f32[2,512,512]{2,1,0:T(8,128)S(1)}, f32[2,512,512]{2,1,0:T(8,128)}, u32[]{:S(2)}, u32[]{:S(2)}) collective-permute-start(f32[2,512,512]{2,1,0:T(8,128)S(1)} %dynamic-slice_bitcast_fusion.2), channel_id=1, source_target_pairs={{0,5},{1,4},{2,7},{3,6},{4,1},{5,0},{6,3},{7,2},{8,13},{9,12},{10,... | collective-permute-start | bytes 6291464 | tf_op jit(solution)/shard_map/ppermute | solution.py:156
  7.7 110.0 %collective-permute-start.3 = (f32[2,512,512]{2,1,0:T(8,128)}, f32[2,512,512]{2,1,0:T(8,128)}, u32[]{:S(2)}, u32[]{:S(2)}) collective-permute-start(f32[2,512,512]{2,1,0:T(8,128)} %bitcast.245), channel_id=1, source_target_pairs={{20,2},{24,6},{28,10},{32,14},{36,18},{40,22},{44,26},{48,30},{52,... | collective-permute-start | bytes 6291464 | tf_op jit(solution)/shard_map/ppermute | solution.py:169
  71.6 46.1 %collective-permute-start.2 = (f32[2,512,512]{2,1,0:T(8,128)}, f32[2,512,512]{2,1,0:T(8,128)}, u32[]{:S(2)}, u32[]{:S(2)}) collective-permute-start(f32[2,512,512]{2,1,0:T(8,128)} %collective-permute-done.1), channel_id=1, source_target_pairs={{2,0},{6,4},{10,8},{14,12},{18,16},{22,20},{26,24},{30,28},{34,32}... | collective-permute-start | bytes 6291464 | tf_op jit(solution)/shard_map/ppermute | solution.py:173
  76.4 43.5 %collective-permute-start = (f32[2,512,512]{2,1,0:T(8,128)}, f32[2,512,512]{2,1,0:T(8,128)}, u32[]{:S(2)}, u32[]{:S(2)}) collective-permute-start(f32[2,512,512]{2,1,0:T(8,128)} %bitcast.246), channel_id=1, source_target_pairs={{0,126},{2,0},{4,2},{6,4},{8,6},{10,8},{12,10},{14,12},{16,14},{18... | collective-permute-start | bytes 6291464 | tf_op jit(solution)/shard_map/ppermute | solution.py:21
  92.4 51.4 %collective-permute-start.5 = (f32[2,512,512]{2,1,0:T(8,128)}, f32[2,512,512]{2,1,0:T(8,128)}, u32[]{:S(2)}, u32[]{:S(2)}) collective-permute-start(f32[2,512,512]{2,1,0:T(8,128)} %collective-permute-done.4), channel_id=1, source_target_pairs={{0,2},{2,0},{4,6},{6,4},{8,10},{10,8},{12,14},{14,12},{16,18},{18,... | collective-permute-start | bytes 6291464 | tf_op jit(solution)/shard_map/ppermute | solution.py:157
  117.7 2.3 copy-start.12
  139.7 4.1 copy-start
  143.8 21.2 %copy-start.5 = (f32[3,512,512]{1,2,0:T(8,128)}, f32[3,512,512]{1,2,0:T(8,128)S(1)}, u32[]{:S(2)}) copy-start(f32[3,512,512]{1,2,0:T(8,128)S(1)} %get-tuple-element.37) | copy-start | bytes 9437188
  143.8 4.6 copy-start.8
  215.8 8.3 %copy-start.6 = (f32[1,3,512,512]{2,3,1,0:T(8,128)S(1)}, f32[1,3,512,512]{2,3,1,0:T(8,128)}, u32[]{:S(2)}) copy-start(f32[1,3,512,512]{2,3,1,0:T(8,128)} %copy.46) | copy-start | bytes 9437188
  227.1 6.1 %copy-start.13 = (bf16[1,2,512,512]{3,2,1,0:T(8,128)(2,1)S(1)}, bf16[1,2,512,512]{3,2,1,0:T(8,128)(2,1)}, u32[]{:S(2)}) copy-start(bf16[1,2,512,512]{3,2,1,0:T(8,128)(2,1)} %get-tuple-element.52) | copy-start | bytes 3145732
  227.2 6.1 %copy-start.14 = (bf16[1,2,512,512]{3,2,1,0:T(8,128)(2,1)S(1)}, bf16[1,2,512,512]{3,2,1,0:T(8,128)(2,1)}, u32[]{:S(2)}) copy-start(bf16[1,2,512,512]{3,2,1,0:T(8,128)(2,1)} %get-tuple-element.55) | copy-start | bytes 3145732
  233.2 33.9 %copy-start.16 = (f32[3]{0:T(128)S(1)}, f32[3]{0:T(128)}, u32[]{:S(2)}) copy-start(f32[3]{0:T(128)} %compare_convert_fusion) | copy-start | bytes 40
  267.1 19.3 %copy-start.1 = (f32[4,512,512]{1,2,0:T(8,128)S(1)}, f32[4,512,512]{1,2,0:T(8,128)}, u32[]{:S(2)}) copy-start(f32[4,512,512]{1,2,0:T(8,128)} %copy.42) | copy-start | bytes 12582916
  267.1 19.3 %copy-start.2 = (f32[4,512,512]{1,2,0:T(8,128)S(1)}, f32[4,512,512]{1,2,0:T(8,128)}, u32[]{:S(2)}) copy-start(f32[4,512,512]{1,2,0:T(8,128)} %copy.43) | copy-start | bytes 12582916
  297.0 1.6 copy-start.3
  298.6 1.6 copy-start.7
  352.7 4.5 collective-permute-start.6
  359.9 1.3 copy-start.9
  362.4 14.7 %collective-permute-start.7 = (f32[256,512]{1,0:T(8,128)}, f32[256,512]{1,0:T(8,128)}, u32[]{:S(2)}, u32[]{:S(2)}) collective-permute-start(f32[256,512]{1,0:T(8,128)} %get-tuple-element.46), channel_id=1, source_target_pairs={{0,32},{2,34},{4,36},{6,38},{8,40},{10,42},{12,44},{14,46},{16,48}... | collective-permute-start | bytes 1572872 | tf_op jit(solution)/shard_map/ppermute | solution.py:31
  363.6 25.7 %collective-permute-start.8 = (f32[256,512]{1,0:T(8,128)}, f32[256,512]{1,0:T(8,128)}, u32[]{:S(2)}, u32[]{:S(2)}) collective-permute-start(f32[256,512]{1,0:T(8,128)} %get-tuple-element.48), channel_id=1, source_target_pairs={{0,64},{2,66},{4,68},{6,70},{8,72},{10,74},{12,76},{14,78},{16,80}... | collective-permute-start | bytes 1572872 | tf_op jit(solution)/shard_map/ppermute | solution.py:31
  366.1 23.2 %collective-permute-start.9 = (f32[256,512]{1,0:T(8,128)}, f32[256,512]{1,0:T(8,128)}, u32[]{:S(2)}, u32[]{:S(2)}) collective-permute-start(f32[256,512]{1,0:T(8,128)} %get-tuple-element.47), channel_id=1, source_target_pairs={{0,96},{2,98},{4,100},{6,102},{8,104},{10,106},{12,108},{14,110},{... | collective-permute-start | bytes 1572872 | tf_op jit(solution)/shard_map/ppermute | solution.py:31
  370.9 74.9 %collective-permute-start.14 = (f32[512,512]{0,1:T(8,128)}, f32[512,512]{0,1:T(8,128)}, u32[]{:S(2)}, u32[]{:S(2)}) collective-permute-start(f32[512,512]{0,1:T(8,128)} %get-tuple-element.43), channel_id=1, source_target_pairs={{0,2},{2,4},{4,6},{6,8},{8,10},{10,12},{12,14},{14,16},{16,18},{18... | collective-permute-start | bytes 3145736 | tf_op jit(solution)/shard_map/ppermute | solution.py:21
  373.5 72.3 %collective-permute-start.15 = (f32[512,512]{0,1:T(8,128)}, f32[512,512]{0,1:T(8,128)}, u32[]{:S(2)}, u32[]{:S(2)}) collective-permute-start(f32[512,512]{0,1:T(8,128)} %get-tuple-element.42), channel_id=1, source_target_pairs={{0,16},{2,18},{4,20},{6,22},{8,24},{10,26},{12,28},{14,30},{16,32}... | collective-permute-start | bytes 3145736 | tf_op jit(solution)/shard_map/ppermute | solution.py:21
  377.1 68.7 %collective-permute-start.16 = (f32[512,512]{0,1:T(8,128)}, f32[512,512]{0,1:T(8,128)}, u32[]{:S(2)}, u32[]{:S(2)}) collective-permute-start(f32[512,512]{0,1:T(8,128)} %get-tuple-element.41), channel_id=1, source_target_pairs={{0,18},{2,20},{4,22},{6,24},{8,26},{10,28},{12,30},{14,32},{16,34}... | collective-permute-start | bytes 3145736 | tf_op jit(solution)/shard_map/ppermute | solution.py:21
  391.1 0.8 copy-start.11
  391.9 44.9 %collective-permute-start.10 = (f32[64,512]{1,0:T(8,128)S(1)}, f32[64,512]{1,0:T(8,128)S(1)}, u32[]{:S(2)}, u32[]{:S(2)}) collective-permute-start(f32[64,512]{1,0:T(8,128)S(1)} %get-tuple-element.49), channel_id=1, source_target_pairs={{0,8},{2,10},{4,12},{6,14},{8,16},{10,18},{12,20},{14,22},{16,24},... | collective-permute-start | bytes 393224 | tf_op jit(solution)/shard_map/ppermute | solution.py:31
  392.0 47.6 %collective-permute-start.11 = (f32[64,512]{1,0:T(8,128)S(1)}, f32[64,512]{1,0:T(8,128)}, u32[]{:S(2)}, u32[]{:S(2)}) collective-permute-start(f32[64,512]{1,0:T(8,128)S(1)} %get-tuple-element.51), channel_id=1, source_target_pairs={{0,16},{2,18},{4,20},{6,22},{8,24},{10,26},{12,28},{14,30},{16,0},... | collective-permute-start | bytes 393224 | tf_op jit(solution)/shard_map/ppermute | solution.py:31
  436.8 4.7 collective-permute-start.12
  442.6 3.2 collective-permute-start.13
  445.8 3.2 collective-permute-start.17
  449.1 6.5 %collective-permute-start.18 = (f32[64,512]{1,0:T(8,128)S(1)}, f32[64,512]{1,0:T(8,128)S(1)}, u32[]{:S(2)}, u32[]{:S(2)}) collective-permute-start(f32[64,512]{1,0:T(8,128)S(1)} %pad_maximum_fusion.14), channel_id=1, source_target_pairs={{0,8},{2,10},{4,12},{6,14},{8,16},{10,18},{12,20},{14,22},{16,24},... | collective-permute-start | bytes 393224 | tf_op jit(solution)/shard_map/ppermute | solution.py:31
  449.2 7.0 %collective-permute-start.19 = (f32[64,512]{1,0:T(8,128)S(1)}, f32[64,512]{1,0:T(8,128)S(1)}, u32[]{:S(2)}, u32[]{:S(2)}) collective-permute-start(f32[64,512]{1,0:T(8,128)S(1)} %pad_maximum_fusion.14), channel_id=1, source_target_pairs={{0,16},{2,18},{4,20},{6,22},{8,24},{10,26},{12,28},{14,30},{16,0},... | collective-permute-start | bytes 393224 | tf_op jit(solution)/shard_map/ppermute | solution.py:31
  451.5 5.4 %collective-permute-start.20 = (f32[64,512]{1,0:T(8,128)S(1)}, f32[64,512]{1,0:T(8,128)S(1)}, u32[]{:S(2)}, u32[]{:S(2)}) collective-permute-start(f32[64,512]{1,0:T(8,128)S(1)} %pad_maximum_fusion.14), channel_id=1, source_target_pairs={{0,24},{2,26},{4,28},{6,30},{8,0},{10,2},{12,4},{14,6},{16,8},{18,... | collective-permute-start | bytes 393224 | tf_op jit(solution)/shard_map/ppermute | solution.py:31
  457.6 11.1 %collective-permute-start.21 = (f32[256,512]{1,0:T(8,128)}, f32[256,512]{1,0:T(8,128)}, u32[]{:S(2)}, u32[]{:S(2)}) collective-permute-start(f32[256,512]{1,0:T(8,128)} %bitcast.81), channel_id=1, source_target_pairs={{0,32},{2,34},{4,36},{6,38},{8,40},{10,42},{12,44},{14,46},{16,48}... | collective-permute-start | bytes 1572872 | tf_op jit(solution)/shard_map/ppermute | solution.py:31
  457.6 20.6 %collective-permute-start.22 = (f32[256,512]{1,0:T(8,128)}, f32[256,512]{1,0:T(8,128)}, u32[]{:S(2)}, u32[]{:S(2)}) collective-permute-start(f32[256,512]{1,0:T(8,128)} %bitcast.81), channel_id=1, source_target_pairs={{0,64},{2,66},{4,68},{6,70},{8,72},{10,74},{12,76},{14,78},{16,80}... | collective-permute-start | bytes 1572872 | tf_op jit(solution)/shard_map/ppermute | solution.py:31
  459.3 30.0 %copy-start.4 = (f32[3,512,512]{1,2,0:T(8,128)S(1)}, f32[3,512,512]{1,2,0:T(8,128)}, u32[]{:S(2)}) copy-start(f32[3,512,512]{1,2,0:T(8,128)} %copy-done.3) | copy-start | bytes 9437188
  459.3 23.8 %collective-permute-start.23 = (f32[256,512]{1,0:T(8,128)}, f32[256,512]{1,0:T(8,128)S(1)}, u32[]{:S(2)}, u32[]{:S(2)}) collective-permute-start(f32[256,512]{1,0:T(8,128)} %bitcast.81), channel_id=1, source_target_pairs={{0,96},{2,98},{4,100},{6,102},{8,104},{10,106},{12,108},{14,110},{... | collective-permute-start | bytes 1572872 | tf_op jit(solution)/shard_map/ppermute | solution.py:31
  483.9 23.0 %collective-permute-start.24 = (f32[1024,512]{1,0:T(8,128)}, f32[1024,512]{1,0:T(8,128)}, u32[]{:S(2)}, u32[]{:S(2)}) collective-permute-start(f32[1024,512]{1,0:T(8,128)} %bitcast.85), channel_id=1, source_target_pairs={{0,2},{2,0},{4,6},{6,4},{8,10},{10,8},{12,14},{14,12},{16,18},{18,... | collective-permute-start | bytes 6291464 | tf_op jit(solution)/shard_map/ppermute | solution.py:31

commit v3 on v2

--- a/solution.py
+++ b/solution.py
@@ -3,6 +3,8 @@
 import jax
 import jax.numpy as jnp
 from jax import lax
+from jax.experimental import pallas as pl
+from jax.experimental.pallas import tpu as pltpu
 from jax.sharding import PartitionSpec as P
 
 GCOLS = 8
@@ -142,6 +144,71 @@
     return jnp.einsum(
         "bcpq,dcqk->bdpk", first_section, matrix_table, preferred_element_type=jnp.float32
     )
+
+
+def complex_table(matrix_table, transposed):
+    if transposed:
+        rows = [jnp.concatenate([matrix_table[0, c], matrix_table[1, c]], axis=1) for c in range(2)]
+    else:
+        rows = [jnp.concatenate([matrix_table[d, 0], matrix_table[d, 1]], axis=1) for d in range(2)]
+    return jnp.concatenate(rows, axis=0)
+
+
+def forward_kernel(patch_ref, probe_ref, amp_ref, left_ref, right_ref, out_ref, far_ref):
+    side = patch_ref.shape[-1]
+    modes = probe_ref.shape[0]
+    obj_real = patch_ref[0, 0]
+    obj_imag = patch_ref[0, 1]
+
+    def one_mode(mode, intensity):
+        probe_real = probe_ref[mode, 0]
+        probe_imag = probe_ref[mode, 1]
+        exit_real = (obj_real * probe_real - obj_imag * probe_imag).astype(jnp.bfloat16)
+        exit_imag = (obj_real * probe_imag + obj_imag * probe_real).astype(jnp.bfloat16)
+        stacked = jnp.concatenate([exit_real, exit_imag], axis=0)
+        half = jnp.dot(left_ref[...], stacked, preferred_element_type=jnp.float32).astype(jnp.bfloat16)
+        wide = jnp.concatenate([half[:side], half[side:]], axis=1)
+        far = jnp.dot(wide, right_ref[...], preferred_element_type=jnp.float32)
+        far_ref[mode] = far
+        return intensity + far[:, :side] * far[:, :side] + far[:, side:] * far[:, side:]
+
+    intensity = lax.fori_loop(0, modes, one_mode, jnp.zeros((side, side), jnp.float32))
+    ratio = amp_ref[0] / jnp.maximum(jnp.sqrt(intensity), amp_floor) - 1.0
+
+    def store(mode, carry):
+        far = far_ref[mode]
+        out_ref[0, mode, 0] = (far[:, :side] * ratio).astype(jnp.bfloat16)
+        out_ref[0, mode, 1] = (far[:, side:] * ratio).astype(jnp.bfloat16)
+        return carry
+
+    lax.fori_loop(0, modes, store, 0)
+
+
+def forward_correction(patch, all_modes, amplitudes, forward_table):
+    slots, _, side, _ = patch.shape
+    modes = all_modes.shape[0]
+    left = complex_table(forward_table, False)
+    right = complex_table(forward_table, True)
+    return pl.pallas_call(
+        forward_kernel,
+        grid=(slots,),
+        in_specs=[
+            pl.BlockSpec((1, 2, side, side), lambda s: (s, 0, 0, 0)),
+            pl.BlockSpec((modes, 2, side, side), lambda s: (0, 0, 0, 0), pipeline_mode=pl.Buffered(1)),
+            pl.BlockSpec((1, side, side), lambda s: (s, 0, 0)),
+            pl.BlockSpec((2 * side, 2 * side), lambda s: (0, 0), pipeline_mode=pl.Buffered(1)),
+            pl.BlockSpec((2 * side, 2 * side), lambda s: (0, 0), pipeline_mode=pl.Buffered(1)),
+        ],
+        out_specs=pl.BlockSpec((1, modes, 2, side, side), lambda s: (s, 0, 0, 0, 0)),
+        out_shape=jax.ShapeDtypeStruct((slots, modes, 2, side, side), jnp.bfloat16),
+        scratch_shapes=[pltpu.VMEM((modes, side, 2 * side), jnp.float32)],
+        compiler_params=pltpu.CompilerParams(vmem_limit_bytes=64 * 1024 * 1024),
+        cost_estimate=pl.CostEstimate(
+            flops=slots * modes * 4 * (2 * side) ** 2 * side,
+            bytes_accessed=slots * (modes + 3) * 2 * side * side * 4,
+            transcendentals=slots * side * side,
+        ),
+    )(patch, all_modes, amplitudes, left, right)
 
 
 def shards(object_tiles, probe_modes, amplitudes, offsets, counts):
@@ -193,16 +260,9 @@
     obj_imag = patch[:, 1][:, None]
     probe_real = all_modes[:, 0][None]
     probe_imag = all_modes[:, 1][None]
-    exit_real = obj_real * probe_real - obj_imag * probe_imag
-    exit_imag = obj_real * probe_imag + obj_imag * probe_real
-    exit_wave = jnp.stack([exit_real, exit_imag], axis=2).astype(jnp.bfloat16)
     forward_table = dft_tables(side, -1.0)
     inverse_table = dft_tables(side, 1.0)
-    far_field = transform(exit_wave.reshape(slots * modes_here, 2, side, side), forward_table)
-    far_field = far_field.reshape(slots, modes_here, 2, side, side)
-    intensity = jnp.sum(far_field * far_field, axis=(1, 2))
-    ratio = amplitudes[0] / jnp.maximum(jnp.sqrt(intensity), amp_floor)
-    correction = (far_field * (ratio - 1.0)[:, None, None]).astype(jnp.bfloat16)
+    correction = forward_correction(patch, all_modes, amplitudes[0], forward_table)
     live_slots = (jnp.arange(slots, dtype=jnp.int32) < counts[0]).astype(jnp.float32)
     back_wave = transform(
         correction.reshape(slots * modes_here, 2, side, side), inverse_table

time: 519 us -> 511 us (0.985)
  Pallas kernels: 0 us -> 42.1 us
  matrix products: 73.5 us -> 34.9 us
  other arithmetic: 131 us -> 119 us
  local copies, waits for them, and re-layouts: 102 us -> 96.8 us
    pallas_call x0 -> x1, Pallas kernels: none -> 42.1 us  [forward_correction(): pl.pallas_call(forward_kernel, grid=(slots,), in_specs=[pl.BlockSpec((1,...]
    dot_general x2 -> x1, matrix products: 73.5 us -> 34.9 us  [transform(): jnp.einsum('bcpq,dcqk->bdpk', first_section, matrix_table, preferred_elem...]
    dynamic_slice x4 -> x0, local copies, waits for them, and re-layouts: 13.5 us -> none  [shards(): lax.dynamic_slice(extended, (0, slot_offsets[slot_id, 0] - 1, slot_offset...]
    concatenate x0 -> x1, other arithmetic: none -> 10.1 us  [complex_table(): return jnp.concatenate(rows, axis=0)]
    reduce_sum x1 -> x0, other arithmetic: 8.31 us -> none  [shards(): intensity = jnp.sum(far_field * far_field, axis=(1, 2))]
    reduce_sum x0 -> x2, local copies, waits for them, and re-layouts: none -> 6.09 us  [the longest x1 3.72 us: shards(): grad_imag = jnp.sum(probe_real * back_imag - probe_imag * back_real, axis=1)]
    another operation x4 -> x5, other arithmetic: 25.9 us -> 20 us
where the time goes in v3:
time: 511 us; the launch traced here: 504 us
  waiting for transfers between devices  157 us (31%)
  other arithmetic  119 us (23%)
  local copies, waits for them, and re-layouts  96.8 us (19%)
  Pallas kernels  42.1 us (8%)
  matrix products  34.9 us (7%)
  starting transfers between devices  31.9 us (6%)
  between operations  21 us (4%)
    ppermute x16, waiting for transfers between devices, sub_shift(): return lax.ppermute(value, 'scan', pairs)  96.1 us
    ppermute x5, waiting for transfers between devices, from_behind(): return lax.ppermute(value, axis, pairs)  61.4 us
    pallas_call x1, Pallas kernels, forward_correction(): pl.pallas_call(forward_kernel, grid=(slots,), in_specs=[pl.BlockSpec((1,...  42.1 us
    dot_general x1, matrix products, transform(): jnp.einsum('bcpq,dcqk->bdpk', first_section, matrix_table, preferred_elem...  34.9 us
    dynamic_update_slice x3, local copies, waits for them, and re-layouts, shards(): lax.dynamic_update_slice(gradient_plane, current + mine[slot_id, 0], start)  23.8 us
    another operation x5, other arithmetic  20 us
    mul x1, other arithmetic, shards(): back_wave = back_wave * live_slots[:, None, None, None, None]  19.3 us
    ppermute x16, starting transfers between devices, sub_shift(): return lax.ppermute(value, 'scan', pairs)  16.5 us
  transfers between devices with their start and end apart: 25, of which 13 were waited for; matrix products, arithmetic and copies ran while one was open for 16% of the time, Pallas kernels for 0%

profile of v3, /device:TPU:65, one launch (start us, length us, event | category | flops | bytes accessed | tf_op | source)
XLA Modules:
  0.0 503.7 jit_solution(17950680519568713096)
XLA Ops:
  0.6 5.2 %collective-permute-start.1 = (f32[2,512,512]{2,1,0:T(8,128)}, f32[2,512,512]{2,1,0:T(8,128)}, u32[]{:S(2)}, u32[]{:S(2)}) collective-permute-start(f32[2,512,512]{2,1,0:T(8,128)} %bitcast), channel_id=1, source_target_pairs={{0,112},{2,114},{4,116},{6,118},{8,120},{10,122},{12,124},{14,126}... | collective-permute-start | bytes 6291464 | tf_op jit(solution)/shard_map/ppermute | solution.py:23
  5.8 3.1 dynamic-slice_bitcast_fusion.5
  10.2 61.4 %collective-permute-done.1 = f32[2,512,512]{2,1,0:T(8,128)} collective-permute-done((f32[2,512,512]{2,1,0:T(8,128)}, f32[2,512,512]{2,1,0:T(8,128)}, u32[]{:S(2)}, u32[]{:S(2)}) %collective-permute-start.1) | collective-permute-done | bytes 2097184 | tf_op jit(solution)/shard_map/ppermute | solution.py:23
  71.5 4.9 collective-permute-start.2
  97.1 4.0 multiply_convert_fusion
  101.0 4.0 multiply_convert_fusion.1
  105.0 4.0 multiply_convert_fusion.2
  109.0 4.0 negate_convert_fusion
  113.1 4.0 negate_convert_fusion.1
  119.2 10.1 %fusion.13 = (bf16[1024,1024]{1,0:T(8,128)(2,1)}, bf16[1024,1024]{1,0:T(8,128)(2,1)}) fusion(bf16[512,512]{1,0:T(8,128)(2,1)S(1)} %get-tuple-element.59, bf16[512,512]{1,0:T(8,128)(2,1)S(1)} %get-tuple-element.43, bf16[512,512]{1,0:T(8,128)(2,1)S(1)} %get-tuple-element.60, bf16[512,512]{1,0:T(8,128)(2,1)S(1)} %get-tuple-element.42), kind=kLoop, calls=%fused_computation.42 | loop fusion | flops 14680064 | bytes 6291456 | tf_op jit(solution)/shard_map/concatenate | solution.py:154
  129.8 3.2 maximum_maximum_fusion
  136.2 5.1 %slice.139.patch_ref = f32[3,2,512,512]{3,2,1,0:T(8,128)} slice(f32[3,2,514,514]{3,2,1,0:T(8,128)S(1)} %pad_maximum_fusion), slice={[0:3], [0:2], [1:513], [1:513]} | slice | bytes 12582912 | tf_op jit(solution)/shard_map/slice | solution.py:256
  141.2 4.9 slice_bitcast_fusion.5
  146.1 2.9 select_bitcast_fusion.1
  151.3 4.8 slice_bitcast_fusion.3
  157.2 5.2 %copy.25 = f32[4,512,512]{1,2,0:T(8,128)} copy(f32[4,512,512]{2,1,0:T(8,128)} %get-tuple-element.21) | data formatting | bytes 8388608 | tf_op jit(solution)/shard_map/mul | solution.py:277
  162.4 5.2 %copy.26 = f32[4,512,512]{1,2,0:T(8,128)} copy(f32[4,512,512]{2,1,0:T(8,128)} %get-tuple-element.22) | data formatting | bytes 8388608 | tf_op jit(solution)/shard_map/mul | solution.py:277
  167.6 42.1 %shard_map.76 = bf16[3,4,2,512,512]{4,3,2,1,0:T(8,128)(2,1)} custom-call(f32[3,2,512,512]{3,2,1,0:T(8,128)} %slice.139.patch_ref, f32[4,2,512,512]{3,2,1,0:T(8,128)} %copy-done.1, f32[3,512,512]{2,1,0:T(8,128)} %bitcast.188, bf16[1024,1024]{1,0:T(8,128)(2,1)} %get-tuple-element.39.left_ref, bf16[1024,1024]{1,0:T(8,128)(2,1)} %get-tuple-element.38.right_ref), custom_call_target="tpu_custom_call" | custom-call | flops 25769803776 | bytes 44040192 | tf_op jit(solution)/shard_map/pallas_call | solution.py:192
  209.7 34.9 %fusion.1 = f32[2,512,12,512,1]{3,1,4,2,0:T(8,128)} fusion(bf16[12,2,512,512,1]{3,2,1,4,0:T(8,128)(2,1)} %bitcast.189, bf16[1,2,512,512]{3,2,1,0:T(8,128)(2,1)} %get-tuple-element.50, bf16[1,2,512,512]{3,2,1,0:T(8,128)(2,1)} %get-tuple-element.47), kind=kOutput, calls=%fused_computation.2 | convolution fusion | flops 25784483840 | bytes 39845888 | tf_op jit(solution)/shard_map/bcpq,dcqk->bdpk/dot_general | solution.py:144
  244.6 19.3 %broadcast_multiply_fusion = f32[3,4,2,512,512]{3,4,1,0,2:T(8,128)} fusion(f32[3,4,2,512,512]{3,4,1,0,2:T(8,128)} %bitcast.174, f32[3]{0:T(128)S(1)} %copy-done.10), kind=kLoop, calls=%fused_computation.7 | loop fusion | flops 6291456 | bytes 50331660 | tf_op jit(solution)/shard_map/mul | solution.py:270
  263.9 13.2 %subtract_reduce_fusion = (f32[3,512,512]{1,2,0:T(8,128)}, f32[3,512,512]{1,2,0:T(8,128)}) fusion(f32[3,4,2,512,512]{3,4,1,0,2:T(8,128)} %broadcast_multiply_fusion, f32[4,512,512]{1,2,0:T(8,128)S(1)} %copy-done.4, f32[4,512,512]{1,2,0:T(8,128)S(1)} %copy-done.3), kind=kLoop, calls=%fused_computation.5 | loop fusion | flops 23592960 | bytes 39845888 | tf_op jit(solution)/shard_map/reduce_sum | solution.py:278
  279.4 3.7 copy.28
  283.2 2.7 fusion.11
  291.1 7.8 %dynamic_update_slice.35 = f32[1024,1024]{1,0:T(8,128)} dynamic-update-slice(f32[1024,1024]{1,0:T(8,128)} %broadcast_in_dim.44, f32[512,512]{1,0:T(8,128)} %slice_bitcast_fusion.8, s32[]{:T(128)S(6)} %select_n.312, s32[]{:T(128)S(6)} %select_n.313) | dynamic-update-slice | bytes 2097156 | tf_op jit(solution)/shard_map/dynamic_update_slice | solution.py:288
  298.9 3.0 fusion.25
  301.9 8.0 %dynamic_update_slice.36 = f32[1024,1024]{1,0:T(8,128)} dynamic-update-slice(f32[1024,1024]{1,0:T(8,128)} %dynamic_update_slice.35, f32[512,512]{1,0:T(8,128)} %fusion.25, s32[]{:T(128)S(6)} %select_n.314, s32[]{:T(128)S(6)} %select_n.315) | dynamic-update-slice | bytes 2097156 | tf_op jit(solution)/shard_map/dynamic_update_slice | solution.py:288
  309.9 3.0 fusion.24
  312.8 8.0 %dynamic_update_slice.37 = f32[1024,1024]{1,0:T(8,128)} dynamic-update-slice(f32[1024,1024]{1,0:T(8,128)} %dynamic_update_slice.36, f32[512,512]{1,0:T(8,128)} %fusion.24, s32[]{:T(128)S(6)} %select_n.316, s32[]{:T(128)S(6)} %select_n.317) | dynamic-update-slice | bytes 2097156 | tf_op jit(solution)/shard_map/dynamic_update_slice | solution.py:288
  320.8 3.5 copy.20
  324.3 3.6 copy.24
  327.9 8.1 %add_reduce_fusion.1 = (f32[2,512,512]{1,2,0:T(8,128)S(1)}, f32[2,512,512]{1,2,0:T(8,128)S(1)}) fusion(f32[3,4,2,512,512]{3,4,1,0,2:T(8,128)} %broadcast_multiply_fusion, s32[]{:T(128)S(6)} %select_n.310, s32[]{:T(128)S(6)} %add.370, f32[3,512,512]{1,2,0:T(8,128)} %copy.24, f32[3,512,512]{1,2,0:T(8,128)} %copy.20), kind=kLoop, calls=%fused_computation.25 | loop fusion | flops 11534336 | bytes 23068680 | tf_op jit(solution)/shard_map/reduce_sum | solution.py:272
  338.5 5.2 %copy.29 = f32[2,2,512,512]{3,2,1,0:T(8,128)} copy(f32[2,2,512,512]{2,3,0,1:T(8,128)} %pad_maximum_fusion.2) | data formatting | bytes 8388608 | tf_op jit(solution)/shard_map/optimization_barrier | solution.py:289
  343.7 3.2 constant_dynamic-slice_fusion.1
  348.8 4.1 collective-permute-done.6
  352.9 2.7 dynamic-slice_add_fusion
  362.8 3.6 fusion.36
  368.8 4.0 collective-permute-done.7
  374.3 10.9 %collective-permute-done.8 = f32[256,512]{1,0:T(8,128)} collective-permute-done((f32[256,512]{1,0:T(8,128)}, f32[256,512]{1,0:T(8,128)}, u32[]{:S(2)}, u32[]{:S(2)}) %collective-permute-start.8) | collective-permute-done | bytes 524320 | tf_op jit(solution)/shard_map/ppermute | solution.py:33
  387.9 44.7 %collective-permute-done.10 = f32[64,512]{1,0:T(8,128)S(1)} collective-permute-done((f32[64,512]{1,0:T(8,128)S(1)}, f32[64,512]{1,0:T(8,128)S(1)}, u32[]{:S(2)}, u32[]{:S(2)}) %collective-permute-start.10) | collective-permute-done | bytes 131104 | tf_op jit(solution)/shard_map/ppermute | solution.py:33
  432.7 2.7 collective-permute-done.11
  438.5 3.1 collective-permute-done.13
  441.7 3.1 collective-permute-done.17
  457.6 7.1 %collective-permute-done.21 = f32[256,512]{1,0:T(8,128)} collective-permute-done((f32[256,512]{1,0:T(8,128)}, f32[256,512]{1,0:T(8,128)}, u32[]{:S(2)}, u32[]{:S(2)}) %collective-permute-start.21) | collective-permute-done | bytes 524320 | tf_op jit(solution)/shard_map/ppermute | solution.py:33
  465.8 8.4 %collective-permute-done.22 = f32[256,512]{1,0:T(8,128)} collective-permute-done((f32[256,512]{1,0:T(8,128)}, f32[256,512]{1,0:T(8,128)}, u32[]{:S(2)}, u32[]{:S(2)}) %collective-permute-start.22) | collective-permute-done | bytes 524320 | tf_op jit(solution)/shard_map/ppermute | solution.py:33
  475.2 3.9 collective-permute-done.23
  479.2 3.9 collective-permute-start.24
  483.0 13.0 %fusion.8 = (f32[3]{0:T(128)S(1)}, f32[3]{0:T(128)S(1)}) fusion(f32[3,2,514,514]{3,2,1,0:T(8,128)} %copy-done, f32[3,1,512,512]{3,2,1,0:T(8,128)S(1)} %bitcast.173, f32[3,1,512,512]{3,2,1,0:T(8,128)S(1)} %bitcast.171), kind=kLoop, calls=%fused_computation.21 | loop fusion | flops 14155770 | bytes 31457304 | tf_op jit(solution)/shard_map/reduce_sum | solution.py:280
  496.6 3.6 add_bitcast_fusion
  (91 shorter events, 58.9 us)
Async XLA Ops:
  0.6 75.8 %copy-start.9 = (s32[1,3,2]{1,2,0:T(2,128)S(1)}, s32[1,3,2]{1,2,0:T(2,128)}, u32[]{:S(2)}) copy-start(s32[1,3,2]{1,2,0:T(2,128)} %param.8) | copy-start | bytes 76
  0.6 70.9 %collective-permute-start.1 = (f32[2,512,512]{2,1,0:T(8,128)}, f32[2,512,512]{2,1,0:T(8,128)}, u32[]{:S(2)}, u32[]{:S(2)}) collective-permute-start(f32[2,512,512]{2,1,0:T(8,128)} %bitcast), channel_id=1, source_target_pairs={{0,112},{2,114},{4,116},{6,118},{8,120},{10,122},{12,124},{14,126}... | collective-permute-start | bytes 6291464 | tf_op jit(solution)/shard_map/ppermute | solution.py:23
  8.9 109.9 %collective-permute-start.4 = (f32[2,512,512]{2,1,0:T(8,128)}, f32[2,512,512]{2,1,0:T(8,128)}, u32[]{:S(2)}, u32[]{:S(2)}) collective-permute-start(f32[2,512,512]{2,1,0:T(8,128)} %dynamic-slice_bitcast_fusion.5), channel_id=1, source_target_pairs={{0,5},{1,4},{2,7},{3,6},{4,1},{5,0},{6,3},{7,2},{8,13},{9,12},{10,... | collective-permute-start | bytes 6291464 | tf_op jit(solution)/shard_map/ppermute | solution.py:223
  8.9 120.4 %collective-permute-start.3 = (f32[2,512,512]{2,1,0:T(8,128)}, f32[2,512,512]{2,1,0:T(8,128)S(1)}, u32[]{:S(2)}, u32[]{:S(2)}) collective-permute-start(f32[2,512,512]{2,1,0:T(8,128)} %bitcast), channel_id=1, source_target_pairs={{20,2},{24,6},{28,10},{32,14},{36,18},{40,22},{44,26},{48,30},{52,... | collective-permute-start | bytes 6291464 | tf_op jit(solution)/shard_map/ppermute | solution.py:236
  71.5 57.7 %collective-permute-start.2 = (f32[2,512,512]{2,1,0:T(8,128)}, f32[2,512,512]{2,1,0:T(8,128)}, u32[]{:S(2)}, u32[]{:S(2)}) collective-permute-start(f32[2,512,512]{2,1,0:T(8,128)} %collective-permute-done.1), channel_id=1, source_target_pairs={{2,0},{6,4},{10,8},{14,12},{18,16},{22,20},{26,24},{30,28},{34,32}... | collective-permute-start | bytes 6291464 | tf_op jit(solution)/shard_map/ppermute | solution.py:240
  76.4 53.3 %collective-permute-start = (f32[2,512,512]{2,1,0:T(8,128)}, f32[2,512,512]{2,1,0:T(8,128)}, u32[]{:S(2)}, u32[]{:S(2)}) collective-permute-start(f32[2,512,512]{2,1,0:T(8,128)} %bitcast), channel_id=1, source_target_pairs={{0,126},{2,0},{4,2},{6,4},{8,6},{10,8},{12,10},{14,12},{16,14},{18... | collective-permute-start | bytes 6291464 | tf_op jit(solution)/shard_map/ppermute | solution.py:23
  118.8 27.3 %collective-permute-start.5 = (f32[2,512,512]{2,1,0:T(8,128)}, f32[2,512,512]{2,1,0:T(8,128)}, u32[]{:S(2)}, u32[]{:S(2)}) collective-permute-start(f32[2,512,512]{2,1,0:T(8,128)} %collective-permute-done.4), channel_id=1, source_target_pairs={{0,2},{2,0},{4,6},{6,4},{8,10},{10,8},{12,14},{14,12},{16,18},{18,... | collective-permute-start | bytes 6291464 | tf_op jit(solution)/shard_map/ppermute | solution.py:224
  136.2 5.1 %copy-start = (f32[3,2,514,514]{3,2,1,0:T(8,128)}, f32[3,2,514,514]{3,2,1,0:T(8,128)S(1)}, u32[]{:S(2)}) copy-start(f32[3,2,514,514]{3,2,1,0:T(8,128)S(1)} %pad_maximum_fusion) | copy-start | bytes 19022116
  146.1 3.4 copy-start.6
  151.3 5.9 %copy-start.1 = (f32[4,2,512,512]{3,2,1,0:T(8,128)}, f32[4,2,512,512]{3,2,1,0:T(8,128)S(1)}, u32[]{:S(2)}) copy-start(f32[4,2,512,512]{3,2,1,0:T(8,128)S(1)} %maximum_select_fusion.probe_ref) | copy-start | bytes 25165828
  209.7 34.9 %copy-start.10 = (f32[3]{0:T(128)S(1)}, f32[3]{0:T(128)}, u32[]{:S(2)}) copy-start(f32[3]{0:T(128)} %compare_convert_fusion) | copy-start | bytes 40
  244.6 19.3 %copy-start.3 = (f32[4,512,512]{1,2,0:T(8,128)S(1)}, f32[4,512,512]{1,2,0:T(8,128)}, u32[]{:S(2)}) copy-start(f32[4,512,512]{1,2,0:T(8,128)} %copy.25) | copy-start | bytes 12582916
  244.6 19.3 %copy-start.4 = (f32[4,512,512]{1,2,0:T(8,128)S(1)}, f32[4,512,512]{1,2,0:T(8,128)}, u32[]{:S(2)}) copy-start(f32[4,512,512]{1,2,0:T(8,128)} %copy.26) | copy-start | bytes 12582916
  285.9 1.6 copy-start.5
  346.8 6.1 %collective-permute-start.6 = (f32[1024,512]{1,0:T(8,128)}, f32[1024,512]{1,0:T(8,128)}, u32[]{:S(2)}, u32[]{:S(2)}) collective-permute-start(f32[1024,512]{1,0:T(8,128)} %constant_dynamic-slice_fusion.1), channel_id=1, source_target_pairs={{0,2},{2,0},{4,6},{6,4},{8,10},{10,8},{12,14},{14,12},{16,18},{18,... | collective-permute-start | bytes 6291464 | tf_op jit(solution)/shard_map/ppermute | solution.py:33
  355.6 1.4 copy-start.7
  358.2 14.7 %collective-permute-start.7 = (f32[256,512]{1,0:T(8,128)}, f32[256,512]{1,0:T(8,128)}, u32[]{:S(2)}, u32[]{:S(2)}) collective-permute-start(f32[256,512]{1,0:T(8,128)} %get-tuple-element.35), channel_id=1, source_target_pairs={{0,32},{2,34},{4,36},{6,38},{8,40},{10,42},{12,44},{14,46},{16,48}... | collective-permute-start | bytes 1572872 | tf_op jit(solution)/shard_map/ppermute | solution.py:33
  359.4 25.7 %collective-permute-start.8 = (f32[256,512]{1,0:T(8,128)}, f32[256,512]{1,0:T(8,128)}, u32[]{:S(2)}, u32[]{:S(2)}) collective-permute-start(f32[256,512]{1,0:T(8,128)} %get-tuple-element.37), channel_id=1, source_target_pairs={{0,64},{2,66},{4,68},{6,70},{8,72},{10,74},{12,76},{14,78},{16,80}... | collective-permute-start | bytes 1572872 | tf_op jit(solution)/shard_map/ppermute | solution.py:33
  361.9 23.2 %collective-permute-start.9 = (f32[256,512]{1,0:T(8,128)}, f32[256,512]{1,0:T(8,128)}, u32[]{:S(2)}, u32[]{:S(2)}) collective-permute-start(f32[256,512]{1,0:T(8,128)} %get-tuple-element.36), channel_id=1, source_target_pairs={{0,96},{2,98},{4,100},{6,102},{8,104},{10,106},{12,108},{14,110},{... | collective-permute-start | bytes 1572872 | tf_op jit(solution)/shard_map/ppermute | solution.py:33
  366.4 75.2 %collective-permute-start.14 = (f32[512,512]{1,0:T(8,128)}, f32[512,512]{1,0:T(8,128)}, u32[]{:S(2)}, u32[]{:S(2)}) collective-permute-start(f32[512,512]{1,0:T(8,128)} %get-tuple-element.32), channel_id=1, source_target_pairs={{0,2},{2,4},{4,6},{6,8},{8,10},{10,12},{12,14},{14,16},{16,18},{18... | collective-permute-start | bytes 3145736 | tf_op jit(solution)/shard_map/ppermute | solution.py:23
  368.8 72.8 %collective-permute-start.15 = (f32[512,512]{1,0:T(8,128)}, f32[512,512]{1,0:T(8,128)}, u32[]{:S(2)}, u32[]{:S(2)}) collective-permute-start(f32[512,512]{1,0:T(8,128)} %get-tuple-element.31), channel_id=1, source_target_pairs={{0,16},{2,18},{4,20},{6,22},{8,24},{10,26},{12,28},{14,30},{16,32}... | collective-permute-start | bytes 3145736 | tf_op jit(solution)/shard_map/ppermute | solution.py:23
  372.8 68.7 %collective-permute-start.16 = (f32[512,512]{1,0:T(8,128)}, f32[512,512]{1,0:T(8,128)}, u32[]{:S(2)}, u32[]{:S(2)}) collective-permute-start(f32[512,512]{1,0:T(8,128)} %get-tuple-element.30), channel_id=1, source_target_pairs={{0,18},{2,20},{4,22},{6,24},{8,26},{10,28},{12,30},{14,32},{16,34}... | collective-permute-start | bytes 3145736 | tf_op jit(solution)/shard_map/ppermute | solution.py:23
  386.9 0.8 copy-start.8
  387.7 44.9 %collective-permute-start.10 = (f32[64,512]{1,0:T(8,128)S(1)}, f32[64,512]{1,0:T(8,128)S(1)}, u32[]{:S(2)}, u32[]{:S(2)}) collective-permute-start(f32[64,512]{1,0:T(8,128)S(1)} %get-tuple-element.44), channel_id=1, source_target_pairs={{0,8},{2,10},{4,12},{6,14},{8,16},{10,18},{12,20},{14,22},{16,24},... | collective-permute-start | bytes 393224 | tf_op jit(solution)/shard_map/ppermute | solution.py:33
  387.8 47.6 %collective-permute-start.11 = (f32[64,512]{1,0:T(8,128)S(1)}, f32[64,512]{1,0:T(8,128)}, u32[]{:S(2)}, u32[]{:S(2)}) collective-permute-start(f32[64,512]{1,0:T(8,128)S(1)} %get-tuple-element.46), channel_id=1, source_target_pairs={{0,16},{2,18},{4,20},{6,22},{8,24},{10,26},{12,28},{14,30},{16,0},... | collective-permute-start | bytes 393224 | tf_op jit(solution)/shard_map/ppermute | solution.py:33
  432.6 4.7 collective-permute-start.12
  438.4 3.2 collective-permute-start.13
  441.6 3.2 collective-permute-start.17
  444.8 6.8 %collective-permute-start.18 = (f32[64,512]{1,0:T(8,128)S(1)}, f32[64,512]{1,0:T(8,128)S(1)}, u32[]{:S(2)}, u32[]{:S(2)}) collective-permute-start(f32[64,512]{1,0:T(8,128)S(1)} %pad_maximum_fusion.15), channel_id=1, source_target_pairs={{0,8},{2,10},{4,12},{6,14},{8,16},{10,18},{12,20},{14,22},{16,24},... | collective-permute-start | bytes 393224 | tf_op jit(solution)/shard_map/ppermute | solution.py:33
  445.2 7.0 %collective-permute-start.19 = (f32[64,512]{1,0:T(8,128)S(1)}, f32[64,512]{1,0:T(8,128)S(1)}, u32[]{:S(2)}, u32[]{:S(2)}) collective-permute-start(f32[64,512]{1,0:T(8,128)S(1)} %pad_maximum_fusion.15), channel_id=1, source_target_pairs={{0,16},{2,18},{4,20},{6,22},{8,24},{10,26},{12,28},{14,30},{16,0},... | collective-permute-start | bytes 393224 | tf_op jit(solution)/shard_map/ppermute | solution.py:33
  447.6 5.4 %collective-permute-start.20 = (f32[64,512]{1,0:T(8,128)S(1)}, f32[64,512]{1,0:T(8,128)S(1)}, u32[]{:S(2)}, u32[]{:S(2)}) collective-permute-start(f32[64,512]{1,0:T(8,128)S(1)} %pad_maximum_fusion.15), channel_id=1, source_target_pairs={{0,24},{2,26},{4,28},{6,30},{8,0},{10,2},{12,4},{14,6},{16,8},{18,... | collective-permute-start | bytes 393224 | tf_op jit(solution)/shard_map/ppermute | solution.py:33
  453.6 11.1 %collective-permute-start.21 = (f32[256,512]{1,0:T(8,128)}, f32[256,512]{1,0:T(8,128)}, u32[]{:S(2)}, u32[]{:S(2)}) collective-permute-start(f32[256,512]{1,0:T(8,128)} %bitcast.68), channel_id=1, source_target_pairs={{0,32},{2,34},{4,36},{6,38},{8,40},{10,42},{12,44},{14,46},{16,48}... | collective-permute-start | bytes 1572872 | tf_op jit(solution)/shard_map/ppermute | solution.py:33
  453.6 20.6 %collective-permute-start.22 = (f32[256,512]{1,0:T(8,128)}, f32[256,512]{1,0:T(8,128)}, u32[]{:S(2)}, u32[]{:S(2)}) collective-permute-start(f32[256,512]{1,0:T(8,128)} %bitcast.68), channel_id=1, source_target_pairs={{0,64},{2,66},{4,68},{6,70},{8,72},{10,74},{12,76},{14,78},{16,80}... | collective-permute-start | bytes 1572872 | tf_op jit(solution)/shard_map/ppermute | solution.py:33
  455.3 27.7 %copy-start.2 = (f32[3,512,512]{2,1,0:T(8,128)S(1)}, f32[3,512,512]{2,1,0:T(8,128)}, u32[]{:S(2)}) copy-start(f32[3,512,512]{2,1,0:T(8,128)} %copy.28) | copy-start | bytes 9437188
  455.3 23.8 %collective-permute-start.23 = (f32[256,512]{1,0:T(8,128)}, f32[256,512]{1,0:T(8,128)S(1)}, u32[]{:S(2)}, u32[]{:S(2)}) collective-permute-start(f32[256,512]{1,0:T(8,128)} %bitcast.68), channel_id=1, source_target_pairs={{0,96},{2,98},{4,100},{6,102},{8,104},{10,106},{12,108},{14,110},{... | collective-permute-start | bytes 1572872 | tf_op jit(solution)/shard_map/ppermute | solution.py:33
  479.2 21.0 %collective-permute-start.24 = (f32[1024,512]{1,0:T(8,128)S(1)}, f32[1024,512]{1,0:T(8,128)S(1)}, u32[]{:S(2)}, u32[]{:S(2)}) collective-permute-start(f32[1024,512]{1,0:T(8,128)S(1)} %bitcast.181), channel_id=1, source_target_pairs={{0,2},{2,0},{4,6},{6,4},{8,10},{10,8},{12,14},{14,12},{16,18},{18,... | collective-permute-start | bytes 6291464 | tf_op jit(solution)/shard_map/ppermute | solution.py:33

commit v4 on v3

--- a/solution.py
+++ b/solution.py
@@ -211,6 +211,94 @@
     )(patch, all_modes, amplitudes, left, right)
 
 
+def backward_kernel(comp_ref, count_ref, corr_ref, probe_ref, patch_ref, left_ref, right_ref, grad_ref, part_ref):
+    side = patch_ref.shape[-1]
+    modes = probe_ref.shape[0]
+    own_modes = part_ref.shape[0]
+    slot = pl.program_id(0)
+
+    @pl.when(slot == 0)
+    def _():
+        part_ref[...] = jnp.zeros(part_ref.shape, part_ref.dtype)
+
+    live = (slot < count_ref[0]).astype(jnp.float32)
+    first_own = comp_ref[0] * own_modes
+    obj_real = patch_ref[0, 0]
+    obj_imag = patch_ref[0, 1]
+
+    def one_mode(mode, carry):
+        grad_real, grad_imag = carry
+        stacked = jnp.concatenate([corr_ref[0, mode, 0], corr_ref[0, mode, 1]], axis=0)
+        half = jnp.dot(left_ref[...], stacked, preferred_element_type=jnp.float32).astype(jnp.bfloat16)
+        wide = jnp.concatenate([half[:side], half[side:]], axis=1)
+        back = jnp.dot(wide, right_ref[...], preferred_element_type=jnp.float32) * live
+        back_real = back[:, :side]
+        back_imag = back[:, side:]
+        probe_real = probe_ref[mode, 0]
+        probe_imag = probe_ref[mode, 1]
+        own = mode - first_own
+
+        @pl.when((own >= 0) & (own < own_modes))
+        def _():
+            index = jnp.clip(own, 0, own_modes - 1)
+            part_ref[index, 0] += obj_real * back_real + obj_imag * back_imag
+            part_ref[index, 1] += obj_real * back_imag - obj_imag * back_real
+
+        grad_real = grad_real + (probe_real * back_real + probe_imag * back_imag)
+        grad_imag = grad_imag + (probe_real * back_imag - probe_imag * back_real)
+        return grad_real, grad_imag
+
+    zeros = jnp.zeros((side, side), jnp.float32)
+    grad_real, grad_imag = lax.fori_loop(0, modes, one_mode, (zeros, zeros))
+    grad_ref[0, 0] = grad_real
+    grad_ref[0, 1] = grad_imag
+
+
+def backward_gradients(correction, all_modes, patch, component, count, own_modes, inverse_table):
+    slots, modes, _, side, _ = correction.shape
+    left = complex_table(inverse_table, False)
+    right = complex_table(inverse_table, True)
+    grid_spec = pltpu.PrefetchScalarGridSpec(
+        num_scalar_prefetch=2,
+        grid=(slots,),
+        in_specs=[
+            pl.BlockSpec((1, modes, 2, side, side), lambda s, c, n: (s, 0, 0, 0, 0)),
+            pl.BlockSpec((modes, 2, side, side), lambda s, c, n: (0, 0, 0, 0), pipeline_mode=pl.Buffered(1)),
+            pl.BlockSpec((1, 2, side, side), lambda s, c, n: (s, 0, 0, 0)),
+            pl.BlockSpec((2 * side, 2 * side), lambda s, c, n: (0, 0), pipeline_mode=pl.Buffered(1)),
+            pl.BlockSpec((2 * side, 2 * side), lambda s, c, n: (0, 0), pipeline_mode=pl.Buffered(1)),
+        ],
+        out_specs=[
+            pl.BlockSpec((1, 2, side, side), lambda s, c, n: (s, 0, 0, 0)),
+            pl.BlockSpec((own_modes, 2, side, side), lambda s, c, n: (0, 0, 0, 0)),
+        ],
+    )
+    return pl.pallas_call(
+        backward_kernel,
+        grid_spec=grid_spec,
+        out_shape=[
+            jax.ShapeDtypeStruct((slots, 2, side, side), jnp.float32),
+            jax.ShapeDtypeStruct((own_modes, 2, side, side), jnp.float32),
+        ],
+        compiler_params=pltpu.CompilerParams(
+            vmem_limit_bytes=64 * 1024 * 1024, dimension_semantics=("arbitrary",)
+        ),
+        cost_estimate=pl.CostEstimate(
+            flops=slots * modes * 4 * (2 * side) ** 2 * side,
+            bytes_accessed=slots * (modes + 4) * 2 * side * side * 4,
+            transcendentals=0,
+        ),
+    )(
+        jnp.reshape(component, (1,)).astype(jnp.int32),
+        jnp.reshape(count, (1,)).astype(jnp.int32),
+        correction,
+        all_modes,
+        patch,
+        left,
+        right,
+    )
+
+
 def shards(object_tiles, probe_modes, amplitudes, offsets, counts):
     side = probe_modes.shape[-1]
     tile_side = object_tiles.shape[-1]
@@ -263,20 +351,9 @@
     forward_table = dft_tables(side, -1.0)
     inverse_table = dft_tables(side, 1.0)
     correction = forward_correction(patch, all_modes, amplitudes[0], forward_table)
-    live_slots = (jnp.arange(slots, dtype=jnp.int32) < counts[0]).astype(jnp.float32)
-    back_wave = transform(
-        correction.reshape(slots * modes_here, 2, side, side), inverse_table
-    ).reshape(slots, modes_here, 2, side, side)
-    back_wave = back_wave * live_slots[:, None, None, None, None]
-    back_own = lax.dynamic_slice_in_dim(back_wave, component * own_modes, own_modes, axis=1)
-    probe_real_grad = jnp.sum(obj_real * back_own[:, :, 0] + obj_imag * back_own[:, :, 1], axis=0)
-    probe_imag_grad = jnp.sum(obj_real * back_own[:, :, 1] - obj_imag * back_own[:, :, 0], axis=0)
-    probe_partial = jnp.stack([probe_real_grad, probe_imag_grad], axis=1)
-    back_real = back_wave[:, :, 0]
-    back_imag = back_wave[:, :, 1]
-    grad_real = jnp.sum(probe_real * back_real + probe_imag * back_imag, axis=1)
-    grad_imag = jnp.sum(probe_real * back_imag - probe_imag * back_real, axis=1)
-    whole_grad = jnp.stack([grad_real, grad_imag], axis=1)
+    whole_grad, probe_partial = backward_gradients(
+        correction, all_modes, patch, component, counts[0], own_modes, inverse_table
+    )
     position_y = jnp.sum(whole_grad * grad_y, axis=(1, 2, 3))
     position_x = jnp.sum(whole_grad * grad_x, axis=(1, 2, 3))
     positions = jnp.stack([position_y, position_x], axis=1) / side

time: 511 us -> 438 us (0.86)
  Pallas kernels: 42.1 us -> 96.5 us
  local copies, waits for them, and re-layouts: 96.8 us -> 47.7 us
  other arithmetic: 119 us -> 76.6 us
  matrix products: 34.9 us -> 0 us
    pallas_call x0 -> x1, Pallas kernels: none -> 54.2 us  [backward_gradients(): pl.pallas_call(backward_kernel, grid_spec=grid_spec, out_shape=[jax.Shape...]
    dot_general x1 -> x0, matrix products: 34.9 us -> none  [transform(): jnp.einsum('bcpq,dcqk->bdpk', first_section, matrix_table, preferred_elem...]
    mul x6 -> x0, local copies, waits for them, and re-layouts: 27.2 us -> none  [the longest x3 15.2 us: shards(): grad_real = jnp.sum(probe_real * back_real + probe_imag * back_imag, axis=1)]
    reduce_sum x2 -> x0, other arithmetic: 21.3 us -> none  [the longest x1 13.2 us: shards(): grad_imag = jnp.sum(probe_real * back_imag - probe_imag * back_real, axis=1)]
    mul x1 -> x0, other arithmetic: 19.3 us -> none  [shards(): back_wave = back_wave * live_slots[:, None, None, None, None]]
    ppermute x16, waiting for transfers between devices: 96.1 us -> 104 us  [sub_shift(): return lax.ppermute(value, 'scan', pairs)]
    ppermute x5, waiting for transfers between devices: 61.4 us -> 54.5 us  [from_behind(): return lax.ppermute(value, axis, pairs)]
    reduce_sum x2 -> x0, local copies, waits for them, and re-layouts: 6.09 us -> none  [the longest x1 3.72 us: shards(): grad_imag = jnp.sum(probe_real * back_imag - probe_imag * back_real, axis=1)]
  transfers between devices with their start and end apart: 25 -> 25, of which waited for: 13 -> 14; matrix products, arithmetic and copies ran while one was open for 16% -> 18% of each run, Pallas kernels for 0% -> 0%
where the time goes in v4:
time: 438 us; the launch traced here: 430 us
  waiting for transfers between devices  159 us (36%)
  Pallas kernels  96.5 us (22%)
  other arithmetic  76.6 us (17%)
  local copies, waits for them, and re-layouts  47.7 us (11%)
  starting transfers between devices  29.8 us (7%)
  between operations  20.8 us (5%)
    ppermute x16, waiting for transfers between devices, sub_shift(): return lax.ppermute(value, 'scan', pairs)  104 us
    ppermute x5, waiting for transfers between devices, from_behind(): return lax.ppermute(value, axis, pairs)  54.5 us
    pallas_call x1, Pallas kernels, backward_gradients(): pl.pallas_call(backward_kernel, grid_spec=grid_spec, out_shape=[jax.Shape...  54.2 us
    pallas_call x1, Pallas kernels, forward_correction(): pl.pallas_call(forward_kernel, grid=(slots,), in_specs=[pl.BlockSpec((1,...  42.3 us
    dynamic_update_slice x3, local copies, waits for them, and re-layouts, shards(): lax.dynamic_update_slice(gradient_plane, current + mine[slot_id, 0], start)  22.9 us
    another operation x5, other arithmetic  19.9 us
    ppermute x16, starting transfers between devices, sub_shift(): return lax.ppermute(value, 'scan', pairs)  15.2 us
    reduce_sum x1, other arithmetic, shards(): position_y = jnp.sum(whole_grad * grad_y, axis=(1, 2, 3))  14.8 us
  transfers between devices with their start and end apart: 25, of which 14 were waited for; matrix products, arithmetic and copies ran while one was open for 18% of the time, Pallas kernels for 0%

profile of v4, /device:TPU:65, one launch (start us, length us, event | category | flops | bytes accessed | tf_op | source)
XLA Modules:
  0.0 429.9 jit_solution(7606449966415242740)
XLA Ops:
  0.6 5.2 %collective-permute-start.1 = (f32[2,512,512]{2,1,0:T(8,128)}, f32[2,512,512]{2,1,0:T(8,128)}, u32[]{:S(2)}, u32[]{:S(2)}) collective-permute-start(f32[2,512,512]{2,1,0:T(8,128)} %bitcast.1), channel_id=1, source_target_pairs={{0,112},{2,114},{4,116},{6,118},{8,120},{10,122},{12,124},{14,126}... | collective-permute-start | bytes 6291464 | tf_op jit(solution)/shard_map/ppermute | solution.py:23
  5.8 3.1 dynamic-slice_bitcast_fusion.3
  10.2 2.9 collective-permute-start
  13.1 4.0 multiply_convert_fusion
  17.1 54.4 %collective-permute-done.1 = f32[2,512,512]{2,1,0:T(8,128)} collective-permute-done((f32[2,512,512]{2,1,0:T(8,128)}, f32[2,512,512]{2,1,0:T(8,128)}, u32[]{:S(2)}, u32[]{:S(2)}) %collective-permute-start.1) | collective-permute-done | bytes 2097184 | tf_op jit(solution)/shard_map/ppermute | solution.py:23
  71.5 4.9 %collective-permute-start.2 = (f32[2,512,512]{2,1,0:T(8,128)}, f32[2,512,512]{2,1,0:T(8,128)}, u32[]{:S(2)}, u32[]{:S(2)}) collective-permute-start(f32[2,512,512]{2,1,0:T(8,128)} %collective-permute-done.1), channel_id=1, source_target_pairs={{2,0},{6,4},{10,8},{14,12},{18,16},{22,20},{26,24},{30,28},{34,32}... | collective-permute-start | bytes 6291464 | tf_op jit(solution)/shard_map/ppermute | solution.py:328
  76.4 4.0 multiply_convert_fusion.1
  80.4 4.0 multiply_convert_fusion.2
  84.4 4.0 negate_convert_fusion
  88.4 4.0 negate_convert_fusion.1
  115.5 4.1 fusion.9
  119.6 10.5 %fusion.7 = (bf16[1024,1024]{1,0:T(8,128)(2,1)}, bf16[1024,1024]{1,0:T(8,128)(2,1)}) fusion(bf16[512,512]{1,0:T(8,128)(2,1)S(1)} %copy-done.4, bf16[512,512]{1,0:T(8,128)(2,1)S(1)} %copy-done.3, bf16[512,512]{1,0:T(8,128)(2,1)S(1)} %copy-done.5, bf16[512,512]{1,0:T(8,128)(2,1)S(1)} %copy-done.2), kind=kLoop, calls=%fused_computation.24 | loop fusion | flops 14680064 | bytes 6291456 | tf_op jit(solution)/shard_map/concatenate | solution.py:154
  130.7 3.3 maximum_maximum_fusion
  134.0 2.1 dynamic-slice_bitcast_fusion.2
  136.7 5.1 %slice.126.patch_ref = f32[3,2,512,512]{3,2,1,0:T(8,128)} slice(f32[3,2,514,514]{3,2,1,0:T(8,128)S(1)} %pad_maximum_fusion), slice={[0:3], [0:2], [1:513], [1:513]} | slice | bytes 12582912 | tf_op jit(solution)/shard_map/slice | solution.py:344
  141.8 2.9 select_bitcast_fusion.1
  145.3 4.0 maximum_select_fusion.probe_ref
  149.3 42.3 %shard_map.76.corr_ref = bf16[3,4,2,512,512]{4,3,2,1,0:T(8,128)(2,1)} custom-call(f32[3,2,512,512]{3,2,1,0:T(8,128)} %slice.126.patch_ref, f32[4,2,512,512]{3,2,1,0:T(8,128)} %maximum_select_fusion.probe_ref, f32[3,512,512]{2,1,0:T(8,128)} %bitcast.124, bf16[1024,1024]{1,0:T(8,128)(2,1)} %get-tuple-element.37.left_ref, ...), custom_call_target="tpu_custom_call" | custom-call | flops 25769803776 | bytes 44040192 | tf_op jit(solution)/shard_map/pallas_call | solution.py:192
  191.6 54.2 %shard_map.77 = (f32[3,2,512,512]{3,2,1,0:T(8,128)}, f32[2,2,512,512]{3,2,1,0:T(8,128)}) custom-call(s32[1]{0:T(128)} %bitcast.comp_ref, s32[1]{0:T(128)S(6)} %copy.19.count_ref, bf16[3,4,2,512,512]{4,3,2,1,0:T(8,128)(2,1)} %shard_map.76.corr_ref, f32[4,2,512,512]{3,2,1,0:T(8,128)} %maximum_select_fusion.probe_ref, f32[3,2,512,512]{3,2,1,0:T(8,128)} %slice.126.patch_ref, ...), custom_call_target="tpu_custom_call" | custom-call | flops 25769803776 | bytes 50331648 | tf_op jit(solution)/shard_map/pallas_call | solution.py:276
  247.1 2.5 broadcast_in_dim.43
  249.6 7.5 %dynamic_update_slice.35 = f32[1024,1024]{1,0:T(8,128)} dynamic-update-slice(f32[1024,1024]{1,0:T(8,128)} %broadcast_in_dim.43, f32[512,512]{1,0:T(8,128)S(1)} %dynamic-slice_bitcast_fusion.6, s32[]{:T(128)S(6)} %select_n.308, s32[]{:T(128)S(6)} %select_n.309) | dynamic-update-slice | bytes 2097156 | tf_op jit(solution)/shard_map/dynamic_update_slice | solution.py:365
  257.1 2.0 fusion.18
  259.1 7.6 %dynamic_update_slice.36 = f32[1024,1024]{1,0:T(8,128)} dynamic-update-slice(f32[1024,1024]{1,0:T(8,128)} %dynamic_update_slice.35, f32[512,512]{1,0:T(8,128)S(1)} %fusion.18, s32[]{:T(128)S(6)} %select_n.310, s32[]{:T(128)S(6)} %select_n.311) | dynamic-update-slice | bytes 2097156 | tf_op jit(solution)/shard_map/dynamic_update_slice | solution.py:365
  266.7 2.0 fusion.17
  268.7 7.8 %dynamic_update_slice.37 = f32[1024,1024]{1,0:T(8,128)} dynamic-update-slice(f32[1024,1024]{1,0:T(8,128)} %dynamic_update_slice.36, f32[512,512]{1,0:T(8,128)S(1)} %fusion.17, s32[]{:T(128)S(6)} %select_n.312, s32[]{:T(128)S(6)} %select_n.313) | dynamic-update-slice | bytes 2097156 | tf_op jit(solution)/shard_map/dynamic_update_slice | solution.py:365
  276.5 1.8 constant_dynamic-slice_fusion.1
  278.2 1.6 collective-permute-start.6
  279.8 3.9 collective-permute-done.6
  283.7 2.7 dynamic-slice_add_fusion
  288.8 2.7 collective-permute-start.8
  292.5 3.6 fusion.27
  296.4 6.2 %collective-permute-done.7 = f32[256,512]{1,0:T(8,128)} collective-permute-done((f32[256,512]{1,0:T(8,128)}, f32[256,512]{1,0:T(8,128)}, u32[]{:S(2)}, u32[]{:S(2)}) %collective-permute-start.7) | collective-permute-done | bytes 524320 | tf_op jit(solution)/shard_map/ppermute | solution.py:33
  302.6 12.1 %collective-permute-done.8 = f32[256,512]{1,0:T(8,128)} collective-permute-done((f32[256,512]{1,0:T(8,128)S(1)}, f32[256,512]{1,0:T(8,128)}, u32[]{:S(2)}, u32[]{:S(2)}) %collective-permute-start.8) | collective-permute-done | bytes 524320 | tf_op jit(solution)/shard_map/ppermute | solution.py:33
  316.5 45.2 %collective-permute-done.10 = f32[64,512]{1,0:T(8,128)S(1)} collective-permute-done((f32[64,512]{1,0:T(8,128)S(1)}, f32[64,512]{1,0:T(8,128)S(1)}, u32[]{:S(2)}, u32[]{:S(2)}) %collective-permute-start.10) | collective-permute-done | bytes 131104 | tf_op jit(solution)/shard_map/ppermute | solution.py:33
  361.8 2.6 collective-permute-done.11
  364.4 1.9 collective-permute-done.12
  366.5 3.1 collective-permute-done.13
  369.7 3.1 collective-permute-done.17
  373.0 2.3 collective-permute-start.19
  375.7 3.7 collective-permute-done.18
  380.1 2.0 collective-permute-start.22
  383.6 7.2 %collective-permute-done.21 = f32[256,512]{1,0:T(8,128)S(1)} collective-permute-done((f32[256,512]{1,0:T(8,128)S(1)}, f32[256,512]{1,0:T(8,128)S(1)}, u32[]{:S(2)}, u32[]{:S(2)}) %collective-permute-start.21) | collective-permute-done | bytes 524320 | tf_op jit(solution)/shard_map/ppermute | solution.py:33
  390.8 9.4 %collective-permute-done.22 = f32[256,512]{1,0:T(8,128)S(1)} collective-permute-done((f32[256,512]{1,0:T(8,128)S(1)}, f32[256,512]{1,0:T(8,128)S(1)}, u32[]{:S(2)}, u32[]{:S(2)}) %collective-permute-start.22) | collective-permute-done | bytes 524320 | tf_op jit(solution)/shard_map/ppermute | solution.py:33
  400.2 5.2 %collective-permute-done.23 = f32[256,512]{1,0:T(8,128)S(1)} collective-permute-done((f32[256,512]{1,0:T(8,128)S(1)}, f32[256,512]{1,0:T(8,128)S(1)}, u32[]{:S(2)}, u32[]{:S(2)}) %collective-permute-start.23) | collective-permute-done | bytes 524320 | tf_op jit(solution)/shard_map/ppermute | solution.py:33
  405.5 2.1 collective-permute-start.24
  407.6 14.8 %fusion.5 = (f32[3]{0:T(128)S(1)}, f32[3]{0:T(128)S(1)}) fusion(f32[3,2,512,512]{3,2,1,0:T(8,128)} %get-tuple-element.12, f32[3,2,514,514]{3,2,1,0:T(8,128)} %copy-done), kind=kLoop, calls=%fused_computation.10 | loop fusion | flops 12582906 | bytes 31457304 | tf_op jit(solution)/shard_map/reduce_sum | solution.py:357
  423.0 3.6 add_bitcast_fusion
  427.2 2.5 pad_maximum_fusion.1
  (70 shorter events, 17.4 us)
Async XLA Ops:
  0.6 70.9 %collective-permute-start.1 = (f32[2,512,512]{2,1,0:T(8,128)}, f32[2,512,512]{2,1,0:T(8,128)}, u32[]{:S(2)}, u32[]{:S(2)}) collective-permute-start(f32[2,512,512]{2,1,0:T(8,128)} %bitcast.1), channel_id=1, source_target_pairs={{0,112},{2,114},{4,116},{6,118},{8,120},{10,122},{12,124},{14,126}... | collective-permute-start | bytes 6291464 | tf_op jit(solution)/shard_map/ppermute | solution.py:23
  8.9 86.4 %collective-permute-start.4 = (f32[2,512,512]{2,1,0:T(8,128)}, f32[2,512,512]{2,1,0:T(8,128)}, u32[]{:S(2)}, u32[]{:S(2)}) collective-permute-start(f32[2,512,512]{2,1,0:T(8,128)} %dynamic-slice_bitcast_fusion.3), channel_id=1, source_target_pairs={{0,5},{1,4},{2,7},{3,6},{4,1},{5,0},{6,3},{7,2},{8,13},{9,12},{10,... | collective-permute-start | bytes 6291464 | tf_op jit(solution)/shard_map/ppermute | solution.py:311
  8.9 121.3 %collective-permute-start.3 = (f32[2,512,512]{2,1,0:T(8,128)}, f32[2,512,512]{2,1,0:T(8,128)S(1)}, u32[]{:S(2)}, u32[]{:S(2)}) collective-permute-start(f32[2,512,512]{2,1,0:T(8,128)} %bitcast.1), channel_id=1, source_target_pairs={{20,2},{24,6},{28,10},{32,14},{36,18},{40,22},{44,26},{48,30},{52,... | collective-permute-start | bytes 6291464 | tf_op jit(solution)/shard_map/ppermute | solution.py:324
  10.2 120.5 %collective-permute-start = (f32[2,512,512]{2,1,0:T(8,128)}, f32[2,512,512]{2,1,0:T(8,128)}, u32[]{:S(2)}, u32[]{:S(2)}) collective-permute-start(f32[2,512,512]{2,1,0:T(8,128)} %bitcast.1), channel_id=1, source_target_pairs={{0,126},{2,0},{4,2},{6,4},{8,6},{10,8},{12,10},{14,12},{16,14},{18... | collective-permute-start | bytes 6291464 | tf_op jit(solution)/shard_map/ppermute | solution.py:23
  71.5 58.6 %collective-permute-start.2 = (f32[2,512,512]{2,1,0:T(8,128)}, f32[2,512,512]{2,1,0:T(8,128)}, u32[]{:S(2)}, u32[]{:S(2)}) collective-permute-start(f32[2,512,512]{2,1,0:T(8,128)} %collective-permute-done.1), channel_id=1, source_target_pairs={{2,0},{6,4},{10,8},{14,12},{18,16},{22,20},{26,24},{30,28},{34,32}... | collective-permute-start | bytes 6291464 | tf_op jit(solution)/shard_map/ppermute | solution.py:328
  92.7 2.6 copy-start.6
  95.3 46.5 %collective-permute-start.5 = (f32[2,512,512]{2,1,0:T(8,128)}, f32[2,512,512]{2,1,0:T(8,128)}, u32[]{:S(2)}, u32[]{:S(2)}) collective-permute-start(f32[2,512,512]{2,1,0:T(8,128)} %collective-permute-done.4), channel_id=1, source_target_pairs={{0,2},{2,0},{4,6},{6,4},{8,10},{10,8},{12,14},{14,12},{16,18},{18,... | collective-permute-start | bytes 6291464 | tf_op jit(solution)/shard_map/ppermute | solution.py:312
  115.4 4.2 copy-start.2
  115.5 4.2 copy-start.3
  115.5 4.2 copy-start.4
  115.5 4.1 copy-start.5
  136.7 5.1 %copy-start = (f32[3,2,514,514]{3,2,1,0:T(8,128)}, f32[3,2,514,514]{3,2,1,0:T(8,128)S(1)}, u32[]{:S(2)}) copy-start(f32[3,2,514,514]{3,2,1,0:T(8,128)S(1)} %pad_maximum_fusion) | copy-start | bytes 19022116
  141.8 3.4 copy-start.1
  278.2 5.5 %collective-permute-start.6 = (f32[1024,512]{1,0:T(8,128)S(1)}, f32[1024,512]{1,0:T(8,128)}, u32[]{:S(2)}, u32[]{:S(2)}) collective-permute-start(f32[1024,512]{1,0:T(8,128)S(1)} %constant_dynamic-slice_fusion.1), channel_id=1, source_target_pairs={{0,2},{2,0},{4,6},{6,4},{8,10},{10,8},{12,14},{14,12},{16,18},{18,... | collective-permute-start | bytes 6291464 | tf_op jit(solution)/shard_map/ppermute | solution.py:33
  287.4 15.2 %collective-permute-start.7 = (f32[256,512]{1,0:T(8,128)}, f32[256,512]{1,0:T(8,128)}, u32[]{:S(2)}, u32[]{:S(2)}) collective-permute-start(f32[256,512]{1,0:T(8,128)} %get-tuple-element.31), channel_id=1, source_target_pairs={{0,32},{2,34},{4,36},{6,38},{8,40},{10,42},{12,44},{14,46},{16,48}... | collective-permute-start | bytes 1572872 | tf_op jit(solution)/shard_map/ppermute | solution.py:33
  288.8 26.0 %collective-permute-start.8 = (f32[256,512]{1,0:T(8,128)S(1)}, f32[256,512]{1,0:T(8,128)}, u32[]{:S(2)}, u32[]{:S(2)}) collective-permute-start(f32[256,512]{1,0:T(8,128)S(1)} %get-tuple-element.33), channel_id=1, source_target_pairs={{0,64},{2,66},{4,68},{6,70},{8,72},{10,74},{12,76},{14,78},{16,80}... | collective-permute-start | bytes 1572872 | tf_op jit(solution)/shard_map/ppermute | solution.py:33
  291.5 23.2 %collective-permute-start.9 = (f32[256,512]{1,0:T(8,128)S(1)}, f32[256,512]{1,0:T(8,128)}, u32[]{:S(2)}, u32[]{:S(2)}) collective-permute-start(f32[256,512]{1,0:T(8,128)S(1)} %get-tuple-element.32), channel_id=1, source_target_pairs={{0,96},{2,98},{4,100},{6,102},{8,104},{10,106},{12,108},{14,110},{... | collective-permute-start | bytes 1572872 | tf_op jit(solution)/shard_map/ppermute | solution.py:33
  296.2 73.4 %collective-permute-start.14 = (f32[512,512]{1,0:T(8,128)}, f32[512,512]{1,0:T(8,128)}, u32[]{:S(2)}, u32[]{:S(2)}) collective-permute-start(f32[512,512]{1,0:T(8,128)} %get-tuple-element.28), channel_id=1, source_target_pairs={{0,2},{2,4},{4,6},{6,8},{8,10},{10,12},{12,14},{14,16},{16,18},{18... | collective-permute-start | bytes 3145736 | tf_op jit(solution)/shard_map/ppermute | solution.py:23
  296.2 73.4 %collective-permute-start.15 = (f32[512,512]{1,0:T(8,128)}, f32[512,512]{1,0:T(8,128)}, u32[]{:S(2)}, u32[]{:S(2)}) collective-permute-start(f32[512,512]{1,0:T(8,128)} %get-tuple-element.27), channel_id=1, source_target_pairs={{0,16},{2,18},{4,20},{6,22},{8,24},{10,26},{12,28},{14,30},{16,32}... | collective-permute-start | bytes 3145736 | tf_op jit(solution)/shard_map/ppermute | solution.py:23
  302.6 67.0 %collective-permute-start.16 = (f32[512,512]{1,0:T(8,128)}, f32[512,512]{1,0:T(8,128)}, u32[]{:S(2)}, u32[]{:S(2)}) collective-permute-start(f32[512,512]{1,0:T(8,128)} %get-tuple-element.26), channel_id=1, source_target_pairs={{0,18},{2,20},{4,22},{6,24},{8,26},{10,28},{12,30},{14,32},{16,34}... | collective-permute-start | bytes 3145736 | tf_op jit(solution)/shard_map/ppermute | solution.py:23
  316.4 45.4 %collective-permute-start.10 = (f32[64,512]{1,0:T(8,128)S(1)}, f32[64,512]{1,0:T(8,128)S(1)}, u32[]{:S(2)}, u32[]{:S(2)}) collective-permute-start(f32[64,512]{1,0:T(8,128)S(1)} %get-tuple-element.46), channel_id=1, source_target_pairs={{0,8},{2,10},{4,12},{6,14},{8,16},{10,18},{12,20},{14,22},{16,24},... | collective-permute-start | bytes 393224 | tf_op jit(solution)/shard_map/ppermute | solution.py:33
  316.4 48.0 %collective-permute-start.11 = (f32[64,512]{1,0:T(8,128)S(1)}, f32[64,512]{1,0:T(8,128)S(1)}, u32[]{:S(2)}, u32[]{:S(2)}) collective-permute-start(f32[64,512]{1,0:T(8,128)S(1)} %get-tuple-element.48), channel_id=1, source_target_pairs={{0,16},{2,18},{4,20},{6,22},{8,24},{10,26},{12,28},{14,30},{16,0},... | collective-permute-start | bytes 393224 | tf_op jit(solution)/shard_map/ppermute | solution.py:33
  361.7 4.6 %collective-permute-start.12 = (f32[64,512]{1,0:T(8,128)S(1)}, f32[64,512]{1,0:T(8,128)S(1)}, u32[]{:S(2)}, u32[]{:S(2)}) collective-permute-start(f32[64,512]{1,0:T(8,128)S(1)} %get-tuple-element.47), channel_id=1, source_target_pairs={{0,24},{2,26},{4,28},{6,30},{8,0},{10,2},{12,4},{14,6},{16,8},{18,... | collective-permute-start | bytes 393224 | tf_op jit(solution)/shard_map/ppermute | solution.py:33
  366.4 3.2 collective-permute-start.13
  369.6 3.2 collective-permute-start.17
  372.8 6.5 %collective-permute-start.18 = (f32[64,512]{1,0:T(8,128)S(1)}, f32[64,512]{1,0:T(8,128)S(1)}, u32[]{:S(2)}, u32[]{:S(2)}) collective-permute-start(f32[64,512]{1,0:T(8,128)S(1)} %pad_maximum_fusion.14), channel_id=1, source_target_pairs={{0,8},{2,10},{4,12},{6,14},{8,16},{10,18},{12,20},{14,22},{16,24},... | collective-permute-start | bytes 393224 | tf_op jit(solution)/shard_map/ppermute | solution.py:33
  373.0 6.4 %collective-permute-start.19 = (f32[64,512]{1,0:T(8,128)S(1)}, f32[64,512]{1,0:T(8,128)S(1)}, u32[]{:S(2)}, u32[]{:S(2)}) collective-permute-start(f32[64,512]{1,0:T(8,128)S(1)} %pad_maximum_fusion.14), channel_id=1, source_target_pairs={{0,16},{2,18},{4,20},{6,22},{8,24},{10,26},{12,28},{14,30},{16,0},... | collective-permute-start | bytes 393224 | tf_op jit(solution)/shard_map/ppermute | solution.py:33
  375.3 4.7 %collective-permute-start.20 = (f32[64,512]{1,0:T(8,128)S(1)}, f32[64,512]{1,0:T(8,128)S(1)}, u32[]{:S(2)}, u32[]{:S(2)}) collective-permute-start(f32[64,512]{1,0:T(8,128)S(1)} %pad_maximum_fusion.14), channel_id=1, source_target_pairs={{0,24},{2,26},{4,28},{6,30},{8,0},{10,2},{12,4},{14,6},{16,8},{18,... | collective-permute-start | bytes 393224 | tf_op jit(solution)/shard_map/ppermute | solution.py:33
  380.0 10.8 %collective-permute-start.21 = (f32[256,512]{1,0:T(8,128)S(1)}, f32[256,512]{1,0:T(8,128)S(1)}, u32[]{:S(2)}, u32[]{:S(2)}) collective-permute-start(f32[256,512]{1,0:T(8,128)S(1)} %bitcast.115), channel_id=1, source_target_pairs={{0,32},{2,34},{4,36},{6,38},{8,40},{10,42},{12,44},{14,46},{16,48}... | collective-permute-start | bytes 1572872 | tf_op jit(solution)/shard_map/ppermute | solution.py:33
  380.1 20.1 %collective-permute-start.22 = (f32[256,512]{1,0:T(8,128)S(1)}, f32[256,512]{1,0:T(8,128)S(1)}, u32[]{:S(2)}, u32[]{:S(2)}) collective-permute-start(f32[256,512]{1,0:T(8,128)S(1)} %bitcast.116), channel_id=1, source_target_pairs={{0,64},{2,66},{4,68},{6,70},{8,72},{10,74},{12,76},{14,78},{16,80}... | collective-permute-start | bytes 1572872 | tf_op jit(solution)/shard_map/ppermute | solution.py:33
  382.1 23.4 %collective-permute-start.23 = (f32[256,512]{1,0:T(8,128)S(1)}, f32[256,512]{1,0:T(8,128)S(1)}, u32[]{:S(2)}, u32[]{:S(2)}) collective-permute-start(f32[256,512]{1,0:T(8,128)S(1)} %bitcast.117), channel_id=1, source_target_pairs={{0,96},{2,98},{4,100},{6,102},{8,104},{10,106},{12,108},{14,110},{... | collective-permute-start | bytes 1572872 | tf_op jit(solution)/shard_map/ppermute | solution.py:33
  405.5 21.1 %collective-permute-start.24 = (f32[1024,512]{1,0:T(8,128)S(1)}, f32[1024,512]{1,0:T(8,128)S(1)}, u32[]{:S(2)}, u32[]{:S(2)}) collective-permute-start(f32[1024,512]{1,0:T(8,128)S(1)} %bitcast.111), channel_id=1, source_target_pairs={{0,2},{2,0},{4,6},{6,4},{8,10},{10,8},{12,14},{14,12},{16,18},{18,... | collective-permute-start | bytes 6291464 | tf_op jit(solution)/shard_map/ppermute | solution.py:33

commit v5 on v4

--- a/solution.py
+++ b/solution.py
@@ -109,19 +109,20 @@
     return jnp.concatenate([out_f.reshape(size * rows, -1), out_b.reshape(size * rows, -1)], axis=0)
 
 
-def scan_all_reduce(value, tied):
+def scan_all_reduce(value, early, tied):
     shape = value.shape
     data = value.reshape(-1, shape[-1])
     data = pair_reduce_scatter(data, CORE)
     data = direct_reduce_scatter(data, XAX)
     data = direct_reduce_scatter(data, YAX)
     data = pair_reduce_scatter(data, ZLO)
-    data, tied = lax.optimization_barrier((data, tied))
+    data, early = lax.optimization_barrier((data, early))
     data = pair_all_gather(data, ZLO)
     data = direct_all_gather(data, YAX)
+    data, tied = lax.optimization_barrier((data, tied))
     data = direct_all_gather(data, XAX)
     data = pair_all_gather(data, CORE)
-    return data.reshape(shape), tied
+    return data.reshape(shape), early, tied
 
 
 def dft_tables(length_side, direction_sign):
@@ -367,8 +368,8 @@
     received_east = from_behind(gradient_plane[:tile_side, tile_side:], "scan", 1)
     received_south = from_behind(gradient_plane[tile_side:, :tile_side], "scan", GCOLS)
     received_corner = from_behind(gradient_plane[tile_side:, tile_side:], "scan", GCOLS + 1)
-    probe_grad, (received_east, received_south, received_corner) = scan_all_reduce(
-        probe_partial, (received_east, received_south, received_corner)
+    probe_grad, positions, (received_east, received_south, received_corner) = scan_all_reduce(
+        probe_partial, positions, (received_east, received_south, received_corner)
     )
     total_grad = (
         gradient_plane[:tile_side, :tile_side] + received_east + received_south + received_corner

time: 438 us -> 454 us (1.037)
  the two profiles are of different devices: /device:TPU:65 before, /device:TPU:81 now
where the time goes in v5:
time: 454 us; the launch traced here: 447 us
  waiting for transfers between devices  142 us (31%)
  Pallas kernels  96.5 us (21%)
  other arithmetic  75.8 us (17%)
  starting transfers between devices  64.3 us (14%)
  local copies, waits for them, and re-layouts  46.5 us (10%)
  between operations  20.8 us (5%)
    ppermute x16, waiting for transfers between devices, sub_shift(): return lax.ppermute(value, 'scan', pairs)  90 us
    pallas_call x1, Pallas kernels, backward_gradients(): pl.pallas_call(backward_kernel, grid_spec=grid_spec, out_shape=[jax.Shape...  54.2 us
    ppermute x5, waiting for transfers between devices, from_behind(): return lax.ppermute(value, axis, pairs)  52.4 us
    ppermute x16, starting transfers between devices, sub_shift(): return lax.ppermute(value, 'scan', pairs)  43.3 us
    pallas_call x1, Pallas kernels, forward_correction(): pl.pallas_call(forward_kernel, grid=(slots,), in_specs=[pl.BlockSpec((1,...  42.3 us
    dynamic_update_slice x3, local copies, waits for them, and re-layouts, shards(): lax.dynamic_update_slice(gradient_plane, current + mine[slot_id, 0], start)  22.5 us
    another operation x5, other arithmetic  19.9 us
    ppermute x5, starting transfers between devices, from_behind(): return lax.ppermute(value, axis, pairs)  14.9 us
  transfers between devices with their start and end apart: 25, of which 12 were waited for; matrix products, arithmetic and copies ran while one was open for 17% of the time, Pallas kernels for 0%

profile of v5, /device:TPU:81, one launch (start us, length us, event | category | flops | bytes accessed | tf_op | source)
XLA Modules:
  0.0 446.5 jit_solution(12801708464667811274)
XLA Ops:
  0.8 3.1 dynamic-slice_bitcast_fusion.3
  5.1 6.4 %collective-permute-start = (f32[2,512,512]{2,1,0:T(8,128)}, f32[2,512,512]{2,1,0:T(8,128)}, u32[]{:S(2)}, u32[]{:S(2)}) collective-permute-start(f32[2,512,512]{2,1,0:T(8,128)} %bitcast.1), channel_id=1, source_target_pairs={{0,126},{2,0},{4,2},{6,4},{8,6},{10,8},{12,10},{14,12},{16,14},{18... | collective-permute-start | bytes 6291464 | tf_op jit(solution)/shard_map/ppermute | solution.py:23
  11.5 4.0 multiply_convert_fusion
  15.5 52.4 %collective-permute-done.1 = f32[2,512,512]{2,1,0:T(8,128)} collective-permute-done((f32[2,512,512]{2,1,0:T(8,128)}, f32[2,512,512]{2,1,0:T(8,128)}, u32[]{:S(2)}, u32[]{:S(2)}) %collective-permute-start.1) | collective-permute-done | bytes 2097184 | tf_op jit(solution)/shard_map/ppermute | solution.py:23
  67.9 4.8 %collective-permute-start.2 = (f32[2,512,512]{2,1,0:T(8,128)}, f32[2,512,512]{2,1,0:T(8,128)}, u32[]{:S(2)}, u32[]{:S(2)}) collective-permute-start(f32[2,512,512]{2,1,0:T(8,128)} %collective-permute-done.1), channel_id=1, source_target_pairs={{2,0},{6,4},{10,8},{14,12},{18,16},{22,20},{26,24},{30,28},{34,32}... | collective-permute-start | bytes 6291464 | tf_op jit(solution)/shard_map/ppermute | solution.py:329
  72.7 4.0 multiply_convert_fusion.1
  76.7 4.0 multiply_convert_fusion.2
  80.7 4.0 negate_convert_fusion
  84.7 4.0 negate_convert_fusion.1
  111.9 4.1 fusion.9
  116.0 10.5 %fusion.7 = (bf16[1024,1024]{1,0:T(8,128)(2,1)}, bf16[1024,1024]{1,0:T(8,128)(2,1)}) fusion(bf16[512,512]{1,0:T(8,128)(2,1)S(1)} %copy-done.5, bf16[512,512]{1,0:T(8,128)(2,1)S(1)} %copy-done.4, bf16[512,512]{1,0:T(8,128)(2,1)S(1)} %copy-done.6, bf16[512,512]{1,0:T(8,128)(2,1)S(1)} %copy-done.3), kind=kLoop, calls=%fused_computation.24 | loop fusion | flops 14680064 | bytes 6291456 | tf_op jit(solution)/shard_map/concatenate | solution.py:155
  127.0 3.3 maximum_maximum_fusion
  130.4 2.1 dynamic-slice_bitcast_fusion.2
  133.1 5.1 %slice.126.patch_ref = f32[3,2,512,512]{3,2,1,0:T(8,128)} slice(f32[3,2,514,514]{3,2,1,0:T(8,128)S(1)} %pad_maximum_fusion), slice={[0:3], [0:2], [1:513], [1:513]} | slice | bytes 12582912 | tf_op jit(solution)/shard_map/slice | solution.py:345
  138.2 2.9 select_bitcast_fusion.1
  141.7 4.0 maximum_select_fusion.probe_ref
  145.7 42.3 %shard_map.76.corr_ref = bf16[3,4,2,512,512]{4,3,2,1,0:T(8,128)(2,1)} custom-call(f32[3,2,512,512]{3,2,1,0:T(8,128)} %slice.126.patch_ref, f32[4,2,512,512]{3,2,1,0:T(8,128)} %maximum_select_fusion.probe_ref, f32[3,512,512]{2,1,0:T(8,128)} %bitcast.125, bf16[1024,1024]{1,0:T(8,128)(2,1)} %get-tuple-element.41.left_ref, ...), custom_call_target="tpu_custom_call" | custom-call | flops 25769803776 | bytes 44040192 | tf_op jit(solution)/shard_map/pallas_call | solution.py:193
  188.0 54.2 %shard_map.77 = (f32[3,2,512,512]{3,2,1,0:T(8,128)}, f32[2,2,512,512]{3,2,1,0:T(8,128)}) custom-call(s32[1]{0:T(128)} %bitcast.comp_ref, s32[1]{0:T(128)S(6)} %copy.19.count_ref, bf16[3,4,2,512,512]{4,3,2,1,0:T(8,128)(2,1)} %shard_map.76.corr_ref, f32[4,2,512,512]{3,2,1,0:T(8,128)} %maximum_select_fusion.probe_ref, f32[3,2,512,512]{3,2,1,0:T(8,128)} %slice.126.patch_ref, ...), custom_call_target="tpu_custom_call" | custom-call | flops 25769803776 | bytes 50331648 | tf_op jit(solution)/shard_map/pallas_call | solution.py:277
  243.5 2.5 broadcast_in_dim.45
  246.0 7.5 %dynamic_update_slice.35 = f32[1024,1024]{1,0:T(8,128)} dynamic-update-slice(f32[1024,1024]{1,0:T(8,128)} %broadcast_in_dim.45, f32[512,512]{1,0:T(8,128)S(1)} %dynamic-slice_bitcast_fusion.6, s32[]{:T(128)S(6)} %select_n.308, s32[]{:T(128)S(6)} %select_n.309) | dynamic-update-slice | bytes 2097156 | tf_op jit(solution)/shard_map/dynamic_update_slice | solution.py:366
  253.6 2.0 fusion.18
  255.5 7.5 %dynamic_update_slice.36 = f32[1024,1024]{1,0:T(8,128)} dynamic-update-slice(f32[1024,1024]{1,0:T(8,128)} %dynamic_update_slice.35, f32[512,512]{1,0:T(8,128)S(1)} %fusion.18, s32[]{:T(128)S(6)} %select_n.310, s32[]{:T(128)S(6)} %select_n.311) | dynamic-update-slice | bytes 2097156 | tf_op jit(solution)/shard_map/dynamic_update_slice | solution.py:366
  263.1 2.0 fusion.17
  265.1 7.5 %dynamic_update_slice.37 = f32[1024,1024]{1,0:T(8,128)} dynamic-update-slice(f32[1024,1024]{1,0:T(8,128)} %dynamic_update_slice.36, f32[512,512]{1,0:T(8,128)S(1)} %fusion.17, s32[]{:T(128)S(6)} %select_n.312, s32[]{:T(128)S(6)} %select_n.313) | dynamic-update-slice | bytes 2097156 | tf_op jit(solution)/shard_map/dynamic_update_slice | solution.py:366
  272.5 1.8 constant_dynamic-slice_fusion.1
  274.3 2.0 collective-permute-start.6
  276.3 3.9 collective-permute-done.6
  280.3 2.7 dynamic-slice_add_fusion
  284.6 3.2 collective-permute-start.8
  287.7 1.6 collective-permute-start.9
  289.4 9.2 %collective-permute-done.7 = f32[256,512]{1,0:T(8,128)} collective-permute-done((f32[256,512]{1,0:T(8,128)}, f32[256,512]{1,0:T(8,128)}, u32[]{:S(2)}, u32[]{:S(2)}) %collective-permute-start.7) | collective-permute-done | bytes 524320 | tf_op jit(solution)/shard_map/ppermute | solution.py:33
  298.6 12.4 %collective-permute-done.8 = f32[256,512]{1,0:T(8,128)} collective-permute-done((f32[256,512]{1,0:T(8,128)S(1)}, f32[256,512]{1,0:T(8,128)}, u32[]{:S(2)}, u32[]{:S(2)}) %collective-permute-start.8) | collective-permute-done | bytes 524320 | tf_op jit(solution)/shard_map/ppermute | solution.py:33
  311.0 1.6 fusion.23
  312.9 4.2 collective-permute-start.11
  317.0 2.0 collective-permute-start.12
  319.0 14.7 %fusion.5 = (f32[3]{0:T(128)S(1)}, f32[3]{0:T(128)S(1)}) fusion(f32[3,2,512,512]{3,2,1,0:T(8,128)} %get-tuple-element.14, f32[3,2,514,514]{3,2,1,0:T(8,128)} %copy-done), kind=kLoop, calls=%fused_computation.10 | loop fusion | flops 12582906 | bytes 31457304 | tf_op jit(solution)/shard_map/reduce_sum | solution.py:358
  334.5 2.5 collective-permute-done.13
  337.1 1.8 fusion.27
  338.9 4.8 %collective-permute-start.18 = (f32[512,512]{1,0:T(8,128)}, f32[512,512]{1,0:T(8,128)S(1)}, u32[]{:S(2)}, u32[]{:S(2)}) collective-permute-start(f32[512,512]{1,0:T(8,128)} %get-tuple-element.32), channel_id=1, source_target_pairs={{0,2},{2,4},{4,6},{6,8},{8,10},{10,12},{12,14},{14,16},{16,18},{18... | collective-permute-start | bytes 3145736 | tf_op jit(solution)/shard_map/ppermute | solution.py:23
  344.7 2.6 collective-permute-start.20
  348.5 47.2 %collective-permute-done.15 = f32[64,512]{1,0:T(8,128)S(1)} collective-permute-done((f32[64,512]{1,0:T(8,128)S(1)}, f32[64,512]{1,0:T(8,128)S(1)}, u32[]{:S(2)}, u32[]{:S(2)}) %collective-permute-start.15) | collective-permute-done | bytes 131104 | tf_op jit(solution)/shard_map/ppermute | solution.py:33
  397.7 2.6 collective-permute-done.17
  401.3 2.1 collective-permute-start.22
  405.1 4.9 %collective-permute-done.21 = f32[256,512]{1,0:T(8,128)} collective-permute-done((f32[256,512]{1,0:T(8,128)S(1)}, f32[256,512]{1,0:T(8,128)}, u32[]{:S(2)}, u32[]{:S(2)}) %collective-permute-start.21) | collective-permute-done | bytes 524320 | tf_op jit(solution)/shard_map/ppermute | solution.py:33
  411.1 4.8 %collective-permute-done.22 = f32[256,512]{1,0:T(8,128)S(1)} collective-permute-done((f32[256,512]{1,0:T(8,128)S(1)}, f32[256,512]{1,0:T(8,128)S(1)}, u32[]{:S(2)}, u32[]{:S(2)}) %collective-permute-start.22) | collective-permute-done | bytes 524320 | tf_op jit(solution)/shard_map/ppermute | solution.py:33
  416.3 23.1 %collective-permute-start.24 = (f32[1024,512]{1,0:T(8,128)S(1)}, f32[1024,512]{1,0:T(8,128)S(1)}, u32[]{:S(2)}, u32[]{:S(2)}) collective-permute-start(f32[1024,512]{1,0:T(8,128)S(1)} %bitcast.111), channel_id=1, source_target_pairs={{0,2},{2,0},{4,6},{6,4},{8,10},{10,8},{12,14},{14,12},{16,18},{18,... | collective-permute-start | bytes 6291464 | tf_op jit(solution)/shard_map/ppermute | solution.py:33
  439.5 3.0 add_bitcast_fusion
  443.9 2.5 pad_maximum_fusion.1
  (72 shorter events, 20.1 us)
Async XLA Ops:
  0.6 67.3 %collective-permute-start.1 = (f32[2,512,512]{2,1,0:T(8,128)}, f32[2,512,512]{2,1,0:T(8,128)}, u32[]{:S(2)}, u32[]{:S(2)}) collective-permute-start(f32[2,512,512]{2,1,0:T(8,128)} %bitcast.1), channel_id=1, source_target_pairs={{0,112},{2,114},{4,116},{6,118},{8,120},{10,122},{12,124},{14,126}... | collective-permute-start | bytes 6291464 | tf_op jit(solution)/shard_map/ppermute | solution.py:23
  3.8 87.8 %collective-permute-start.4 = (f32[2,512,512]{2,1,0:T(8,128)}, f32[2,512,512]{2,1,0:T(8,128)}, u32[]{:S(2)}, u32[]{:S(2)}) collective-permute-start(f32[2,512,512]{2,1,0:T(8,128)} %dynamic-slice_bitcast_fusion.3), channel_id=1, source_target_pairs={{0,5},{1,4},{2,7},{3,6},{4,1},{5,0},{6,3},{7,2},{8,13},{9,12},{10,... | collective-permute-start | bytes 6291464 | tf_op jit(solution)/shard_map/ppermute | solution.py:312
  3.8 122.7 %collective-permute-start.3 = (f32[2,512,512]{2,1,0:T(8,128)}, f32[2,512,512]{2,1,0:T(8,128)S(1)}, u32[]{:S(2)}, u32[]{:S(2)}) collective-permute-start(f32[2,512,512]{2,1,0:T(8,128)} %bitcast.1), channel_id=1, source_target_pairs={{20,2},{24,6},{28,10},{32,14},{36,18},{40,22},{44,26},{48,30},{52,... | collective-permute-start | bytes 6291464 | tf_op jit(solution)/shard_map/ppermute | solution.py:325
  5.1 121.9 %collective-permute-start = (f32[2,512,512]{2,1,0:T(8,128)}, f32[2,512,512]{2,1,0:T(8,128)}, u32[]{:S(2)}, u32[]{:S(2)}) collective-permute-start(f32[2,512,512]{2,1,0:T(8,128)} %bitcast.1), channel_id=1, source_target_pairs={{0,126},{2,0},{4,2},{6,4},{8,6},{10,8},{12,10},{14,12},{16,14},{18... | collective-permute-start | bytes 6291464 | tf_op jit(solution)/shard_map/ppermute | solution.py:23
  67.9 58.7 %collective-permute-start.2 = (f32[2,512,512]{2,1,0:T(8,128)}, f32[2,512,512]{2,1,0:T(8,128)}, u32[]{:S(2)}, u32[]{:S(2)}) collective-permute-start(f32[2,512,512]{2,1,0:T(8,128)} %collective-permute-done.1), channel_id=1, source_target_pairs={{2,0},{6,4},{10,8},{14,12},{18,16},{22,20},{26,24},{30,28},{34,32}... | collective-permute-start | bytes 6291464 | tf_op jit(solution)/shard_map/ppermute | solution.py:329
  89.0 2.6 copy-start.7
  91.6 46.6 %collective-permute-start.5 = (f32[2,512,512]{2,1,0:T(8,128)}, f32[2,512,512]{2,1,0:T(8,128)}, u32[]{:S(2)}, u32[]{:S(2)}) collective-permute-start(f32[2,512,512]{2,1,0:T(8,128)} %collective-permute-done.4), channel_id=1, source_target_pairs={{0,2},{2,0},{4,6},{6,4},{8,10},{10,8},{12,14},{14,12},{16,18},{18,... | collective-permute-start | bytes 6291464 | tf_op jit(solution)/shard_map/ppermute | solution.py:313
  111.8 4.2 copy-start.3
  111.8 4.2 copy-start.4
  111.8 4.1 copy-start.5
  111.8 4.1 copy-start.6
  133.1 5.1 %copy-start = (f32[3,2,514,514]{3,2,1,0:T(8,128)}, f32[3,2,514,514]{3,2,1,0:T(8,128)S(1)}, u32[]{:S(2)}) copy-start(f32[3,2,514,514]{3,2,1,0:T(8,128)S(1)} %pad_maximum_fusion) | copy-start | bytes 19022116
  138.2 3.4 copy-start.2
  274.3 5.9 %collective-permute-start.6 = (f32[1024,512]{1,0:T(8,128)S(1)}, f32[1024,512]{1,0:T(8,128)}, u32[]{:S(2)}, u32[]{:S(2)}) collective-permute-start(f32[1024,512]{1,0:T(8,128)S(1)} %constant_dynamic-slice_fusion.1), channel_id=1, source_target_pairs={{0,2},{2,0},{4,6},{6,4},{8,10},{10,8},{12,14},{14,12},{16,18},{18,... | collective-permute-start | bytes 6291464 | tf_op jit(solution)/shard_map/ppermute | solution.py:33
  283.9 14.7 %collective-permute-start.7 = (f32[256,512]{1,0:T(8,128)}, f32[256,512]{1,0:T(8,128)}, u32[]{:S(2)}, u32[]{:S(2)}) collective-permute-start(f32[256,512]{1,0:T(8,128)} %get-tuple-element.35), channel_id=1, source_target_pairs={{0,32},{2,34},{4,36},{6,38},{8,40},{10,42},{12,44},{14,46},{16,48}... | collective-permute-start | bytes 1572872 | tf_op jit(solution)/shard_map/ppermute | solution.py:33
  284.6 26.4 %collective-permute-start.8 = (f32[256,512]{1,0:T(8,128)S(1)}, f32[256,512]{1,0:T(8,128)}, u32[]{:S(2)}, u32[]{:S(2)}) collective-permute-start(f32[256,512]{1,0:T(8,128)S(1)} %get-tuple-element.37), channel_id=1, source_target_pairs={{0,64},{2,66},{4,68},{6,70},{8,72},{10,74},{12,76},{14,78},{16,80}... | collective-permute-start | bytes 1572872 | tf_op jit(solution)/shard_map/ppermute | solution.py:33
  287.7 23.2 %collective-permute-start.9 = (f32[256,512]{1,0:T(8,128)S(1)}, f32[256,512]{1,0:T(8,128)}, u32[]{:S(2)}, u32[]{:S(2)}) collective-permute-start(f32[256,512]{1,0:T(8,128)S(1)} %get-tuple-element.36), channel_id=1, source_target_pairs={{0,96},{2,98},{4,100},{6,102},{8,104},{10,106},{12,108},{14,110},{... | collective-permute-start | bytes 1572872 | tf_op jit(solution)/shard_map/ppermute | solution.py:33
  312.6 21.1 %collective-permute-start.10 = (f32[64,512]{1,0:T(8,128)S(1)}, f32[64,512]{1,0:T(8,128)S(1)}, u32[]{:S(2)}, u32[]{:S(2)}) collective-permute-start(f32[64,512]{1,0:T(8,128)S(1)} %get-tuple-element.50), channel_id=1, source_target_pairs={{0,8},{2,10},{4,12},{6,14},{8,16},{10,18},{12,20},{14,22},{16,24},... | collective-permute-start | bytes 393224 | tf_op jit(solution)/shard_map/ppermute | solution.py:33
  312.9 20.8 %collective-permute-start.11 = (f32[64,512]{1,0:T(8,128)S(1)}, f32[64,512]{1,0:T(8,128)S(1)}, u32[]{:S(2)}, u32[]{:S(2)}) collective-permute-start(f32[64,512]{1,0:T(8,128)S(1)} %get-tuple-element.52), channel_id=1, source_target_pairs={{0,16},{2,18},{4,20},{6,22},{8,24},{10,26},{12,28},{14,30},{16,0},... | collective-permute-start | bytes 393224 | tf_op jit(solution)/shard_map/ppermute | solution.py:33
  317.0 20.1 %copy-start.1 = (f32[1024,1024]{1,0:T(8,128)S(1)}, f32[1024,1024]{1,0:T(8,128)}, u32[]{:S(2)}) copy-start(f32[1024,1024]{1,0:T(8,128)} %dynamic_update_slice.37) | copy-start | bytes 12582916
  317.0 16.7 %collective-permute-start.12 = (f32[64,512]{1,0:T(8,128)S(1)}, f32[64,512]{1,0:T(8,128)S(1)}, u32[]{:S(2)}, u32[]{:S(2)}) collective-permute-start(f32[64,512]{1,0:T(8,128)S(1)} %get-tuple-element.51), channel_id=1, source_target_pairs={{0,24},{2,26},{4,28},{6,30},{8,0},{10,2},{12,4},{14,6},{16,8},{18,... | collective-permute-start | bytes 393224 | tf_op jit(solution)/shard_map/ppermute | solution.py:33
  333.8 3.2 collective-permute-start.13
  337.0 10.3 %collective-permute-start.14 = (f32[32,512]{1,0:T(8,128)S(1)}, f32[32,512]{1,0:T(8,128)S(1)}, u32[]{:S(2)}, u32[]{:S(2)}) collective-permute-start(f32[32,512]{1,0:T(8,128)S(1)} %dynamic-slice_add_fusion.1), channel_id=1, source_target_pairs={{0,4},{2,6},{4,0},{6,2},{8,12},{10,14},{12,8},{14,10},{16,20},{18,... | collective-permute-start | bytes 196616 | tf_op jit(solution)/shard_map/ppermute | solution.py:33
  338.9 61.4 %collective-permute-start.18 = (f32[512,512]{1,0:T(8,128)}, f32[512,512]{1,0:T(8,128)S(1)}, u32[]{:S(2)}, u32[]{:S(2)}) collective-permute-start(f32[512,512]{1,0:T(8,128)} %get-tuple-element.32), channel_id=1, source_target_pairs={{0,2},{2,4},{4,6},{6,8},{8,10},{10,12},{12,14},{14,16},{16,18},{18... | collective-permute-start | bytes 3145736 | tf_op jit(solution)/shard_map/ppermute | solution.py:23
  343.7 56.6 %collective-permute-start.19 = (f32[512,512]{1,0:T(8,128)}, f32[512,512]{1,0:T(8,128)S(1)}, u32[]{:S(2)}, u32[]{:S(2)}) collective-permute-start(f32[512,512]{1,0:T(8,128)} %get-tuple-element.31), channel_id=1, source_target_pairs={{0,16},{2,18},{4,20},{6,22},{8,24},{10,26},{12,28},{14,30},{16,32}... | collective-permute-start | bytes 3145736 | tf_op jit(solution)/shard_map/ppermute | solution.py:23
  344.7 55.6 %collective-permute-start.20 = (f32[512,512]{1,0:T(8,128)}, f32[512,512]{1,0:T(8,128)}, u32[]{:S(2)}, u32[]{:S(2)}) collective-permute-start(f32[512,512]{1,0:T(8,128)} %get-tuple-element.30), channel_id=1, source_target_pairs={{0,18},{2,20},{4,22},{6,24},{8,26},{10,28},{12,30},{14,32},{16,34}... | collective-permute-start | bytes 3145736 | tf_op jit(solution)/shard_map/ppermute | solution.py:23
  347.4 48.3 %collective-permute-start.15 = (f32[64,512]{1,0:T(8,128)S(1)}, f32[64,512]{1,0:T(8,128)S(1)}, u32[]{:S(2)}, u32[]{:S(2)}) collective-permute-start(f32[64,512]{1,0:T(8,128)S(1)} %pad_maximum_fusion.14), channel_id=1, source_target_pairs={{0,8},{2,10},{4,12},{6,14},{8,16},{10,18},{12,20},{14,22},{16,24},... | collective-permute-start | bytes 393224 | tf_op jit(solution)/shard_map/ppermute | solution.py:33
  347.5 50.2 %collective-permute-start.16 = (f32[64,512]{1,0:T(8,128)S(1)}, f32[64,512]{1,0:T(8,128)S(1)}, u32[]{:S(2)}, u32[]{:S(2)}) collective-permute-start(f32[64,512]{1,0:T(8,128)S(1)} %pad_maximum_fusion.14), channel_id=1, source_target_pairs={{0,16},{2,18},{4,20},{6,22},{8,24},{10,26},{12,28},{14,30},{16,0},... | collective-permute-start | bytes 393224 | tf_op jit(solution)/shard_map/ppermute | solution.py:33
  395.7 4.6 %collective-permute-start.17 = (f32[64,512]{1,0:T(8,128)S(1)}, f32[64,512]{1,0:T(8,128)S(1)}, u32[]{:S(2)}, u32[]{:S(2)}) collective-permute-start(f32[64,512]{1,0:T(8,128)S(1)} %pad_maximum_fusion.14), channel_id=1, source_target_pairs={{0,24},{2,26},{4,28},{6,30},{8,0},{10,2},{12,4},{14,6},{16,8},{18,... | collective-permute-start | bytes 393224 | tf_op jit(solution)/shard_map/ppermute | solution.py:33
  400.3 9.7 %collective-permute-start.21 = (f32[256,512]{1,0:T(8,128)S(1)}, f32[256,512]{1,0:T(8,128)}, u32[]{:S(2)}, u32[]{:S(2)}) collective-permute-start(f32[256,512]{1,0:T(8,128)S(1)} %bitcast.115), channel_id=1, source_target_pairs={{0,32},{2,34},{4,36},{6,38},{8,40},{10,42},{12,44},{14,46},{16,48}... | collective-permute-start | bytes 1572872 | tf_op jit(solution)/shard_map/ppermute | solution.py:33
  401.3 14.7 %collective-permute-start.22 = (f32[256,512]{1,0:T(8,128)S(1)}, f32[256,512]{1,0:T(8,128)S(1)}, u32[]{:S(2)}, u32[]{:S(2)}) collective-permute-start(f32[256,512]{1,0:T(8,128)S(1)} %bitcast.116), channel_id=1, source_target_pairs={{0,64},{2,66},{4,68},{6,70},{8,72},{10,74},{12,76},{14,78},{16,80}... | collective-permute-start | bytes 1572872 | tf_op jit(solution)/shard_map/ppermute | solution.py:33
  403.4 12.9 %collective-permute-start.23 = (f32[256,512]{1,0:T(8,128)S(1)}, f32[256,512]{1,0:T(8,128)S(1)}, u32[]{:S(2)}, u32[]{:S(2)}) collective-permute-start(f32[256,512]{1,0:T(8,128)S(1)} %bitcast.117), channel_id=1, source_target_pairs={{0,96},{2,98},{4,100},{6,102},{8,104},{10,106},{12,108},{14,110},{... | collective-permute-start | bytes 1572872 | tf_op jit(solution)/shard_map/ppermute | solution.py:33
  416.3 26.9 %collective-permute-start.24 = (f32[1024,512]{1,0:T(8,128)S(1)}, f32[1024,512]{1,0:T(8,128)S(1)}, u32[]{:S(2)}, u32[]{:S(2)}) collective-permute-start(f32[1024,512]{1,0:T(8,128)S(1)} %bitcast.111), channel_id=1, source_target_pairs={{0,2},{2,0},{4,6},{6,4},{8,10},{10,8},{12,14},{14,12},{16,18},{18,... | collective-permute-start | bytes 6291464 | tf_op jit(solution)/shard_map/ppermute | solution.py:33

commit v6 on v5

--- a/solution.py
+++ b/solution.py
@@ -116,10 +116,9 @@
     data = direct_reduce_scatter(data, XAX)
     data = direct_reduce_scatter(data, YAX)
     data = pair_reduce_scatter(data, ZLO)
-    data, early = lax.optimization_barrier((data, early))
+    data, early, tied = lax.optimization_barrier((data, early, tied))
     data = pair_all_gather(data, ZLO)
     data = direct_all_gather(data, YAX)
-    data, tied = lax.optimization_barrier((data, tied))
     data = direct_all_gather(data, XAX)
     data = pair_all_gather(data, CORE)
     return data.reshape(shape), early, tied

time: 454 us -> 435 us (0.958)
  the two profiles are of different devices: /device:TPU:81 before, /device:TPU:65 now
where the time goes in v6:
time: 435 us; the launch traced here: 426 us
  waiting for transfers between devices  158 us (36%)
  Pallas kernels  96.6 us (22%)
  other arithmetic  74.9 us (17%)
  local copies, waits for them, and re-layouts  47.6 us (11%)
  starting transfers between devices  28.9 us (7%)
  between operations  20.8 us (5%)
    ppermute x16, waiting for transfers between devices, sub_shift(): return lax.ppermute(value, 'scan', pairs)  103 us
    ppermute x5, waiting for transfers between devices, from_behind(): return lax.ppermute(value, axis, pairs)  54.5 us
    pallas_call x1, Pallas kernels, backward_gradients(): pl.pallas_call(backward_kernel, grid_spec=grid_spec, out_shape=[jax.Shape...  54.2 us
    pallas_call x1, Pallas kernels, forward_correction(): pl.pallas_call(forward_kernel, grid=(slots,), in_specs=[pl.BlockSpec((1,...  42.3 us
    dynamic_update_slice x3, local copies, waits for them, and re-layouts, shards(): lax.dynamic_update_slice(gradient_plane, current + mine[slot_id, 0], start)  22.9 us
    another operation x5, other arithmetic  19.9 us
    concatenate x2, other arithmetic, complex_table(): return jnp.concatenate(rows, axis=0)  14.6 us
    ppermute x16, starting transfers between devices, sub_shift(): return lax.ppermute(value, 'scan', pairs)  14.4 us
  transfers between devices with their start and end apart: 25, of which 16 were waited for; matrix products, arithmetic and copies ran while one was open for 17% of the time, Pallas kernels for 0%

profile of v6, /device:TPU:65, one launch (start us, length us, event | category | flops | bytes accessed | tf_op | source)
XLA Modules:
  0.0 426.3 jit_solution(7664155033135775025)
XLA Ops:
  0.6 5.2 %collective-permute-start.1 = (f32[2,512,512]{2,1,0:T(8,128)}, f32[2,512,512]{2,1,0:T(8,128)}, u32[]{:S(2)}, u32[]{:S(2)}) collective-permute-start(f32[2,512,512]{2,1,0:T(8,128)} %bitcast.1), channel_id=1, source_target_pairs={{0,112},{2,114},{4,116},{6,118},{8,120},{10,122},{12,124},{14,126}... | collective-permute-start | bytes 6291464 | tf_op jit(solution)/shard_map/ppermute | solution.py:23
  5.8 3.1 dynamic-slice_bitcast_fusion.3
  10.2 2.9 collective-permute-start
  13.1 4.0 multiply_convert_fusion
  17.1 54.4 %collective-permute-done.1 = f32[2,512,512]{2,1,0:T(8,128)} collective-permute-done((f32[2,512,512]{2,1,0:T(8,128)}, f32[2,512,512]{2,1,0:T(8,128)}, u32[]{:S(2)}, u32[]{:S(2)}) %collective-permute-start.1) | collective-permute-done | bytes 2097184 | tf_op jit(solution)/shard_map/ppermute | solution.py:23
  71.5 4.9 %collective-permute-start.2 = (f32[2,512,512]{2,1,0:T(8,128)}, f32[2,512,512]{2,1,0:T(8,128)}, u32[]{:S(2)}, u32[]{:S(2)}) collective-permute-start(f32[2,512,512]{2,1,0:T(8,128)} %collective-permute-done.1), channel_id=1, source_target_pairs={{2,0},{6,4},{10,8},{14,12},{18,16},{22,20},{26,24},{30,28},{34,32}... | collective-permute-start | bytes 6291464 | tf_op jit(solution)/shard_map/ppermute | solution.py:328
  76.4 4.0 multiply_convert_fusion.1
  80.4 4.0 negate_convert_fusion
  84.4 4.0 multiply_convert_fusion.2
  88.4 4.0 negate_convert_fusion.1
  115.5 4.1 fusion.9
  119.6 10.5 %fusion.7 = (bf16[1024,1024]{1,0:T(8,128)(2,1)}, bf16[1024,1024]{1,0:T(8,128)(2,1)}) fusion(bf16[512,512]{1,0:T(8,128)(2,1)S(1)} %copy-done.5, bf16[512,512]{1,0:T(8,128)(2,1)S(1)} %copy-done.4, bf16[512,512]{1,0:T(8,128)(2,1)S(1)} %copy-done.6, bf16[512,512]{1,0:T(8,128)(2,1)S(1)} %copy-done.3), kind=kLoop, calls=%fused_computation.24 | loop fusion | flops 14680064 | bytes 6291456 | tf_op jit(solution)/shard_map/concatenate | solution.py:154
  130.7 3.3 maximum_maximum_fusion
  134.0 2.1 dynamic-slice_bitcast_fusion.2
  136.7 5.1 %slice.126.patch_ref = f32[3,2,512,512]{3,2,1,0:T(8,128)} slice(f32[3,2,514,514]{3,2,1,0:T(8,128)S(1)} %pad_maximum_fusion), slice={[0:3], [0:2], [1:513], [1:513]} | slice | bytes 12582912 | tf_op jit(solution)/shard_map/slice | solution.py:344
  141.8 2.9 select_bitcast_fusion.1
  145.3 4.0 maximum_select_fusion.probe_ref
  149.3 42.3 %shard_map.76.corr_ref = bf16[3,4,2,512,512]{4,3,2,1,0:T(8,128)(2,1)} custom-call(f32[3,2,512,512]{3,2,1,0:T(8,128)} %slice.126.patch_ref, f32[4,2,512,512]{3,2,1,0:T(8,128)} %maximum_select_fusion.probe_ref, f32[3,512,512]{2,1,0:T(8,128)} %bitcast.128, bf16[1024,1024]{1,0:T(8,128)(2,1)} %get-tuple-element.39.left_ref, ...), custom_call_target="tpu_custom_call" | custom-call | flops 25769803776 | bytes 44040192 | tf_op jit(solution)/shard_map/pallas_call | solution.py:192
  191.6 54.2 %shard_map.77 = (f32[3,2,512,512]{3,2,1,0:T(8,128)}, f32[2,2,512,512]{3,2,1,0:T(8,128)}) custom-call(s32[1]{0:T(128)} %bitcast.comp_ref, s32[1]{0:T(128)S(6)} %copy.19.count_ref, bf16[3,4,2,512,512]{4,3,2,1,0:T(8,128)(2,1)} %shard_map.76.corr_ref, f32[4,2,512,512]{3,2,1,0:T(8,128)} %maximum_select_fusion.probe_ref, f32[3,2,512,512]{3,2,1,0:T(8,128)} %slice.126.patch_ref, ...), custom_call_target="tpu_custom_call" | custom-call | flops 25769803776 | bytes 50331648 | tf_op jit(solution)/shard_map/pallas_call | solution.py:276
  247.1 2.5 broadcast_in_dim.45
  249.7 7.5 %dynamic_update_slice.35 = f32[1024,1024]{1,0:T(8,128)} dynamic-update-slice(f32[1024,1024]{1,0:T(8,128)} %broadcast_in_dim.45, f32[512,512]{1,0:T(8,128)S(1)} %dynamic-slice_bitcast_fusion.6, s32[]{:T(128)S(6)} %select_n.308, s32[]{:T(128)S(6)} %select_n.309) | dynamic-update-slice | bytes 2097156 | tf_op jit(solution)/shard_map/dynamic_update_slice | solution.py:365
  257.2 2.0 fusion.18
  259.2 7.8 %dynamic_update_slice.36 = f32[1024,1024]{1,0:T(8,128)} dynamic-update-slice(f32[1024,1024]{1,0:T(8,128)} %dynamic_update_slice.35, f32[512,512]{1,0:T(8,128)S(1)} %fusion.18, s32[]{:T(128)S(6)} %select_n.310, s32[]{:T(128)S(6)} %select_n.311) | dynamic-update-slice | bytes 2097156 | tf_op jit(solution)/shard_map/dynamic_update_slice | solution.py:365
  266.9 2.0 fusion.17
  268.9 7.6 %dynamic_update_slice.37 = f32[1024,1024]{1,0:T(8,128)} dynamic-update-slice(f32[1024,1024]{1,0:T(8,128)} %dynamic_update_slice.36, f32[512,512]{1,0:T(8,128)S(1)} %fusion.17, s32[]{:T(128)S(6)} %select_n.312, s32[]{:T(128)S(6)} %select_n.313) | dynamic-update-slice | bytes 2097156 | tf_op jit(solution)/shard_map/dynamic_update_slice | solution.py:365
  276.6 1.8 constant_dynamic-slice_fusion.1
  278.3 2.0 collective-permute-start.6
  280.3 3.9 collective-permute-done.6
  284.2 2.8 dynamic-slice_add_fusion
  289.3 2.4 collective-permute-start.9
  292.8 10.8 %collective-permute-done.9 = f32[256,512]{1,0:T(8,128)} collective-permute-done((f32[256,512]{1,0:T(8,128)}, f32[256,512]{1,0:T(8,128)}, u32[]{:S(2)}, u32[]{:S(2)}) %collective-permute-start.9) | collective-permute-done | bytes 524320 | tf_op jit(solution)/shard_map/ppermute | solution.py:33
  303.7 2.5 collective-permute-done.8
  306.2 12.2 %collective-permute-done.7 = f32[256,512]{1,0:T(8,128)} collective-permute-done((f32[256,512]{1,0:T(8,128)S(1)}, f32[256,512]{1,0:T(8,128)}, u32[]{:S(2)}, u32[]{:S(2)}) %collective-permute-start.7) | collective-permute-done | bytes 524320 | tf_op jit(solution)/shard_map/ppermute | solution.py:33
  318.4 1.7 fusion.23
  320.5 2.2 fusion.27
  325.1 13.2 %fusion.5 = (f32[3]{0:T(128)S(1)}, f32[3]{0:T(128)S(1)}) fusion(f32[3,2,512,512]{3,2,1,0:T(8,128)S(1)} %bitcast.111, f32[3,2,514,514]{3,2,1,0:T(8,128)} %copy-done), kind=kLoop, calls=%fused_computation.10 | loop fusion | flops 12582906 | bytes 31457304 | tf_op jit(solution)/shard_map/reduce_sum | solution.py:357
  338.2 32.3 %collective-permute-done.11 = f32[64,512]{1,0:T(8,128)S(1)} collective-permute-done((f32[64,512]{1,0:T(8,128)S(1)}, f32[64,512]{1,0:T(8,128)S(1)}, u32[]{:S(2)}, u32[]{:S(2)}) %collective-permute-start.11) | collective-permute-done | bytes 131104 | tf_op jit(solution)/shard_map/ppermute | solution.py:33
  370.5 7.2 %collective-permute-done.10 = f32[64,512]{1,0:T(8,128)S(1)} collective-permute-done((f32[64,512]{1,0:T(8,128)S(1)}, f32[64,512]{1,0:T(8,128)S(1)}, u32[]{:S(2)}, u32[]{:S(2)}) %collective-permute-start.10) | collective-permute-done | bytes 131104 | tf_op jit(solution)/shard_map/ppermute | solution.py:33
  378.4 2.5 collective-permute-done.13
  381.4 2.7 collective-permute-done.17
  385.1 1.9 collective-permute-start.20
  387.0 3.7 collective-permute-done.18
  394.7 9.3 %collective-permute-done.21 = f32[256,512]{1,0:T(8,128)S(1)} collective-permute-done((f32[256,512]{1,0:T(8,128)S(1)}, f32[256,512]{1,0:T(8,128)S(1)}, u32[]{:S(2)}, u32[]{:S(2)}) %collective-permute-start.21) | collective-permute-done | bytes 524320 | tf_op jit(solution)/shard_map/ppermute | solution.py:33
  404.0 8.1 %collective-permute-done.22 = f32[256,512]{1,0:T(8,128)S(1)} collective-permute-done((f32[256,512]{1,0:T(8,128)S(1)}, f32[256,512]{1,0:T(8,128)S(1)}, u32[]{:S(2)}, u32[]{:S(2)}) %collective-permute-start.22) | collective-permute-done | bytes 524320 | tf_op jit(solution)/shard_map/ppermute | solution.py:33
  412.2 4.7 %collective-permute-done.23 = f32[256,512]{1,0:T(8,128)S(1)} collective-permute-done((f32[256,512]{1,0:T(8,128)S(1)}, f32[256,512]{1,0:T(8,128)S(1)}, u32[]{:S(2)}, u32[]{:S(2)}) %collective-permute-start.23) | collective-permute-done | bytes 524320 | tf_op jit(solution)/shard_map/ppermute | solution.py:33
  417.0 2.3 collective-permute-start.24
  419.2 3.3 add_bitcast_fusion
  423.6 2.5 pad_maximum_fusion.1
  (77 shorter events, 20.9 us)
Async XLA Ops:
  0.6 70.9 %collective-permute-start.1 = (f32[2,512,512]{2,1,0:T(8,128)}, f32[2,512,512]{2,1,0:T(8,128)}, u32[]{:S(2)}, u32[]{:S(2)}) collective-permute-start(f32[2,512,512]{2,1,0:T(8,128)} %bitcast.1), channel_id=1, source_target_pairs={{0,112},{2,114},{4,116},{6,118},{8,120},{10,122},{12,124},{14,126}... | collective-permute-start | bytes 6291464 | tf_op jit(solution)/shard_map/ppermute | solution.py:23
  8.9 86.4 %collective-permute-start.4 = (f32[2,512,512]{2,1,0:T(8,128)}, f32[2,512,512]{2,1,0:T(8,128)}, u32[]{:S(2)}, u32[]{:S(2)}) collective-permute-start(f32[2,512,512]{2,1,0:T(8,128)} %dynamic-slice_bitcast_fusion.3), channel_id=1, source_target_pairs={{0,5},{1,4},{2,7},{3,6},{4,1},{5,0},{6,3},{7,2},{8,13},{9,12},{10,... | collective-permute-start | bytes 6291464 | tf_op jit(solution)/shard_map/ppermute | solution.py:311
  8.9 121.3 %collective-permute-start.3 = (f32[2,512,512]{2,1,0:T(8,128)}, f32[2,512,512]{2,1,0:T(8,128)S(1)}, u32[]{:S(2)}, u32[]{:S(2)}) collective-permute-start(f32[2,512,512]{2,1,0:T(8,128)} %bitcast.1), channel_id=1, source_target_pairs={{20,2},{24,6},{28,10},{32,14},{36,18},{40,22},{44,26},{48,30},{52,... | collective-permute-start | bytes 6291464 | tf_op jit(solution)/shard_map/ppermute | solution.py:324
  10.2 120.5 %collective-permute-start = (f32[2,512,512]{2,1,0:T(8,128)}, f32[2,512,512]{2,1,0:T(8,128)}, u32[]{:S(2)}, u32[]{:S(2)}) collective-permute-start(f32[2,512,512]{2,1,0:T(8,128)} %bitcast.1), channel_id=1, source_target_pairs={{0,126},{2,0},{4,2},{6,4},{8,6},{10,8},{12,10},{14,12},{16,14},{18... | collective-permute-start | bytes 6291464 | tf_op jit(solution)/shard_map/ppermute | solution.py:23
  71.5 58.6 %collective-permute-start.2 = (f32[2,512,512]{2,1,0:T(8,128)}, f32[2,512,512]{2,1,0:T(8,128)}, u32[]{:S(2)}, u32[]{:S(2)}) collective-permute-start(f32[2,512,512]{2,1,0:T(8,128)} %collective-permute-done.1), channel_id=1, source_target_pairs={{2,0},{6,4},{10,8},{14,12},{18,16},{22,20},{26,24},{30,28},{34,32}... | collective-permute-start | bytes 6291464 | tf_op jit(solution)/shard_map/ppermute | solution.py:328
  92.7 2.6 copy-start.7
  95.3 46.5 %collective-permute-start.5 = (f32[2,512,512]{2,1,0:T(8,128)}, f32[2,512,512]{2,1,0:T(8,128)}, u32[]{:S(2)}, u32[]{:S(2)}) collective-permute-start(f32[2,512,512]{2,1,0:T(8,128)} %collective-permute-done.4), channel_id=1, source_target_pairs={{0,2},{2,0},{4,6},{6,4},{8,10},{10,8},{12,14},{14,12},{16,18},{18,... | collective-permute-start | bytes 6291464 | tf_op jit(solution)/shard_map/ppermute | solution.py:312
  115.5 4.2 copy-start.3
  115.5 4.2 copy-start.4
  115.5 4.1 copy-start.5
  115.5 4.1 copy-start.6
  136.7 5.1 %copy-start = (f32[3,2,514,514]{3,2,1,0:T(8,128)}, f32[3,2,514,514]{3,2,1,0:T(8,128)S(1)}, u32[]{:S(2)}) copy-start(f32[3,2,514,514]{3,2,1,0:T(8,128)S(1)} %pad_maximum_fusion) | copy-start | bytes 19022116
  141.8 3.4 copy-start.1
  278.3 5.9 %collective-permute-start.6 = (f32[1024,512]{1,0:T(8,128)S(1)}, f32[1024,512]{1,0:T(8,128)}, u32[]{:S(2)}, u32[]{:S(2)}) collective-permute-start(f32[1024,512]{1,0:T(8,128)S(1)} %constant_dynamic-slice_fusion.1), channel_id=1, source_target_pairs={{0,2},{2,0},{4,6},{6,4},{8,10},{10,8},{12,14},{14,12},{16,18},{18,... | collective-permute-start | bytes 6291464 | tf_op jit(solution)/shard_map/ppermute | solution.py:33
  284.2 40.8 %slice-start = ((s8[6291456]{0:T(1024)(128)(4,1)}), s8[2097152]{0:T(1024)(128)(4,1)S(1)}, s32[]{:S(2)}) async-start(s8[6291456]{0:T(1024)(128)(4,1)} %bitcast.110), calls=%async_computation | async-start | bytes 4194304
  287.1 1.3 copy-start.2
  289.3 14.3 %collective-permute-start.9 = (f32[256,512]{1,0:T(8,128)}, f32[256,512]{1,0:T(8,128)}, u32[]{:S(2)}, u32[]{:S(2)}) collective-permute-start(f32[256,512]{1,0:T(8,128)} %get-tuple-element.34), channel_id=1, source_target_pairs={{0,96},{2,98},{4,100},{6,102},{8,104},{10,106},{12,108},{14,110},{... | collective-permute-start | bytes 1572872 | tf_op jit(solution)/shard_map/ppermute | solution.py:33
  291.7 14.5 %collective-permute-start.8 = (f32[256,512]{1,0:T(8,128)S(1)}, f32[256,512]{1,0:T(8,128)}, u32[]{:S(2)}, u32[]{:S(2)}) collective-permute-start(f32[256,512]{1,0:T(8,128)S(1)} %get-tuple-element.35), channel_id=1, source_target_pairs={{0,64},{2,66},{4,68},{6,70},{8,72},{10,74},{12,76},{14,78},{16,80}... | collective-permute-start | bytes 1572872 | tf_op jit(solution)/shard_map/ppermute | solution.py:33
  292.0 26.4 %collective-permute-start.7 = (f32[256,512]{1,0:T(8,128)S(1)}, f32[256,512]{1,0:T(8,128)}, u32[]{:S(2)}, u32[]{:S(2)}) collective-permute-start(f32[256,512]{1,0:T(8,128)S(1)} %get-tuple-element.33), channel_id=1, source_target_pairs={{0,32},{2,34},{4,36},{6,38},{8,40},{10,42},{12,44},{14,46},{16,48}... | collective-permute-start | bytes 1572872 | tf_op jit(solution)/shard_map/ppermute | solution.py:33
  292.8 32.3 %slice-start.1 = ((s8[6291456]{0:T(1024)(128)(4,1)}), s8[4194304]{0:T(1024)(128)(4,1)S(1)}, s32[]{:S(2)}) async-start(s8[6291456]{0:T(1024)(128)(4,1)} %bitcast.110), calls=%async_computation.1 | async-start | bytes 8388608
  320.2 4.9 %collective-permute-start.12 = (f32[64,512]{1,0:T(8,128)S(1)}, f32[64,512]{1,0:T(8,128)S(1)}, u32[]{:S(2)}, u32[]{:S(2)}) collective-permute-start(f32[64,512]{1,0:T(8,128)S(1)} %get-tuple-element.49), channel_id=1, source_target_pairs={{0,24},{2,26},{4,28},{6,30},{8,0},{10,2},{12,4},{14,6},{16,8},{18,... | collective-permute-start | bytes 393224 | tf_op jit(solution)/shard_map/ppermute | solution.py:33
  322.7 58.3 %collective-permute-start.14 = (f32[512,512]{1,0:T(8,128)S(1)}, f32[512,512]{1,0:T(8,128)S(1)}, u32[]{:S(2)}, u32[]{:S(2)}) collective-permute-start(f32[512,512]{1,0:T(8,128)S(1)} %get-tuple-element.30), channel_id=1, source_target_pairs={{0,2},{2,4},{4,6},{6,8},{8,10},{10,12},{12,14},{14,16},{16,18},{18... | collective-permute-start | bytes 3145736 | tf_op jit(solution)/shard_map/ppermute | solution.py:23
  322.7 58.2 %collective-permute-start.15 = (f32[512,512]{1,0:T(8,128)S(1)}, f32[512,512]{1,0:T(8,128)}, u32[]{:S(2)}, u32[]{:S(2)}) collective-permute-start(f32[512,512]{1,0:T(8,128)S(1)} %get-tuple-element.29), channel_id=1, source_target_pairs={{0,16},{2,18},{4,20},{6,22},{8,24},{10,26},{12,28},{14,30},{16,32}... | collective-permute-start | bytes 3145736 | tf_op jit(solution)/shard_map/ppermute | solution.py:23
  322.8 58.1 %collective-permute-start.16 = (f32[512,512]{1,0:T(8,128)S(1)}, f32[512,512]{1,0:T(8,128)}, u32[]{:S(2)}, u32[]{:S(2)}) collective-permute-start(f32[512,512]{1,0:T(8,128)S(1)} %get-tuple-element.28), channel_id=1, source_target_pairs={{0,18},{2,20},{4,22},{6,24},{8,26},{10,28},{12,30},{14,32},{16,34}... | collective-permute-start | bytes 3145736 | tf_op jit(solution)/shard_map/ppermute | solution.py:23
  322.9 47.6 %collective-permute-start.11 = (f32[64,512]{1,0:T(8,128)S(1)}, f32[64,512]{1,0:T(8,128)S(1)}, u32[]{:S(2)}, u32[]{:S(2)}) collective-permute-start(f32[64,512]{1,0:T(8,128)S(1)} %get-tuple-element.50), channel_id=1, source_target_pairs={{0,16},{2,18},{4,20},{6,22},{8,24},{10,26},{12,28},{14,30},{16,0},... | collective-permute-start | bytes 393224 | tf_op jit(solution)/shard_map/ppermute | solution.py:33
  325.1 52.6 %collective-permute-start.10 = (f32[64,512]{1,0:T(8,128)S(1)}, f32[64,512]{1,0:T(8,128)S(1)}, u32[]{:S(2)}, u32[]{:S(2)}) collective-permute-start(f32[64,512]{1,0:T(8,128)S(1)} %get-tuple-element.48), channel_id=1, source_target_pairs={{0,8},{2,10},{4,12},{6,14},{8,16},{10,18},{12,20},{14,22},{16,24},... | collective-permute-start | bytes 393224 | tf_op jit(solution)/shard_map/ppermute | solution.py:33
  377.7 3.2 collective-permute-start.13
  381.0 3.2 collective-permute-start.17
  384.2 6.5 %collective-permute-start.18 = (f32[64,512]{1,0:T(8,128)S(1)}, f32[64,512]{1,0:T(8,128)S(1)}, u32[]{:S(2)}, u32[]{:S(2)}) collective-permute-start(f32[64,512]{1,0:T(8,128)S(1)} %pad_maximum_fusion.14), channel_id=1, source_target_pairs={{0,8},{2,10},{4,12},{6,14},{8,16},{10,18},{12,20},{14,22},{16,24},... | collective-permute-start | bytes 393224 | tf_op jit(solution)/shard_map/ppermute | solution.py:33
  384.4 6.4 %collective-permute-start.19 = (f32[64,512]{1,0:T(8,128)S(1)}, f32[64,512]{1,0:T(8,128)S(1)}, u32[]{:S(2)}, u32[]{:S(2)}) collective-permute-start(f32[64,512]{1,0:T(8,128)S(1)} %pad_maximum_fusion.14), channel_id=1, source_target_pairs={{0,16},{2,18},{4,20},{6,22},{8,24},{10,26},{12,28},{14,30},{16,0},... | collective-permute-start | bytes 393224 | tf_op jit(solution)/shard_map/ppermute | solution.py:33
  385.1 6.6 %collective-permute-start.20 = (f32[64,512]{1,0:T(8,128)S(1)}, f32[64,512]{1,0:T(8,128)S(1)}, u32[]{:S(2)}, u32[]{:S(2)}) collective-permute-start(f32[64,512]{1,0:T(8,128)S(1)} %pad_maximum_fusion.14), channel_id=1, source_target_pairs={{0,24},{2,26},{4,28},{6,30},{8,0},{10,2},{12,4},{14,6},{16,8},{18,... | collective-permute-start | bytes 393224 | tf_op jit(solution)/shard_map/ppermute | solution.py:33
  391.6 12.3 %collective-permute-start.21 = (f32[256,512]{1,0:T(8,128)S(1)}, f32[256,512]{1,0:T(8,128)S(1)}, u32[]{:S(2)}, u32[]{:S(2)}) collective-permute-start(f32[256,512]{1,0:T(8,128)S(1)} %bitcast.118), channel_id=1, source_target_pairs={{0,32},{2,34},{4,36},{6,38},{8,40},{10,42},{12,44},{14,46},{16,48}... | collective-permute-start | bytes 1572872 | tf_op jit(solution)/shard_map/ppermute | solution.py:33
  391.7 20.4 %collective-permute-start.22 = (f32[256,512]{1,0:T(8,128)S(1)}, f32[256,512]{1,0:T(8,128)S(1)}, u32[]{:S(2)}, u32[]{:S(2)}) collective-permute-start(f32[256,512]{1,0:T(8,128)S(1)} %bitcast.119), channel_id=1, source_target_pairs={{0,64},{2,66},{4,68},{6,70},{8,72},{10,74},{12,76},{14,78},{16,80}... | collective-permute-start | bytes 1572872 | tf_op jit(solution)/shard_map/ppermute | solution.py:33
  392.9 24.0 %collective-permute-start.23 = (f32[256,512]{1,0:T(8,128)S(1)}, f32[256,512]{1,0:T(8,128)S(1)}, u32[]{:S(2)}, u32[]{:S(2)}) collective-permute-start(f32[256,512]{1,0:T(8,128)S(1)} %bitcast.120), channel_id=1, source_target_pairs={{0,96},{2,98},{4,100},{6,102},{8,104},{10,106},{12,108},{14,110},{... | collective-permute-start | bytes 1572872 | tf_op jit(solution)/shard_map/ppermute | solution.py:33
  417.0 6.1 %collective-permute-start.24 = (f32[1024,512]{1,0:T(8,128)S(1)}, f32[1024,512]{1,0:T(8,128)S(1)}, u32[]{:S(2)}, u32[]{:S(2)}) collective-permute-start(f32[1024,512]{1,0:T(8,128)S(1)} %bitcast.114), channel_id=1, source_target_pairs={{0,2},{2,0},{4,6},{6,4},{8,10},{10,8},{12,14},{14,12},{16,18},{18,... | collective-permute-start | bytes 6291464 | tf_op jit(solution)/shard_map/ppermute | solution.py:33

commit v7 on v6

--- a/solution.py
+++ b/solution.py
@@ -211,18 +211,18 @@
     )(patch, all_modes, amplitudes, left, right)
 
 
-def backward_kernel(comp_ref, count_ref, corr_ref, probe_ref, patch_ref, left_ref, right_ref, grad_ref, part_ref):
+def backward_kernel(block_ref, count_ref, corr_ref, probe_ref, patch_ref, left_ref, right_ref, grad_ref, *part):
     side = patch_ref.shape[-1]
     modes = probe_ref.shape[0]
-    own_modes = part_ref.shape[0]
     slot = pl.program_id(0)
-
-    @pl.when(slot == 0)
-    def _():
-        part_ref[...] = jnp.zeros(part_ref.shape, part_ref.dtype)
+    if part:
+        part_ref = part[0]
+
+        @pl.when(slot == 0)
+        def _():
+            part_ref[...] = jnp.zeros(part_ref.shape, part_ref.dtype)
 
     live = (slot < count_ref[0]).astype(jnp.float32)
-    first_own = comp_ref[0] * own_modes
     obj_real = patch_ref[0, 0]
     obj_imag = patch_ref[0, 1]
 
@@ -236,13 +236,9 @@
         back_imag = back[:, side:]
         probe_real = probe_ref[mode, 0]
         probe_imag = probe_ref[mode, 1]
-        own = mode - first_own
-
-        @pl.when((own >= 0) & (own < own_modes))
-        def _():
-            index = jnp.clip(own, 0, own_modes - 1)
-            part_ref[index, 0] += obj_real * back_real + obj_imag * back_imag
-            part_ref[index, 1] += obj_real * back_imag - obj_imag * back_real
+        if part:
+            part_ref[mode, 0] += obj_real * back_real + obj_imag * back_imag
+            part_ref[mode, 1] += obj_real * back_imag - obj_imag * back_real
 
         grad_real = grad_real + (probe_real * back_real + probe_imag * back_imag)
         grad_imag = grad_imag + (probe_real * back_imag - probe_imag * back_real)
@@ -254,42 +250,41 @@
     grad_ref[0, 1] = grad_imag
 
 
-def backward_gradients(correction, all_modes, patch, component, count, own_modes, inverse_table):
+def backward_gradients(correction, all_modes, patch, block, count, block_modes, inverse_table, with_partial):
     slots, modes, _, side, _ = correction.shape
     left = complex_table(inverse_table, False)
     right = complex_table(inverse_table, True)
+    out_specs = [pl.BlockSpec((1, 2, side, side), lambda s, b, n: (s, 0, 0, 0))]
+    out_shape = [jax.ShapeDtypeStruct((slots, 2, side, side), jnp.float32)]
+    if with_partial:
+        out_specs.append(pl.BlockSpec((block_modes, 2, side, side), lambda s, b, n: (0, 0, 0, 0)))
+        out_shape.append(jax.ShapeDtypeStruct((block_modes, 2, side, side), jnp.float32))
     grid_spec = pltpu.PrefetchScalarGridSpec(
         num_scalar_prefetch=2,
         grid=(slots,),
         in_specs=[
-            pl.BlockSpec((1, modes, 2, side, side), lambda s, c, n: (s, 0, 0, 0, 0)),
-            pl.BlockSpec((modes, 2, side, side), lambda s, c, n: (0, 0, 0, 0), pipeline_mode=pl.Buffered(1)),
-            pl.BlockSpec((1, 2, side, side), lambda s, c, n: (s, 0, 0, 0)),
-            pl.BlockSpec((2 * side, 2 * side), lambda s, c, n: (0, 0), pipeline_mode=pl.Buffered(1)),
-            pl.BlockSpec((2 * side, 2 * side), lambda s, c, n: (0, 0), pipeline_mode=pl.Buffered(1)),
+            pl.BlockSpec((1, block_modes, 2, side, side), lambda s, b, n: (s, b[0], 0, 0, 0)),
+            pl.BlockSpec((block_modes, 2, side, side), lambda s, b, n: (b[0], 0, 0, 0), pipeline_mode=pl.Buffered(1)),
+            pl.BlockSpec((1, 2, side, side), lambda s, b, n: (s, 0, 0, 0)),
+            pl.BlockSpec((2 * side, 2 * side), lambda s, b, n: (0, 0), pipeline_mode=pl.Buffered(1)),
+            pl.BlockSpec((2 * side, 2 * side), lambda s, b, n: (0, 0), pipeline_mode=pl.Buffered(1)),
         ],
-        out_specs=[
-            pl.BlockSpec((1, 2, side, side), lambda s, c, n: (s, 0, 0, 0)),
-            pl.BlockSpec((own_modes, 2, side, side), lambda s, c, n: (0, 0, 0, 0)),
-        ],
+        out_specs=out_specs,
     )
     return pl.pallas_call(
         backward_kernel,
         grid_spec=grid_spec,
-        out_shape=[
-            jax.ShapeDtypeStruct((slots, 2, side, side), jnp.float32),
-            jax.ShapeDtypeStruct((own_modes, 2, side, side), jnp.float32),
-        ],
+        out_shape=out_shape,
         compiler_params=pltpu.CompilerParams(
             vmem_limit_bytes=64 * 1024 * 1024, dimension_semantics=("arbitrary",)
         ),
         cost_estimate=pl.CostEstimate(
-            flops=slots * modes * 4 * (2 * side) ** 2 * side,
-            bytes_accessed=slots * (modes + 4) * 2 * side * side * 4,
+            flops=slots * block_modes * 4 * (2 * side) ** 2 * side,
+            bytes_accessed=slots * (block_modes + 4) * 2 * side * side * 4,
             transcendentals=0,
         ),
     )(
-        jnp.reshape(component, (1,)).astype(jnp.int32),
+        jnp.reshape(block, (1,)).astype(jnp.int32),
         jnp.reshape(count, (1,)).astype(jnp.int32),
         correction,
         all_modes,
@@ -351,9 +346,13 @@
     forward_table = dft_tables(side, -1.0)
     inverse_table = dft_tables(side, 1.0)
     correction = forward_correction(patch, all_modes, amplitudes[0], forward_table)
-    whole_grad, probe_partial = backward_gradients(
-        correction, all_modes, patch, component, counts[0], own_modes, inverse_table
-    )
+    own_grad, probe_partial = backward_gradients(
+        correction, all_modes, patch, component, counts[0], own_modes, inverse_table, True
+    )
+    (partner_grad,) = backward_gradients(
+        correction, all_modes, patch, 1 - component, counts[0], own_modes, inverse_table, False
+    )
+    whole_grad = own_grad + partner_grad
     position_y = jnp.sum(whole_grad * grad_y, axis=(1, 2, 3))
     position_x = jnp.sum(whole_grad * grad_x, axis=(1, 2, 3))
     positions = jnp.stack([position_y, position_x], axis=1) / side
@@ -363,7 +362,6 @@
         start = (slot_offsets[slot_id, 0], slot_offsets[slot_id, 1])
         current = lax.dynamic_slice(gradient_plane, start, (side, side))
         gradient_plane = lax.dynamic_update_slice(gradient_plane, current + mine[slot_id, 0], start)
-    probe_partial, gradient_plane = lax.optimization_barrier((probe_partial, gradient_plane))
     received_east = from_behind(gradient_plane[:tile_side, tile_side:], "scan", 1)
     received_south = from_behind(gradient_plane[tile_side:, :tile_side], "scan", GCOLS)
     received_corner = from_behind(gradient_plane[tile_side:, tile_side:], "scan", GCOLS + 1)

time: 435 us -> 424 us (0.975)
  waiting for transfers between devices: 158 us -> 138 us
    ppermute x16, waiting for transfers between devices: 103 us -> 83.3 us  [sub_shift(): return lax.ppermute(value, 'scan', pairs)]
    pallas_call x1 -> x2, Pallas kernels: 54.2 us -> 52.2 us  [backward_gradients(): pl.pallas_call(backward_kernel, grid_spec=grid_spec, out_shape=out_shape,...]
  transfers between devices with their start and end apart: 25 -> 25, of which waited for: 16 -> 13; matrix products, arithmetic and copies ran while one was open for 17% -> 26% of each run, Pallas kernels for 0% -> 6%
where the time goes in v7:
time: 424 us; the launch traced here: 415 us
  waiting for transfers between devices  138 us (33%)
  Pallas kernels  94.5 us (22%)
  other arithmetic  78.7 us (19%)
  local copies, waits for them, and re-layouts  50.6 us (12%)
  starting transfers between devices  32.3 us (8%)
  between operations  21.4 us (5%)
    ppermute x16, waiting for transfers between devices, sub_shift(): return lax.ppermute(value, 'scan', pairs)  83.3 us
    ppermute x5, waiting for transfers between devices, from_behind(): return lax.ppermute(value, axis, pairs)  54.5 us
    pallas_call x2, Pallas kernels, backward_gradients(): pl.pallas_call(backward_kernel, grid_spec=grid_spec, out_shape=out_shape,...  52.2 us
    pallas_call x1, Pallas kernels, forward_correction(): pl.pallas_call(forward_kernel, grid=(slots,), in_specs=[pl.BlockSpec((1,...  42.3 us
    dynamic_update_slice x3, local copies, waits for them, and re-layouts, shards(): lax.dynamic_update_slice(gradient_plane, current + mine[slot_id, 0], start)  22.8 us
    another operation x5, other arithmetic  19.9 us
    ppermute x16, starting transfers between devices, sub_shift(): return lax.ppermute(value, 'scan', pairs)  17.9 us
    reduce_sum x1, other arithmetic, shards(): position_y = jnp.sum(whole_grad * grad_y, axis=(1, 2, 3))  17.1 us
  transfers between devices with their start and end apart: 25, of which 13 were waited for; matrix products, arithmetic and copies ran while one was open for 26% of the time, Pallas kernels for 6%

profile of v7, /device:TPU:65, one launch (start us, length us, event | category | flops | bytes accessed | tf_op | source)
XLA Modules:
  0.0 415.4 jit_solution(11052587698070073132)
XLA Ops:
  0.6 5.2 %collective-permute-start.1 = (f32[2,512,512]{2,1,0:T(8,128)}, f32[2,512,512]{2,1,0:T(8,128)}, u32[]{:S(2)}, u32[]{:S(2)}) collective-permute-start(f32[2,512,512]{2,1,0:T(8,128)} %bitcast.1), channel_id=1, source_target_pairs={{0,112},{2,114},{4,116},{6,118},{8,120},{10,122},{12,124},{14,126}... | collective-permute-start | bytes 6291464 | tf_op jit(solution)/shard_map/ppermute | solution.py:23
  5.8 3.1 dynamic-slice_bitcast_fusion.3
  10.2 2.9 collective-permute-start
  13.1 4.0 multiply_convert_fusion
  17.1 54.4 %collective-permute-done.1 = f32[2,512,512]{2,1,0:T(8,128)} collective-permute-done((f32[2,512,512]{2,1,0:T(8,128)}, f32[2,512,512]{2,1,0:T(8,128)}, u32[]{:S(2)}, u32[]{:S(2)}) %collective-permute-start.1) | collective-permute-done | bytes 2097184 | tf_op jit(solution)/shard_map/ppermute | solution.py:23
  71.5 4.9 %collective-permute-start.2 = (f32[2,512,512]{2,1,0:T(8,128)}, f32[2,512,512]{2,1,0:T(8,128)}, u32[]{:S(2)}, u32[]{:S(2)}) collective-permute-start(f32[2,512,512]{2,1,0:T(8,128)} %collective-permute-done.1), channel_id=1, source_target_pairs={{2,0},{6,4},{10,8},{14,12},{18,16},{22,20},{26,24},{30,28},{34,32}... | collective-permute-start | bytes 6291464 | tf_op jit(solution)/shard_map/ppermute | solution.py:323
  76.4 4.0 multiply_convert_fusion.1
  80.4 4.0 negate_convert_fusion
  84.5 4.0 multiply_convert_fusion.2
  88.5 4.0 negate_convert_fusion.1
  116.0 4.2 %fusion.9 = (bf16[1024,1024]{1,0:T(8,128)(2,1)}, bf16[1024,1024]{1,0:T(8,128)(2,1)}) fusion(bf16[512,512]{1,0:T(8,128)(2,1)} %get-tuple-element.62, bf16[512,512]{1,0:T(8,128)(2,1)S(1)} %get-tuple-element.44, bf16[512,512]{1,0:T(8,128)(2,1)} %get-tuple-element.63, bf16[512,512]{1,0:T(8,128)(2,1)S(1)} %get-tuple-element.43), kind=kLoop, calls=%fused_computation.26 | loop fusion | flops 14680064 | bytes 6291456 | tf_op jit(solution)/shard_map/concatenate | solution.py:154
  120.2 10.2 %fusion.7 = (bf16[1024,1024]{1,0:T(8,128)(2,1)}, bf16[1024,1024]{1,0:T(8,128)(2,1)}) fusion(bf16[512,512]{1,0:T(8,128)(2,1)S(1)} %copy-done.5, bf16[512,512]{1,0:T(8,128)(2,1)S(1)} %copy-done.4, bf16[512,512]{1,0:T(8,128)(2,1)S(1)} %copy-done.6, bf16[512,512]{1,0:T(8,128)(2,1)S(1)} %copy-done.3), kind=kLoop, calls=%fused_computation.24 | loop fusion | flops 14680064 | bytes 6291456 | tf_op jit(solution)/shard_map/concatenate | solution.py:154
  131.0 3.3 maximum_maximum_fusion
  134.3 2.1 dynamic-slice_bitcast_fusion.2
  137.0 5.0 %slice.134.patch_ref = f32[3,2,512,512]{3,2,1,0:T(8,128)} slice(f32[3,2,514,514]{3,2,1,0:T(8,128)S(1)} %pad_maximum_fusion), slice={[0:3], [0:2], [1:513], [1:513]} | slice | bytes 12582912 | tf_op jit(solution)/shard_map/slice | solution.py:339
  142.0 2.9 select_bitcast_fusion.1
  145.5 4.0 maximum_select_fusion.probe_ref
  149.5 42.3 %shard_map.76.corr_ref = bf16[3,4,2,512,512]{4,3,2,1,0:T(8,128)(2,1)} custom-call(f32[3,2,512,512]{3,2,1,0:T(8,128)} %slice.134.patch_ref, f32[4,2,512,512]{3,2,1,0:T(8,128)} %maximum_select_fusion.probe_ref, f32[3,512,512]{2,1,0:T(8,128)} %bitcast.127, bf16[1024,1024]{1,0:T(8,128)(2,1)} %get-tuple-element.36.left_ref, ...), custom_call_target="tpu_custom_call" | custom-call | flops 25769803776 | bytes 44040192 | tf_op jit(solution)/shard_map/pallas_call | solution.py:192
  191.8 28.3 %shard_map.77 = (f32[3,2,512,512]{3,2,1,0:T(8,128)}, f32[2,2,512,512]{3,2,1,0:T(8,128)}) custom-call(s32[1]{0:T(128)} %bitcast.block_ref, s32[1]{0:T(128)S(6)} %copy.19.count_ref, bf16[3,4,2,512,512]{4,3,2,1,0:T(8,128)(2,1)} %shard_map.76.corr_ref, f32[4,2,512,512]{3,2,1,0:T(8,128)} %maximum_select_fusion.probe_ref, f32[3,2,512,512]{3,2,1,0:T(8,128)} %slice.134.patch_ref, ...), custom_call_target="tpu_custom_call" | custom-call | flops 12884901888 | bytes 37748736 | tf_op jit(solution)/shard_map/pallas_call | solution.py:274
  220.1 3.1 constant_dynamic-slice_fusion.1
  223.3 2.1 collective-permute-start.6
  225.4 23.9 %shard_map.78 = f32[3,2,512,512]{3,2,1,0:T(8,128)} custom-call(s32[1]{0:T(128)} %bitcast.28.block_ref, s32[1]{0:T(128)S(6)} %copy.19.count_ref, bf16[3,4,2,512,512]{4,3,2,1,0:T(8,128)(2,1)} %shard_map.76.corr_ref, f32[4,2,512,512]{3,2,1,0:T(8,128)} %maximum_select_fusion.probe_ref, f32[3,2,512,512]{3,2,1,0:T(8,128)} %slice.134.patch_ref, ...), custom_call_target="tpu_custom_call" | custom-call | flops 12884901888 | bytes 37748736 | tf_op jit(solution)/shard_map/pallas_call | solution.py:274
  249.3 17.1 %fusion.5 = (f32[3]{0:T(128)S(1)}, f32[3]{0:T(128)S(1)}, f32[3,2,512,512]{3,2,1,0:T(8,128)S(1)}) fusion(f32[3,2,514,514]{3,2,1,0:T(8,128)} %copy-done, f32[3,2,512,512]{3,2,1,0:T(8,128)} %get-tuple-element.10, f32[3,2,512,512]{3,2,1,0:T(8,128)} %shard_map.78), kind=kLoop, calls=%fused_computation.10 | loop fusion | flops 14155770 | bytes 44040216 | tf_op jit(solution)/shard_map/reduce_sum | solution.py:356
  266.4 2.6 copy-done.1
  269.1 2.5 broadcast_in_dim.45
  271.6 7.6 %dynamic_update_slice.35 = f32[1024,1024]{1,0:T(8,128)} dynamic-update-slice(f32[1024,1024]{1,0:T(8,128)} %broadcast_in_dim.45, f32[512,512]{1,0:T(8,128)S(1)} %dynamic-slice_bitcast_fusion.6, s32[]{:T(128)S(6)} %select_n.308, s32[]{:T(128)S(6)} %select_n.309) | dynamic-update-slice | bytes 2097156 | tf_op jit(solution)/shard_map/dynamic_update_slice | solution.py:364
  279.3 2.7 dynamic-slice_add_fusion
  283.1 2.3 collective-permute-start.9
  286.7 2.0 fusion.21
  288.6 7.7 %dynamic_update_slice.36 = f32[1024,1024]{1,0:T(8,128)} dynamic-update-slice(f32[1024,1024]{1,0:T(8,128)} %dynamic_update_slice.35, f32[512,512]{1,0:T(8,128)S(1)} %fusion.21, s32[]{:T(128)S(6)} %select_n.310, s32[]{:T(128)S(6)} %select_n.311) | dynamic-update-slice | bytes 2097156 | tf_op jit(solution)/shard_map/dynamic_update_slice | solution.py:364
  296.3 2.0 fusion.20
  298.3 7.5 %dynamic_update_slice.37 = f32[1024,1024]{1,0:T(8,128)} dynamic-update-slice(f32[1024,1024]{1,0:T(8,128)} %dynamic_update_slice.36, f32[512,512]{1,0:T(8,128)S(1)} %fusion.20, s32[]{:T(128)S(6)} %select_n.312, s32[]{:T(128)S(6)} %select_n.313) | dynamic-update-slice | bytes 2097156 | tf_op jit(solution)/shard_map/dynamic_update_slice | solution.py:364
  305.8 3.6 fusion.30
  309.5 2.9 collective-permute-done.7
  312.4 1.6 fusion.26
  315.4 27.7 %collective-permute-done.12 = f32[64,512]{1,0:T(8,128)S(1)} collective-permute-done((f32[64,512]{1,0:T(8,128)S(1)}, f32[64,512]{1,0:T(8,128)S(1)}, u32[]{:S(2)}, u32[]{:S(2)}) %collective-permute-start.12) | collective-permute-done | bytes 131104 | tf_op jit(solution)/shard_map/ppermute | solution.py:33
  344.1 19.6 %collective-permute-done.11 = f32[64,512]{1,0:T(8,128)S(1)} collective-permute-done((f32[64,512]{1,0:T(8,128)S(1)}, f32[64,512]{1,0:T(8,128)S(1)}, u32[]{:S(2)}, u32[]{:S(2)}) %collective-permute-start.11) | collective-permute-done | bytes 131104 | tf_op jit(solution)/shard_map/ppermute | solution.py:33
  363.7 2.8 collective-permute-done.10
  367.2 2.5 collective-permute-done.13
  370.3 2.7 collective-permute-done.17
  375.8 3.7 collective-permute-done.18
  380.5 2.0 collective-permute-start.22
  383.5 10.4 %collective-permute-done.21 = f32[256,512]{1,0:T(8,128)S(1)} collective-permute-done((f32[256,512]{1,0:T(8,128)S(1)}, f32[256,512]{1,0:T(8,128)S(1)}, u32[]{:S(2)}, u32[]{:S(2)}) %collective-permute-start.21) | collective-permute-done | bytes 524320 | tf_op jit(solution)/shard_map/ppermute | solution.py:33
  394.0 4.9 %collective-permute-done.22 = f32[256,512]{1,0:T(8,128)S(1)} collective-permute-done((f32[256,512]{1,0:T(8,128)S(1)}, f32[256,512]{1,0:T(8,128)S(1)}, u32[]{:S(2)}, u32[]{:S(2)}) %collective-permute-start.22) | collective-permute-done | bytes 524320 | tf_op jit(solution)/shard_map/ppermute | solution.py:33
  399.0 5.1 %collective-permute-done.23 = f32[256,512]{1,0:T(8,128)S(1)} collective-permute-done((f32[256,512]{1,0:T(8,128)S(1)}, f32[256,512]{1,0:T(8,128)S(1)}, u32[]{:S(2)}, u32[]{:S(2)}) %collective-permute-start.23) | collective-permute-done | bytes 524320 | tf_op jit(solution)/shard_map/ppermute | solution.py:33
  404.1 4.0 collective-permute-start.24
  408.0 3.6 fusion.19
  412.4 2.5 pad_maximum_fusion.1
  (73 shorter events, 18.2 us)
Async XLA Ops:
  0.6 70.9 %collective-permute-start.1 = (f32[2,512,512]{2,1,0:T(8,128)}, f32[2,512,512]{2,1,0:T(8,128)}, u32[]{:S(2)}, u32[]{:S(2)}) collective-permute-start(f32[2,512,512]{2,1,0:T(8,128)} %bitcast.1), channel_id=1, source_target_pairs={{0,112},{2,114},{4,116},{6,118},{8,120},{10,122},{12,124},{14,126}... | collective-permute-start | bytes 6291464 | tf_op jit(solution)/shard_map/ppermute | solution.py:23
  8.9 86.5 %collective-permute-start.4 = (f32[2,512,512]{2,1,0:T(8,128)}, f32[2,512,512]{2,1,0:T(8,128)}, u32[]{:S(2)}, u32[]{:S(2)}) collective-permute-start(f32[2,512,512]{2,1,0:T(8,128)} %dynamic-slice_bitcast_fusion.3), channel_id=1, source_target_pairs={{0,5},{1,4},{2,7},{3,6},{4,1},{5,0},{6,3},{7,2},{8,13},{9,12},{10,... | collective-permute-start | bytes 6291464 | tf_op jit(solution)/shard_map/ppermute | solution.py:306
  8.9 121.6 %collective-permute-start.3 = (f32[2,512,512]{2,1,0:T(8,128)}, f32[2,512,512]{2,1,0:T(8,128)S(1)}, u32[]{:S(2)}, u32[]{:S(2)}) collective-permute-start(f32[2,512,512]{2,1,0:T(8,128)} %bitcast.1), channel_id=1, source_target_pairs={{20,2},{24,6},{28,10},{32,14},{36,18},{40,22},{44,26},{48,30},{52,... | collective-permute-start | bytes 6291464 | tf_op jit(solution)/shard_map/ppermute | solution.py:319
  10.2 120.8 %collective-permute-start = (f32[2,512,512]{2,1,0:T(8,128)}, f32[2,512,512]{2,1,0:T(8,128)}, u32[]{:S(2)}, u32[]{:S(2)}) collective-permute-start(f32[2,512,512]{2,1,0:T(8,128)} %bitcast.1), channel_id=1, source_target_pairs={{0,126},{2,0},{4,2},{6,4},{8,6},{10,8},{12,10},{14,12},{16,14},{18... | collective-permute-start | bytes 6291464 | tf_op jit(solution)/shard_map/ppermute | solution.py:23
  71.5 58.9 %collective-permute-start.2 = (f32[2,512,512]{2,1,0:T(8,128)}, f32[2,512,512]{2,1,0:T(8,128)}, u32[]{:S(2)}, u32[]{:S(2)}) collective-permute-start(f32[2,512,512]{2,1,0:T(8,128)} %collective-permute-done.1), channel_id=1, source_target_pairs={{2,0},{6,4},{10,8},{14,12},{18,16},{22,20},{26,24},{30,28},{34,32}... | collective-permute-start | bytes 6291464 | tf_op jit(solution)/shard_map/ppermute | solution.py:323
  92.8 2.7 copy-start.7
  95.4 46.6 %collective-permute-start.5 = (f32[2,512,512]{2,1,0:T(8,128)}, f32[2,512,512]{2,1,0:T(8,128)}, u32[]{:S(2)}, u32[]{:S(2)}) collective-permute-start(f32[2,512,512]{2,1,0:T(8,128)} %collective-permute-done.4), channel_id=1, source_target_pairs={{0,2},{2,0},{4,6},{6,4},{8,10},{10,8},{12,14},{14,12},{16,18},{18,... | collective-permute-start | bytes 6291464 | tf_op jit(solution)/shard_map/ppermute | solution.py:307
  115.9 4.3 %copy-start.3 = (bf16[512,512]{1,0:T(8,128)(2,1)S(1)}, bf16[512,512]{1,0:T(8,128)(2,1)}, u32[]{:S(2)}) copy-start(bf16[512,512]{1,0:T(8,128)(2,1)} %get-tuple-element.39) | copy-start | bytes 1572868
  115.9 4.3 %copy-start.4 = (bf16[512,512]{1,0:T(8,128)(2,1)S(1)}, bf16[512,512]{1,0:T(8,128)(2,1)}, u32[]{:S(2)}) copy-start(bf16[512,512]{1,0:T(8,128)(2,1)} %get-tuple-element.40) | copy-start | bytes 1572868
  116.0 4.2 %copy-start.5 = (bf16[512,512]{1,0:T(8,128)(2,1)S(1)}, bf16[512,512]{1,0:T(8,128)(2,1)}, u32[]{:S(2)}) copy-start(bf16[512,512]{1,0:T(8,128)(2,1)} %get-tuple-element.60) | copy-start | bytes 1572868
  116.0 4.2 %copy-start.6 = (bf16[512,512]{1,0:T(8,128)(2,1)S(1)}, bf16[512,512]{1,0:T(8,128)(2,1)}, u32[]{:S(2)}) copy-start(bf16[512,512]{1,0:T(8,128)(2,1)} %get-tuple-element.61) | copy-start | bytes 1572868
  137.0 5.0 %copy-start = (f32[3,2,514,514]{3,2,1,0:T(8,128)}, f32[3,2,514,514]{3,2,1,0:T(8,128)S(1)}, u32[]{:S(2)}) copy-start(f32[3,2,514,514]{3,2,1,0:T(8,128)S(1)} %pad_maximum_fusion) | copy-start | bytes 19022116
  142.0 3.4 copy-start.2
  223.3 56.0 %collective-permute-start.6 = (f32[1024,512]{1,0:T(8,128)}, f32[1024,512]{1,0:T(8,128)}, u32[]{:S(2)}, u32[]{:S(2)}) collective-permute-start(f32[1024,512]{1,0:T(8,128)} %constant_dynamic-slice_fusion.1), channel_id=1, source_target_pairs={{0,2},{2,0},{4,6},{6,4},{8,10},{10,8},{12,14},{14,12},{16,18},{18,... | collective-permute-start | bytes 6291464 | tf_op jit(solution)/shard_map/ppermute | solution.py:33
  266.4 2.7 copy-start.1
  283.1 26.3 %collective-permute-start.9 = (f32[256,512]{1,0:T(8,128)}, f32[256,512]{1,0:T(8,128)}, u32[]{:S(2)}, u32[]{:S(2)}) collective-permute-start(f32[256,512]{1,0:T(8,128)} %get-tuple-element.31), channel_id=1, source_target_pairs={{0,96},{2,98},{4,100},{6,102},{8,104},{10,106},{12,108},{14,110},{... | collective-permute-start | bytes 1572872 | tf_op jit(solution)/shard_map/ppermute | solution.py:33
  285.5 24.0 %collective-permute-start.8 = (f32[256,512]{1,0:T(8,128)}, f32[256,512]{1,0:T(8,128)}, u32[]{:S(2)}, u32[]{:S(2)}) collective-permute-start(f32[256,512]{1,0:T(8,128)} %get-tuple-element.32), channel_id=1, source_target_pairs={{0,64},{2,66},{4,68},{6,70},{8,72},{10,74},{12,76},{14,78},{16,80}... | collective-permute-start | bytes 1572872 | tf_op jit(solution)/shard_map/ppermute | solution.py:33
  286.0 26.4 %collective-permute-start.7 = (f32[256,512]{1,0:T(8,128)}, f32[256,512]{1,0:T(8,128)}, u32[]{:S(2)}, u32[]{:S(2)}) collective-permute-start(f32[256,512]{1,0:T(8,128)} %get-tuple-element.30), channel_id=1, source_target_pairs={{0,32},{2,34},{4,36},{6,38},{8,40},{10,42},{12,44},{14,46},{16,48}... | collective-permute-start | bytes 1572872 | tf_op jit(solution)/shard_map/ppermute | solution.py:33
  309.4 60.3 %collective-permute-start.14 = (f32[512,512]{1,0:T(8,128)}, f32[512,512]{1,0:T(8,128)}, u32[]{:S(2)}, u32[]{:S(2)}) collective-permute-start(f32[512,512]{1,0:T(8,128)} %get-tuple-element.27), channel_id=1, source_target_pairs={{0,2},{2,4},{4,6},{6,8},{8,10},{10,12},{12,14},{14,16},{16,18},{18... | collective-permute-start | bytes 3145736 | tf_op jit(solution)/shard_map/ppermute | solution.py:23
  309.4 60.3 %collective-permute-start.15 = (f32[512,512]{1,0:T(8,128)}, f32[512,512]{1,0:T(8,128)}, u32[]{:S(2)}, u32[]{:S(2)}) collective-permute-start(f32[512,512]{1,0:T(8,128)} %get-tuple-element.26), channel_id=1, source_target_pairs={{0,16},{2,18},{4,20},{6,22},{8,24},{10,26},{12,28},{14,30},{16,32}... | collective-permute-start | bytes 3145736 | tf_op jit(solution)/shard_map/ppermute | solution.py:23
  309.4 60.3 %collective-permute-start.16 = (f32[512,512]{1,0:T(8,128)}, f32[512,512]{1,0:T(8,128)}, u32[]{:S(2)}, u32[]{:S(2)}) collective-permute-start(f32[512,512]{1,0:T(8,128)} %get-tuple-element.25), channel_id=1, source_target_pairs={{0,18},{2,20},{4,22},{6,24},{8,26},{10,28},{12,30},{14,32},{16,34}... | collective-permute-start | bytes 3145736 | tf_op jit(solution)/shard_map/ppermute | solution.py:23
  314.0 29.0 %collective-permute-start.12 = (f32[64,512]{1,0:T(8,128)S(1)}, f32[64,512]{1,0:T(8,128)S(1)}, u32[]{:S(2)}, u32[]{:S(2)}) collective-permute-start(f32[64,512]{1,0:T(8,128)S(1)} %get-tuple-element.46), channel_id=1, source_target_pairs={{0,24},{2,26},{4,28},{6,30},{8,0},{10,2},{12,4},{14,6},{16,8},{18,... | collective-permute-start | bytes 393224 | tf_op jit(solution)/shard_map/ppermute | solution.py:33
  314.1 49.6 %collective-permute-start.11 = (f32[64,512]{1,0:T(8,128)S(1)}, f32[64,512]{1,0:T(8,128)S(1)}, u32[]{:S(2)}, u32[]{:S(2)}) collective-permute-start(f32[64,512]{1,0:T(8,128)S(1)} %get-tuple-element.47), channel_id=1, source_target_pairs={{0,16},{2,18},{4,20},{6,22},{8,24},{10,26},{12,28},{14,30},{16,0},... | collective-permute-start | bytes 393224 | tf_op jit(solution)/shard_map/ppermute | solution.py:33
  343.1 23.4 %collective-permute-start.10 = (f32[64,512]{1,0:T(8,128)S(1)}, f32[64,512]{1,0:T(8,128)S(1)}, u32[]{:S(2)}, u32[]{:S(2)}) collective-permute-start(f32[64,512]{1,0:T(8,128)S(1)} %get-tuple-element.45), channel_id=1, source_target_pairs={{0,8},{2,10},{4,12},{6,14},{8,16},{10,18},{12,20},{14,22},{16,24},... | collective-permute-start | bytes 393224 | tf_op jit(solution)/shard_map/ppermute | solution.py:33
  366.5 3.2 collective-permute-start.13
  369.8 3.2 collective-permute-start.17
  373.0 6.5 %collective-permute-start.18 = (f32[64,512]{1,0:T(8,128)S(1)}, f32[64,512]{1,0:T(8,128)S(1)}, u32[]{:S(2)}, u32[]{:S(2)}) collective-permute-start(f32[64,512]{1,0:T(8,128)S(1)} %pad_maximum_fusion.14), channel_id=1, source_target_pairs={{0,8},{2,10},{4,12},{6,14},{8,16},{10,18},{12,20},{14,22},{16,24},... | collective-permute-start | bytes 393224 | tf_op jit(solution)/shard_map/ppermute | solution.py:33
  373.2 6.4 %collective-permute-start.19 = (f32[64,512]{1,0:T(8,128)S(1)}, f32[64,512]{1,0:T(8,128)S(1)}, u32[]{:S(2)}, u32[]{:S(2)}) collective-permute-start(f32[64,512]{1,0:T(8,128)S(1)} %pad_maximum_fusion.14), channel_id=1, source_target_pairs={{0,16},{2,18},{4,20},{6,22},{8,24},{10,26},{12,28},{14,30},{16,0},... | collective-permute-start | bytes 393224 | tf_op jit(solution)/shard_map/ppermute | solution.py:33
  374.5 5.9 %collective-permute-start.20 = (f32[64,512]{1,0:T(8,128)S(1)}, f32[64,512]{1,0:T(8,128)S(1)}, u32[]{:S(2)}, u32[]{:S(2)}) collective-permute-start(f32[64,512]{1,0:T(8,128)S(1)} %pad_maximum_fusion.14), channel_id=1, source_target_pairs={{0,24},{2,26},{4,28},{6,30},{8,0},{10,2},{12,4},{14,6},{16,8},{18,... | collective-permute-start | bytes 393224 | tf_op jit(solution)/shard_map/ppermute | solution.py:33
  380.4 13.5 %collective-permute-start.21 = (f32[256,512]{1,0:T(8,128)S(1)}, f32[256,512]{1,0:T(8,128)S(1)}, u32[]{:S(2)}, u32[]{:S(2)}) collective-permute-start(f32[256,512]{1,0:T(8,128)S(1)} %bitcast.117), channel_id=1, source_target_pairs={{0,32},{2,34},{4,36},{6,38},{8,40},{10,42},{12,44},{14,46},{16,48}... | collective-permute-start | bytes 1572872 | tf_op jit(solution)/shard_map/ppermute | solution.py:33
  380.5 18.4 %collective-permute-start.22 = (f32[256,512]{1,0:T(8,128)S(1)}, f32[256,512]{1,0:T(8,128)S(1)}, u32[]{:S(2)}, u32[]{:S(2)}) collective-permute-start(f32[256,512]{1,0:T(8,128)S(1)} %bitcast.118), channel_id=1, source_target_pairs={{0,64},{2,66},{4,68},{6,70},{8,72},{10,74},{12,76},{14,78},{16,80}... | collective-permute-start | bytes 1572872 | tf_op jit(solution)/shard_map/ppermute | solution.py:33
  382.5 21.5 %collective-permute-start.23 = (f32[256,512]{1,0:T(8,128)S(1)}, f32[256,512]{1,0:T(8,128)S(1)}, u32[]{:S(2)}, u32[]{:S(2)}) collective-permute-start(f32[256,512]{1,0:T(8,128)S(1)} %bitcast.119), channel_id=1, source_target_pairs={{0,96},{2,98},{4,100},{6,102},{8,104},{10,106},{12,108},{14,110},{... | collective-permute-start | bytes 1572872 | tf_op jit(solution)/shard_map/ppermute | solution.py:33
  404.1 7.7 %collective-permute-start.24 = (f32[1024,512]{1,0:T(8,128)S(1)}, f32[1024,512]{1,0:T(8,128)S(1)}, u32[]{:S(2)}, u32[]{:S(2)}) collective-permute-start(f32[1024,512]{1,0:T(8,128)S(1)} %bitcast.113), channel_id=1, source_target_pairs={{0,2},{2,0},{4,6},{6,4},{8,10},{10,8},{12,14},{14,12},{16,18},{18,... | collective-permute-start | bytes 6291464 | tf_op jit(solution)/shard_map/ppermute | solution.py:33

commit v8 on v7

--- a/solution.py
+++ b/solution.py
@@ -304,7 +304,8 @@
     sent = lax.dynamic_index_in_dim(probe_modes, core, 0, keepdims=False)
     pairs = [(s * 2 + m, (s ^ 2) * 2 + 1 - m) for s in range(count) for m in range(2)]
     got = lax.ppermute(sent, ("scan", "mode"), pairs)
-    mate = lax.ppermute(got, "scan", [(s, s ^ 1) for s in range(count)])
+    other = lax.dynamic_index_in_dim(probe_modes, 1 - core, 0, keepdims=False)
+    mate = lax.ppermute(other, "mode", [(0, 1), (1, 0)])
     partner_modes = jnp.stack([jnp.where(core == 0, got, mate), jnp.where(core == 0, mate, got)])
     component = lax.axis_index("mode")
     all_modes = jnp.where(

time: 424 us -> 414 us (0.976)
  waiting for transfers between devices: 138 us -> 111 us
  starting transfers between devices: 32.3 us -> 47.2 us
    ppermute x5, waiting for transfers between devices: 54.5 us -> 33.9 us  [from_behind(): return lax.ppermute(value, axis, pairs)]
    ppermute x16, starting transfers between devices: 17.9 us -> 31.5 us  [sub_shift(): return lax.ppermute(value, 'scan', pairs)]
    ppermute x16, waiting for transfers between devices: 83.3 us -> 77.4 us  [sub_shift(): return lax.ppermute(value, 'scan', pairs)]
where the time goes in v8:
time: 414 us; the launch traced here: 406 us
  waiting for transfers between devices  111 us (27%)
  Pallas kernels  94.5 us (23%)
  other arithmetic  77.9 us (19%)
  local copies, waits for them, and re-layouts  53.2 us (13%)
  starting transfers between devices  47.2 us (11%)
  between operations  21.6 us (5%)
    ppermute x16, waiting for transfers between devices, sub_shift(): return lax.ppermute(value, 'scan', pairs)  77.4 us
    pallas_call x2, Pallas kernels, backward_gradients(): pl.pallas_call(backward_kernel, grid_spec=grid_spec, out_shape=out_shape,...  52.2 us
    pallas_call x1, Pallas kernels, forward_correction(): pl.pallas_call(forward_kernel, grid=(slots,), in_specs=[pl.BlockSpec((1,...  42.3 us
    ppermute x5, waiting for transfers between devices, from_behind(): return lax.ppermute(value, axis, pairs)  33.9 us
    ppermute x16, starting transfers between devices, sub_shift(): return lax.ppermute(value, 'scan', pairs)  31.5 us
    dynamic_update_slice x3, local copies, waits for them, and re-layouts, shards(): lax.dynamic_update_slice(gradient_plane, current + mine[slot_id, 0], start)  22.7 us
    another operation x5, other arithmetic  20 us
    reduce_sum x1, other arithmetic, shards(): position_y = jnp.sum(whole_grad * grad_y, axis=(1, 2, 3))  17.1 us
  transfers between devices with their start and end apart: 25, of which 13 were waited for; matrix products, arithmetic and copies ran while one was open for 26% of the time, Pallas kernels for 6%

profile of v8, /device:TPU:65, one launch (start us, length us, event | category | flops | bytes accessed | tf_op | source)
XLA Modules:
  0.0 405.7 jit_solution(11838468156946625781)
XLA Ops:
  0.6 5.2 %collective-permute-start.1 = (f32[2,512,512]{2,1,0:T(8,128)}, f32[2,512,512]{2,1,0:T(8,128)}, u32[]{:S(2)}, u32[]{:S(2)}) collective-permute-start(f32[2,512,512]{2,1,0:T(8,128)} %bitcast.125), channel_id=1, source_target_pairs={{0,112},{2,114},{4,116},{6,118},{8,120},{10,122},{12,124},{14,126}... | collective-permute-start | bytes 6291464 | tf_op jit(solution)/shard_map/ppermute | solution.py:23
  7.1 2.9 collective-permute-start
  10.0 4.8 %dynamic-slice_bitcast_fusion.4 = (f32[2,512,512]{2,1,0:T(8,128)}, f32[2,512,512]{2,1,0:T(8,128)}) fusion(f32[2,2,512,512]{3,2,1,0:T(8,128)} %param.6, s32[]{:T(128)S(6)} %select_n.305, s32[]{:T(128)S(6)} %select_n.306), kind=kLoop, calls=%fused_computation.31 | loop fusion | bytes 8388616 | tf_op jit(solution)/shard_map/jit(dynamic_index_in_dim)/squeeze | solution.py:304
  16.1 4.0 multiply_convert_fusion
  20.1 4.0 multiply_convert_fusion.1
  24.1 4.0 negate_convert_fusion
  28.1 4.0 multiply_convert_fusion.2
  32.1 4.0 negate_convert_fusion.1
  37.6 33.9 %collective-permute-done.1 = f32[2,512,512]{2,1,0:T(8,128)} collective-permute-done((f32[2,512,512]{2,1,0:T(8,128)}, f32[2,512,512]{2,1,0:T(8,128)}, u32[]{:S(2)}, u32[]{:S(2)}) %collective-permute-start.1) | collective-permute-done | bytes 2097184 | tf_op jit(solution)/shard_map/ppermute | solution.py:23
  71.5 4.9 %collective-permute-start.2 = (f32[2,512,512]{2,1,0:T(8,128)}, f32[2,512,512]{2,1,0:T(8,128)}, u32[]{:S(2)}, u32[]{:S(2)}) collective-permute-start(f32[2,512,512]{2,1,0:T(8,128)} %collective-permute-done.1), channel_id=1, source_target_pairs={{2,0},{6,4},{10,8},{14,12},{18,16},{22,20},{26,24},{30,28},{34,32}... | collective-permute-start | bytes 6291464 | tf_op jit(solution)/shard_map/ppermute | solution.py:324
  98.4 4.1 %fusion.9 = (bf16[1024,1024]{1,0:T(8,128)(2,1)}, bf16[1024,1024]{1,0:T(8,128)(2,1)}) fusion(bf16[512,512]{1,0:T(8,128)(2,1)} %get-tuple-element.64, bf16[512,512]{1,0:T(8,128)(2,1)S(1)} %get-tuple-element.46, bf16[512,512]{1,0:T(8,128)(2,1)} %get-tuple-element.65, bf16[512,512]{1,0:T(8,128)(2,1)S(1)} %get-tuple-element.45), kind=kLoop, calls=%fused_computation.26 | loop fusion | flops 14680064 | bytes 6291456 | tf_op jit(solution)/shard_map/concatenate | solution.py:154
  102.6 10.2 %fusion.7 = (bf16[1024,1024]{1,0:T(8,128)(2,1)}, bf16[1024,1024]{1,0:T(8,128)(2,1)}) fusion(bf16[512,512]{1,0:T(8,128)(2,1)S(1)} %copy-done.5, bf16[512,512]{1,0:T(8,128)(2,1)S(1)} %copy-done.4, bf16[512,512]{1,0:T(8,128)(2,1)S(1)} %copy-done.6, bf16[512,512]{1,0:T(8,128)(2,1)S(1)} %copy-done.3), kind=kLoop, calls=%fused_computation.24 | loop fusion | flops 14680064 | bytes 6291456 | tf_op jit(solution)/shard_map/concatenate | solution.py:154
  112.8 2.9 select_bitcast_fusion.1
  116.3 4.1 maximum_select_fusion.probe_ref
  121.9 2.6 maximum_maximum_fusion
  124.6 2.1 dynamic-slice_bitcast_fusion.2
  127.3 5.0 %slice.134.patch_ref = f32[3,2,512,512]{3,2,1,0:T(8,128)} slice(f32[3,2,514,514]{3,2,1,0:T(8,128)S(1)} %pad_maximum_fusion), slice={[0:3], [0:2], [1:513], [1:513]} | slice | bytes 12582912 | tf_op jit(solution)/shard_map/slice | solution.py:340
  132.3 42.3 %shard_map.76.corr_ref = bf16[3,4,2,512,512]{4,3,2,1,0:T(8,128)(2,1)} custom-call(f32[3,2,512,512]{3,2,1,0:T(8,128)} %slice.134.patch_ref, f32[4,2,512,512]{3,2,1,0:T(8,128)} %maximum_select_fusion.probe_ref, f32[3,512,512]{2,1,0:T(8,128)} %bitcast.133, bf16[1024,1024]{1,0:T(8,128)(2,1)} %get-tuple-element.38.left_ref, ...), custom_call_target="tpu_custom_call" | custom-call | flops 25769803776 | bytes 44040192 | tf_op jit(solution)/shard_map/pallas_call | solution.py:192
  174.7 28.3 %shard_map.77 = (f32[3,2,512,512]{3,2,1,0:T(8,128)}, f32[2,2,512,512]{3,2,1,0:T(8,128)}) custom-call(s32[1]{0:T(128)} %bitcast.block_ref, s32[1]{0:T(128)S(6)} %copy.19.count_ref, bf16[3,4,2,512,512]{4,3,2,1,0:T(8,128)(2,1)} %shard_map.76.corr_ref, f32[4,2,512,512]{3,2,1,0:T(8,128)} %maximum_select_fusion.probe_ref, f32[3,2,512,512]{3,2,1,0:T(8,128)} %slice.134.patch_ref, ...), custom_call_target="tpu_custom_call" | custom-call | flops 12884901888 | bytes 37748736 | tf_op jit(solution)/shard_map/pallas_call | solution.py:274
  203.0 3.1 constant_dynamic-slice_fusion.1
  206.1 23.9 %shard_map.78 = f32[3,2,512,512]{3,2,1,0:T(8,128)} custom-call(s32[1]{0:T(128)} %bitcast.29.block_ref, s32[1]{0:T(128)S(6)} %copy.19.count_ref, bf16[3,4,2,512,512]{4,3,2,1,0:T(8,128)(2,1)} %shard_map.76.corr_ref, f32[4,2,512,512]{3,2,1,0:T(8,128)} %maximum_select_fusion.probe_ref, f32[3,2,512,512]{3,2,1,0:T(8,128)} %slice.134.patch_ref, ...), custom_call_target="tpu_custom_call" | custom-call | flops 12884901888 | bytes 37748736 | tf_op jit(solution)/shard_map/pallas_call | solution.py:274
  230.0 17.1 %fusion.5 = (f32[3]{0:T(128)S(1)}, f32[3]{0:T(128)S(1)}, f32[3,2,512,512]{3,2,1,0:T(8,128)S(1)}) fusion(f32[3,2,514,514]{3,2,1,0:T(8,128)} %copy-done, f32[3,2,512,512]{3,2,1,0:T(8,128)} %get-tuple-element.10, f32[3,2,512,512]{3,2,1,0:T(8,128)} %shard_map.78), kind=kLoop, calls=%fused_computation.10 | loop fusion | flops 14155770 | bytes 44040216 | tf_op jit(solution)/shard_map/reduce_sum | solution.py:357
  247.1 2.7 copy-done.2
  249.9 2.5 broadcast_in_dim.45
  252.4 7.4 %dynamic_update_slice.35 = f32[1024,1024]{1,0:T(8,128)} dynamic-update-slice(f32[1024,1024]{1,0:T(8,128)} %broadcast_in_dim.45, f32[512,512]{1,0:T(8,128)S(1)} %dynamic-slice_bitcast_fusion.7, s32[]{:T(128)S(6)} %select_n.312, s32[]{:T(128)S(6)} %select_n.313) | dynamic-update-slice | bytes 2097156 | tf_op jit(solution)/shard_map/dynamic_update_slice | solution.py:365
  259.9 2.7 dynamic-slice_add_fusion
  263.8 2.6 collective-permute-start.9
  267.5 2.0 fusion.21
  269.4 7.7 %dynamic_update_slice.36 = f32[1024,1024]{1,0:T(8,128)} dynamic-update-slice(f32[1024,1024]{1,0:T(8,128)} %dynamic_update_slice.35, f32[512,512]{1,0:T(8,128)S(1)} %fusion.21, s32[]{:T(128)S(6)} %select_n.314, s32[]{:T(128)S(6)} %select_n.315) | dynamic-update-slice | bytes 2097156 | tf_op jit(solution)/shard_map/dynamic_update_slice | solution.py:365
  277.1 2.0 fusion.20
  279.1 7.5 %dynamic_update_slice.37 = f32[1024,1024]{1,0:T(8,128)} dynamic-update-slice(f32[1024,1024]{1,0:T(8,128)} %dynamic_update_slice.36, f32[512,512]{1,0:T(8,128)S(1)} %fusion.20, s32[]{:T(128)S(6)} %select_n.316, s32[]{:T(128)S(6)} %select_n.317) | dynamic-update-slice | bytes 2097156 | tf_op jit(solution)/shard_map/dynamic_update_slice | solution.py:365
  286.7 3.6 fusion.30
  290.4 2.9 collective-permute-done.7
  296.2 41.0 %collective-permute-done.12 = f32[64,512]{1,0:T(8,128)S(1)} collective-permute-done((f32[64,512]{1,0:T(8,128)S(1)}, f32[64,512]{1,0:T(8,128)S(1)}, u32[]{:S(2)}, u32[]{:S(2)}) %collective-permute-start.12) | collective-permute-done | bytes 131104 | tf_op jit(solution)/shard_map/ppermute | solution.py:33
  337.2 3.1 collective-permute-start.10
  340.3 4.2 %collective-permute-done.11 = f32[64,512]{1,0:T(8,128)S(1)} collective-permute-done((f32[64,512]{1,0:T(8,128)S(1)}, f32[64,512]{1,0:T(8,128)S(1)}, u32[]{:S(2)}, u32[]{:S(2)}) %collective-permute-start.11) | collective-permute-done | bytes 131104 | tf_op jit(solution)/shard_map/ppermute | solution.py:33
  344.5 2.8 collective-permute-done.10
  354.0 9.3 %collective-permute-start.19 = (f32[64,512]{1,0:T(8,128)S(1)}, f32[64,512]{1,0:T(8,128)S(1)}, u32[]{:S(2)}, u32[]{:S(2)}) collective-permute-start(f32[64,512]{1,0:T(8,128)S(1)} %pad_maximum_fusion.14), channel_id=1, source_target_pairs={{0,16},{2,18},{4,20},{6,22},{8,24},{10,26},{12,28},{14,30},{16,0},... | collective-permute-start | bytes 393224 | tf_op jit(solution)/shard_map/ppermute | solution.py:33
  363.3 1.9 collective-permute-start.20
  365.3 2.6 collective-permute-done.19
  368.7 3.3 collective-permute-start.21
  372.0 2.2 collective-permute-start.22
  374.2 2.0 collective-permute-start.23
  376.5 5.8 %collective-permute-done.21 = f32[256,512]{1,0:T(8,128)S(1)} collective-permute-done((f32[256,512]{1,0:T(8,128)S(1)}, f32[256,512]{1,0:T(8,128)S(1)}, u32[]{:S(2)}, u32[]{:S(2)}) %collective-permute-start.21) | collective-permute-done | bytes 524320 | tf_op jit(solution)/shard_map/ppermute | solution.py:33
  382.3 13.3 %collective-permute-done.22 = f32[256,512]{1,0:T(8,128)S(1)} collective-permute-done((f32[256,512]{1,0:T(8,128)S(1)}, f32[256,512]{1,0:T(8,128)S(1)}, u32[]{:S(2)}, u32[]{:S(2)}) %collective-permute-start.22) | collective-permute-done | bytes 524320 | tf_op jit(solution)/shard_map/ppermute | solution.py:33
  396.4 2.0 collective-permute-start.24
  398.4 3.6 fusion.19
  402.8 2.5 pad_maximum_fusion.1
  (75 shorter events, 23.7 us)
Async XLA Ops:
  0.6 70.9 %collective-permute-start.1 = (f32[2,512,512]{2,1,0:T(8,128)}, f32[2,512,512]{2,1,0:T(8,128)}, u32[]{:S(2)}, u32[]{:S(2)}) collective-permute-start(f32[2,512,512]{2,1,0:T(8,128)} %bitcast.125), channel_id=1, source_target_pairs={{0,112},{2,114},{4,116},{6,118},{8,120},{10,122},{12,124},{14,126}... | collective-permute-start | bytes 6291464 | tf_op jit(solution)/shard_map/ppermute | solution.py:23
  5.8 114.5 %collective-permute-start.3 = (f32[2,512,512]{2,1,0:T(8,128)}, f32[2,512,512]{2,1,0:T(8,128)S(1)}, u32[]{:S(2)}, u32[]{:S(2)}) collective-permute-start(f32[2,512,512]{2,1,0:T(8,128)} %bitcast.126), channel_id=1, source_target_pairs={{20,2},{24,6},{28,10},{32,14},{36,18},{40,22},{44,26},{48,30},{52,... | collective-permute-start | bytes 6291464 | tf_op jit(solution)/shard_map/ppermute | solution.py:320
  7.1 113.7 %collective-permute-start = (f32[2,512,512]{2,1,0:T(8,128)}, f32[2,512,512]{2,1,0:T(8,128)}, u32[]{:S(2)}, u32[]{:S(2)}) collective-permute-start(f32[2,512,512]{2,1,0:T(8,128)} %bitcast.127), channel_id=1, source_target_pairs={{0,126},{2,0},{4,2},{6,4},{8,6},{10,8},{12,10},{14,12},{16,14},{18... | collective-permute-start | bytes 6291464 | tf_op jit(solution)/shard_map/ppermute | solution.py:23
  14.8 98.0 %collective-permute-start.4 = (f32[2,512,512]{2,1,0:T(8,128)}, f32[2,512,512]{2,1,0:T(8,128)}, u32[]{:S(2)}, u32[]{:S(2)}) collective-permute-start(f32[2,512,512]{2,1,0:T(8,128)} %get-tuple-element.30), channel_id=1, source_target_pairs={{0,5},{1,4},{2,7},{3,6},{4,1},{5,0},{6,3},{7,2},{8,13},{9,12},{10,... | collective-permute-start | bytes 6291464 | tf_op jit(solution)/shard_map/ppermute | solution.py:306
  14.8 98.0 %collective-permute-start.5 = (f32[2,512,512]{2,1,0:T(8,128)}, f32[2,512,512]{2,1,0:T(8,128)}, u32[]{:S(2)}, u32[]{:S(2)}) collective-permute-start(f32[2,512,512]{2,1,0:T(8,128)} %get-tuple-element.31), channel_id=1, source_target_pairs={{0,1},{1,0},{2,3},{3,2},{4,5},{5,4},{6,7},{7,6},{8,9},{9,8},{10,11... | collective-permute-start | bytes 6291464 | tf_op jit(solution)/shard_map/ppermute | solution.py:308
  36.4 41.3 %copy-start.8 = (s32[1,3,2]{1,2,0:T(2,128)S(1)}, s32[1,3,2]{1,2,0:T(2,128)}, u32[]{:S(2)}) copy-start(s32[1,3,2]{1,2,0:T(2,128)} %param.8) | copy-start | bytes 76
  71.5 48.8 %collective-permute-start.2 = (f32[2,512,512]{2,1,0:T(8,128)}, f32[2,512,512]{2,1,0:T(8,128)}, u32[]{:S(2)}, u32[]{:S(2)}) collective-permute-start(f32[2,512,512]{2,1,0:T(8,128)} %collective-permute-done.1), channel_id=1, source_target_pairs={{2,0},{6,4},{10,8},{14,12},{18,16},{22,20},{26,24},{30,28},{34,32}... | collective-permute-start | bytes 6291464 | tf_op jit(solution)/shard_map/ppermute | solution.py:324
  98.4 4.2 %copy-start.3 = (bf16[512,512]{1,0:T(8,128)(2,1)S(1)}, bf16[512,512]{1,0:T(8,128)(2,1)}, u32[]{:S(2)}) copy-start(bf16[512,512]{1,0:T(8,128)(2,1)} %get-tuple-element.41) | copy-start | bytes 1572868
  98.4 4.1 %copy-start.4 = (bf16[512,512]{1,0:T(8,128)(2,1)S(1)}, bf16[512,512]{1,0:T(8,128)(2,1)}, u32[]{:S(2)}) copy-start(bf16[512,512]{1,0:T(8,128)(2,1)} %get-tuple-element.42) | copy-start | bytes 1572868
  98.4 4.1 %copy-start.5 = (bf16[512,512]{1,0:T(8,128)(2,1)S(1)}, bf16[512,512]{1,0:T(8,128)(2,1)}, u32[]{:S(2)}) copy-start(bf16[512,512]{1,0:T(8,128)(2,1)} %get-tuple-element.62) | copy-start | bytes 1572868
  98.4 4.1 %copy-start.6 = (bf16[512,512]{1,0:T(8,128)(2,1)S(1)}, bf16[512,512]{1,0:T(8,128)(2,1)}, u32[]{:S(2)}) copy-start(bf16[512,512]{1,0:T(8,128)(2,1)} %get-tuple-element.63) | copy-start | bytes 1572868
  112.8 3.4 copy-start.1
  120.3 1.6 copy-start.7
  127.3 5.0 %copy-start = (f32[3,2,514,514]{3,2,1,0:T(8,128)}, f32[3,2,514,514]{3,2,1,0:T(8,128)S(1)}, u32[]{:S(2)}) copy-start(f32[3,2,514,514]{3,2,1,0:T(8,128)S(1)} %pad_maximum_fusion) | copy-start | bytes 19022116
  206.1 53.8 %collective-permute-start.6 = (f32[1024,512]{1,0:T(8,128)}, f32[1024,512]{1,0:T(8,128)}, u32[]{:S(2)}, u32[]{:S(2)}) collective-permute-start(f32[1024,512]{1,0:T(8,128)} %constant_dynamic-slice_fusion.1), channel_id=1, source_target_pairs={{0,2},{2,0},{4,6},{6,4},{8,10},{10,8},{12,14},{14,12},{16,18},{18,... | collective-permute-start | bytes 6291464 | tf_op jit(solution)/shard_map/ppermute | solution.py:33
  247.1 2.7 copy-start.2
  263.8 26.5 %collective-permute-start.9 = (f32[256,512]{1,0:T(8,128)}, f32[256,512]{1,0:T(8,128)}, u32[]{:S(2)}, u32[]{:S(2)}) collective-permute-start(f32[256,512]{1,0:T(8,128)} %get-tuple-element.33), channel_id=1, source_target_pairs={{0,96},{2,98},{4,100},{6,102},{8,104},{10,106},{12,108},{14,110},{... | collective-permute-start | bytes 1572872 | tf_op jit(solution)/shard_map/ppermute | solution.py:33
  266.3 24.0 %collective-permute-start.8 = (f32[256,512]{1,0:T(8,128)}, f32[256,512]{1,0:T(8,128)}, u32[]{:S(2)}, u32[]{:S(2)}) collective-permute-start(f32[256,512]{1,0:T(8,128)} %get-tuple-element.34), channel_id=1, source_target_pairs={{0,64},{2,66},{4,68},{6,70},{8,72},{10,74},{12,76},{14,78},{16,80}... | collective-permute-start | bytes 1572872 | tf_op jit(solution)/shard_map/ppermute | solution.py:33
  266.8 26.4 %collective-permute-start.7 = (f32[256,512]{1,0:T(8,128)}, f32[256,512]{1,0:T(8,128)}, u32[]{:S(2)}, u32[]{:S(2)}) collective-permute-start(f32[256,512]{1,0:T(8,128)} %get-tuple-element.32), channel_id=1, source_target_pairs={{0,32},{2,34},{4,36},{6,38},{8,40},{10,42},{12,44},{14,46},{16,48}... | collective-permute-start | bytes 1572872 | tf_op jit(solution)/shard_map/ppermute | solution.py:33
  290.3 60.3 %collective-permute-start.14 = (f32[512,512]{1,0:T(8,128)}, f32[512,512]{1,0:T(8,128)}, u32[]{:S(2)}, u32[]{:S(2)}) collective-permute-start(f32[512,512]{1,0:T(8,128)} %get-tuple-element.27), channel_id=1, source_target_pairs={{0,2},{2,4},{4,6},{6,8},{8,10},{10,12},{12,14},{14,16},{16,18},{18... | collective-permute-start | bytes 3145736 | tf_op jit(solution)/shard_map/ppermute | solution.py:23
  290.3 60.3 %collective-permute-start.15 = (f32[512,512]{1,0:T(8,128)}, f32[512,512]{1,0:T(8,128)}, u32[]{:S(2)}, u32[]{:S(2)}) collective-permute-start(f32[512,512]{1,0:T(8,128)} %get-tuple-element.26), channel_id=1, source_target_pairs={{0,16},{2,18},{4,20},{6,22},{8,24},{10,26},{12,28},{14,30},{16,32}... | collective-permute-start | bytes 3145736 | tf_op jit(solution)/shard_map/ppermute | solution.py:23
  290.3 60.3 %collective-permute-start.16 = (f32[512,512]{1,0:T(8,128)}, f32[512,512]{1,0:T(8,128)}, u32[]{:S(2)}, u32[]{:S(2)}) collective-permute-start(f32[512,512]{1,0:T(8,128)} %get-tuple-element.25), channel_id=1, source_target_pairs={{0,18},{2,20},{4,22},{6,24},{8,26},{10,28},{12,30},{14,32},{16,34}... | collective-permute-start | bytes 3145736 | tf_op jit(solution)/shard_map/ppermute | solution.py:23
  294.8 42.4 %collective-permute-start.12 = (f32[64,512]{1,0:T(8,128)S(1)}, f32[64,512]{1,0:T(8,128)S(1)}, u32[]{:S(2)}, u32[]{:S(2)}) collective-permute-start(f32[64,512]{1,0:T(8,128)S(1)} %get-tuple-element.48), channel_id=1, source_target_pairs={{0,24},{2,26},{4,28},{6,30},{8,0},{10,2},{12,4},{14,6},{16,8},{18,... | collective-permute-start | bytes 393224 | tf_op jit(solution)/shard_map/ppermute | solution.py:33
  294.9 49.6 %collective-permute-start.11 = (f32[64,512]{1,0:T(8,128)S(1)}, f32[64,512]{1,0:T(8,128)S(1)}, u32[]{:S(2)}, u32[]{:S(2)}) collective-permute-start(f32[64,512]{1,0:T(8,128)S(1)} %get-tuple-element.49), channel_id=1, source_target_pairs={{0,16},{2,18},{4,20},{6,22},{8,24},{10,26},{12,28},{14,30},{16,0},... | collective-permute-start | bytes 393224 | tf_op jit(solution)/shard_map/ppermute | solution.py:33
  337.2 10.1 %collective-permute-start.10 = (f32[64,512]{1,0:T(8,128)S(1)}, f32[64,512]{1,0:T(8,128)S(1)}, u32[]{:S(2)}, u32[]{:S(2)}) collective-permute-start(f32[64,512]{1,0:T(8,128)S(1)} %get-tuple-element.47), channel_id=1, source_target_pairs={{0,8},{2,10},{4,12},{6,14},{8,16},{10,18},{12,20},{14,22},{16,24},... | collective-permute-start | bytes 393224 | tf_op jit(solution)/shard_map/ppermute | solution.py:33
  347.4 3.2 collective-permute-start.13
  350.6 3.2 collective-permute-start.17
  353.8 11.4 %collective-permute-start.18 = (f32[64,512]{1,0:T(8,128)S(1)}, f32[64,512]{1,0:T(8,128)S(1)}, u32[]{:S(2)}, u32[]{:S(2)}) collective-permute-start(f32[64,512]{1,0:T(8,128)S(1)} %pad_maximum_fusion.14), channel_id=1, source_target_pairs={{0,8},{2,10},{4,12},{6,14},{8,16},{10,18},{12,20},{14,22},{16,24},... | collective-permute-start | bytes 393224 | tf_op jit(solution)/shard_map/ppermute | solution.py:33
  354.0 13.9 %collective-permute-start.19 = (f32[64,512]{1,0:T(8,128)S(1)}, f32[64,512]{1,0:T(8,128)S(1)}, u32[]{:S(2)}, u32[]{:S(2)}) collective-permute-start(f32[64,512]{1,0:T(8,128)S(1)} %pad_maximum_fusion.14), channel_id=1, source_target_pairs={{0,16},{2,18},{4,20},{6,22},{8,24},{10,26},{12,28},{14,30},{16,0},... | collective-permute-start | bytes 393224 | tf_op jit(solution)/shard_map/ppermute | solution.py:33
  363.3 5.4 %collective-permute-start.20 = (f32[64,512]{1,0:T(8,128)S(1)}, f32[64,512]{1,0:T(8,128)S(1)}, u32[]{:S(2)}, u32[]{:S(2)}) collective-permute-start(f32[64,512]{1,0:T(8,128)S(1)} %pad_maximum_fusion.14), channel_id=1, source_target_pairs={{0,24},{2,26},{4,28},{6,30},{8,0},{10,2},{12,4},{14,6},{16,8},{18,... | collective-permute-start | bytes 393224 | tf_op jit(solution)/shard_map/ppermute | solution.py:33
  368.7 13.5 %collective-permute-start.21 = (f32[256,512]{1,0:T(8,128)S(1)}, f32[256,512]{1,0:T(8,128)S(1)}, u32[]{:S(2)}, u32[]{:S(2)}) collective-permute-start(f32[256,512]{1,0:T(8,128)S(1)} %bitcast.119), channel_id=1, source_target_pairs={{0,32},{2,34},{4,36},{6,38},{8,40},{10,42},{12,44},{14,46},{16,48}... | collective-permute-start | bytes 1572872 | tf_op jit(solution)/shard_map/ppermute | solution.py:33
  372.0 23.5 %collective-permute-start.22 = (f32[256,512]{1,0:T(8,128)S(1)}, f32[256,512]{1,0:T(8,128)S(1)}, u32[]{:S(2)}, u32[]{:S(2)}) collective-permute-start(f32[256,512]{1,0:T(8,128)S(1)} %bitcast.120), channel_id=1, source_target_pairs={{0,64},{2,66},{4,68},{6,70},{8,72},{10,74},{12,76},{14,78},{16,80}... | collective-permute-start | bytes 1572872 | tf_op jit(solution)/shard_map/ppermute | solution.py:33
  374.2 22.2 %collective-permute-start.23 = (f32[256,512]{1,0:T(8,128)S(1)}, f32[256,512]{1,0:T(8,128)S(1)}, u32[]{:S(2)}, u32[]{:S(2)}) collective-permute-start(f32[256,512]{1,0:T(8,128)S(1)} %bitcast.121), channel_id=1, source_target_pairs={{0,96},{2,98},{4,100},{6,102},{8,104},{10,106},{12,108},{14,110},{... | collective-permute-start | bytes 1572872 | tf_op jit(solution)/shard_map/ppermute | solution.py:33
  396.4 5.8 %collective-permute-start.24 = (f32[1024,512]{1,0:T(8,128)S(1)}, f32[1024,512]{1,0:T(8,128)S(1)}, u32[]{:S(2)}, u32[]{:S(2)}) collective-permute-start(f32[1024,512]{1,0:T(8,128)S(1)} %bitcast.115), channel_id=1, source_target_pairs={{0,2},{2,0},{4,6},{6,4},{8,10},{10,8},{12,14},{14,12},{16,18},{18,... | collective-permute-start | bytes 6291464 | tf_op jit(solution)/shard_map/ppermute | solution.py:33

commit v9 on v8

--- a/solution.py
+++ b/solution.py
@@ -109,11 +109,13 @@
     return jnp.concatenate([out_f.reshape(size * rows, -1), out_b.reshape(size * rows, -1)], axis=0)
 
 
-def scan_all_reduce(value, early, tied):
+def scan_all_reduce(value, early_inputs, early_work, tied):
     shape = value.shape
     data = value.reshape(-1, shape[-1])
     data = pair_reduce_scatter(data, CORE)
     data = direct_reduce_scatter(data, XAX)
+    data, early_inputs = lax.optimization_barrier((data, early_inputs))
+    early = early_work(*early_inputs)
     data = direct_reduce_scatter(data, YAX)
     data = pair_reduce_scatter(data, ZLO)
     data, early, tied = lax.optimization_barrier((data, early, tied))
@@ -354,9 +356,11 @@
         correction, all_modes, patch, 1 - component, counts[0], own_modes, inverse_table, False
     )
     whole_grad = own_grad + partner_grad
-    position_y = jnp.sum(whole_grad * grad_y, axis=(1, 2, 3))
-    position_x = jnp.sum(whole_grad * grad_x, axis=(1, 2, 3))
-    positions = jnp.stack([position_y, position_x], axis=1) / side
+    def position_work(whole_grad, grad_y, grad_x):
+        position_y = jnp.sum(whole_grad * grad_y, axis=(1, 2, 3))
+        position_x = jnp.sum(whole_grad * grad_x, axis=(1, 2, 3))
+        return jnp.stack([position_y, position_x], axis=1) / side
+
     mine = lax.dynamic_slice_in_dim(whole_grad, component, 1, axis=1)
     gradient_plane = jnp.zeros((2 * tile_side, 2 * tile_side), jnp.float32)
     for slot_id in range(slots):
@@ -367,7 +371,7 @@
     received_south = from_behind(gradient_plane[tile_side:, :tile_side], "scan", GCOLS)
     received_corner = from_behind(gradient_plane[tile_side:, tile_side:], "scan", GCOLS + 1)
     probe_grad, positions, (received_east, received_south, received_corner) = scan_all_reduce(
-        probe_partial, positions, (received_east, received_south, received_corner)
+        probe_partial, (whole_grad, grad_y, grad_x), position_work, (received_east, received_south, received_corner)
     )
     total_grad = (
         gradient_plane[:tile_side, :tile_side] + received_east + received_south + received_corner

time: 414 us -> 434 us (1.048)
  other arithmetic: 77.9 us -> 95.1 us
  starting transfers between devices: 47.2 us -> 54.6 us
  local copies, waits for them, and re-layouts: 53.2 us -> 47.8 us
    mul x0 -> x1, other arithmetic: none -> 19.8 us  [shards(): grad_x = (windows[:, :, 1:-1, 2:] - windows[:, :, 1:-1, :-2]) * 0.5]
    reduce_sum x1, other arithmetic: 17.1 us -> 6.14 us  [position_work(): position_y = jnp.sum(whole_grad * grad_y, axis=(1, 2, 3))]
    ppermute x5, starting transfers between devices: 8.19 us -> 15.1 us  [from_behind(): return lax.ppermute(value, axis, pairs)]
    add x0 -> x1, other arithmetic: none -> 6.16 us  [shards(): whole_grad = own_grad + partner_grad]
    ppermute x1, waiting for transfers between devices: 0.01 us -> 5.97 us  [shards(): got = lax.ppermute(sent, ('scan', 'mode'), pairs)]
    slice x1 -> x0, local copies, waits for them, and re-layouts: 5.04 us -> none  [shards(): patch = windows[:, :, 1:-1, 1:-1]]
  transfers between devices with their start and end apart: 25 -> 25, of which waited for: 13 -> 12; matrix products, arithmetic and copies ran while one was open for 26% -> 23% of each run, Pallas kernels for 6% -> 6%
where the time goes in v9:
time: 434 us; the launch traced here: 427 us
  waiting for transfers between devices  114 us (26%)
  other arithmetic  95.1 us (22%)
  Pallas kernels  94.2 us (22%)
  starting transfers between devices  54.6 us (13%)
  local copies, waits for them, and re-layouts  47.8 us (11%)
  between operations  20.7 us (5%)
    ppermute x16, waiting for transfers between devices, sub_shift(): return lax.ppermute(value, 'scan', pairs)  74.6 us
    pallas_call x2, Pallas kernels, backward_gradients(): pl.pallas_call(backward_kernel, grid_spec=grid_spec, out_shape=out_shape,...  52.1 us
    pallas_call x1, Pallas kernels, forward_correction(): pl.pallas_call(forward_kernel, grid=(slots,), in_specs=[pl.BlockSpec((1,...  42.2 us
    ppermute x5, waiting for transfers between devices, from_behind(): return lax.ppermute(value, axis, pairs)  33.9 us
    ppermute x16, starting transfers between devices, sub_shift(): return lax.ppermute(value, 'scan', pairs)  31.4 us
    dynamic_update_slice x3, local copies, waits for them, and re-layouts, shards(): lax.dynamic_update_slice(gradient_plane, current + mine[slot_id, 0], start)  22.9 us
    another operation x5, other arithmetic  20 us
    mul x1, other arithmetic, shards(): grad_x = (windows[:, :, 1:-1, 2:] - windows[:, :, 1:-1, :-2]) * 0.5  19.8 us
  transfers between devices with their start and end apart: 25, of which 12 were waited for; matrix products, arithmetic and copies ran while one was open for 23% of the time, Pallas kernels for 6%

profile of v9, /device:TPU:65, one launch (start us, length us, event | category | flops | bytes accessed | tf_op | source)
XLA Modules:
  0.0 426.8 jit_solution(2109759119020849892)
XLA Ops:
  0.6 5.2 %collective-permute-start.1 = (f32[2,512,512]{2,1,0:T(8,128)}, f32[2,512,512]{2,1,0:T(8,128)}, u32[]{:S(2)}, u32[]{:S(2)}) collective-permute-start(f32[2,512,512]{2,1,0:T(8,128)} %bitcast.127), channel_id=1, source_target_pairs={{0,112},{2,114},{4,116},{6,118},{8,120},{10,122},{12,124},{14,126}... | collective-permute-start | bytes 6291464 | tf_op jit(solution)/shard_map/ppermute | solution.py:23
  7.1 2.9 collective-permute-start
  10.0 4.7 %dynamic-slice_bitcast_fusion.4 = (f32[2,512,512]{2,1,0:T(8,128)}, f32[2,512,512]{2,1,0:T(8,128)}) fusion(f32[2,2,512,512]{3,2,1,0:T(8,128)} %param.6, s32[]{:T(128)S(6)} %select_n.305, s32[]{:T(128)S(6)} %select_n.306), kind=kLoop, calls=%fused_computation.29 | loop fusion | bytes 8388616 | tf_op jit(solution)/shard_map/jit(dynamic_index_in_dim)/squeeze | solution.py:306
  16.1 4.0 multiply_convert_fusion
  20.1 4.0 multiply_convert_fusion.1
  24.1 4.0 negate_convert_fusion
  28.1 4.0 multiply_convert_fusion.2
  32.1 4.0 negate_convert_fusion.1
  37.6 33.9 %collective-permute-done.1 = f32[2,512,512]{2,1,0:T(8,128)} collective-permute-done((f32[2,512,512]{2,1,0:T(8,128)}, f32[2,512,512]{2,1,0:T(8,128)}, u32[]{:S(2)}, u32[]{:S(2)}) %collective-permute-start.1) | collective-permute-done | bytes 2097184 | tf_op jit(solution)/shard_map/ppermute | solution.py:23
  71.5 5.4 %collective-permute-start.2 = (f32[2,512,512]{2,1,0:T(8,128)}, f32[2,512,512]{2,1,0:T(8,128)}, u32[]{:S(2)}, u32[]{:S(2)}) collective-permute-start(f32[2,512,512]{2,1,0:T(8,128)} %collective-permute-done.1), channel_id=1, source_target_pairs={{2,0},{6,4},{10,8},{14,12},{18,16},{22,20},{26,24},{30,28},{34,32}... | collective-permute-start | bytes 6291464 | tf_op jit(solution)/shard_map/ppermute | solution.py:326
  87.0 4.1 fusion.5
  91.2 10.1 %fusion.3 = (bf16[1024,1024]{1,0:T(8,128)(2,1)}, bf16[1024,1024]{1,0:T(8,128)(2,1)}) fusion(bf16[512,512]{1,0:T(8,128)(2,1)S(1)} %copy-done.5, bf16[512,512]{1,0:T(8,128)(2,1)S(1)} %copy-done.4, bf16[512,512]{1,0:T(8,128)(2,1)S(1)} %copy-done.6, bf16[512,512]{1,0:T(8,128)(2,1)S(1)} %copy-done.3), kind=kLoop, calls=%fused_computation.22 | loop fusion | flops 14680064 | bytes 6291456 | tf_op jit(solution)/shard_map/concatenate | solution.py:156
  101.3 6.0 %collective-permute-done.4 = f32[2,512,512]{2,1,0:T(8,128)} collective-permute-done((f32[2,512,512]{2,1,0:T(8,128)}, f32[2,512,512]{2,1,0:T(8,128)}, u32[]{:S(2)}, u32[]{:S(2)}) %collective-permute-start.4) | collective-permute-done | bytes 2097184 | tf_op jit(solution)/shard_map/ppermute | solution.py:308
  107.2 2.7 select_bitcast_fusion.1
  110.0 4.0 maximum_select_fusion.probe_ref
  115.6 2.6 maximum_maximum_fusion
  118.2 2.1 dynamic-slice_bitcast_fusion.2
  120.4 3.5 pad_maximum_fusion
  123.9 19.8 %fusion = (f32[3,2,512,512]{3,2,1,0:T(8,128)}, f32[3,2,512,512]{3,2,1,0:T(8,128)}, f32[3,2,512,512]{3,2,1,0:T(8,128)}) fusion(f32[3,2,514,514]{3,2,1,0:T(8,128)} %pad_maximum_fusion), kind=kLoop, calls=%fused_computation.4 | loop fusion | flops 6291456 | bytes 50331648 | tf_op jit(solution)/shard_map/mul | solution.py:344
  143.7 42.2 %shard_map.76.corr_ref = bf16[3,4,2,512,512]{4,3,2,1,0:T(8,128)(2,1)} custom-call(f32[3,2,512,512]{3,2,1,0:T(8,128)} %get-tuple-element.32.patch_ref, f32[4,2,512,512]{3,2,1,0:T(8,128)} %maximum_select_fusion.probe_ref, f32[3,512,512]{2,1,0:T(8,128)} %bitcast.135, bf16[1024,1024]{1,0:T(8,128)(2,1)} %get-tuple-element.48.left_ref, ...), custom_call_target="tpu_custom_call" | custom-call | flops 25769803776 | bytes 44040192 | tf_op jit(solution)/shard_map/pallas_call | solution.py:194
  185.9 28.4 %shard_map.77 = (f32[3,2,512,512]{3,2,1,0:T(8,128)}, f32[2,2,512,512]{3,2,1,0:T(8,128)}) custom-call(s32[1]{0:T(128)} %bitcast.block_ref, s32[1]{0:T(128)S(6)} %copy.19.count_ref, bf16[3,4,2,512,512]{4,3,2,1,0:T(8,128)(2,1)} %shard_map.76.corr_ref, f32[4,2,512,512]{3,2,1,0:T(8,128)} %maximum_select_fusion.probe_ref, ...), custom_call_target="tpu_custom_call" | custom-call | flops 12884901888 | bytes 37748736 | tf_op jit(solution)/shard_map/pallas_call | solution.py:276
  214.3 3.1 constant_dynamic-slice_fusion.1
  230.0 2.1 dynamic-slice_add_fusion
  234.9 2.6 collective-permute-start.8
  237.6 23.6 %shard_map.78 = f32[3,2,512,512]{3,2,1,0:T(8,128)} custom-call(s32[1]{0:T(128)} %bitcast.29.block_ref, s32[1]{0:T(128)S(6)} %copy.19.count_ref, bf16[3,4,2,512,512]{4,3,2,1,0:T(8,128)(2,1)} %shard_map.76.corr_ref, f32[4,2,512,512]{3,2,1,0:T(8,128)} %maximum_select_fusion.probe_ref, f32[3,2,512,512]{3,2,1,0:T(8,128)} %get-tuple-element.32.patch_ref, ...), custom_call_target="tpu_custom_call" | custom-call | flops 12884901888 | bytes 37748736 | tf_op jit(solution)/shard_map/pallas_call | solution.py:276
  261.2 6.2 %add.307 = f32[3,2,512,512]{3,2,1,0:T(8,128)S(1)} add(f32[3,2,512,512]{3,2,1,0:T(8,128)} %get-tuple-element.14, f32[3,2,512,512]{3,2,1,0:T(8,128)} %shard_map.78) | non-fusion elementwise | flops 1572864 | bytes 18874368 | tf_op jit(solution)/shard_map/add | solution.py:358
  267.4 2.7 copy-done
  270.1 2.5 broadcast_in_dim.45
  272.7 7.6 %dynamic_update_slice.35 = f32[1024,1024]{1,0:T(8,128)} dynamic-update-slice(f32[1024,1024]{1,0:T(8,128)} %broadcast_in_dim.45, f32[512,512]{1,0:T(8,128)S(1)} %dynamic-slice_bitcast_fusion.7, s32[]{:T(128)S(6)} %select_n.312, s32[]{:T(128)S(6)} %select_n.313) | dynamic-update-slice | bytes 2097156 | tf_op jit(solution)/shard_map/dynamic_update_slice | solution.py:369
  280.3 2.0 fusion.17
  282.3 7.7 %dynamic_update_slice.36 = f32[1024,1024]{1,0:T(8,128)} dynamic-update-slice(f32[1024,1024]{1,0:T(8,128)} %dynamic_update_slice.35, f32[512,512]{1,0:T(8,128)S(1)} %fusion.17, s32[]{:T(128)S(6)} %select_n.314, s32[]{:T(128)S(6)} %select_n.315) | dynamic-update-slice | bytes 2097156 | tf_op jit(solution)/shard_map/dynamic_update_slice | solution.py:369
  290.0 2.1 fusion.16
  292.1 7.6 %dynamic_update_slice.37 = f32[1024,1024]{1,0:T(8,128)} dynamic-update-slice(f32[1024,1024]{1,0:T(8,128)} %dynamic_update_slice.36, f32[512,512]{1,0:T(8,128)S(1)} %fusion.16, s32[]{:T(128)S(6)} %select_n.316, s32[]{:T(128)S(6)} %select_n.317) | dynamic-update-slice | bytes 2097156 | tf_op jit(solution)/shard_map/dynamic_update_slice | solution.py:369
  302.3 2.2 fusion.26
  304.5 2.5 collective-permute-start.14
  307.5 4.0 collective-permute-start.16
  312.6 6.1 %multiply_reduce_fusion.1 = (f32[3]{0:T(128)S(1)}, f32[3]{0:T(128)S(1)}) fusion(f32[3,2,512,512]{3,2,1,0:T(8,128)S(1)} %bitcast.114, f32[3,2,512,512]{3,2,1,0:T(8,128)} %get-tuple-element.18, f32[3,2,512,512]{3,2,1,0:T(8,128)} %get-tuple-element.19), kind=kLoop, calls=%fused_computation.8 | loop fusion | flops 6291450 | bytes 18874392 | tf_op jit(solution)/shard_map/reduce_sum | solution.py:360
  318.7 41.7 %collective-permute-done.11 = f32[64,512]{1,0:T(8,128)S(1)} collective-permute-done((f32[64,512]{1,0:T(8,128)S(1)}, f32[64,512]{1,0:T(8,128)S(1)}, u32[]{:S(2)}, u32[]{:S(2)}) %collective-permute-start.11) | collective-permute-done | bytes 131104 | tf_op jit(solution)/shard_map/ppermute | solution.py:33
  360.4 2.7 collective-permute-done.10
  363.2 6.3 %collective-permute-start.13 = (f32[32,512]{1,0:T(8,128)S(1)}, f32[32,512]{1,0:T(8,128)S(1)}, u32[]{:S(2)}, u32[]{:S(2)}) collective-permute-start(f32[32,512]{1,0:T(8,128)S(1)} %constant_dynamic-slice_fusion), channel_id=1, source_target_pairs={{0,4},{2,6},{4,0},{6,2},{8,12},{10,14},{12,8},{14,10},{16,20},{18,... | collective-permute-start | bytes 196616 | tf_op jit(solution)/shard_map/ppermute | solution.py:33
  372.8 2.1 collective-permute-done.17
  375.3 8.3 %collective-permute-start.19 = (f32[64,512]{1,0:T(8,128)S(1)}, f32[64,512]{1,0:T(8,128)S(1)}, u32[]{:S(2)}, u32[]{:S(2)}) collective-permute-start(f32[64,512]{1,0:T(8,128)S(1)} %pad_maximum_fusion.14), channel_id=1, source_target_pairs={{0,16},{2,18},{4,20},{6,22},{8,24},{10,26},{12,28},{14,30},{16,0},... | collective-permute-start | bytes 393224 | tf_op jit(solution)/shard_map/ppermute | solution.py:33
  384.9 5.1 %collective-permute-done.19 = f32[64,512]{1,0:T(8,128)S(1)} collective-permute-done((f32[64,512]{1,0:T(8,128)S(1)}, f32[64,512]{1,0:T(8,128)S(1)}, u32[]{:S(2)}, u32[]{:S(2)}) %collective-permute-start.19) | collective-permute-done | bytes 131104 | tf_op jit(solution)/shard_map/ppermute | solution.py:33
  390.0 3.7 collective-permute-start.21
  397.6 6.7 %collective-permute-done.21 = f32[256,512]{1,0:T(8,128)S(1)} collective-permute-done((f32[256,512]{1,0:T(8,128)S(1)}, f32[256,512]{1,0:T(8,128)S(1)}, u32[]{:S(2)}, u32[]{:S(2)}) %collective-permute-start.21) | collective-permute-done | bytes 524320 | tf_op jit(solution)/shard_map/ppermute | solution.py:33
  404.3 12.9 %collective-permute-done.22 = f32[256,512]{1,0:T(8,128)S(1)} collective-permute-done((f32[256,512]{1,0:T(8,128)S(1)}, f32[256,512]{1,0:T(8,128)S(1)}, u32[]{:S(2)}, u32[]{:S(2)}) %collective-permute-start.22) | collective-permute-done | bytes 524320 | tf_op jit(solution)/shard_map/ppermute | solution.py:33
  419.5 3.3 fusion.15
  423.9 2.5 pad_maximum_fusion.1
  (81 shorter events, 28.1 us)
Async XLA Ops:
  0.6 70.9 %collective-permute-start.1 = (f32[2,512,512]{2,1,0:T(8,128)}, f32[2,512,512]{2,1,0:T(8,128)}, u32[]{:S(2)}, u32[]{:S(2)}) collective-permute-start(f32[2,512,512]{2,1,0:T(8,128)} %bitcast.127), channel_id=1, source_target_pairs={{0,112},{2,114},{4,116},{6,118},{8,120},{10,122},{12,124},{14,126}... | collective-permute-start | bytes 6291464 | tf_op jit(solution)/shard_map/ppermute | solution.py:23
  5.8 108.2 %collective-permute-start.3 = (f32[2,512,512]{2,1,0:T(8,128)}, f32[2,512,512]{2,1,0:T(8,128)S(1)}, u32[]{:S(2)}, u32[]{:S(2)}) collective-permute-start(f32[2,512,512]{2,1,0:T(8,128)} %bitcast.128), channel_id=1, source_target_pairs={{20,2},{24,6},{28,10},{32,14},{36,18},{40,22},{44,26},{48,30},{52,... | collective-permute-start | bytes 6291464 | tf_op jit(solution)/shard_map/ppermute | solution.py:322
  7.1 107.4 %collective-permute-start = (f32[2,512,512]{2,1,0:T(8,128)}, f32[2,512,512]{2,1,0:T(8,128)}, u32[]{:S(2)}, u32[]{:S(2)}) collective-permute-start(f32[2,512,512]{2,1,0:T(8,128)} %bitcast.129), channel_id=1, source_target_pairs={{0,126},{2,0},{4,2},{6,4},{8,6},{10,8},{12,10},{14,12},{16,14},{18... | collective-permute-start | bytes 6291464 | tf_op jit(solution)/shard_map/ppermute | solution.py:23
  14.8 92.5 %collective-permute-start.4 = (f32[2,512,512]{2,1,0:T(8,128)}, f32[2,512,512]{2,1,0:T(8,128)}, u32[]{:S(2)}, u32[]{:S(2)}) collective-permute-start(f32[2,512,512]{2,1,0:T(8,128)} %get-tuple-element.40), channel_id=1, source_target_pairs={{0,5},{1,4},{2,7},{3,6},{4,1},{5,0},{6,3},{7,2},{8,13},{9,12},{10,... | collective-permute-start | bytes 6291464 | tf_op jit(solution)/shard_map/ppermute | solution.py:308
  14.8 92.5 %collective-permute-start.5 = (f32[2,512,512]{2,1,0:T(8,128)}, f32[2,512,512]{2,1,0:T(8,128)}, u32[]{:S(2)}, u32[]{:S(2)}) collective-permute-start(f32[2,512,512]{2,1,0:T(8,128)} %get-tuple-element.41), channel_id=1, source_target_pairs={{0,1},{1,0},{2,3},{3,2},{4,5},{5,4},{6,7},{7,6},{8,9},{9,8},{10,11... | collective-permute-start | bytes 6291464 | tf_op jit(solution)/shard_map/ppermute | solution.py:310
  36.4 41.8 %copy-start.8 = (s32[1,3,2]{1,2,0:T(2,128)S(1)}, s32[1,3,2]{1,2,0:T(2,128)}, u32[]{:S(2)}) copy-start(s32[1,3,2]{1,2,0:T(2,128)} %param.8) | copy-start | bytes 76
  71.5 42.5 %collective-permute-start.2 = (f32[2,512,512]{2,1,0:T(8,128)}, f32[2,512,512]{2,1,0:T(8,128)}, u32[]{:S(2)}, u32[]{:S(2)}) collective-permute-start(f32[2,512,512]{2,1,0:T(8,128)} %collective-permute-done.1), channel_id=1, source_target_pairs={{2,0},{6,4},{10,8},{14,12},{18,16},{22,20},{26,24},{30,28},{34,32}... | collective-permute-start | bytes 6291464 | tf_op jit(solution)/shard_map/ppermute | solution.py:326
  87.0 4.2 copy-start.3
  87.0 4.2 copy-start.4
  87.0 4.2 copy-start.5
  87.0 4.2 copy-start.6
  101.3 8.7 %copy-start.1 = (f32[2,2,512,512]{3,2,1,0:T(8,128)S(1)}, f32[2,2,512,512]{3,2,1,0:T(8,128)}, u32[]{:S(2)}) copy-start(f32[2,2,512,512]{3,2,1,0:T(8,128)} %param.6) | copy-start | bytes 12582916
  114.0 1.6 copy-start.7
  217.4 12.6 %collective-permute-start.6 = (f32[1024,512]{1,0:T(8,128)}, f32[1024,512]{1,0:T(8,128)S(1)}, u32[]{:S(2)}, u32[]{:S(2)}) collective-permute-start(f32[1024,512]{1,0:T(8,128)} %constant_dynamic-slice_fusion.1), channel_id=1, source_target_pairs={{0,2},{2,0},{4,6},{6,4},{8,10},{10,8},{12,14},{14,12},{16,18},{18,... | collective-permute-start | bytes 6291464 | tf_op jit(solution)/shard_map/ppermute | solution.py:33
  232.1 1.4 copy-start.2
  234.7 65.1 %collective-permute-start.9 = (f32[256,512]{1,0:T(8,128)}, f32[256,512]{1,0:T(8,128)}, u32[]{:S(2)}, u32[]{:S(2)}) collective-permute-start(f32[256,512]{1,0:T(8,128)} %get-tuple-element.43), channel_id=1, source_target_pairs={{0,96},{2,98},{4,100},{6,102},{8,104},{10,106},{12,108},{14,110},{... | collective-permute-start | bytes 1572872 | tf_op jit(solution)/shard_map/ppermute | solution.py:33
  234.9 64.8 %collective-permute-start.8 = (f32[256,512]{1,0:T(8,128)}, f32[256,512]{1,0:T(8,128)}, u32[]{:S(2)}, u32[]{:S(2)}) collective-permute-start(f32[256,512]{1,0:T(8,128)} %get-tuple-element.44), channel_id=1, source_target_pairs={{0,64},{2,66},{4,68},{6,70},{8,72},{10,74},{12,76},{14,78},{16,80}... | collective-permute-start | bytes 1572872 | tf_op jit(solution)/shard_map/ppermute | solution.py:33
  237.6 62.2 %collective-permute-start.7 = (f32[256,512]{1,0:T(8,128)}, f32[256,512]{1,0:T(8,128)}, u32[]{:S(2)}, u32[]{:S(2)}) collective-permute-start(f32[256,512]{1,0:T(8,128)} %get-tuple-element.42), channel_id=1, source_target_pairs={{0,32},{2,34},{4,36},{6,38},{8,40},{10,42},{12,44},{14,46},{16,48}... | collective-permute-start | bytes 1572872 | tf_op jit(solution)/shard_map/ppermute | solution.py:33
  267.4 2.7 copy-start
  289.9 22.6 %slice-start = ((s8[6291456]{0:T(1024)(128)(4,1)}), s8[2097152]{0:T(1024)(128)(4,1)S(1)}, s32[]{:S(2)}) async-start(s8[6291456]{0:T(1024)(128)(4,1)} %bitcast.113), calls=%async_computation | async-start | bytes 4194304
  299.7 12.8 %slice-start.1 = ((s8[6291456]{0:T(1024)(128)(4,1)}), s8[4194304]{0:T(1024)(128)(4,1)S(1)}, s32[]{:S(2)}) async-start(s8[6291456]{0:T(1024)(128)(4,1)} %bitcast.113), calls=%async_computation.1 | async-start | bytes 8388608
  301.7 9.8 %collective-permute-start.12 = (f32[64,512]{1,0:T(8,128)S(1)}, f32[64,512]{1,0:T(8,128)S(1)}, u32[]{:S(2)}, u32[]{:S(2)}) collective-permute-start(f32[64,512]{1,0:T(8,128)S(1)} %get-tuple-element.58), channel_id=1, source_target_pairs={{0,24},{2,26},{4,28},{6,30},{8,0},{10,2},{12,4},{14,6},{16,8},{18,... | collective-permute-start | bytes 393224 | tf_op jit(solution)/shard_map/ppermute | solution.py:33
  304.5 67.2 %collective-permute-start.14 = (f32[512,512]{1,0:T(8,128)S(1)}, f32[512,512]{1,0:T(8,128)S(1)}, u32[]{:S(2)}, u32[]{:S(2)}) collective-permute-start(f32[512,512]{1,0:T(8,128)S(1)} %get-tuple-element.37), channel_id=1, source_target_pairs={{0,2},{2,4},{4,6},{6,8},{8,10},{10,12},{12,14},{14,16},{16,18},{18... | collective-permute-start | bytes 3145736 | tf_op jit(solution)/shard_map/ppermute | solution.py:23
  307.0 64.7 %collective-permute-start.15 = (f32[512,512]{1,0:T(8,128)S(1)}, f32[512,512]{1,0:T(8,128)}, u32[]{:S(2)}, u32[]{:S(2)}) collective-permute-start(f32[512,512]{1,0:T(8,128)S(1)} %get-tuple-element.36), channel_id=1, source_target_pairs={{0,16},{2,18},{4,20},{6,22},{8,24},{10,26},{12,28},{14,30},{16,32}... | collective-permute-start | bytes 3145736 | tf_op jit(solution)/shard_map/ppermute | solution.py:23
  307.5 64.2 %collective-permute-start.16 = (f32[512,512]{1,0:T(8,128)S(1)}, f32[512,512]{1,0:T(8,128)}, u32[]{:S(2)}, u32[]{:S(2)}) collective-permute-start(f32[512,512]{1,0:T(8,128)S(1)} %get-tuple-element.35), channel_id=1, source_target_pairs={{0,18},{2,20},{4,22},{6,24},{8,26},{10,28},{12,30},{14,32},{16,34}... | collective-permute-start | bytes 3145736 | tf_op jit(solution)/shard_map/ppermute | solution.py:23
  311.5 49.0 %collective-permute-start.11 = (f32[64,512]{1,0:T(8,128)S(1)}, f32[64,512]{1,0:T(8,128)S(1)}, u32[]{:S(2)}, u32[]{:S(2)}) collective-permute-start(f32[64,512]{1,0:T(8,128)S(1)} %get-tuple-element.59), channel_id=1, source_target_pairs={{0,16},{2,18},{4,20},{6,22},{8,24},{10,26},{12,28},{14,30},{16,0},... | collective-permute-start | bytes 393224 | tf_op jit(solution)/shard_map/ppermute | solution.py:33
  311.5 51.7 %collective-permute-start.10 = (f32[64,512]{1,0:T(8,128)S(1)}, f32[64,512]{1,0:T(8,128)S(1)}, u32[]{:S(2)}, u32[]{:S(2)}) collective-permute-start(f32[64,512]{1,0:T(8,128)S(1)} %get-tuple-element.57), channel_id=1, source_target_pairs={{0,8},{2,10},{4,12},{6,14},{8,16},{10,18},{12,20},{14,22},{16,24},... | collective-permute-start | bytes 393224 | tf_op jit(solution)/shard_map/ppermute | solution.py:33
  363.2 8.4 %collective-permute-start.13 = (f32[32,512]{1,0:T(8,128)S(1)}, f32[32,512]{1,0:T(8,128)S(1)}, u32[]{:S(2)}, u32[]{:S(2)}) collective-permute-start(f32[32,512]{1,0:T(8,128)S(1)} %constant_dynamic-slice_fusion), channel_id=1, source_target_pairs={{0,4},{2,6},{4,0},{6,2},{8,12},{10,14},{12,8},{14,10},{16,20},{18,... | collective-permute-start | bytes 196616 | tf_op jit(solution)/shard_map/ppermute | solution.py:33
  371.7 3.2 collective-permute-start.17
  374.9 9.9 %collective-permute-start.18 = (f32[64,512]{1,0:T(8,128)S(1)}, f32[64,512]{1,0:T(8,128)S(1)}, u32[]{:S(2)}, u32[]{:S(2)}) collective-permute-start(f32[64,512]{1,0:T(8,128)S(1)} %pad_maximum_fusion.14), channel_id=1, source_target_pairs={{0,8},{2,10},{4,12},{6,14},{8,16},{10,18},{12,20},{14,22},{16,24},... | collective-permute-start | bytes 393224 | tf_op jit(solution)/shard_map/ppermute | solution.py:33
  375.3 14.7 %collective-permute-start.19 = (f32[64,512]{1,0:T(8,128)S(1)}, f32[64,512]{1,0:T(8,128)S(1)}, u32[]{:S(2)}, u32[]{:S(2)}) collective-permute-start(f32[64,512]{1,0:T(8,128)S(1)} %pad_maximum_fusion.14), channel_id=1, source_target_pairs={{0,16},{2,18},{4,20},{6,22},{8,24},{10,26},{12,28},{14,30},{16,0},... | collective-permute-start | bytes 393224 | tf_op jit(solution)/shard_map/ppermute | solution.py:33
  383.7 6.3 %collective-permute-start.20 = (f32[64,512]{1,0:T(8,128)S(1)}, f32[64,512]{1,0:T(8,128)S(1)}, u32[]{:S(2)}, u32[]{:S(2)}) collective-permute-start(f32[64,512]{1,0:T(8,128)S(1)} %pad_maximum_fusion.14), channel_id=1, source_target_pairs={{0,24},{2,26},{4,28},{6,30},{8,0},{10,2},{12,4},{14,6},{16,8},{18,... | collective-permute-start | bytes 393224 | tf_op jit(solution)/shard_map/ppermute | solution.py:33
  390.0 14.3 %collective-permute-start.21 = (f32[256,512]{1,0:T(8,128)S(1)}, f32[256,512]{1,0:T(8,128)S(1)}, u32[]{:S(2)}, u32[]{:S(2)}) collective-permute-start(f32[256,512]{1,0:T(8,128)S(1)} %bitcast.121), channel_id=1, source_target_pairs={{0,32},{2,34},{4,36},{6,38},{8,40},{10,42},{12,44},{14,46},{16,48}... | collective-permute-start | bytes 1572872 | tf_op jit(solution)/shard_map/ppermute | solution.py:33
  393.8 23.4 %collective-permute-start.22 = (f32[256,512]{1,0:T(8,128)S(1)}, f32[256,512]{1,0:T(8,128)S(1)}, u32[]{:S(2)}, u32[]{:S(2)}) collective-permute-start(f32[256,512]{1,0:T(8,128)S(1)} %bitcast.122), channel_id=1, source_target_pairs={{0,64},{2,66},{4,68},{6,70},{8,72},{10,74},{12,76},{14,78},{16,80}... | collective-permute-start | bytes 1572872 | tf_op jit(solution)/shard_map/ppermute | solution.py:33
  395.3 22.2 %collective-permute-start.23 = (f32[256,512]{1,0:T(8,128)S(1)}, f32[256,512]{1,0:T(8,128)S(1)}, u32[]{:S(2)}, u32[]{:S(2)}) collective-permute-start(f32[256,512]{1,0:T(8,128)S(1)} %bitcast.123), channel_id=1, source_target_pairs={{0,96},{2,98},{4,100},{6,102},{8,104},{10,106},{12,108},{14,110},{... | collective-permute-start | bytes 1572872 | tf_op jit(solution)/shard_map/ppermute | solution.py:33
  417.5 5.8 %collective-permute-start.24 = (f32[1024,512]{1,0:T(8,128)S(1)}, f32[1024,512]{1,0:T(8,128)S(1)}, u32[]{:S(2)}, u32[]{:S(2)}) collective-permute-start(f32[1024,512]{1,0:T(8,128)S(1)} %bitcast.117), channel_id=1, source_target_pairs={{0,2},{2,0},{4,6},{6,4},{8,10},{10,8},{12,14},{14,12},{16,18},{18,... | collective-permute-start | bytes 6291464 | tf_op jit(solution)/shard_map/ppermute | solution.py:33

commit v10 on v8

--- a/solution.py
+++ b/solution.py
@@ -113,13 +113,13 @@
     shape = value.shape
     data = value.reshape(-1, shape[-1])
     data = pair_reduce_scatter(data, CORE)
-    data = direct_reduce_scatter(data, XAX)
+    data = ring_reduce_scatter(data, XAX)
     data = direct_reduce_scatter(data, YAX)
     data = pair_reduce_scatter(data, ZLO)
     data, early, tied = lax.optimization_barrier((data, early, tied))
     data = pair_all_gather(data, ZLO)
     data = direct_all_gather(data, YAX)
-    data = direct_all_gather(data, XAX)
+    data = ring_all_gather(data, XAX)
     data = pair_all_gather(data, CORE)
     return data.reshape(shape), early, tied
 

time: 414 us -> 426 us (1.029)
  the two profiles are of different devices: /device:TPU:65 before, /device:TPU:73 now
where the time goes in v10:
time: 426 us; the launch traced here: 418 us
  waiting for transfers between devices  106 us (25%)
  Pallas kernels  94.8 us (22%)
  other arithmetic  83.1 us (20%)
  starting transfers between devices  62.4 us (15%)
  local copies, waits for them, and re-layouts  51.3 us (12%)
  between operations  21.2 us (5%)
    ppermute x22, waiting for transfers between devices, sub_shift(): return lax.ppermute(value, 'scan', pairs)  77.6 us
    pallas_call x2, Pallas kernels, backward_gradients(): pl.pallas_call(backward_kernel, grid_spec=grid_spec, out_shape=out_shape,...  52.5 us
    ppermute x22, starting transfers between devices, sub_shift(): return lax.ppermute(value, 'scan', pairs)  43 us
    pallas_call x1, Pallas kernels, forward_correction(): pl.pallas_call(forward_kernel, grid=(slots,), in_specs=[pl.BlockSpec((1,...  42.4 us
    dynamic_update_slice x3, local copies, waits for them, and re-layouts, shards(): lax.dynamic_update_slice(gradient_plane, current + mine[slot_id, 0], start)  23.1 us
    another operation x5, other arithmetic  20 us
    reduce_sum x1, other arithmetic, shards(): position_y = jnp.sum(whole_grad * grad_y, axis=(1, 2, 3))  17.1 us
    concatenate x2, other arithmetic, complex_table(): return jnp.concatenate(rows, axis=0)  14.4 us
  transfers between devices with their start and end apart: 31, of which 16 were waited for; matrix products, arithmetic and copies ran while one was open for 26% of the time, Pallas kernels for 6%

profile of v10, /device:TPU:73, one launch (start us, length us, event | category | flops | bytes accessed | tf_op | source)
XLA Modules:
  0.0 418.4 jit_solution(3567854031714049911)
XLA Ops:
  0.6 4.3 %collective-permute-start.1 = (f32[2,512,512]{2,1,0:T(8,128)}, f32[2,512,512]{2,1,0:T(8,128)}, u32[]{:S(2)}, u32[]{:S(2)}) collective-permute-start(f32[2,512,512]{2,1,0:T(8,128)} %bitcast.144), channel_id=1, source_target_pairs={{0,112},{2,114},{4,116},{6,118},{8,120},{10,122},{12,124},{14,126}... | collective-permute-start | bytes 6291464 | tf_op jit(solution)/shard_map/ppermute | solution.py:23
  7.8 4.7 %dynamic-slice_bitcast_fusion.4 = (f32[2,512,512]{2,1,0:T(8,128)}, f32[2,512,512]{2,1,0:T(8,128)}) fusion(f32[2,2,512,512]{3,2,1,0:T(8,128)} %param.6, s32[]{:T(128)S(6)} %select_n.337, s32[]{:T(128)S(6)} %select_n.338), kind=kLoop, calls=%fused_computation.32 | loop fusion | bytes 8388616 | tf_op jit(solution)/shard_map/jit(dynamic_index_in_dim)/squeeze | solution.py:304
  12.5 3.5 collective-permute-start.5
  16.1 4.0 multiply_convert_fusion
  20.0 4.0 multiply_convert_fusion.1
  24.0 4.0 negate_convert_fusion
  28.1 4.0 multiply_convert_fusion.2
  32.1 4.0 negate_convert_fusion.1
  37.6 12.0 %collective-permute-done.1 = f32[2,512,512]{2,1,0:T(8,128)} collective-permute-done((f32[2,512,512]{2,1,0:T(8,128)}, f32[2,512,512]{2,1,0:T(8,128)}, u32[]{:S(2)}, u32[]{:S(2)}) %collective-permute-start.1) | collective-permute-done | bytes 2097184 | tf_op jit(solution)/shard_map/ppermute | solution.py:23
  49.6 4.8 %collective-permute-start.2 = (f32[2,512,512]{2,1,0:T(8,128)}, f32[2,512,512]{2,1,0:T(8,128)}, u32[]{:S(2)}, u32[]{:S(2)}) collective-permute-start(f32[2,512,512]{2,1,0:T(8,128)} %collective-permute-done.1), channel_id=1, source_target_pairs={{2,0},{6,4},{10,8},{14,12},{18,16},{22,20},{26,24},{30,28},{34,32}... | collective-permute-start | bytes 6291464 | tf_op jit(solution)/shard_map/ppermute | solution.py:324
  76.3 4.1 fusion.9
  80.4 10.3 %fusion.7 = (bf16[1024,1024]{1,0:T(8,128)(2,1)}, bf16[1024,1024]{1,0:T(8,128)(2,1)}) fusion(bf16[512,512]{1,0:T(8,128)(2,1)S(1)} %copy-done.8, bf16[512,512]{1,0:T(8,128)(2,1)S(1)} %copy-done.7, bf16[512,512]{1,0:T(8,128)(2,1)S(1)} %copy-done.9, bf16[512,512]{1,0:T(8,128)(2,1)S(1)} %copy-done.6), kind=kLoop, calls=%fused_computation.24 | loop fusion | flops 14680064 | bytes 6291456 | tf_op jit(solution)/shard_map/concatenate | solution.py:154
  90.7 11.4 %collective-permute-done.4 = f32[2,512,512]{2,1,0:T(8,128)} collective-permute-done((f32[2,512,512]{2,1,0:T(8,128)}, f32[2,512,512]{2,1,0:T(8,128)}, u32[]{:S(2)}, u32[]{:S(2)}) %collective-permute-start.4) | collective-permute-done | bytes 2097184 | tf_op jit(solution)/shard_map/ppermute | solution.py:306
  102.1 4.5 %collective-permute-done.5 = f32[2,512,512]{2,1,0:T(8,128)} collective-permute-done((f32[2,512,512]{2,1,0:T(8,128)}, f32[2,512,512]{2,1,0:T(8,128)}, u32[]{:S(2)}, u32[]{:S(2)}) %collective-permute-start.5) | collective-permute-done | bytes 2097184 | tf_op jit(solution)/shard_map/ppermute | solution.py:308
  106.6 2.7 select_bitcast_fusion.1
  109.3 4.0 maximum_select_fusion.probe_ref
  115.0 2.6 maximum_maximum_fusion
  120.3 5.0 %slice.158.patch_ref = f32[3,2,512,512]{3,2,1,0:T(8,128)} slice(f32[3,2,514,514]{3,2,1,0:T(8,128)S(1)} %pad_maximum_fusion), slice={[0:3], [0:2], [1:513], [1:513]} | slice | bytes 12582912 | tf_op jit(solution)/shard_map/slice | solution.py:340
  125.4 42.4 %shard_map.76.corr_ref = bf16[3,4,2,512,512]{4,3,2,1,0:T(8,128)(2,1)} custom-call(f32[3,2,512,512]{3,2,1,0:T(8,128)} %slice.158.patch_ref, f32[4,2,512,512]{3,2,1,0:T(8,128)} %maximum_select_fusion.probe_ref, f32[3,512,512]{2,1,0:T(8,128)} %bitcast.156, bf16[1024,1024]{1,0:T(8,128)(2,1)} %get-tuple-element.37.left_ref, ...), custom_call_target="tpu_custom_call" | custom-call | flops 25769803776 | bytes 44040192 | tf_op jit(solution)/shard_map/pallas_call | solution.py:192
  167.7 28.4 %shard_map.77 = (f32[3,2,512,512]{3,2,1,0:T(8,128)}, f32[2,2,512,512]{3,2,1,0:T(8,128)}) custom-call(s32[1]{0:T(128)} %bitcast.block_ref, s32[1]{0:T(128)S(6)} %copy.23.count_ref, bf16[3,4,2,512,512]{4,3,2,1,0:T(8,128)(2,1)} %shard_map.76.corr_ref, f32[4,2,512,512]{3,2,1,0:T(8,128)} %maximum_select_fusion.probe_ref, f32[3,2,512,512]{3,2,1,0:T(8,128)} %slice.158.patch_ref, ...), custom_call_target="tpu_custom_call" | custom-call | flops 12884901888 | bytes 37748736 | tf_op jit(solution)/shard_map/pallas_call | solution.py:274
  196.1 3.1 constant_dynamic-slice_fusion.1
  201.2 24.1 %shard_map.78 = f32[3,2,512,512]{3,2,1,0:T(8,128)} custom-call(s32[1]{0:T(128)} %bitcast.29.block_ref, s32[1]{0:T(128)S(6)} %copy.23.count_ref, bf16[3,4,2,512,512]{4,3,2,1,0:T(8,128)(2,1)} %shard_map.76.corr_ref, f32[4,2,512,512]{3,2,1,0:T(8,128)} %maximum_select_fusion.probe_ref, f32[3,2,512,512]{3,2,1,0:T(8,128)} %slice.158.patch_ref, ...), custom_call_target="tpu_custom_call" | custom-call | flops 12884901888 | bytes 37748736 | tf_op jit(solution)/shard_map/pallas_call | solution.py:274
  225.3 17.1 %fusion.5 = (f32[3]{0:T(128)S(1)}, f32[3]{0:T(128)S(1)}, f32[3,2,512,512]{3,2,1,0:T(8,128)S(1)}) fusion(f32[3,2,514,514]{3,2,1,0:T(8,128)} %copy-done, f32[3,2,512,512]{3,2,1,0:T(8,128)} %get-tuple-element.10, f32[3,2,512,512]{3,2,1,0:T(8,128)} %shard_map.78), kind=kLoop, calls=%fused_computation.10 | loop fusion | flops 14155770 | bytes 44040216 | tf_op jit(solution)/shard_map/reduce_sum | solution.py:357
  242.4 5.0 %dynamic-slice_add_fusion = f32[1024,512]{1,0:T(8,128)S(1)} fusion(f32[1024,512]{1,0:T(8,128)} %collective-permute-done.6, f32[2048,512]{1,0:T(8,128)} %bitcast.132, s32[]{:T(128)S(6)} %select_n.350), kind=kLoop, calls=%fused_computation.28 | loop fusion | flops 524288 | bytes 6291460 | tf_op jit(solution)/shard_map/add | solution.py:46
  249.5 2.5 broadcast_in_dim.54
  252.1 7.6 %dynamic_update_slice.47 = f32[1024,1024]{1,0:T(8,128)} dynamic-update-slice(f32[1024,1024]{1,0:T(8,128)} %broadcast_in_dim.54, f32[512,512]{1,0:T(8,128)S(1)} %dynamic-slice_bitcast_fusion.7, s32[]{:T(128)S(6)} %select_n.344, s32[]{:T(128)S(6)} %select_n.345) | dynamic-update-slice | bytes 2097156 | tf_op jit(solution)/shard_map/dynamic_update_slice | solution.py:365
  262.8 7.7 %dynamic_update_slice.48 = f32[1024,1024]{1,0:T(8,128)} dynamic-update-slice(f32[1024,1024]{1,0:T(8,128)} %dynamic_update_slice.47, f32[512,512]{1,0:T(8,128)S(1)} %fusion.21, s32[]{:T(128)S(6)} %select_n.346, s32[]{:T(128)S(6)} %select_n.347) | dynamic-update-slice | bytes 2097156 | tf_op jit(solution)/shard_map/dynamic_update_slice | solution.py:365
  271.5 2.3 collective-permute-start.11
  277.5 7.8 %dynamic_update_slice.49 = f32[1024,1024]{1,0:T(8,128)} dynamic-update-slice(f32[1024,1024]{1,0:T(8,128)} %dynamic_update_slice.48, f32[512,512]{1,0:T(8,128)S(1)} %fusion.20, s32[]{:T(128)S(6)} %select_n.348, s32[]{:T(128)S(6)} %select_n.349) | dynamic-update-slice | bytes 2097156 | tf_op jit(solution)/shard_map/dynamic_update_slice | solution.py:365
  286.3 2.7 collective-permute-start.12
  290.0 3.6 fusion.28
  298.5 4.2 collective-permute-start.15
  302.7 46.4 %collective-permute-done.15 = f32[64,512]{1,0:T(8,128)S(1)} collective-permute-done((f32[64,512]{1,0:T(8,128)S(1)}, f32[64,512]{1,0:T(8,128)S(1)}, u32[]{:S(2)}, u32[]{:S(2)}) %collective-permute-start.15) | collective-permute-done | bytes 131104 | tf_op jit(solution)/shard_map/ppermute | solution.py:33
  349.3 2.6 collective-permute-done.14
  354.5 4.5 %collective-permute-done.16 = f32[32,512]{1,0:T(8,128)S(1)} collective-permute-done((f32[32,512]{1,0:T(8,128)S(1)}, f32[32,512]{1,0:T(8,128)S(1)}, u32[]{:S(2)}, u32[]{:S(2)}) %collective-permute-start.16) | collective-permute-done | bytes 65568 | tf_op jit(solution)/shard_map/ppermute | solution.py:33
  359.1 3.1 collective-permute-done.20
  362.3 10.3 %collective-permute-start.21 = (f32[64,512]{1,0:T(8,128)S(1)}, f32[64,512]{1,0:T(8,128)S(1)}, u32[]{:S(2)}, u32[]{:S(2)}) collective-permute-start(f32[64,512]{1,0:T(8,128)S(1)} %pad_maximum_fusion.16), channel_id=1, source_target_pairs={{0,8},{2,10},{4,12},{6,14},{8,16},{10,18},{12,20},{14,22},{16,24},... | collective-permute-start | bytes 393224 | tf_op jit(solution)/shard_map/ppermute | solution.py:33
  374.6 3.3 collective-permute-done.22
  378.1 4.8 %collective-permute-start.27 = (f32[128,512]{1,0:T(8,128)S(1)}, f32[128,512]{1,0:T(8,128)S(1)}, u32[]{:S(2)}, u32[]{:S(2)}) collective-permute-start(f32[128,512]{1,0:T(8,128)S(1)} %bitcast.150), channel_id=1, source_target_pairs={{0,96},{2,98},{4,100},{6,102},{8,104},{10,106},{12,108},{14,110},{... | collective-permute-start | bytes 786440 | tf_op jit(solution)/shard_map/ppermute | solution.py:33
  383.2 3.0 collective-permute-done.27
  386.2 3.1 collective-permute-start.28
  389.5 3.4 collective-permute-done.28
  392.9 3.1 collective-permute-start.29
  396.3 4.3 %collective-permute-done.29 = f32[128,512]{1,0:T(8,128)S(1)} collective-permute-done((f32[128,512]{1,0:T(8,128)S(1)}, f32[128,512]{1,0:T(8,128)S(1)}, u32[]{:S(2)}, u32[]{:S(2)}) %collective-permute-start.29) | collective-permute-done | bytes 262176 | tf_op jit(solution)/shard_map/ppermute | solution.py:33
  400.6 3.5 collective-permute-done.26
  404.4 7.0 %collective-permute-start.30 = (f32[1024,512]{1,0:T(8,128)S(1)}, f32[1024,512]{1,0:T(8,128)S(1)}, u32[]{:S(2)}, u32[]{:S(2)}) collective-permute-start(f32[1024,512]{1,0:T(8,128)S(1)} %pad_maximum_fusion.10), channel_id=1, source_target_pairs={{0,2},{2,0},{4,6},{6,4},{8,10},{10,8},{12,14},{14,12},{16,18},{18,... | collective-permute-start | bytes 6291464 | tf_op jit(solution)/shard_map/ppermute | solution.py:33
  411.4 3.3 fusion.19
  415.8 2.5 pad_maximum_fusion.1
  (108 shorter events, 36.5 us)
Async XLA Ops:
  0.6 48.9 %collective-permute-start.1 = (f32[2,512,512]{2,1,0:T(8,128)}, f32[2,512,512]{2,1,0:T(8,128)}, u32[]{:S(2)}, u32[]{:S(2)}) collective-permute-start(f32[2,512,512]{2,1,0:T(8,128)} %bitcast.144), channel_id=1, source_target_pairs={{0,112},{2,114},{4,116},{6,118},{8,120},{10,122},{12,124},{14,126}... | collective-permute-start | bytes 6291464 | tf_op jit(solution)/shard_map/ppermute | solution.py:23
  4.9 108.5 %collective-permute-start.3 = (f32[2,512,512]{2,1,0:T(8,128)}, f32[2,512,512]{2,1,0:T(8,128)S(1)}, u32[]{:S(2)}, u32[]{:S(2)}) collective-permute-start(f32[2,512,512]{2,1,0:T(8,128)} %bitcast.145), channel_id=1, source_target_pairs={{20,2},{24,6},{28,10},{32,14},{36,18},{40,22},{44,26},{48,30},{52,... | collective-permute-start | bytes 6291464 | tf_op jit(solution)/shard_map/ppermute | solution.py:320
  6.2 107.7 %collective-permute-start = (f32[2,512,512]{2,1,0:T(8,128)}, f32[2,512,512]{2,1,0:T(8,128)}, u32[]{:S(2)}, u32[]{:S(2)}) collective-permute-start(f32[2,512,512]{2,1,0:T(8,128)} %bitcast.146), channel_id=1, source_target_pairs={{0,126},{2,0},{4,2},{6,4},{8,6},{10,8},{12,10},{14,12},{16,14},{18... | collective-permute-start | bytes 6291464 | tf_op jit(solution)/shard_map/ppermute | solution.py:23
  12.5 89.5 %collective-permute-start.4 = (f32[2,512,512]{2,1,0:T(8,128)}, f32[2,512,512]{2,1,0:T(8,128)}, u32[]{:S(2)}, u32[]{:S(2)}) collective-permute-start(f32[2,512,512]{2,1,0:T(8,128)} %get-tuple-element.30), channel_id=1, source_target_pairs={{0,5},{1,4},{2,7},{3,6},{4,1},{5,0},{6,3},{7,2},{8,13},{9,12},{10,... | collective-permute-start | bytes 6291464 | tf_op jit(solution)/shard_map/ppermute | solution.py:306
  12.5 94.0 %collective-permute-start.5 = (f32[2,512,512]{2,1,0:T(8,128)}, f32[2,512,512]{2,1,0:T(8,128)}, u32[]{:S(2)}, u32[]{:S(2)}) collective-permute-start(f32[2,512,512]{2,1,0:T(8,128)} %get-tuple-element.31), channel_id=1, source_target_pairs={{0,1},{1,0},{2,3},{3,2},{4,5},{5,4},{6,7},{7,6},{8,9},{9,8},{10,11... | collective-permute-start | bytes 6291464 | tf_op jit(solution)/shard_map/ppermute | solution.py:308
  36.4 19.3 %copy-start.11 = (s32[1,3,2]{1,2,0:T(2,128)S(1)}, s32[1,3,2]{1,2,0:T(2,128)}, u32[]{:S(2)}) copy-start(s32[1,3,2]{1,2,0:T(2,128)} %param.8) | copy-start | bytes 76
  49.6 63.8 %collective-permute-start.2 = (f32[2,512,512]{2,1,0:T(8,128)}, f32[2,512,512]{2,1,0:T(8,128)}, u32[]{:S(2)}, u32[]{:S(2)}) collective-permute-start(f32[2,512,512]{2,1,0:T(8,128)} %collective-permute-done.1), channel_id=1, source_target_pairs={{2,0},{6,4},{10,8},{14,12},{18,16},{22,20},{26,24},{30,28},{34,32}... | collective-permute-start | bytes 6291464 | tf_op jit(solution)/shard_map/ppermute | solution.py:324
  76.3 4.1 copy-start.6
  76.3 4.1 copy-start.7
  76.3 4.1 copy-start.8
  76.3 4.1 copy-start.9
  90.7 18.6 %copy-start.1 = (f32[2,2,512,512]{3,2,1,0:T(8,128)S(1)}, f32[2,2,512,512]{3,2,1,0:T(8,128)}, u32[]{:S(2)}) copy-start(f32[2,2,512,512]{3,2,1,0:T(8,128)} %param.6) | copy-start | bytes 12582916
  113.4 1.6 copy-start.10
  120.3 5.0 %copy-start = (f32[3,2,514,514]{3,2,1,0:T(8,128)}, f32[3,2,514,514]{3,2,1,0:T(8,128)S(1)}, u32[]{:S(2)}) copy-start(f32[3,2,514,514]{3,2,1,0:T(8,128)S(1)} %pad_maximum_fusion) | copy-start | bytes 19022116
  199.2 43.2 %collective-permute-start.6 = (f32[1024,512]{1,0:T(8,128)}, f32[1024,512]{1,0:T(8,128)}, u32[]{:S(2)}, u32[]{:S(2)}) collective-permute-start(f32[1024,512]{1,0:T(8,128)} %constant_dynamic-slice_fusion.1), channel_id=1, source_target_pairs={{0,2},{2,0},{4,6},{6,4},{8,10},{10,8},{12,14},{14,12},{16,18},{18,... | collective-permute-start | bytes 6291464 | tf_op jit(solution)/shard_map/ppermute | solution.py:33
  242.4 6.8 %copy-start.2 = (f32[3,2,512,512]{3,2,1,0:T(8,128)}, f32[3,2,512,512]{3,2,1,0:T(8,128)S(1)}, u32[]{:S(2)}) copy-start(f32[3,2,512,512]{3,2,1,0:T(8,128)S(1)} %get-tuple-element.19) | copy-start | bytes 18874372
  248.5 1.0 copy-start.4
  248.6 22.0 %collective-permute-start.10 = (f32[128,512]{1,0:T(8,128)S(1)}, f32[128,512]{1,0:T(8,128)}, u32[]{:S(2)}, u32[]{:S(2)}) collective-permute-start(f32[128,512]{1,0:T(8,128)S(1)} %dynamic-slice_bitcast_fusion.8), channel_id=1, source_target_pairs={{0,96},{2,98},{4,100},{6,102},{8,104},{10,106},{12,108},{14,110},{... | collective-permute-start | bytes 786440 | tf_op jit(solution)/shard_map/ppermute | solution.py:33
  249.5 10.1 %copy-start.3 = (f32[512,512]{1,0:T(8,128)S(1)}, f32[512,512]{1,0:T(8,128)}, u32[]{:S(2)}) copy-start(f32[512,512]{1,0:T(8,128)} %get-tuple-element.32) | copy-start | bytes 3145732
  259.7 10.9 %copy-start.5 = (f32[512,512]{1,0:T(8,128)S(1)}, f32[512,512]{1,0:T(8,128)}, u32[]{:S(2)}) copy-start(f32[512,512]{1,0:T(8,128)} %copy-done.4) | copy-start | bytes 3145732
  260.4 13.4 %collective-permute-start.7 = (f32[128,512]{1,0:T(8,128)}, f32[128,512]{1,0:T(8,128)}, u32[]{:S(2)}, u32[]{:S(2)}) collective-permute-start(f32[128,512]{1,0:T(8,128)} %dynamic-slice_bitcast_fusion.9), channel_id=1, source_target_pairs={{0,32},{2,34},{4,36},{6,38},{8,40},{10,42},{12,44},{14,46},{16,48}... | collective-permute-start | bytes 786440 | tf_op jit(solution)/shard_map/ppermute | solution.py:33
  271.5 13.7 %collective-permute-start.11 = (f32[128,512]{1,0:T(8,128)S(1)}, f32[128,512]{1,0:T(8,128)}, u32[]{:S(2)}, u32[]{:S(2)}) collective-permute-start(f32[128,512]{1,0:T(8,128)S(1)} %bitcast_add_fusion.2), channel_id=1, source_target_pairs={{0,96},{2,98},{4,100},{6,102},{8,104},{10,106},{12,108},{14,110},{... | collective-permute-start | bytes 786440 | tf_op jit(solution)/shard_map/ppermute | solution.py:33
  275.5 13.4 %collective-permute-start.8 = (f32[128,512]{1,0:T(8,128)}, f32[128,512]{1,0:T(8,128)}, u32[]{:S(2)}, u32[]{:S(2)}) collective-permute-start(f32[128,512]{1,0:T(8,128)} %bitcast_add_fusion.5), channel_id=1, source_target_pairs={{0,32},{2,34},{4,36},{6,38},{8,40},{10,42},{12,44},{14,46},{16,48}... | collective-permute-start | bytes 786440 | tf_op jit(solution)/shard_map/ppermute | solution.py:33
  286.3 11.2 %collective-permute-start.12 = (f32[128,512]{1,0:T(8,128)S(1)}, f32[128,512]{1,0:T(8,128)S(1)}, u32[]{:S(2)}, u32[]{:S(2)}) collective-permute-start(f32[128,512]{1,0:T(8,128)S(1)} %bitcast_add_fusion.1), channel_id=1, source_target_pairs={{0,96},{2,98},{4,100},{6,102},{8,104},{10,106},{12,108},{14,110},{... | collective-permute-start | bytes 786440 | tf_op jit(solution)/shard_map/ppermute | solution.py:33
  289.9 8.5 %collective-permute-start.9 = (f32[128,512]{1,0:T(8,128)S(1)}, f32[128,512]{1,0:T(8,128)S(1)}, u32[]{:S(2)}, u32[]{:S(2)}) collective-permute-start(f32[128,512]{1,0:T(8,128)S(1)} %bitcast_add_fusion.4), channel_id=1, source_target_pairs={{0,32},{2,34},{4,36},{6,38},{8,40},{10,42},{12,44},{14,46},{16,48}... | collective-permute-start | bytes 786440 | tf_op jit(solution)/shard_map/ppermute | solution.py:33
  293.6 65.4 %collective-permute-start.17 = (f32[512,512]{1,0:T(8,128)}, f32[512,512]{1,0:T(8,128)S(1)}, u32[]{:S(2)}, u32[]{:S(2)}) collective-permute-start(f32[512,512]{1,0:T(8,128)} %get-tuple-element.27), channel_id=1, source_target_pairs={{0,2},{2,4},{4,6},{6,8},{8,10},{10,12},{12,14},{14,16},{16,18},{18... | collective-permute-start | bytes 3145736 | tf_op jit(solution)/shard_map/ppermute | solution.py:23
  295.4 63.6 %collective-permute-start.18 = (f32[512,512]{1,0:T(8,128)}, f32[512,512]{1,0:T(8,128)}, u32[]{:S(2)}, u32[]{:S(2)}) collective-permute-start(f32[512,512]{1,0:T(8,128)} %get-tuple-element.26), channel_id=1, source_target_pairs={{0,16},{2,18},{4,20},{6,22},{8,24},{10,26},{12,28},{14,30},{16,32}... | collective-permute-start | bytes 3145736 | tf_op jit(solution)/shard_map/ppermute | solution.py:23
  297.5 61.6 %collective-permute-start.19 = (f32[512,512]{1,0:T(8,128)}, f32[512,512]{1,0:T(8,128)}, u32[]{:S(2)}, u32[]{:S(2)}) collective-permute-start(f32[512,512]{1,0:T(8,128)} %get-tuple-element.25), channel_id=1, source_target_pairs={{0,18},{2,20},{4,22},{6,24},{8,26},{10,28},{12,30},{14,32},{16,34}... | collective-permute-start | bytes 3145736 | tf_op jit(solution)/shard_map/ppermute | solution.py:23
  298.5 50.6 %collective-permute-start.15 = (f32[64,512]{1,0:T(8,128)S(1)}, f32[64,512]{1,0:T(8,128)S(1)}, u32[]{:S(2)}, u32[]{:S(2)}) collective-permute-start(f32[64,512]{1,0:T(8,128)S(1)} %get-tuple-element.49), channel_id=1, source_target_pairs={{0,24},{2,26},{4,28},{6,30},{8,0},{10,2},{12,4},{14,6},{16,8},{18,... | collective-permute-start | bytes 393224 | tf_op jit(solution)/shard_map/ppermute | solution.py:33
  302.7 49.2 %collective-permute-start.14 = (f32[64,512]{1,0:T(8,128)S(1)}, f32[64,512]{1,0:T(8,128)S(1)}, u32[]{:S(2)}, u32[]{:S(2)}) collective-permute-start(f32[64,512]{1,0:T(8,128)S(1)} %get-tuple-element.50), channel_id=1, source_target_pairs={{0,16},{2,18},{4,20},{6,22},{8,24},{10,26},{12,28},{14,30},{16,0},... | collective-permute-start | bytes 393224 | tf_op jit(solution)/shard_map/ppermute | solution.py:33
  349.1 4.6 %collective-permute-start.13 = (f32[64,512]{1,0:T(8,128)S(1)}, f32[64,512]{1,0:T(8,128)S(1)}, u32[]{:S(2)}, u32[]{:S(2)}) collective-permute-start(f32[64,512]{1,0:T(8,128)S(1)} %get-tuple-element.48), channel_id=1, source_target_pairs={{0,8},{2,10},{4,12},{6,14},{8,16},{10,18},{12,20},{14,22},{16,24},... | collective-permute-start | bytes 393224 | tf_op jit(solution)/shard_map/ppermute | solution.py:33
  353.8 5.2 %collective-permute-start.16 = (f32[32,512]{1,0:T(8,128)S(1)}, f32[32,512]{1,0:T(8,128)S(1)}, u32[]{:S(2)}, u32[]{:S(2)}) collective-permute-start(f32[32,512]{1,0:T(8,128)S(1)} %constant_dynamic-slice_fusion), channel_id=1, source_target_pairs={{0,4},{2,6},{4,0},{6,2},{8,12},{10,14},{12,8},{14,10},{16,20},{18,... | collective-permute-start | bytes 196616 | tf_op jit(solution)/shard_map/ppermute | solution.py:33
  359.1 3.2 collective-permute-start.20
  362.3 12.3 %collective-permute-start.21 = (f32[64,512]{1,0:T(8,128)S(1)}, f32[64,512]{1,0:T(8,128)S(1)}, u32[]{:S(2)}, u32[]{:S(2)}) collective-permute-start(f32[64,512]{1,0:T(8,128)S(1)} %pad_maximum_fusion.16), channel_id=1, source_target_pairs={{0,8},{2,10},{4,12},{6,14},{8,16},{10,18},{12,20},{14,22},{16,24},... | collective-permute-start | bytes 393224 | tf_op jit(solution)/shard_map/ppermute | solution.py:33
  372.6 5.4 %collective-permute-start.22 = (f32[64,512]{1,0:T(8,128)S(1)}, f32[64,512]{1,0:T(8,128)S(1)}, u32[]{:S(2)}, u32[]{:S(2)}) collective-permute-start(f32[64,512]{1,0:T(8,128)S(1)} %pad_maximum_fusion.16), channel_id=1, source_target_pairs={{0,16},{2,18},{4,20},{6,22},{8,24},{10,26},{12,28},{14,30},{16,0},... | collective-permute-start | bytes 393224 | tf_op jit(solution)/shard_map/ppermute | solution.py:33
  372.6 5.4 %collective-permute-start.23 = (f32[64,512]{1,0:T(8,128)S(1)}, f32[64,512]{1,0:T(8,128)S(1)}, u32[]{:S(2)}, u32[]{:S(2)}) collective-permute-start(f32[64,512]{1,0:T(8,128)S(1)} %pad_maximum_fusion.16), channel_id=1, source_target_pairs={{0,24},{2,26},{4,28},{6,30},{8,0},{10,2},{12,4},{14,6},{16,8},{18,... | collective-permute-start | bytes 393224 | tf_op jit(solution)/shard_map/ppermute | solution.py:33
  378.1 8.1 %collective-permute-start.27 = (f32[128,512]{1,0:T(8,128)S(1)}, f32[128,512]{1,0:T(8,128)S(1)}, u32[]{:S(2)}, u32[]{:S(2)}) collective-permute-start(f32[128,512]{1,0:T(8,128)S(1)} %bitcast.150), channel_id=1, source_target_pairs={{0,96},{2,98},{4,100},{6,102},{8,104},{10,106},{12,108},{14,110},{... | collective-permute-start | bytes 786440 | tf_op jit(solution)/shard_map/ppermute | solution.py:33
  382.9 6.5 %collective-permute-start.24 = (f32[128,512]{1,0:T(8,128)S(1)}, f32[128,512]{1,0:T(8,128)S(1)}, u32[]{:S(2)}, u32[]{:S(2)}) collective-permute-start(f32[128,512]{1,0:T(8,128)S(1)} %bitcast.148), channel_id=1, source_target_pairs={{0,32},{2,34},{4,36},{6,38},{8,40},{10,42},{12,44},{14,46},{16,48}... | collective-permute-start | bytes 786440 | tf_op jit(solution)/shard_map/ppermute | solution.py:33
  386.2 6.7 %collective-permute-start.28 = (f32[128,512]{1,0:T(8,128)S(1)}, f32[128,512]{1,0:T(8,128)S(1)}, u32[]{:S(2)}, u32[]{:S(2)}) collective-permute-start(f32[128,512]{1,0:T(8,128)S(1)} %collective-permute-done.27), channel_id=1, source_target_pairs={{0,96},{2,98},{4,100},{6,102},{8,104},{10,106},{12,108},{14,110},{... | collective-permute-start | bytes 786440 | tf_op jit(solution)/shard_map/ppermute | solution.py:33
  389.4 6.9 %collective-permute-start.25 = (f32[128,512]{1,0:T(8,128)S(1)}, f32[128,512]{1,0:T(8,128)S(1)}, u32[]{:S(2)}, u32[]{:S(2)}) collective-permute-start(f32[128,512]{1,0:T(8,128)S(1)} %collective-permute-done.24), channel_id=1, source_target_pairs={{0,32},{2,34},{4,36},{6,38},{8,40},{10,42},{12,44},{14,46},{16,48}... | collective-permute-start | bytes 786440 | tf_op jit(solution)/shard_map/ppermute | solution.py:33
  392.9 7.7 %collective-permute-start.29 = (f32[128,512]{1,0:T(8,128)S(1)}, f32[128,512]{1,0:T(8,128)S(1)}, u32[]{:S(2)}, u32[]{:S(2)}) collective-permute-start(f32[128,512]{1,0:T(8,128)S(1)} %collective-permute-done.28), channel_id=1, source_target_pairs={{0,96},{2,98},{4,100},{6,102},{8,104},{10,106},{12,108},{14,110},{... | collective-permute-start | bytes 786440 | tf_op jit(solution)/shard_map/ppermute | solution.py:33
  396.3 7.9 %collective-permute-start.26 = (f32[128,512]{1,0:T(8,128)S(1)}, f32[128,512]{1,0:T(8,128)S(1)}, u32[]{:S(2)}, u32[]{:S(2)}) collective-permute-start(f32[128,512]{1,0:T(8,128)S(1)} %collective-permute-done.25), channel_id=1, source_target_pairs={{0,32},{2,34},{4,36},{6,38},{8,40},{10,42},{12,44},{14,46},{16,48}... | collective-permute-start | bytes 786440 | tf_op jit(solution)/shard_map/ppermute | solution.py:33
  404.4 10.8 %collective-permute-start.30 = (f32[1024,512]{1,0:T(8,128)S(1)}, f32[1024,512]{1,0:T(8,128)S(1)}, u32[]{:S(2)}, u32[]{:S(2)}) collective-permute-start(f32[1024,512]{1,0:T(8,128)S(1)} %pad_maximum_fusion.10), channel_id=1, source_target_pairs={{0,2},{2,0},{4,6},{6,4},{8,10},{10,8},{12,14},{14,12},{16,18},{18,... | collective-permute-start | bytes 6291464 | tf_op jit(solution)/shard_map/ppermute | solution.py:33

commit v11 on v8

--- a/solution.py
+++ b/solution.py
@@ -115,9 +115,8 @@
     data = pair_reduce_scatter(data, CORE)
     data = direct_reduce_scatter(data, XAX)
     data = direct_reduce_scatter(data, YAX)
-    data = pair_reduce_scatter(data, ZLO)
+    data = data + sub_shift(data, ZLO, 1)
     data, early, tied = lax.optimization_barrier((data, early, tied))
-    data = pair_all_gather(data, ZLO)
     data = direct_all_gather(data, YAX)
     data = direct_all_gather(data, XAX)
     data = pair_all_gather(data, CORE)

time: 414 us -> 412 us (level)
  the two profiles are of different devices: /device:TPU:65 before, /device:TPU:69 now
where the time goes in v11:
time: 412 us; the launch traced here: 405 us
  waiting for transfers between devices  115 us (28%)
  Pallas kernels  94.7 us (23%)
  other arithmetic  77.9 us (19%)
  local copies, waits for them, and re-layouts  53.3 us (13%)
  starting transfers between devices  42.6 us (10%)
  between operations  20.9 us (5%)
    ppermute x15, waiting for transfers between devices, sub_shift(): return lax.ppermute(value, 'scan', pairs)  79.2 us
    pallas_call x2, Pallas kernels, backward_gradients(): pl.pallas_call(backward_kernel, grid_spec=grid_spec, out_shape=out_shape,...  52.2 us
    pallas_call x1, Pallas kernels, forward_correction(): pl.pallas_call(forward_kernel, grid=(slots,), in_specs=[pl.BlockSpec((1,...  42.5 us
    ppermute x5, waiting for transfers between devices, from_behind(): return lax.ppermute(value, axis, pairs)  36.1 us
    ppermute x15, starting transfers between devices, sub_shift(): return lax.ppermute(value, 'scan', pairs)  29.1 us
    dynamic_update_slice x3, local copies, waits for them, and re-layouts, shards(): lax.dynamic_update_slice(gradient_plane, current + mine[slot_id, 0], start)  22.9 us
    another operation x5, other arithmetic  20 us
    reduce_sum x1, other arithmetic, shards(): position_y = jnp.sum(whole_grad * grad_y, axis=(1, 2, 3))  17.1 us
  transfers between devices with their start and end apart: 24, of which 11 were waited for; matrix products, arithmetic and copies ran while one was open for 26% of the time, Pallas kernels for 6%

profile of v11, /device:TPU:69, one launch (start us, length us, event | category | flops | bytes accessed | tf_op | source)
XLA Modules:
  0.0 404.6 jit_solution(17453757671070664695)
XLA Ops:
  0.6 3.0 collective-permute-start.1
  4.9 2.6 collective-permute-start
  7.5 4.8 %dynamic-slice_bitcast_fusion.4 = (f32[2,512,512]{2,1,0:T(8,128)}, f32[2,512,512]{2,1,0:T(8,128)}) fusion(f32[2,2,512,512]{3,2,1,0:T(8,128)} %param.6, s32[]{:T(128)S(6)} %select_n.277, s32[]{:T(128)S(6)} %select_n.278), kind=kLoop, calls=%fused_computation.31 | loop fusion | bytes 8388616 | tf_op jit(solution)/shard_map/jit(dynamic_index_in_dim)/squeeze | solution.py:303
  12.3 1.6 collective-permute-start.5
  13.9 4.0 multiply_convert_fusion
  17.9 4.0 multiply_convert_fusion.1
  21.9 4.0 negate_convert_fusion
  25.9 4.0 multiply_convert_fusion.2
  29.9 4.0 negate_convert_fusion.1
  35.4 36.0 %collective-permute-done.1 = f32[2,512,512]{2,1,0:T(8,128)} collective-permute-done((f32[2,512,512]{2,1,0:T(8,128)}, f32[2,512,512]{2,1,0:T(8,128)}, u32[]{:S(2)}, u32[]{:S(2)}) %collective-permute-start.1) | collective-permute-done | bytes 2097184 | tf_op jit(solution)/shard_map/ppermute | solution.py:23
  71.5 4.9 %collective-permute-start.2 = (f32[2,512,512]{2,1,0:T(8,128)}, f32[2,512,512]{2,1,0:T(8,128)}, u32[]{:S(2)}, u32[]{:S(2)}) collective-permute-start(f32[2,512,512]{2,1,0:T(8,128)} %collective-permute-done.1), channel_id=1, source_target_pairs={{2,0},{6,4},{10,8},{14,12},{18,16},{22,20},{26,24},{30,28},{34,32}... | collective-permute-start | bytes 6291464 | tf_op jit(solution)/shard_map/ppermute | solution.py:323
  98.0 4.1 %fusion.9 = (bf16[1024,1024]{1,0:T(8,128)(2,1)}, bf16[1024,1024]{1,0:T(8,128)(2,1)}) fusion(bf16[512,512]{1,0:T(8,128)(2,1)} %get-tuple-element.62, bf16[512,512]{1,0:T(8,128)(2,1)S(1)} %get-tuple-element.46, bf16[512,512]{1,0:T(8,128)(2,1)} %get-tuple-element.63, bf16[512,512]{1,0:T(8,128)(2,1)S(1)} %get-tuple-element.45), kind=kLoop, calls=%fused_computation.26 | loop fusion | flops 14680064 | bytes 6291456 | tf_op jit(solution)/shard_map/concatenate | solution.py:153
  102.1 10.3 %fusion.7 = (bf16[1024,1024]{1,0:T(8,128)(2,1)}, bf16[1024,1024]{1,0:T(8,128)(2,1)}) fusion(bf16[512,512]{1,0:T(8,128)(2,1)S(1)} %copy-done.5, bf16[512,512]{1,0:T(8,128)(2,1)S(1)} %copy-done.4, bf16[512,512]{1,0:T(8,128)(2,1)S(1)} %copy-done.6, bf16[512,512]{1,0:T(8,128)(2,1)S(1)} %copy-done.3), kind=kLoop, calls=%fused_computation.24 | loop fusion | flops 14680064 | bytes 6291456 | tf_op jit(solution)/shard_map/concatenate | solution.py:153
  112.4 2.9 select_bitcast_fusion.1
  115.8 4.0 maximum_select_fusion.probe_ref
  121.5 2.6 maximum_maximum_fusion
  124.1 2.1 dynamic-slice_bitcast_fusion.2
  126.8 5.0 %slice.134.patch_ref = f32[3,2,512,512]{3,2,1,0:T(8,128)} slice(f32[3,2,514,514]{3,2,1,0:T(8,128)S(1)} %pad_maximum_fusion), slice={[0:3], [0:2], [1:513], [1:513]} | slice | bytes 12582912 | tf_op jit(solution)/shard_map/slice | solution.py:339
  131.9 42.5 %shard_map.76.corr_ref = bf16[3,4,2,512,512]{4,3,2,1,0:T(8,128)(2,1)} custom-call(f32[3,2,512,512]{3,2,1,0:T(8,128)} %slice.134.patch_ref, f32[4,2,512,512]{3,2,1,0:T(8,128)} %maximum_select_fusion.probe_ref, f32[3,512,512]{2,1,0:T(8,128)} %bitcast.133, bf16[1024,1024]{1,0:T(8,128)(2,1)} %get-tuple-element.38.left_ref, ...), custom_call_target="tpu_custom_call" | custom-call | flops 25769803776 | bytes 44040192 | tf_op jit(solution)/shard_map/pallas_call | solution.py:191
  174.4 28.3 %shard_map.77 = (f32[3,2,512,512]{3,2,1,0:T(8,128)}, f32[2,2,512,512]{3,2,1,0:T(8,128)}) custom-call(s32[1]{0:T(128)} %bitcast.block_ref, s32[1]{0:T(128)S(6)} %copy.19.count_ref, bf16[3,4,2,512,512]{4,3,2,1,0:T(8,128)(2,1)} %shard_map.76.corr_ref, f32[4,2,512,512]{3,2,1,0:T(8,128)} %maximum_select_fusion.probe_ref, f32[3,2,512,512]{3,2,1,0:T(8,128)} %slice.134.patch_ref, ...), custom_call_target="tpu_custom_call" | custom-call | flops 12884901888 | bytes 37748736 | tf_op jit(solution)/shard_map/pallas_call | solution.py:273
  202.7 3.1 constant_dynamic-slice_fusion
  205.8 23.9 %shard_map.78 = f32[3,2,512,512]{3,2,1,0:T(8,128)} custom-call(s32[1]{0:T(128)} %bitcast.29.block_ref, s32[1]{0:T(128)S(6)} %copy.19.count_ref, bf16[3,4,2,512,512]{4,3,2,1,0:T(8,128)(2,1)} %shard_map.76.corr_ref, f32[4,2,512,512]{3,2,1,0:T(8,128)} %maximum_select_fusion.probe_ref, f32[3,2,512,512]{3,2,1,0:T(8,128)} %slice.134.patch_ref, ...), custom_call_target="tpu_custom_call" | custom-call | flops 12884901888 | bytes 37748736 | tf_op jit(solution)/shard_map/pallas_call | solution.py:273
  229.7 17.1 %fusion.5 = (f32[3]{0:T(128)S(1)}, f32[3]{0:T(128)S(1)}, f32[3,2,512,512]{3,2,1,0:T(8,128)S(1)}) fusion(f32[3,2,514,514]{3,2,1,0:T(8,128)} %copy-done, f32[3,2,512,512]{3,2,1,0:T(8,128)} %get-tuple-element.10, f32[3,2,512,512]{3,2,1,0:T(8,128)} %shard_map.78), kind=kLoop, calls=%fused_computation.10 | loop fusion | flops 14155770 | bytes 44040216 | tf_op jit(solution)/shard_map/reduce_sum | solution.py:356
  246.8 2.6 copy-done.2
  249.5 2.5 broadcast_in_dim.45
  252.0 7.5 %dynamic_update_slice.35 = f32[1024,1024]{1,0:T(8,128)} dynamic-update-slice(f32[1024,1024]{1,0:T(8,128)} %broadcast_in_dim.45, f32[512,512]{1,0:T(8,128)S(1)} %dynamic-slice_bitcast_fusion.7, s32[]{:T(128)S(6)} %select_n.284, s32[]{:T(128)S(6)} %select_n.285) | dynamic-update-slice | bytes 2097156 | tf_op jit(solution)/shard_map/dynamic_update_slice | solution.py:364
  259.5 2.7 dynamic-slice_add_fusion
  263.7 2.4 collective-permute-start.8
  266.1 2.0 fusion.21
  268.1 7.7 %dynamic_update_slice.36 = f32[1024,1024]{1,0:T(8,128)} dynamic-update-slice(f32[1024,1024]{1,0:T(8,128)} %dynamic_update_slice.35, f32[512,512]{1,0:T(8,128)S(1)} %fusion.21, s32[]{:T(128)S(6)} %select_n.286, s32[]{:T(128)S(6)} %select_n.287) | dynamic-update-slice | bytes 2097156 | tf_op jit(solution)/shard_map/dynamic_update_slice | solution.py:364
  275.8 2.0 fusion.20
  277.8 7.7 %dynamic_update_slice.37 = f32[1024,1024]{1,0:T(8,128)} dynamic-update-slice(f32[1024,1024]{1,0:T(8,128)} %dynamic_update_slice.36, f32[512,512]{1,0:T(8,128)S(1)} %fusion.20, s32[]{:T(128)S(6)} %select_n.288, s32[]{:T(128)S(6)} %select_n.289) | dynamic-update-slice | bytes 2097156 | tf_op jit(solution)/shard_map/dynamic_update_slice | solution.py:364
  285.5 3.6 fusion.30
  292.3 2.6 collective-permute-start.11
  294.9 42.8 %collective-permute-done.12 = f32[64,512]{1,0:T(8,128)S(1)} collective-permute-done((f32[64,512]{1,0:T(8,128)S(1)}, f32[64,512]{1,0:T(8,128)S(1)}, u32[]{:S(2)}, u32[]{:S(2)}) %collective-permute-start.12) | collective-permute-done | bytes 131104 | tf_op jit(solution)/shard_map/ppermute | solution.py:33
  337.7 2.1 collective-permute-start.10
  339.8 2.2 collective-permute-done.11
  342.1 2.6 collective-permute-done.10
  344.7 5.1 %collective-permute-start.13 = (f32[64,512]{1,0:T(8,128)S(1)}, f32[64,512]{1,0:T(8,128)S(1)}, u32[]{:S(2)}, u32[]{:S(2)}) collective-permute-start(f32[64,512]{1,0:T(8,128)S(1)} %fusion.29), channel_id=1, source_target_pairs={{0,4},{2,6},{4,0},{6,2},{8,12},{10,14},{12,8},{14,10},{16,20},{18,... | collective-permute-start | bytes 393224 | tf_op jit(solution)/shard_map/ppermute | solution.py:33
  350.4 2.3 collective-permute-done.13
  352.8 10.8 %collective-permute-start.18 = (f32[64,512]{1,0:T(8,128)S(1)}, f32[64,512]{1,0:T(8,128)S(1)}, u32[]{:S(2)}, u32[]{:S(2)}) collective-permute-start(f32[64,512]{1,0:T(8,128)S(1)} %add.337), channel_id=1, source_target_pairs={{0,16},{2,18},{4,20},{6,22},{8,24},{10,26},{12,28},{14,30},{16,0},... | collective-permute-start | bytes 393224 | tf_op jit(solution)/shard_map/ppermute | solution.py:33
  363.7 2.0 collective-permute-start.19
  365.7 4.2 %collective-permute-done.18 = f32[64,512]{1,0:T(8,128)S(1)} collective-permute-done((f32[64,512]{1,0:T(8,128)S(1)}, f32[64,512]{1,0:T(8,128)S(1)}, u32[]{:S(2)}, u32[]{:S(2)}) %collective-permute-start.18) | collective-permute-done | bytes 131104 | tf_op jit(solution)/shard_map/ppermute | solution.py:33
  371.8 10.8 %collective-permute-done.20 = f32[256,512]{1,0:T(8,128)S(1)} collective-permute-done((f32[256,512]{1,0:T(8,128)S(1)}, f32[256,512]{1,0:T(8,128)S(1)}, u32[]{:S(2)}, u32[]{:S(2)}) %collective-permute-start.20) | collective-permute-done | bytes 524320 | tf_op jit(solution)/shard_map/ppermute | solution.py:33
  382.7 11.0 %collective-permute-done.21 = f32[256,512]{1,0:T(8,128)S(1)} collective-permute-done((f32[256,512]{1,0:T(8,128)S(1)}, f32[256,512]{1,0:T(8,128)S(1)}, u32[]{:S(2)}, u32[]{:S(2)}) %collective-permute-start.21) | collective-permute-done | bytes 524320 | tf_op jit(solution)/shard_map/ppermute | solution.py:33
  395.4 2.1 collective-permute-start.23
  397.6 3.6 fusion.19
  401.9 2.5 pad_maximum_fusion.1
  (70 shorter events, 17.3 us)
Async XLA Ops:
  0.6 70.9 %collective-permute-start.1 = (f32[2,512,512]{2,1,0:T(8,128)}, f32[2,512,512]{2,1,0:T(8,128)}, u32[]{:S(2)}, u32[]{:S(2)}) collective-permute-start(f32[2,512,512]{2,1,0:T(8,128)} %bitcast.125), channel_id=1, source_target_pairs={{0,112},{2,114},{4,116},{6,118},{8,120},{10,122},{12,124},{14,126}... | collective-permute-start | bytes 6291464 | tf_op jit(solution)/shard_map/ppermute | solution.py:23
  3.6 116.3 %collective-permute-start.3 = (f32[2,512,512]{2,1,0:T(8,128)}, f32[2,512,512]{2,1,0:T(8,128)S(1)}, u32[]{:S(2)}, u32[]{:S(2)}) collective-permute-start(f32[2,512,512]{2,1,0:T(8,128)} %bitcast.126), channel_id=1, source_target_pairs={{20,2},{24,6},{28,10},{32,14},{36,18},{40,22},{44,26},{48,30},{52,... | collective-permute-start | bytes 6291464 | tf_op jit(solution)/shard_map/ppermute | solution.py:319
  4.9 115.5 %collective-permute-start = (f32[2,512,512]{2,1,0:T(8,128)}, f32[2,512,512]{2,1,0:T(8,128)}, u32[]{:S(2)}, u32[]{:S(2)}) collective-permute-start(f32[2,512,512]{2,1,0:T(8,128)} %bitcast.127), channel_id=1, source_target_pairs={{0,126},{2,0},{4,2},{6,4},{8,6},{10,8},{12,10},{14,12},{16,14},{18... | collective-permute-start | bytes 6291464 | tf_op jit(solution)/shard_map/ppermute | solution.py:23
  12.3 100.1 %collective-permute-start.4 = (f32[2,512,512]{2,1,0:T(8,128)}, f32[2,512,512]{2,1,0:T(8,128)}, u32[]{:S(2)}, u32[]{:S(2)}) collective-permute-start(f32[2,512,512]{2,1,0:T(8,128)} %get-tuple-element.30), channel_id=1, source_target_pairs={{0,5},{1,4},{2,7},{3,6},{4,1},{5,0},{6,3},{7,2},{8,13},{9,12},{10,... | collective-permute-start | bytes 6291464 | tf_op jit(solution)/shard_map/ppermute | solution.py:305
  12.3 100.1 %collective-permute-start.5 = (f32[2,512,512]{2,1,0:T(8,128)}, f32[2,512,512]{2,1,0:T(8,128)}, u32[]{:S(2)}, u32[]{:S(2)}) collective-permute-start(f32[2,512,512]{2,1,0:T(8,128)} %get-tuple-element.31), channel_id=1, source_target_pairs={{0,1},{1,0},{2,3},{3,2},{4,5},{5,4},{6,7},{7,6},{8,9},{9,8},{10,11... | collective-permute-start | bytes 6291464 | tf_op jit(solution)/shard_map/ppermute | solution.py:307
  34.2 43.5 %copy-start.8 = (s32[1,3,2]{1,2,0:T(2,128)S(1)}, s32[1,3,2]{1,2,0:T(2,128)}, u32[]{:S(2)}) copy-start(s32[1,3,2]{1,2,0:T(2,128)} %param.8) | copy-start | bytes 76
  71.5 48.4 %collective-permute-start.2 = (f32[2,512,512]{2,1,0:T(8,128)}, f32[2,512,512]{2,1,0:T(8,128)}, u32[]{:S(2)}, u32[]{:S(2)}) collective-permute-start(f32[2,512,512]{2,1,0:T(8,128)} %collective-permute-done.1), channel_id=1, source_target_pairs={{2,0},{6,4},{10,8},{14,12},{18,16},{22,20},{26,24},{30,28},{34,32}... | collective-permute-start | bytes 6291464 | tf_op jit(solution)/shard_map/ppermute | solution.py:323
  98.0 4.1 %copy-start.3 = (bf16[512,512]{1,0:T(8,128)(2,1)S(1)}, bf16[512,512]{1,0:T(8,128)(2,1)}, u32[]{:S(2)}) copy-start(bf16[512,512]{1,0:T(8,128)(2,1)} %get-tuple-element.41) | copy-start | bytes 1572868
  98.0 4.1 %copy-start.4 = (bf16[512,512]{1,0:T(8,128)(2,1)S(1)}, bf16[512,512]{1,0:T(8,128)(2,1)}, u32[]{:S(2)}) copy-start(bf16[512,512]{1,0:T(8,128)(2,1)} %get-tuple-element.42) | copy-start | bytes 1572868
  98.0 4.1 %copy-start.5 = (bf16[512,512]{1,0:T(8,128)(2,1)S(1)}, bf16[512,512]{1,0:T(8,128)(2,1)}, u32[]{:S(2)}) copy-start(bf16[512,512]{1,0:T(8,128)(2,1)} %get-tuple-element.60) | copy-start | bytes 1572868
  98.0 4.1 %copy-start.6 = (bf16[512,512]{1,0:T(8,128)(2,1)S(1)}, bf16[512,512]{1,0:T(8,128)(2,1)}, u32[]{:S(2)}) copy-start(bf16[512,512]{1,0:T(8,128)(2,1)} %get-tuple-element.61) | copy-start | bytes 1572868
  112.4 3.4 copy-start.1
  119.9 1.6 copy-start.7
  126.8 5.0 %copy-start = (f32[3,2,514,514]{3,2,1,0:T(8,128)}, f32[3,2,514,514]{3,2,1,0:T(8,128)S(1)}, u32[]{:S(2)}) copy-start(f32[3,2,514,514]{3,2,1,0:T(8,128)S(1)} %pad_maximum_fusion) | copy-start | bytes 19022116
  205.8 53.7 %collective-permute-start.6 = (f32[1024,512]{1,0:T(8,128)}, f32[1024,512]{1,0:T(8,128)}, u32[]{:S(2)}, u32[]{:S(2)}) collective-permute-start(f32[1024,512]{1,0:T(8,128)} %constant_dynamic-slice_fusion), channel_id=1, source_target_pairs={{0,2},{2,0},{4,6},{6,4},{8,10},{10,8},{12,14},{14,12},{16,18},{18,... | collective-permute-start | bytes 6291464 | tf_op jit(solution)/shard_map/ppermute | solution.py:33
  246.8 2.7 copy-start.2
  263.4 25.7 %collective-permute-start.9 = (f32[256,512]{1,0:T(8,128)}, f32[256,512]{1,0:T(8,128)}, u32[]{:S(2)}, u32[]{:S(2)}) collective-permute-start(f32[256,512]{1,0:T(8,128)} %get-tuple-element.33), channel_id=1, source_target_pairs={{0,96},{2,98},{4,100},{6,102},{8,104},{10,106},{12,108},{14,110},{... | collective-permute-start | bytes 1572872 | tf_op jit(solution)/shard_map/ppermute | solution.py:33
  263.7 25.6 %collective-permute-start.8 = (f32[256,512]{1,0:T(8,128)}, f32[256,512]{1,0:T(8,128)}, u32[]{:S(2)}, u32[]{:S(2)}) collective-permute-start(f32[256,512]{1,0:T(8,128)} %get-tuple-element.34), channel_id=1, source_target_pairs={{0,64},{2,66},{4,68},{6,70},{8,72},{10,74},{12,76},{14,78},{16,80}... | collective-permute-start | bytes 1572872 | tf_op jit(solution)/shard_map/ppermute | solution.py:33
  266.1 24.5 %collective-permute-start.7 = (f32[256,512]{1,0:T(8,128)}, f32[256,512]{1,0:T(8,128)}, u32[]{:S(2)}, u32[]{:S(2)}) collective-permute-start(f32[256,512]{1,0:T(8,128)} %get-tuple-element.32), channel_id=1, source_target_pairs={{0,32},{2,34},{4,36},{6,38},{8,40},{10,42},{12,44},{14,46},{16,48}... | collective-permute-start | bytes 1572872 | tf_op jit(solution)/shard_map/ppermute | solution.py:33
  289.1 63.6 %collective-permute-start.14 = (f32[512,512]{1,0:T(8,128)}, f32[512,512]{1,0:T(8,128)}, u32[]{:S(2)}, u32[]{:S(2)}) collective-permute-start(f32[512,512]{1,0:T(8,128)} %get-tuple-element.27), channel_id=1, source_target_pairs={{0,2},{2,4},{4,6},{6,8},{8,10},{10,12},{12,14},{14,16},{16,18},{18... | collective-permute-start | bytes 3145736 | tf_op jit(solution)/shard_map/ppermute | solution.py:23
  289.1 63.7 %collective-permute-start.15 = (f32[512,512]{1,0:T(8,128)}, f32[512,512]{1,0:T(8,128)}, u32[]{:S(2)}, u32[]{:S(2)}) collective-permute-start(f32[512,512]{1,0:T(8,128)} %get-tuple-element.26), channel_id=1, source_target_pairs={{0,16},{2,18},{4,20},{6,22},{8,24},{10,26},{12,28},{14,30},{16,32}... | collective-permute-start | bytes 3145736 | tf_op jit(solution)/shard_map/ppermute | solution.py:23
  289.1 63.7 %collective-permute-start.16 = (f32[512,512]{1,0:T(8,128)}, f32[512,512]{1,0:T(8,128)}, u32[]{:S(2)}, u32[]{:S(2)}) collective-permute-start(f32[512,512]{1,0:T(8,128)} %get-tuple-element.25), channel_id=1, source_target_pairs={{0,18},{2,20},{4,22},{6,24},{8,26},{10,28},{12,30},{14,32},{16,34}... | collective-permute-start | bytes 3145736 | tf_op jit(solution)/shard_map/ppermute | solution.py:23
  292.2 45.5 %collective-permute-start.12 = (f32[64,512]{1,0:T(8,128)S(1)}, f32[64,512]{1,0:T(8,128)S(1)}, u32[]{:S(2)}, u32[]{:S(2)}) collective-permute-start(f32[64,512]{1,0:T(8,128)S(1)} %get-tuple-element.48), channel_id=1, source_target_pairs={{0,24},{2,26},{4,28},{6,30},{8,0},{10,2},{12,4},{14,6},{16,8},{18,... | collective-permute-start | bytes 393224 | tf_op jit(solution)/shard_map/ppermute | solution.py:33
  292.3 49.7 %collective-permute-start.11 = (f32[64,512]{1,0:T(8,128)S(1)}, f32[64,512]{1,0:T(8,128)S(1)}, u32[]{:S(2)}, u32[]{:S(2)}) collective-permute-start(f32[64,512]{1,0:T(8,128)S(1)} %get-tuple-element.49), channel_id=1, source_target_pairs={{0,16},{2,18},{4,20},{6,22},{8,24},{10,26},{12,28},{14,30},{16,0},... | collective-permute-start | bytes 393224 | tf_op jit(solution)/shard_map/ppermute | solution.py:33
  337.7 6.9 %collective-permute-start.10 = (f32[64,512]{1,0:T(8,128)S(1)}, f32[64,512]{1,0:T(8,128)S(1)}, u32[]{:S(2)}, u32[]{:S(2)}) collective-permute-start(f32[64,512]{1,0:T(8,128)S(1)} %get-tuple-element.47), channel_id=1, source_target_pairs={{0,8},{2,10},{4,12},{6,14},{8,16},{10,18},{12,20},{14,22},{16,24},... | collective-permute-start | bytes 393224 | tf_op jit(solution)/shard_map/ppermute | solution.py:33
  344.7 8.0 %collective-permute-start.13 = (f32[64,512]{1,0:T(8,128)S(1)}, f32[64,512]{1,0:T(8,128)S(1)}, u32[]{:S(2)}, u32[]{:S(2)}) collective-permute-start(f32[64,512]{1,0:T(8,128)S(1)} %fusion.29), channel_id=1, source_target_pairs={{0,4},{2,6},{4,0},{6,2},{8,12},{10,14},{12,8},{14,10},{16,20},{18,... | collective-permute-start | bytes 393224 | tf_op jit(solution)/shard_map/ppermute | solution.py:33
  352.8 13.0 %collective-permute-start.17 = (f32[64,512]{1,0:T(8,128)S(1)}, f32[64,512]{1,0:T(8,128)S(1)}, u32[]{:S(2)}, u32[]{:S(2)}) collective-permute-start(f32[64,512]{1,0:T(8,128)S(1)} %add.337), channel_id=1, source_target_pairs={{0,8},{2,10},{4,12},{6,14},{8,16},{10,18},{12,20},{14,22},{16,24},... | collective-permute-start | bytes 393224 | tf_op jit(solution)/shard_map/ppermute | solution.py:33
  352.8 17.1 %collective-permute-start.18 = (f32[64,512]{1,0:T(8,128)S(1)}, f32[64,512]{1,0:T(8,128)S(1)}, u32[]{:S(2)}, u32[]{:S(2)}) collective-permute-start(f32[64,512]{1,0:T(8,128)S(1)} %add.337), channel_id=1, source_target_pairs={{0,16},{2,18},{4,20},{6,22},{8,24},{10,26},{12,28},{14,30},{16,0},... | collective-permute-start | bytes 393224 | tf_op jit(solution)/shard_map/ppermute | solution.py:33
  363.7 6.3 %collective-permute-start.19 = (f32[64,512]{1,0:T(8,128)S(1)}, f32[64,512]{1,0:T(8,128)S(1)}, u32[]{:S(2)}, u32[]{:S(2)}) collective-permute-start(f32[64,512]{1,0:T(8,128)S(1)} %add.337), channel_id=1, source_target_pairs={{0,24},{2,26},{4,28},{6,30},{8,0},{10,2},{12,4},{14,6},{16,8},{18,... | collective-permute-start | bytes 393224 | tf_op jit(solution)/shard_map/ppermute | solution.py:33
  370.0 12.7 %collective-permute-start.20 = (f32[256,512]{1,0:T(8,128)S(1)}, f32[256,512]{1,0:T(8,128)S(1)}, u32[]{:S(2)}, u32[]{:S(2)}) collective-permute-start(f32[256,512]{1,0:T(8,128)S(1)} %bitcast.119), channel_id=1, source_target_pairs={{0,32},{2,34},{4,36},{6,38},{8,40},{10,42},{12,44},{14,46},{16,48}... | collective-permute-start | bytes 1572872 | tf_op jit(solution)/shard_map/ppermute | solution.py:33
  370.0 23.7 %collective-permute-start.21 = (f32[256,512]{1,0:T(8,128)S(1)}, f32[256,512]{1,0:T(8,128)S(1)}, u32[]{:S(2)}, u32[]{:S(2)}) collective-permute-start(f32[256,512]{1,0:T(8,128)S(1)} %bitcast.120), channel_id=1, source_target_pairs={{0,64},{2,66},{4,68},{6,70},{8,72},{10,74},{12,76},{14,78},{16,80}... | collective-permute-start | bytes 1572872 | tf_op jit(solution)/shard_map/ppermute | solution.py:33
  371.4 24.0 %collective-permute-start.22 = (f32[256,512]{1,0:T(8,128)S(1)}, f32[256,512]{1,0:T(8,128)S(1)}, u32[]{:S(2)}, u32[]{:S(2)}) collective-permute-start(f32[256,512]{1,0:T(8,128)S(1)} %bitcast.121), channel_id=1, source_target_pairs={{0,96},{2,98},{4,100},{6,102},{8,104},{10,106},{12,108},{14,110},{... | collective-permute-start | bytes 1572872 | tf_op jit(solution)/shard_map/ppermute | solution.py:33
  395.4 5.9 %collective-permute-start.23 = (f32[1024,512]{1,0:T(8,128)S(1)}, f32[1024,512]{1,0:T(8,128)S(1)}, u32[]{:S(2)}, u32[]{:S(2)}) collective-permute-start(f32[1024,512]{1,0:T(8,128)S(1)} %bitcast.115), channel_id=1, source_target_pairs={{0,2},{2,0},{4,6},{6,4},{8,10},{10,8},{12,14},{14,12},{16,18},{18,... | collective-permute-start | bytes 6291464 | tf_op jit(solution)/shard_map/ppermute | solution.py:33

commit v12 on v11

--- a/solution.py
+++ b/solution.py
@@ -59,7 +59,7 @@
     coord = sub_coord(sub)
     chunks = data.reshape(size, data.shape[0] // size, -1)
     total = chunks[coord]
-    for shift in range(1, size):
+    for shift in sorted(range(1, size), key=lambda k: -min(k, size - k)):
         total = total + sub_shift(chunks[(coord + shift) % size], sub, shift)
     return total
 
@@ -69,7 +69,7 @@
     coord = sub_coord(sub)
     out = jnp.zeros((size,) + data.shape, data.dtype)
     out = lax.dynamic_update_index_in_dim(out, data, coord, 0)
-    for shift in range(1, size):
+    for shift in sorted(range(1, size), key=lambda k: -min(k, size - k)):
         got = sub_shift(data, sub, shift)
         out = lax.dynamic_update_index_in_dim(out, got, (coord - shift) % size, 0)
     return out.reshape(size * data.shape[0], -1)

time: 412 us -> 419 us (1.017)
  the two profiles are of different devices: /device:TPU:69 before, /device:TPU:75 now
where the time goes in v12:
time: 419 us; the launch traced here: 412 us
  waiting for transfers between devices  115 us (27%)
  Pallas kernels  94.5 us (23%)
  other arithmetic  77.7 us (19%)
  local copies, waits for them, and re-layouts  52.7 us (13%)
  starting transfers between devices  50.8 us (12%)
  between operations  21.2 us (5%)
    ppermute x15, waiting for transfers between devices, sub_shift(): return lax.ppermute(value, 'scan', pairs)  86.7 us
    pallas_call x2, Pallas kernels, backward_gradients(): pl.pallas_call(backward_kernel, grid_spec=grid_spec, out_shape=out_shape,...  52.2 us
    pallas_call x1, Pallas kernels, forward_correction(): pl.pallas_call(forward_kernel, grid=(slots,), in_specs=[pl.BlockSpec((1,...  42.3 us
    ppermute x15, starting transfers between devices, sub_shift(): return lax.ppermute(value, 'scan', pairs)  32.7 us
    dynamic_update_slice x3, local copies, waits for them, and re-layouts, shards(): lax.dynamic_update_slice(gradient_plane, current + mine[slot_id, 0], start)  22.7 us
    another operation x5, other arithmetic  20 us
    reduce_sum x1, other arithmetic, shards(): position_y = jnp.sum(whole_grad * grad_y, axis=(1, 2, 3))  17.1 us
    concatenate x2, other arithmetic, complex_table(): return jnp.concatenate(rows, axis=0)  14.3 us
  transfers between devices with their start and end apart: 24, of which 13 were waited for; matrix products, arithmetic and copies ran while one was open for 26% of the time, Pallas kernels for 6%

profile of v12, /device:TPU:75, one launch (start us, length us, event | category | flops | bytes accessed | tf_op | source)
XLA Modules:
  0.0 411.7 jit_solution(3294668427960296583)
XLA Ops:
  0.6 2.1 collective-permute-start.1
  5.6 4.8 %dynamic-slice_bitcast_fusion.4 = (f32[2,512,512]{2,1,0:T(8,128)}, f32[2,512,512]{2,1,0:T(8,128)}) fusion(f32[2,2,512,512]{3,2,1,0:T(8,128)} %param.6, s32[]{:T(128)S(6)} %select_n.277, s32[]{:T(128)S(6)} %select_n.278), kind=kLoop, calls=%fused_computation.31 | loop fusion | bytes 8388616 | tf_op jit(solution)/shard_map/jit(dynamic_index_in_dim)/squeeze | solution.py:303
  10.3 3.5 collective-permute-start.5
  13.9 4.0 multiply_convert_fusion
  17.8 4.0 multiply_convert_fusion.1
  21.8 4.0 negate_convert_fusion
  25.9 4.0 multiply_convert_fusion.2
  29.9 4.0 negate_convert_fusion.1
  35.4 13.7 %collective-permute-done.1 = f32[2,512,512]{2,1,0:T(8,128)} collective-permute-done((f32[2,512,512]{2,1,0:T(8,128)}, f32[2,512,512]{2,1,0:T(8,128)}, u32[]{:S(2)}, u32[]{:S(2)}) %collective-permute-start.1) | collective-permute-done | bytes 2097184 | tf_op jit(solution)/shard_map/ppermute | solution.py:23
  49.1 4.9 %collective-permute-start.2 = (f32[2,512,512]{2,1,0:T(8,128)}, f32[2,512,512]{2,1,0:T(8,128)}, u32[]{:S(2)}, u32[]{:S(2)}) collective-permute-start(f32[2,512,512]{2,1,0:T(8,128)} %collective-permute-done.1), channel_id=1, source_target_pairs={{2,0},{6,4},{10,8},{14,12},{18,16},{22,20},{26,24},{30,28},{34,32}... | collective-permute-start | bytes 6291464 | tf_op jit(solution)/shard_map/ppermute | solution.py:323
  75.6 4.1 fusion.9
  79.7 10.2 %fusion.7 = (bf16[1024,1024]{1,0:T(8,128)(2,1)}, bf16[1024,1024]{1,0:T(8,128)(2,1)}) fusion(bf16[512,512]{1,0:T(8,128)(2,1)S(1)} %copy-done.5, bf16[512,512]{1,0:T(8,128)(2,1)S(1)} %copy-done.4, bf16[512,512]{1,0:T(8,128)(2,1)S(1)} %copy-done.6, bf16[512,512]{1,0:T(8,128)(2,1)S(1)} %copy-done.3), kind=kLoop, calls=%fused_computation.24 | loop fusion | flops 14680064 | bytes 6291456 | tf_op jit(solution)/shard_map/concatenate | solution.py:153
  89.9 9.9 %collective-permute-done.4 = f32[2,512,512]{2,1,0:T(8,128)} collective-permute-done((f32[2,512,512]{2,1,0:T(8,128)}, f32[2,512,512]{2,1,0:T(8,128)}, u32[]{:S(2)}, u32[]{:S(2)}) %collective-permute-start.4) | collective-permute-done | bytes 2097184 | tf_op jit(solution)/shard_map/ppermute | solution.py:305
  99.9 4.5 %collective-permute-done.5 = f32[2,512,512]{2,1,0:T(8,128)} collective-permute-done((f32[2,512,512]{2,1,0:T(8,128)}, f32[2,512,512]{2,1,0:T(8,128)}, u32[]{:S(2)}, u32[]{:S(2)}) %collective-permute-start.5) | collective-permute-done | bytes 2097184 | tf_op jit(solution)/shard_map/ppermute | solution.py:307
  104.4 2.7 select_bitcast_fusion.1
  107.1 4.1 maximum_select_fusion.probe_ref
  112.8 2.6 maximum_maximum_fusion
  115.4 2.1 dynamic-slice_bitcast_fusion.2
  118.2 5.0 %slice.134.patch_ref = f32[3,2,512,512]{3,2,1,0:T(8,128)} slice(f32[3,2,514,514]{3,2,1,0:T(8,128)S(1)} %pad_maximum_fusion), slice={[0:3], [0:2], [1:513], [1:513]} | slice | bytes 12582912 | tf_op jit(solution)/shard_map/slice | solution.py:339
  123.2 42.3 %shard_map.76.corr_ref = bf16[3,4,2,512,512]{4,3,2,1,0:T(8,128)(2,1)} custom-call(f32[3,2,512,512]{3,2,1,0:T(8,128)} %slice.134.patch_ref, f32[4,2,512,512]{3,2,1,0:T(8,128)} %maximum_select_fusion.probe_ref, f32[3,512,512]{2,1,0:T(8,128)} %bitcast.133, bf16[1024,1024]{1,0:T(8,128)(2,1)} %get-tuple-element.38.left_ref, ...), custom_call_target="tpu_custom_call" | custom-call | flops 25769803776 | bytes 44040192 | tf_op jit(solution)/shard_map/pallas_call | solution.py:191
  165.5 28.3 %shard_map.77 = (f32[3,2,512,512]{3,2,1,0:T(8,128)}, f32[2,2,512,512]{3,2,1,0:T(8,128)}) custom-call(s32[1]{0:T(128)} %bitcast.block_ref, s32[1]{0:T(128)S(6)} %copy.19.count_ref, bf16[3,4,2,512,512]{4,3,2,1,0:T(8,128)(2,1)} %shard_map.76.corr_ref, f32[4,2,512,512]{3,2,1,0:T(8,128)} %maximum_select_fusion.probe_ref, f32[3,2,512,512]{3,2,1,0:T(8,128)} %slice.134.patch_ref, ...), custom_call_target="tpu_custom_call" | custom-call | flops 12884901888 | bytes 37748736 | tf_op jit(solution)/shard_map/pallas_call | solution.py:273
  193.8 3.1 constant_dynamic-slice_fusion
  198.9 23.9 %shard_map.78 = f32[3,2,512,512]{3,2,1,0:T(8,128)} custom-call(s32[1]{0:T(128)} %bitcast.29.block_ref, s32[1]{0:T(128)S(6)} %copy.19.count_ref, bf16[3,4,2,512,512]{4,3,2,1,0:T(8,128)(2,1)} %shard_map.76.corr_ref, f32[4,2,512,512]{3,2,1,0:T(8,128)} %maximum_select_fusion.probe_ref, f32[3,2,512,512]{3,2,1,0:T(8,128)} %slice.134.patch_ref, ...), custom_call_target="tpu_custom_call" | custom-call | flops 12884901888 | bytes 37748736 | tf_op jit(solution)/shard_map/pallas_call | solution.py:273
  222.8 17.1 %fusion.5 = (f32[3]{0:T(128)S(1)}, f32[3]{0:T(128)S(1)}, f32[3,2,512,512]{3,2,1,0:T(8,128)S(1)}) fusion(f32[3,2,514,514]{3,2,1,0:T(8,128)} %copy-done, f32[3,2,512,512]{3,2,1,0:T(8,128)} %get-tuple-element.10, f32[3,2,512,512]{3,2,1,0:T(8,128)} %shard_map.78), kind=kLoop, calls=%fused_computation.10 | loop fusion | flops 14155770 | bytes 44040216 | tf_op jit(solution)/shard_map/reduce_sum | solution.py:356
  239.9 2.6 copy-done.2
  242.6 2.5 broadcast_in_dim.45
  245.2 7.4 %dynamic_update_slice.35 = f32[1024,1024]{1,0:T(8,128)} dynamic-update-slice(f32[1024,1024]{1,0:T(8,128)} %broadcast_in_dim.45, f32[512,512]{1,0:T(8,128)S(1)} %dynamic-slice_bitcast_fusion.7, s32[]{:T(128)S(6)} %select_n.284, s32[]{:T(128)S(6)} %select_n.285) | dynamic-update-slice | bytes 2097156 | tf_op jit(solution)/shard_map/dynamic_update_slice | solution.py:364
  252.5 2.7 dynamic-slice_add_fusion
  256.4 2.7 collective-permute-start.9
  259.1 2.2 collective-permute-start.7
  261.3 2.0 fusion.21
  263.3 7.7 %dynamic_update_slice.36 = f32[1024,1024]{1,0:T(8,128)} dynamic-update-slice(f32[1024,1024]{1,0:T(8,128)} %dynamic_update_slice.35, f32[512,512]{1,0:T(8,128)S(1)} %fusion.21, s32[]{:T(128)S(6)} %select_n.286, s32[]{:T(128)S(6)} %select_n.287) | dynamic-update-slice | bytes 2097156 | tf_op jit(solution)/shard_map/dynamic_update_slice | solution.py:364
  271.0 2.0 fusion.20
  273.0 7.7 %dynamic_update_slice.37 = f32[1024,1024]{1,0:T(8,128)} dynamic-update-slice(f32[1024,1024]{1,0:T(8,128)} %dynamic_update_slice.36, f32[512,512]{1,0:T(8,128)S(1)} %fusion.20, s32[]{:T(128)S(6)} %select_n.288, s32[]{:T(128)S(6)} %select_n.289) | dynamic-update-slice | bytes 2097156 | tf_op jit(solution)/shard_map/dynamic_update_slice | solution.py:364
  280.7 3.6 fusion.30
  284.3 1.9 collective-permute-start.14
  290.6 2.5 collective-permute-start.12
  293.5 45.1 %collective-permute-done.12 = f32[64,512]{1,0:T(8,128)S(1)} collective-permute-done((f32[64,512]{1,0:T(8,128)S(1)}, f32[64,512]{1,0:T(8,128)S(1)}, u32[]{:S(2)}, u32[]{:S(2)}) %collective-permute-start.12) | collective-permute-done | bytes 131104 | tf_op jit(solution)/shard_map/ppermute | solution.py:33
  339.5 5.4 %collective-permute-done.10 = f32[64,512]{1,0:T(8,128)S(1)} collective-permute-done((f32[64,512]{1,0:T(8,128)S(1)}, f32[64,512]{1,0:T(8,128)S(1)}, u32[]{:S(2)}, u32[]{:S(2)}) %collective-permute-start.10) | collective-permute-done | bytes 131104 | tf_op jit(solution)/shard_map/ppermute | solution.py:33
  344.9 18.9 %collective-permute-start.13 = (f32[64,512]{1,0:T(8,128)S(1)}, f32[64,512]{1,0:T(8,128)S(1)}, u32[]{:S(2)}, u32[]{:S(2)}) collective-permute-start(f32[64,512]{1,0:T(8,128)S(1)} %fusion.29), channel_id=1, source_target_pairs={{0,4},{2,6},{4,0},{6,2},{8,12},{10,14},{12,8},{14,10},{16,20},{18,... | collective-permute-start | bytes 393224 | tf_op jit(solution)/shard_map/ppermute | solution.py:33
  364.4 2.9 collective-permute-done.13
  369.1 3.8 collective-permute-done.17
  372.9 4.1 collective-permute-done.19
  379.1 12.5 %collective-permute-done.20 = f32[256,512]{1,0:T(8,128)S(1)} collective-permute-done((f32[256,512]{1,0:T(8,128)S(1)}, f32[256,512]{1,0:T(8,128)S(1)}, u32[]{:S(2)}, u32[]{:S(2)}) %collective-permute-start.20) | collective-permute-done | bytes 524320 | tf_op jit(solution)/shard_map/ppermute | solution.py:33
  391.6 9.9 %collective-permute-done.21 = f32[256,512]{1,0:T(8,128)S(1)} collective-permute-done((f32[256,512]{1,0:T(8,128)S(1)}, f32[256,512]{1,0:T(8,128)S(1)}, u32[]{:S(2)}, u32[]{:S(2)}) %collective-permute-start.21) | collective-permute-done | bytes 524320 | tf_op jit(solution)/shard_map/ppermute | solution.py:33
  401.5 2.2 collective-permute-done.22
  404.4 3.6 fusion.19
  408.7 2.5 pad_maximum_fusion.1
  (70 shorter events, 23.1 us)
Async XLA Ops:
  0.6 48.4 %collective-permute-start.1 = (f32[2,512,512]{2,1,0:T(8,128)}, f32[2,512,512]{2,1,0:T(8,128)}, u32[]{:S(2)}, u32[]{:S(2)}) collective-permute-start(f32[2,512,512]{2,1,0:T(8,128)} %bitcast.125), channel_id=1, source_target_pairs={{0,112},{2,114},{4,116},{6,118},{8,120},{10,122},{12,124},{14,126}... | collective-permute-start | bytes 6291464 | tf_op jit(solution)/shard_map/ppermute | solution.py:23
  2.7 108.5 %collective-permute-start.3 = (f32[2,512,512]{2,1,0:T(8,128)}, f32[2,512,512]{2,1,0:T(8,128)S(1)}, u32[]{:S(2)}, u32[]{:S(2)}) collective-permute-start(f32[2,512,512]{2,1,0:T(8,128)} %bitcast.126), channel_id=1, source_target_pairs={{20,2},{24,6},{28,10},{32,14},{36,18},{40,22},{44,26},{48,30},{52,... | collective-permute-start | bytes 6291464 | tf_op jit(solution)/shard_map/ppermute | solution.py:319
  4.0 107.7 %collective-permute-start = (f32[2,512,512]{2,1,0:T(8,128)}, f32[2,512,512]{2,1,0:T(8,128)}, u32[]{:S(2)}, u32[]{:S(2)}) collective-permute-start(f32[2,512,512]{2,1,0:T(8,128)} %bitcast.127), channel_id=1, source_target_pairs={{0,126},{2,0},{4,2},{6,4},{8,6},{10,8},{12,10},{14,12},{16,14},{18... | collective-permute-start | bytes 6291464 | tf_op jit(solution)/shard_map/ppermute | solution.py:23
  10.3 89.5 %collective-permute-start.4 = (f32[2,512,512]{2,1,0:T(8,128)}, f32[2,512,512]{2,1,0:T(8,128)}, u32[]{:S(2)}, u32[]{:S(2)}) collective-permute-start(f32[2,512,512]{2,1,0:T(8,128)} %get-tuple-element.30), channel_id=1, source_target_pairs={{0,5},{1,4},{2,7},{3,6},{4,1},{5,0},{6,3},{7,2},{8,13},{9,12},{10,... | collective-permute-start | bytes 6291464 | tf_op jit(solution)/shard_map/ppermute | solution.py:305
  10.3 94.0 %collective-permute-start.5 = (f32[2,512,512]{2,1,0:T(8,128)}, f32[2,512,512]{2,1,0:T(8,128)}, u32[]{:S(2)}, u32[]{:S(2)}) collective-permute-start(f32[2,512,512]{2,1,0:T(8,128)} %get-tuple-element.31), channel_id=1, source_target_pairs={{0,1},{1,0},{2,3},{3,2},{4,5},{5,4},{6,7},{7,6},{8,9},{9,8},{10,11... | collective-permute-start | bytes 6291464 | tf_op jit(solution)/shard_map/ppermute | solution.py:307
  34.2 21.1 %copy-start.8 = (s32[1,3,2]{1,2,0:T(2,128)S(1)}, s32[1,3,2]{1,2,0:T(2,128)}, u32[]{:S(2)}) copy-start(s32[1,3,2]{1,2,0:T(2,128)} %param.8) | copy-start | bytes 76
  49.1 62.2 %collective-permute-start.2 = (f32[2,512,512]{2,1,0:T(8,128)}, f32[2,512,512]{2,1,0:T(8,128)}, u32[]{:S(2)}, u32[]{:S(2)}) collective-permute-start(f32[2,512,512]{2,1,0:T(8,128)} %collective-permute-done.1), channel_id=1, source_target_pairs={{2,0},{6,4},{10,8},{14,12},{18,16},{22,20},{26,24},{30,28},{34,32}... | collective-permute-start | bytes 6291464 | tf_op jit(solution)/shard_map/ppermute | solution.py:323
  75.5 4.1 %copy-start.3 = (bf16[512,512]{1,0:T(8,128)(2,1)S(1)}, bf16[512,512]{1,0:T(8,128)(2,1)}, u32[]{:S(2)}) copy-start(bf16[512,512]{1,0:T(8,128)(2,1)} %get-tuple-element.41) | copy-start | bytes 1572868
  75.6 4.1 %copy-start.4 = (bf16[512,512]{1,0:T(8,128)(2,1)S(1)}, bf16[512,512]{1,0:T(8,128)(2,1)}, u32[]{:S(2)}) copy-start(bf16[512,512]{1,0:T(8,128)(2,1)} %get-tuple-element.42) | copy-start | bytes 1572868
  75.6 4.1 copy-start.5
  75.6 4.1 copy-start.6
  89.9 17.2 %copy-start.1 = (f32[2,2,512,512]{3,2,1,0:T(8,128)S(1)}, f32[2,2,512,512]{3,2,1,0:T(8,128)}, u32[]{:S(2)}) copy-start(f32[2,2,512,512]{3,2,1,0:T(8,128)} %param.6) | copy-start | bytes 12582916
  111.2 1.6 copy-start.7
  118.2 5.0 %copy-start = (f32[3,2,514,514]{3,2,1,0:T(8,128)}, f32[3,2,514,514]{3,2,1,0:T(8,128)S(1)}, u32[]{:S(2)}) copy-start(f32[3,2,514,514]{3,2,1,0:T(8,128)S(1)} %pad_maximum_fusion) | copy-start | bytes 19022116
  197.0 55.6 %collective-permute-start.6 = (f32[1024,512]{1,0:T(8,128)}, f32[1024,512]{1,0:T(8,128)}, u32[]{:S(2)}, u32[]{:S(2)}) collective-permute-start(f32[1024,512]{1,0:T(8,128)} %constant_dynamic-slice_fusion), channel_id=1, source_target_pairs={{0,2},{2,0},{4,6},{6,4},{8,10},{10,8},{12,14},{14,12},{16,18},{18,... | collective-permute-start | bytes 6291464 | tf_op jit(solution)/shard_map/ppermute | solution.py:33
  239.9 2.7 copy-start.2
  256.4 31.7 %collective-permute-start.9 = (f32[256,512]{1,0:T(8,128)}, f32[256,512]{1,0:T(8,128)}, u32[]{:S(2)}, u32[]{:S(2)}) collective-permute-start(f32[256,512]{1,0:T(8,128)} %get-tuple-element.33), channel_id=1, source_target_pairs={{0,96},{2,98},{4,100},{6,102},{8,104},{10,106},{12,108},{14,110},{... | collective-permute-start | bytes 1572872 | tf_op jit(solution)/shard_map/ppermute | solution.py:33
  259.1 29.8 %collective-permute-start.8 = (f32[256,512]{1,0:T(8,128)}, f32[256,512]{1,0:T(8,128)}, u32[]{:S(2)}, u32[]{:S(2)}) collective-permute-start(f32[256,512]{1,0:T(8,128)} %get-tuple-element.34), channel_id=1, source_target_pairs={{0,32},{2,34},{4,36},{6,38},{8,40},{10,42},{12,44},{14,46},{16,48}... | collective-permute-start | bytes 1572872 | tf_op jit(solution)/shard_map/ppermute | solution.py:33
  259.1 29.8 %collective-permute-start.7 = (f32[256,512]{1,0:T(8,128)}, f32[256,512]{1,0:T(8,128)}, u32[]{:S(2)}, u32[]{:S(2)}) collective-permute-start(f32[256,512]{1,0:T(8,128)} %get-tuple-element.32), channel_id=1, source_target_pairs={{0,64},{2,66},{4,68},{6,70},{8,72},{10,74},{12,76},{14,78},{16,80}... | collective-permute-start | bytes 1572872 | tf_op jit(solution)/shard_map/ppermute | solution.py:33
  284.3 83.1 %collective-permute-start.14 = (f32[512,512]{1,0:T(8,128)}, f32[512,512]{1,0:T(8,128)}, u32[]{:S(2)}, u32[]{:S(2)}) collective-permute-start(f32[512,512]{1,0:T(8,128)} %get-tuple-element.27), channel_id=1, source_target_pairs={{0,2},{2,4},{4,6},{6,8},{8,10},{10,12},{12,14},{14,16},{16,18},{18... | collective-permute-start | bytes 3145736 | tf_op jit(solution)/shard_map/ppermute | solution.py:23
  286.2 81.2 %collective-permute-start.15 = (f32[512,512]{1,0:T(8,128)}, f32[512,512]{1,0:T(8,128)}, u32[]{:S(2)}, u32[]{:S(2)}) collective-permute-start(f32[512,512]{1,0:T(8,128)} %get-tuple-element.26), channel_id=1, source_target_pairs={{0,16},{2,18},{4,20},{6,22},{8,24},{10,26},{12,28},{14,30},{16,32}... | collective-permute-start | bytes 3145736 | tf_op jit(solution)/shard_map/ppermute | solution.py:23
  288.2 79.2 %collective-permute-start.16 = (f32[512,512]{1,0:T(8,128)}, f32[512,512]{1,0:T(8,128)}, u32[]{:S(2)}, u32[]{:S(2)}) collective-permute-start(f32[512,512]{1,0:T(8,128)} %get-tuple-element.25), channel_id=1, source_target_pairs={{0,18},{2,20},{4,22},{6,24},{8,26},{10,28},{12,30},{14,32},{16,34}... | collective-permute-start | bytes 3145736 | tf_op jit(solution)/shard_map/ppermute | solution.py:23
  290.6 48.0 %collective-permute-start.12 = (f32[64,512]{1,0:T(8,128)S(1)}, f32[64,512]{1,0:T(8,128)S(1)}, u32[]{:S(2)}, u32[]{:S(2)}) collective-permute-start(f32[64,512]{1,0:T(8,128)S(1)} %get-tuple-element.48), channel_id=1, source_target_pairs={{0,24},{2,26},{4,28},{6,30},{8,0},{10,2},{12,4},{14,6},{16,8},{18,... | collective-permute-start | bytes 393224 | tf_op jit(solution)/shard_map/ppermute | solution.py:33
  293.1 46.4 %collective-permute-start.11 = (f32[64,512]{1,0:T(8,128)S(1)}, f32[64,512]{1,0:T(8,128)S(1)}, u32[]{:S(2)}, u32[]{:S(2)}) collective-permute-start(f32[64,512]{1,0:T(8,128)S(1)} %get-tuple-element.49), channel_id=1, source_target_pairs={{0,8},{2,10},{4,12},{6,14},{8,16},{10,18},{12,20},{14,22},{16,24},... | collective-permute-start | bytes 393224 | tf_op jit(solution)/shard_map/ppermute | solution.py:33
  338.6 6.3 %collective-permute-start.10 = (f32[64,512]{1,0:T(8,128)S(1)}, f32[64,512]{1,0:T(8,128)S(1)}, u32[]{:S(2)}, u32[]{:S(2)}) collective-permute-start(f32[64,512]{1,0:T(8,128)S(1)} %get-tuple-element.47), channel_id=1, source_target_pairs={{0,16},{2,18},{4,20},{6,22},{8,24},{10,26},{12,28},{14,30},{16,0},... | collective-permute-start | bytes 393224 | tf_op jit(solution)/shard_map/ppermute | solution.py:33
  344.9 22.4 %collective-permute-start.13 = (f32[64,512]{1,0:T(8,128)S(1)}, f32[64,512]{1,0:T(8,128)S(1)}, u32[]{:S(2)}, u32[]{:S(2)}) collective-permute-start(f32[64,512]{1,0:T(8,128)S(1)} %fusion.29), channel_id=1, source_target_pairs={{0,4},{2,6},{4,0},{6,2},{8,12},{10,14},{12,8},{14,10},{16,20},{18,... | collective-permute-start | bytes 393224 | tf_op jit(solution)/shard_map/ppermute | solution.py:33
  367.4 5.5 %collective-permute-start.17 = (f32[64,512]{1,0:T(8,128)S(1)}, f32[64,512]{1,0:T(8,128)S(1)}, u32[]{:S(2)}, u32[]{:S(2)}) collective-permute-start(f32[64,512]{1,0:T(8,128)S(1)} %add.337), channel_id=1, source_target_pairs={{0,16},{2,18},{4,20},{6,22},{8,24},{10,26},{12,28},{14,30},{16,0},... | collective-permute-start | bytes 393224 | tf_op jit(solution)/shard_map/ppermute | solution.py:33
  367.5 5.4 %collective-permute-start.18 = (f32[64,512]{1,0:T(8,128)S(1)}, f32[64,512]{1,0:T(8,128)S(1)}, u32[]{:S(2)}, u32[]{:S(2)}) collective-permute-start(f32[64,512]{1,0:T(8,128)S(1)} %add.337), channel_id=1, source_target_pairs={{0,8},{2,10},{4,12},{6,14},{8,16},{10,18},{12,20},{14,22},{16,24},... | collective-permute-start | bytes 393224 | tf_op jit(solution)/shard_map/ppermute | solution.py:33
  367.6 9.5 %collective-permute-start.19 = (f32[64,512]{1,0:T(8,128)S(1)}, f32[64,512]{1,0:T(8,128)S(1)}, u32[]{:S(2)}, u32[]{:S(2)}) collective-permute-start(f32[64,512]{1,0:T(8,128)S(1)} %add.337), channel_id=1, source_target_pairs={{0,24},{2,26},{4,28},{6,30},{8,0},{10,2},{12,4},{14,6},{16,8},{18,... | collective-permute-start | bytes 393224 | tf_op jit(solution)/shard_map/ppermute | solution.py:33
  377.1 14.5 %collective-permute-start.20 = (f32[256,512]{1,0:T(8,128)S(1)}, f32[256,512]{1,0:T(8,128)S(1)}, u32[]{:S(2)}, u32[]{:S(2)}) collective-permute-start(f32[256,512]{1,0:T(8,128)S(1)} %bitcast.119), channel_id=1, source_target_pairs={{0,64},{2,66},{4,68},{6,70},{8,72},{10,74},{12,76},{14,78},{16,80}... | collective-permute-start | bytes 1572872 | tf_op jit(solution)/shard_map/ppermute | solution.py:33
  377.2 24.3 %collective-permute-start.21 = (f32[256,512]{1,0:T(8,128)S(1)}, f32[256,512]{1,0:T(8,128)S(1)}, u32[]{:S(2)}, u32[]{:S(2)}) collective-permute-start(f32[256,512]{1,0:T(8,128)S(1)} %bitcast.120), channel_id=1, source_target_pairs={{0,32},{2,34},{4,36},{6,38},{8,40},{10,42},{12,44},{14,46},{16,48}... | collective-permute-start | bytes 1572872 | tf_op jit(solution)/shard_map/ppermute | solution.py:33
  377.3 26.4 %collective-permute-start.22 = (f32[256,512]{1,0:T(8,128)S(1)}, f32[256,512]{1,0:T(8,128)S(1)}, u32[]{:S(2)}, u32[]{:S(2)}) collective-permute-start(f32[256,512]{1,0:T(8,128)S(1)} %bitcast.121), channel_id=1, source_target_pairs={{0,96},{2,98},{4,100},{6,102},{8,104},{10,106},{12,108},{14,110},{... | collective-permute-start | bytes 1572872 | tf_op jit(solution)/shard_map/ppermute | solution.py:33
  403.8 4.4 %collective-permute-start.23 = (f32[1024,512]{1,0:T(8,128)S(1)}, f32[1024,512]{1,0:T(8,128)S(1)}, u32[]{:S(2)}, u32[]{:S(2)}) collective-permute-start(f32[1024,512]{1,0:T(8,128)S(1)} %bitcast.115), channel_id=1, source_target_pairs={{0,2},{2,0},{4,6},{6,4},{8,10},{10,8},{12,14},{14,12},{16,18},{18,... | collective-permute-start | bytes 6291464 | tf_op jit(solution)/shard_map/ppermute | solution.py:33
